TPU v7x, 32 devices: a whole 2x2x4 slice. The times are simulated.
32 devices in a mesh: seq: 4 (over z), exp: 8 (over y, x, core).
Axes of the slice: x: 2, y: 2, z: 4, core: 2. Of those that a mesh axis runs over, the one named last changes fastest.
Arguments:
- queries: bfloat16 [8, 512, 2048], P('exp', 'seq'), may hold values from -100 to 100
- keys: bfloat16 [8, 512, 2048], P('exp', 'seq'), may hold values from -4 to 4
- values: bfloat16 [8, 512, 2048], P('exp', 'seq'), may hold values from -6 to 6
- resid: bfloat16 [8, 512, 2048], P('exp', 'seq'), may hold values from -6 to 6
- norm_gain: float32 [2048], replicated, may hold values from 0.1 to 1.9
- w_gate: bfloat16 [8, 2048, 704], P('exp', 'seq'), may hold values from -0.125 to 0.125
- w_up: bfloat16 [8, 2048, 704], P('exp', 'seq'), may hold values from -0.125 to 0.125
- w_down: bfloat16 [8, 704, 2048], P('exp', None, 'seq'), may hold values from -0.21875 to 0.21875
- expert_ids: int32 [8, 512, 2], P('exp', 'seq'), may hold values from 0 to 7, all different within a row; in each aligned block of 128 rows (0 to 127, 128 to 255, ..., all dimensions but the last counted through in order) at most 40 rows name the same one
- route_weights: float32 [8, 512, 2], P('exp', 'seq'), may hold values from 0.25 to 1
- cotangent: bfloat16 [8, 512, 2048], P('exp', 'seq'), may hold values from -6 to 6
Outputs:
- output: bfloat16 [8, 512, 2048], P('exp', 'seq')
- stream_grad: bfloat16 [8, 512, 2048], P('exp', 'seq')
Inputs may be any that keep to these rules, and one draw needn't show every extreme that they name: `expert_ids`: within the positions of one device (aligned blocks of 128 positions, taken in order over sequences and positions) no expert is chosen more than 40 times, a bound that some block reaches; the two choices of a position differ.
All inputs are finite; a program needn't handle non-finite values.
Results may differ from a plain program's by a relative error of at most 0.009.
Values may be sent and summed in bfloat16 or wider, within the bound.
No kernel may reach another device: no remote copies, remote signals or barrier semaphores. Data moves between devices by JAX's collectives and lax.ppermute only.
A program may use at most 64 MiB of HBM per device.

v0:
```python
import jax
import jax.numpy as jnp
from jax import lax
from jax.sharding import PartitionSpec as P

HD = 128


def causal_attention(query_rows, key_rows, value_rows):
    length = query_rows.shape[0]
    block_rows = min(512, length)
    score_scale = HD ** (-0.5)
    row_ids = lax.broadcasted_iota(jnp.int32, (block_rows, block_rows), 0)
    col_ids = lax.broadcasted_iota(jnp.int32, (block_rows, block_rows), 1)
    diag_keep = (col_ids <= row_ids)[None]
    pieces = []
    for block in range(length // block_rows):
        start = block * block_rows
        finish = start + block_rows
        query_part = query_rows[start:finish]
        diag_scores = (
            jnp.einsum(
                "qhd,khd->hqk",
                query_part,
                key_rows[start:finish],
                preferred_element_type=jnp.float32,
            )
            * score_scale
        )
        diag_scores = jnp.where(diag_keep, diag_scores, -jnp.inf)
        row_max = jnp.max(diag_scores, axis=-1, keepdims=True)
        if start > 0:
            early_scores = (
                jnp.einsum(
                    "qhd,khd->hqk", query_part, key_rows[:start], preferred_element_type=jnp.float32
                )
                * score_scale
            )
            row_max = jnp.maximum(row_max, jnp.max(early_scores, axis=-1, keepdims=True))
        diag_exp = jnp.exp(diag_scores - row_max)
        totals = jnp.sum(diag_exp, axis=-1, keepdims=True)
        if start > 0:
            early_exp = jnp.exp(early_scores - row_max)
            totals = totals + jnp.sum(early_exp, axis=-1, keepdims=True)
        diag_probs = (diag_exp / totals).astype(jnp.bfloat16)
        context = jnp.einsum(
            "hqk,khd->qhd", diag_probs, value_rows[start:finish], preferred_element_type=jnp.float32
        )
        if start > 0:
            early_probs = (early_exp / totals).astype(jnp.bfloat16)
            context = context + jnp.einsum(
                "hqk,khd->qhd", early_probs, value_rows[:start], preferred_element_type=jnp.float32
            )
        pieces.append(context.astype(jnp.bfloat16))
    return jnp.concatenate(pieces, axis=0)


def to_experts(buffer):
    return lax.all_to_all(buffer, "exp", split_axis=0, concat_axis=0, tiled=True)


def to_owners(buffer):
    return lax.all_to_all(buffer, "exp", split_axis=0, concat_axis=0, tiled=True)


def per_device(
    queries,
    keys,
    values,
    resid,
    norm_gain,
    w_gate,
    w_up,
    w_down,
    expert_ids,
    route_weights,
    cotangent,
):
    groups = lax.axis_size("seq")
    owners = lax.axis_size("exp")
    tokens_here = queries.shape[1]
    model_width = queries.shape[2]
    heads_here = model_width // (groups * HD)
    split_shape = (tokens_here, groups, heads_here, HD)
    query_part = lax.all_to_all(
        queries.reshape(split_shape), "seq", split_axis=1, concat_axis=0, tiled=True
    )
    key_part = lax.all_to_all(
        keys.reshape(split_shape), "seq", split_axis=1, concat_axis=0, tiled=True
    )
    value_part = lax.all_to_all(
        values.reshape(split_shape), "seq", split_axis=1, concat_axis=0, tiled=True
    )
    context = causal_attention(query_part[:, 0], key_part[:, 0], value_part[:, 0])
    regrouped = lax.all_to_all(context[:, None], "seq", split_axis=0, concat_axis=1, tiled=True)
    context = regrouped.reshape(tokens_here, model_width)
    gate_full, up_full, down_full = (
        lax.all_gather(w_gate, "seq", axis=1, tiled=True),
        lax.all_gather(w_up, "seq", axis=1, tiled=True),
        lax.all_gather(w_down, "seq", axis=2, tiled=True),
    )
    gate_w = gate_full[0]
    up_w = up_full[0]
    down_w = down_full[0]
    stream = (resid[0].astype(jnp.float32) + context.astype(jnp.float32)).astype(jnp.bfloat16)
    stream_f = stream.astype(jnp.float32)
    inv_rms = lax.rsqrt(jnp.mean(stream_f * stream_f, axis=-1, keepdims=True) + 1e-05)
    unit_rows = stream_f * inv_rms
    normed = (unit_rows * norm_gain).astype(jnp.bfloat16)
    capacity = max(2, tokens_here * 10 // (4 * owners))
    pair_count = 2 * tokens_here
    choices_flat = expert_ids[0].reshape(pair_count)
    member = (choices_flat[:, None] == jnp.arange(owners, dtype=jnp.int32)[None]).astype(jnp.int32)
    before = jnp.cumsum(member, axis=0) - member
    slot_of = jnp.sum(before * member, axis=1)
    target = choices_flat * capacity + slot_of
    token_pairs = jnp.repeat(normed, 2, axis=0)
    send_rows = (
        jnp.zeros((owners * capacity, model_width), jnp.bfloat16).at[target].set(token_pairs)
    )
    send_rows = send_rows.reshape(owners, capacity, model_width)
    weights_here = route_weights[0]
    cot_f = cotangent[0].astype(jnp.float32)
    scaled_cot = (
        (weights_here[..., None] * cot_f[:, None, :])
        .astype(jnp.bfloat16)
        .reshape(pair_count, model_width)
    )
    send_cot = jnp.zeros((owners * capacity, model_width), jnp.bfloat16).at[target].set(scaled_cot)
    send_cot = send_cot.reshape(owners, capacity, model_width)
    token_rows = to_experts(send_rows)
    gate_pre = jnp.einsum("scd,df->scf", token_rows, gate_w, preferred_element_type=jnp.float32)
    up_pre = jnp.einsum("scd,df->scf", token_rows, up_w, preferred_element_type=jnp.float32)
    hidden = (jax.nn.silu(gate_pre) * up_pre).astype(jnp.bfloat16)
    out_rows = jnp.einsum("scf,fd->scd", hidden, down_w, preferred_element_type=jnp.float32)
    out_rows, gate_pre, up_pre = (out_rows.astype(jnp.bfloat16), gate_pre, up_pre)
    back_out = to_owners(out_rows)
    d_hidden = jnp.einsum(
        "scd,fd->scf", to_experts(send_cot), down_w, preferred_element_type=jnp.float32
    )
    sigma = jax.nn.sigmoid(gate_pre)
    d_gate = (d_hidden * up_pre * sigma * (1.0 + gate_pre * (1.0 - sigma))).astype(jnp.bfloat16)
    d_up = (d_hidden * gate_pre * sigma).astype(jnp.bfloat16)
    d_rows = jnp.einsum("scf,df->scd", d_gate, gate_w, preferred_element_type=jnp.float32)
    d_rows = d_rows + jnp.einsum("scf,df->scd", d_up, up_w, preferred_element_type=jnp.float32)
    d_rows = d_rows.astype(jnp.bfloat16)
    back_grad = to_owners(d_rows)
    pair_out = back_out.reshape(owners * capacity, model_width)[target]
    pair_out = pair_out.reshape(tokens_here, 2, model_width).astype(jnp.float32)
    pair_grad = back_grad.reshape(owners * capacity, model_width)[target]
    pair_grad = pair_grad.reshape(tokens_here, 2, model_width).astype(jnp.float32)
    output = (stream_f + jnp.sum(weights_here[..., None] * pair_out, axis=1)).astype(jnp.bfloat16)
    d_normed = jnp.sum(pair_grad, axis=1)
    gained = d_normed * norm_gain
    d_stream = inv_rms * (gained - unit_rows * jnp.mean(gained * unit_rows, axis=-1, keepdims=True))
    stream_grad = (cot_f + d_stream).astype(jnp.bfloat16)
    return (output[None], stream_grad[None])


def solution(mesh):
    placed = (
        P("exp", "seq", None),
        P("exp", "seq", None),
        P("exp", "seq", None),
        P("exp", "seq", None),
        P(),
        P("exp", "seq", None),
        P("exp", "seq", None),
        P("exp", None, "seq"),
        P("exp", "seq", None),
        P("exp", "seq", None),
        P("exp", "seq", None),
    )
    return jax.shard_map(
        per_device,
        mesh=mesh,
        in_specs=placed,
        out_specs=(P("exp", "seq", None), P("exp", "seq", None)),
        check_vma=False,
    )
```

profile of v0, /device:TPU:0, one launch (start us, length us, event | category | flops | bytes accessed | tf_op | source)
XLA Modules:
  0.0 304.1 jit_solution(9772625788284379928)
XLA Ops:
  7.2 0.7 all-gather.4.cloned.1.call-update
  8.0 0.7 all-gather.6.cloned.1.call-update
  8.7 1.3 copy.43
  10.0 1.0 copy.44
  11.0 6.4 %all-to-all-start = ((bf16[128,4,4,128]{3,0,2,1:T(8,128)(2,1)}), bf16[128,4,4,128]{3,0,2,1:T(8,128)(2,1)S(1)}, u32[]{:S(2)}, u32[]{:S(2)}) async-start(bf16[128,4,4,128]{3,0,2,1:T(8,128)(2,1)} %copy.44), calls=%async_computation | async-start | bytes 1048576 | tf_op jit(solution)/shard_map/all_to_all | solution.py:85
  17.7 1.0 copy.47
  18.7 26.2 %all-to-all-done = bf16[128,4,4,128]{3,0,2,1:T(8,128)(2,1)S(1)} async-done(((bf16[128,4,4,128]{3,0,2,1:T(8,128)(2,1)}), bf16[128,4,4,128]{3,0,2,1:T(8,128)(2,1)S(1)}, u32[]{:S(2)}, u32[]{:S(2)}) %all-to-all-start) | async-done | bytes 524320 | tf_op jit(solution)/shard_map/all_to_all | solution.py:85
  44.9 3.5 %all-to-all-start.1 = ((bf16[128,4,4,128]{3,0,2,1:T(8,128)(2,1)}), bf16[128,4,4,128]{3,0,2,1:T(8,128)(2,1)S(1)}, u32[]{:S(2)}, u32[]{:S(2)}) async-start(bf16[128,4,4,128]{3,0,2,1:T(8,128)(2,1)} %copy.47), calls=%async_computation.1 | async-start | bytes 1048576 | tf_op jit(solution)/shard_map/all_to_all | solution.py:88
  48.7 1.0 copy.50
  49.7 26.2 %all-to-all-done.1 = bf16[128,4,4,128]{3,0,2,1:T(8,128)(2,1)S(1)} async-done(((bf16[128,4,4,128]{3,0,2,1:T(8,128)(2,1)}), bf16[128,4,4,128]{3,0,2,1:T(8,128)(2,1)S(1)}, u32[]{:S(2)}, u32[]{:S(2)}) %all-to-all-start.1) | async-done | bytes 524320 | tf_op jit(solution)/shard_map/all_to_all | solution.py:88
  75.9 3.5 %all-to-all-start.2 = ((bf16[128,4,4,128]{3,0,2,1:T(8,128)(2,1)}), bf16[128,4,4,128]{3,0,2,1:T(8,128)(2,1)S(1)}, u32[]{:S(2)}, u32[]{:S(2)}) async-start(bf16[128,4,4,128]{3,0,2,1:T(8,128)(2,1)} %copy.50), calls=%async_computation.2 | async-start | bytes 1048576 | tf_op jit(solution)/shard_map/all_to_all | solution.py:91
  79.4 0.7 all-gather.8.cloned.1.call-update
  80.3 19.2 %all-to-all-done.2 = bf16[128,4,4,128]{3,0,2,1:T(8,128)(2,1)S(1)} async-done(((bf16[128,4,4,128]{3,0,2,1:T(8,128)(2,1)}), bf16[128,4,4,128]{3,0,2,1:T(8,128)(2,1)S(1)}, u32[]{:S(2)}, u32[]{:S(2)}) %all-to-all-start.2) | async-done | bytes 524320 | tf_op jit(solution)/shard_map/all_to_all | solution.py:91
  99.6 3.6 %fusion.61 = (f32[4,512]{1,0:T(4,128)S(1)}, f32[4,512,512]{1,2,0:T(8,128)}) fusion(pred[512,512]{0,1:T(8,128)(4,1)S(1)} %iota_compare_fusion, bf16[512,4,128]{2,0,1:T(8,128)(2,1)S(1)} %bitcast.100, bf16[512,4,128]{2,0,1:T(8,128)(2,1)S(1)} %bitcast.101), kind=kOutput, calls=%fused_computation.86 | convolution fusion | flops 272630272 | bytes 5513216 | tf_op jit(solution)/shard_map/sub | solution.py:40
  103.1 3.1 %fusion.30 = bf16[512,1,4,128]{3,0,2,1:T(8,128)(2,1)S(1)} fusion(bf16[512,4,128]{2,0,1:T(8,128)(2,1)S(1)} %bitcast.102, f32[4,512,512]{1,2,0:T(8,128)} %get-tuple-element.7, f32[4,512]{1,0:T(4,128)S(1)} %get-tuple-element.6), kind=kOutput, calls=%fused_computation.41 | convolution fusion | flops 270794752 | bytes 5251072 | tf_op jit(solution)/shard_map/hqk,khd->qhd/dot_general | solution.py:46
  106.2 1.2 copy.53
  107.4 3.5 %all-to-all-start.3 = ((bf16[512,1,4,128]{3,2,1,0:T(4,128)(2,1)}), bf16[512,1,4,128]{3,2,1,0:T(4,128)(2,1)S(1)}, u32[]{:S(2)}, u32[]{:S(2)}) async-start(bf16[512,1,4,128]{3,2,1,0:T(4,128)(2,1)} %copy.53), calls=%async_computation.3 | async-start | bytes 1048576 | tf_op jit(solution)/shard_map/all_to_all | solution.py:95
  112.6 22.5 %all-to-all-done.3 = bf16[512,1,4,128]{3,2,1,0:T(4,128)(2,1)S(1)} async-done(((bf16[512,1,4,128]{3,2,1,0:T(4,128)(2,1)}), bf16[512,1,4,128]{3,2,1,0:T(4,128)(2,1)S(1)}, u32[]{:S(2)}, u32[]{:S(2)}) %all-to-all-start.3) | async-done | bytes 524320 | tf_op jit(solution)/shard_map/all_to_all | solution.py:95
  136.4 0.8 copy-done.1
  137.4 0.6 broadcast_in_dim.19
  138.5 3.3 %scatter_custom_fusion = bf16[320,2048]{1,0:T(8,128)(2,1)} fusion(s32[256]{0:T(256)S(1)} %bitcast.104, bf16[256,2048]{1,0:T(8,128)(2,1)S(1)} %reshape.225, bf16[]{:T(256)} %constant.13.clone.1), kind=kCustom, calls=%fused_computation.63 | custom fusion | bytes 1310722 | tf_op jit(solution)/shard_map/scatter | solution.py:119
  141.8 3.8 %all-to-all-start.4 = ((bf16[8,40,2048]{2,1,0:T(8,128)(2,1)}), bf16[8,40,2048]{2,1,0:T(8,128)(2,1)S(1)}, u32[]{:S(2)}, u32[]{:S(2)}) async-start(bf16[8,40,2048]{2,1,0:T(8,128)(2,1)} %bitcast.23), calls=%async_computation.4 | async-start | bytes 2621440 | tf_op jit(solution)/shard_map/all_to_all | solution.py:59
  146.0 2.5 mul.157
  148.5 2.7 mul.158
  151.2 3.4 %scatter_custom_fusion.1 = bf16[320,2048]{1,0:T(8,128)(2,1)} fusion(s32[256]{0:T(256)S(1)} %bitcast.105, f32[256,2048]{1,0:T(8,128)S(1)} %mul.158, f32[256]{0:T(256)S(1)} %mul.155, bf16[]{:T(256)} %constant.13.clone.1), kind=kCustom, calls=%fused_computation.53 | custom fusion | flops 1048576 | bytes 3408898 | tf_op jit(solution)/shard_map/scatter | solution.py:129
  154.6 9.2 %all-to-all-done.4 = bf16[8,40,2048]{2,1,0:T(8,128)(2,1)S(1)} async-done(((bf16[8,40,2048]{2,1,0:T(8,128)(2,1)}), bf16[8,40,2048]{2,1,0:T(8,128)(2,1)S(1)}, u32[]{:S(2)}, u32[]{:S(2)}) %all-to-all-start.4) | async-done | bytes 1310752 | tf_op jit(solution)/shard_map/all_to_all | solution.py:59
  163.8 3.6 %all-to-all-start.6 = ((bf16[8,40,2048]{2,1,0:T(8,128)(2,1)}), bf16[8,40,2048]{2,1,0:T(8,128)(2,1)S(1)}, u32[]{:S(2)}, u32[]{:S(2)}) async-start(bf16[8,40,2048]{2,1,0:T(8,128)(2,1)} %bitcast.33), calls=%async_computation.6 | async-start | bytes 2621440 | tf_op jit(solution)/shard_map/all_to_all | solution.py:59
  167.4 4.0 %fusion.12 = f32[8,40,704]{2,1,0:T(8,128)} fusion(bf16[8,40,2048]{2,1,0:T(8,128)(2,1)S(1)} %all-to-all-done.4, bf16[1,2048,704]{1,2,0:T(8,128)(2,1)} %all-gather.4.cloned.1.call-done), kind=kOutput, calls=%fused_computation.19 | convolution fusion | flops 922746880 | bytes 5095424 | tf_op jit(solution)/shard_map/scd,df->scf/dot_general | solution.py:132
  171.4 4.0 %fusion.8 = f32[8,40,704]{2,1,0:T(8,128)} fusion(bf16[8,40,2048]{2,1,0:T(8,128)(2,1)S(1)} %all-to-all-done.4, bf16[1,2048,704]{1,2,0:T(8,128)(2,1)} %all-gather.6.cloned.1.call-done), kind=kOutput, calls=%fused_computation.15 | convolution fusion | flops 922746880 | bytes 5095424 | tf_op jit(solution)/shard_map/scd,df->scf/dot_general | solution.py:133
  175.5 10.1 %all-to-all-done.6 = bf16[8,40,2048]{2,1,0:T(8,128)(2,1)S(1)} async-done(((bf16[8,40,2048]{2,1,0:T(8,128)(2,1)}), bf16[8,40,2048]{2,1,0:T(8,128)(2,1)S(1)}, u32[]{:S(2)}, u32[]{:S(2)}) %all-to-all-start.6) | async-done | bytes 1310752 | tf_op jit(solution)/shard_map/all_to_all | solution.py:59
  185.5 43.0 %all-gather.8.cloned.1.call-done = bf16[1,704,2048]{2,1,0:T(8,128)(2,1)} async-done(((bf16[1,704,512]{2,1,0:T(8,128)(2,1)}), bf16[1,704,2048]{2,1,0:T(8,128)(2,1)}) %all-gather.8.cloned.1.call-update) | async-done | bytes 2883600 | tf_op jit(solution)/shard_map/all_gather | solution.py:100
  228.5 3.2 %fusion.2 = f32[8,40,704]{2,1,0:T(8,128)S(1)} fusion(bf16[8,40,2048]{2,1,0:T(8,128)(2,1)S(1)} %all-to-all-done.6, bf16[1,704,2048]{2,1,0:T(8,128)(2,1)} %all-gather.8.cloned.1.call-done), kind=kOutput, calls=%fused_computation.9 | convolution fusion | flops 922746880 | bytes 5095424 | tf_op jit(solution)/shard_map/scd,fd->scf/dot_general | solution.py:138
  231.8 1.3 fusion.6
  233.9 2.6 fusion.17
  236.4 3.6 %all-to-all-start.7 = ((bf16[8,40,2048]{2,1,0:T(8,128)(2,1)}), bf16[8,40,2048]{2,1,0:T(8,128)(2,1)S(1)}, u32[]{:S(2)}, u32[]{:S(2)}) async-start(bf16[8,40,2048]{2,1,0:T(8,128)(2,1)} %fusion.17), calls=%async_computation.7 | async-start | bytes 2621440 | tf_op jit(solution)/shard_map/all_to_all | solution.py:63
  240.1 4.2 %fusion.20 = bf16[8,40,2048]{2,1,0:T(8,128)(2,1)} fusion(bf16[1,704,2048]{2,1,0:T(8,128)(2,1)} %all-gather.8.cloned.1.call-done, f32[8,40,704]{2,1,0:T(8,128)S(1)} %copy-done.16, f32[8,40,704]{2,1,0:T(8,128)S(1)} %copy-done.15), kind=kOutput, calls=%fused_computation.23 | convolution fusion | flops 924753920 | bytes 5996544 | tf_op jit(solution)/shard_map/scf,fd->scd/dot_general | solution.py:135
  244.2 14.0 %all-to-all-done.7 = bf16[8,40,2048]{2,1,0:T(8,128)(2,1)S(1)} async-done(((bf16[8,40,2048]{2,1,0:T(8,128)(2,1)}), bf16[8,40,2048]{2,1,0:T(8,128)(2,1)S(1)}, u32[]{:S(2)}, u32[]{:S(2)}) %all-to-all-start.7) | async-done | bytes 1310752 | tf_op jit(solution)/shard_map/all_to_all | solution.py:63
  258.3 3.8 %all-to-all-start.5 = ((bf16[8,40,2048]{2,1,0:T(8,128)(2,1)}), bf16[8,40,2048]{2,1,0:T(8,128)(2,1)S(1)}, u32[]{:S(2)}, u32[]{:S(2)}) async-start(bf16[8,40,2048]{2,1,0:T(8,128)(2,1)} %fusion.20), calls=%async_computation.5 | async-start | bytes 2621440 | tf_op jit(solution)/shard_map/all_to_all | solution.py:63
  262.2 2.6 reshape.197
  264.8 2.4 gather_fusion.1
  267.2 12.8 %all-to-all-done.5 = bf16[8,40,2048]{2,1,0:T(8,128)(2,1)S(1)} async-done(((bf16[8,40,2048]{2,1,0:T(8,128)(2,1)}), bf16[8,40,2048]{2,1,0:T(8,128)(2,1)S(1)}, u32[]{:S(2)}, u32[]{:S(2)}) %all-to-all-start.5) | async-done | bytes 1310752 | tf_op jit(solution)/shard_map/all_to_all | solution.py:63
  280.0 2.3 gather_fusion
  282.3 2.5 reshape.200
  284.8 2.3 reshape.202
  287.2 4.1 %reduce_sum.66 = f32[128,2048]{1,0:T(8,128)S(1)} reduce(f32[128,2,2048]{2,1,0:T(2,128)} %reshape.202, f32[]{:T(128)} %constant.6.clone.1), dimensions={1}, to_apply=%region_9.10 | reduce | flops 262144 | bytes 3145732 | tf_op jit(solution)/shard_map/reduce_sum | solution.py:153
  291.3 1.5 fusion.32
  292.8 3.2 %multiply_reduce_fusion = f32[128,2048]{1,0:T(8,128)S(1)} fusion(f32[128,2,2048]{2,1,0:T(2,128)S(1)} %reshape.200, f32[128,2]{1,0:T(8,128)S(1)} %copy.55), kind=kLoop, calls=%fused_computation.25 | loop fusion | flops 786432 | bytes 3146752 | tf_op jit(solution)/shard_map/reduce_sum | solution.py:152
  296.0 1.5 fusion.41
  (70 shorter events, 5.7 us)
Async XLA Ops:
  7.2 160.3 %all-gather.4.cloned.1.call-start = ((), (), s32[]{:S(2)}) async-start(), calls=%async_computation.8 | async-start | bytes 3604480 | tf_op jit(solution)/shard_map/all_gather | solution.py:98
  7.9 9.5 %copy-start.8 = (bf16[1,128,2048]{2,1,0:T(8,128)(2,1)S(1)}, bf16[1,128,2048]{2,1,0:T(8,128)(2,1)}, u32[]{:S(2)}) copy-start(bf16[1,128,2048]{2,1,0:T(8,128)(2,1)} %param.12) | copy-start | bytes 1572868
  7.9 163.5 %all-gather.6.cloned.1.call-start = ((), (), s32[]{:S(2)}) async-start(), calls=%async_computation.9 | async-start | bytes 3604480 | tf_op jit(solution)/shard_map/all_gather | solution.py:99
  11.0 37.4 %copy-start.9 = (bf16[1,128,2048]{2,1,0:T(8,128)(2,1)S(1)}, bf16[1,128,2048]{2,1,0:T(8,128)(2,1)}, u32[]{:S(2)}) copy-start(bf16[1,128,2048]{2,1,0:T(8,128)(2,1)} %param.13) | copy-start | bytes 1572868
  11.0 33.9 %all-to-all-start = ((bf16[128,4,4,128]{3,0,2,1:T(8,128)(2,1)}), bf16[128,4,4,128]{3,0,2,1:T(8,128)(2,1)S(1)}, u32[]{:S(2)}, u32[]{:S(2)}) async-start(bf16[128,4,4,128]{3,0,2,1:T(8,128)(2,1)} %copy.44), calls=%async_computation | async-start | bytes 1048576 | tf_op jit(solution)/shard_map/all_to_all | solution.py:85
  44.9 31.0 %all-to-all-start.1 = ((bf16[128,4,4,128]{3,0,2,1:T(8,128)(2,1)}), bf16[128,4,4,128]{3,0,2,1:T(8,128)(2,1)S(1)}, u32[]{:S(2)}, u32[]{:S(2)}) async-start(bf16[128,4,4,128]{3,0,2,1:T(8,128)(2,1)} %copy.47), calls=%async_computation.1 | async-start | bytes 1048576 | tf_op jit(solution)/shard_map/all_to_all | solution.py:88
  75.9 23.6 %all-to-all-start.2 = ((bf16[128,4,4,128]{3,0,2,1:T(8,128)(2,1)}), bf16[128,4,4,128]{3,0,2,1:T(8,128)(2,1)S(1)}, u32[]{:S(2)}, u32[]{:S(2)}) async-start(bf16[128,4,4,128]{3,0,2,1:T(8,128)(2,1)} %copy.50), calls=%async_computation.2 | async-start | bytes 1048576 | tf_op jit(solution)/shard_map/all_to_all | solution.py:91
  79.3 149.2 %all-gather.8.cloned.1.call-start = ((), (), s32[]{:S(2)}) async-start(), calls=%async_computation.10 | async-start | bytes 3604480 | tf_op jit(solution)/shard_map/all_gather | solution.py:100
  106.2 4.7 %copy-start.12 = (s32[1,128,2]{1,2,0:T(2,128)S(1)}, s32[1,128,2]{1,2,0:T(2,128)}, u32[]{:S(2)}) copy-start(s32[1,128,2]{1,2,0:T(2,128)} %param.19) | copy-start | bytes 3076
  107.4 27.6 %all-to-all-start.3 = ((bf16[512,1,4,128]{3,2,1,0:T(4,128)(2,1)}), bf16[512,1,4,128]{3,2,1,0:T(4,128)(2,1)S(1)}, u32[]{:S(2)}, u32[]{:S(2)}) async-start(bf16[512,1,4,128]{3,2,1,0:T(4,128)(2,1)} %copy.53), calls=%async_computation.3 | async-start | bytes 1048576 | tf_op jit(solution)/shard_map/all_to_all | solution.py:95
  135.1 1.0 copy-start.6
  135.3 1.1 copy-start
  135.4 1.9 copy-start.10
  136.4 0.8 copy-start.1
  138.5 7.1 %copy-start.11 = (f32[1,128,2]{1,2,0:T(2,128)S(1)}, f32[1,128,2]{1,2,0:T(2,128)}, u32[]{:S(2)}) copy-start(f32[1,128,2]{1,2,0:T(2,128)} %param.20) | copy-start | bytes 3076
  138.5 7.4 %copy-start.4 = (bf16[1,128,2048]{2,1,0:T(8,128)(2,1)S(1)}, bf16[1,128,2048]{2,1,0:T(8,128)(2,1)}, u32[]{:S(2)}) copy-start(bf16[1,128,2048]{2,1,0:T(8,128)(2,1)} %param.21) | copy-start | bytes 1572868
  141.8 22.0 %all-to-all-start.4 = ((bf16[8,40,2048]{2,1,0:T(8,128)(2,1)}), bf16[8,40,2048]{2,1,0:T(8,128)(2,1)S(1)}, u32[]{:S(2)}, u32[]{:S(2)}) async-start(bf16[8,40,2048]{2,1,0:T(8,128)(2,1)} %bitcast.23), calls=%async_computation.4 | async-start | bytes 2621440 | tf_op jit(solution)/shard_map/all_to_all | solution.py:59
  163.8 21.7 %all-to-all-start.6 = ((bf16[8,40,2048]{2,1,0:T(8,128)(2,1)}), bf16[8,40,2048]{2,1,0:T(8,128)(2,1)S(1)}, u32[]{:S(2)}, u32[]{:S(2)}) async-start(bf16[8,40,2048]{2,1,0:T(8,128)(2,1)} %bitcast.33), calls=%async_computation.6 | async-start | bytes 2621440 | tf_op jit(solution)/shard_map/all_to_all | solution.py:59
  175.5 56.3 %copy-start.15 = (f32[8,40,704]{2,1,0:T(8,128)S(1)}, f32[8,40,704]{2,1,0:T(8,128)}, u32[]{:S(2)}) copy-start(f32[8,40,704]{2,1,0:T(8,128)} %fusion.12) | copy-start | bytes 2703364
  228.5 3.2 %copy-start.14 = (bf16[1,2048,704]{1,2,0:T(8,128)(2,1)S(1)}, bf16[1,2048,704]{1,2,0:T(8,128)(2,1)}, u32[]{:S(2)}) copy-start(bf16[1,2048,704]{1,2,0:T(8,128)(2,1)} %all-gather.6.cloned.1.call-done) | copy-start | bytes 8650756
  231.8 1.8 copy-start.13
  231.8 2.1 copy-start.16
  236.4 21.9 %all-to-all-start.7 = ((bf16[8,40,2048]{2,1,0:T(8,128)(2,1)}), bf16[8,40,2048]{2,1,0:T(8,128)(2,1)S(1)}, u32[]{:S(2)}, u32[]{:S(2)}) async-start(bf16[8,40,2048]{2,1,0:T(8,128)(2,1)} %fusion.17), calls=%async_computation.7 | async-start | bytes 2621440 | tf_op jit(solution)/shard_map/all_to_all | solution.py:63
  258.3 21.7 %all-to-all-start.5 = ((bf16[8,40,2048]{2,1,0:T(8,128)(2,1)}), bf16[8,40,2048]{2,1,0:T(8,128)(2,1)S(1)}, u32[]{:S(2)}, u32[]{:S(2)}) async-start(bf16[8,40,2048]{2,1,0:T(8,128)(2,1)} %fusion.20), calls=%async_computation.5 | async-start | bytes 2621440 | tf_op jit(solution)/shard_map/all_to_all | solution.py:63
  282.3 2.5 copy-start.2
  291.3 4.7 %copy-start.3 = (f32[1,128,2048]{2,1,0:T(8,128)S(1)}, f32[1,128,2048]{2,1,0:T(8,128)}, u32[]{:S(2)}) copy-start(f32[1,128,2048]{2,1,0:T(8,128)} %reshape.197) | copy-start | bytes 3145732
  291.3 4.7 %copy-start.5 = (bf16[1,128,2048]{2,1,0:T(8,128)(2,1)S(1)}, bf16[1,128,2048]{2,1,0:T(8,128)(2,1)}, u32[]{:S(2)}) copy-start(bf16[1,128,2048]{2,1,0:T(8,128)(2,1)} %param.21) | copy-start | bytes 1572868
  291.3 4.7 %copy-start.7 = (bf16[1,128,2048]{2,1,0:T(8,128)(2,1)S(1)}, bf16[1,128,2048]{2,1,0:T(8,128)(2,1)}, u32[]{:S(2)}) copy-start(bf16[1,128,2048]{2,1,0:T(8,128)(2,1)} %param.14) | copy-start | bytes 1572868
Sparse Core Ops, SparseCore 0:
  9.6 91.5 all-gather.3
  102.7 65.8 all-gather.5
  170.2 58.2 all-gather.7
where the time goes:
time: 305 us; the launch traced here: 304 us
  waiting for transfers between devices  185 us (61%)
  starting transfers between devices  31.8 us (10%)
  local copies, waits for them, and re-layouts  31.7 us (10%)
  matrix products  25.9 us (8%)
  other arithmetic  15.1 us (5%)
  between operations  14.2 us (5%)
    all_gather x1, waiting for transfers between devices, per_device(): lax.all_gather(w_down, 'seq', axis=2, tiled=True)  43 us
    all_to_all x2, waiting for transfers between devices, to_owners(): lax.all_to_all(buffer, 'exp', split_axis=0, concat_axis=0, tiled=True)  26.9 us
    all_to_all x1, waiting for transfers between devices, per_device(): lax.all_to_all(keys.reshape(split_shape), 'seq', split_axis=1, concat_axi...  26.2 us
    all_to_all x1, waiting for transfers between devices, per_device(): lax.all_to_all(queries.reshape(split_shape), 'seq', split_axis=1, concat_...  26.2 us
    all_to_all x1, waiting for transfers between devices, per_device(): lax.all_to_all(context[:, None], 'seq', split_axis=0, concat_axis=1, tile...  22.5 us
    all_to_all x2, waiting for transfers between devices, to_experts(): lax.all_to_all(buffer, 'exp', split_axis=0, concat_axis=0, tiled=True)  19.3 us
    all_to_all x1, waiting for transfers between devices, per_device(): lax.all_to_all(values.reshape(split_shape), 'seq', split_axis=1, concat_a...  19.2 us
    all_to_all x2, starting transfers between devices, to_owners(): lax.all_to_all(buffer, 'exp', split_axis=0, concat_axis=0, tiled=True)  7.44 us
  transfers between devices with their start and end apart: 11, of which 9 were waited for; matrix products, arithmetic and copies ran while one was open for 15% of the time, Pallas kernels for 0%

commit v1 on v0

v1 whole, which is shorter than its diff:
```python
import functools

import jax
import jax.numpy as jnp
from jax import lax
from jax.experimental import pallas as pl
from jax.experimental.pallas import tpu as pltpu
from jax.sharding import PartitionSpec as P

HD = 128
BF = jnp.bfloat16
F32 = jnp.float32
MIB = 1 << 20
ANY = pl.BlockSpec(memory_space=pl.ANY)
VMEM = pl.BlockSpec(memory_space=pltpu.VMEM)
SMEM = pl.BlockSpec(memory_space=pltpu.SMEM)
NT = (((1,), (1,)), ((), ()))
NN = (((1,), (0,)), ((), ()))


def mm(a, b, dims):
    return lax.dot_general(a, b, dims, preferred_element_type=F32)


def call(kernel, outs, args, in_specs, scratch=(), flops=0, moved=0, vmem=40):
    return pl.pallas_call(
        kernel,
        out_shape=outs,
        in_specs=in_specs,
        out_specs=jax.tree.map(lambda _: VMEM, outs),
        scratch_shapes=list(scratch),
        compiler_params=pltpu.CompilerParams(vmem_limit_bytes=vmem * MIB),
        cost_estimate=pl.CostEstimate(flops=flops, bytes_accessed=moved, transcendentals=0),
    )(*args)


def sds(shape, dtype=BF):
    return jax.ShapeDtypeStruct(shape, dtype)


def pack_kernel(q_ref, k_ref, v_ref, o_ref):
    rows = q_ref.shape[0]
    o_ref[0, 0:rows] = q_ref[...]
    o_ref[0, rows : 2 * rows] = k_ref[...]
    o_ref[0, 2 * rows : 3 * rows] = v_ref[...]


def pack(q, k, v, groups):
    rows, width = q.shape
    part = width // groups
    spec = pl.BlockSpec((rows, part), lambda g: (0, g))
    return pl.pallas_call(
        pack_kernel,
        grid=(groups,),
        out_shape=sds((groups, 3 * rows, part)),
        in_specs=[spec] * 3,
        out_specs=pl.BlockSpec((1, 3 * rows, part), lambda g: (g, 0, 0)),
        cost_estimate=pl.CostEstimate(
            flops=0, bytes_accessed=12 * rows * width, transcendentals=0
        ),
    )(q, k, v)


def attend_kernel(x_ref, o_ref):
    blocks, three, hd = x_ref.shape
    rows = three // 3
    scale = HD ** (-0.5)
    keys = x_ref[:, rows : 2 * rows, :].reshape(blocks * rows, hd)
    vals = x_ref[:, 2 * rows : 3 * rows, :].reshape(blocks * rows, hd)
    row_ids = lax.broadcasted_iota(jnp.int32, (rows, rows), 0)
    col_ids = lax.broadcasted_iota(jnp.int32, (rows, rows), 1)
    keep = col_ids <= row_ids
    for b in range(blocks):
        query = x_ref[b, 0:rows, :]
        end = b * rows
        diag = mm(query, keys[end : end + rows], NT) * scale
        diag = jnp.where(keep, diag, -jnp.inf)
        top = jnp.max(diag, axis=-1, keepdims=True)
        if b:
            early = mm(query, keys[:end], NT) * scale
            top = jnp.maximum(top, jnp.max(early, axis=-1, keepdims=True))
        diag = jnp.exp(diag - top)
        total = jnp.sum(diag, axis=-1, keepdims=True)
        if b:
            early = jnp.exp(early - top)
            total = total + jnp.sum(early, axis=-1, keepdims=True)
        inverse = 1.0 / total
        ctx = mm((diag * inverse).astype(BF), vals[end : end + rows], NN)
        if b:
            ctx = ctx + mm((early * inverse).astype(BF), vals[:end], NN)
        o_ref[b] = ctx.astype(BF)


def attend(x):
    blocks, three, part = x.shape
    rows = three // 3
    length = blocks * rows
    return pl.pallas_call(
        attend_kernel,
        grid=(part // HD,),
        out_shape=sds((blocks, rows, part)),
        in_specs=[pl.BlockSpec((blocks, three, HD), lambda h: (0, 0, h))],
        out_specs=pl.BlockSpec((blocks, rows, HD), lambda h: (0, 0, h)),
        compiler_params=pltpu.CompilerParams(vmem_limit_bytes=40 * MIB),
        cost_estimate=pl.CostEstimate(
            flops=4 * length * length * part,
            bytes_accessed=8 * length * part,
            transcendentals=length * length * part // HD,
        ),
    )(x)


def slot_rows(ids_t, owners, cap):
    tokens = ids_t.shape[1]
    experts = lax.broadcasted_iota(jnp.int32, (owners, tokens), 0)
    first = (experts == ids_t[0:1]).astype(F32)
    second = (experts == ids_t[1:2]).astype(F32)
    src = lax.broadcasted_iota(jnp.int32, (tokens, tokens), 0)
    dst = lax.broadcasted_iota(jnp.int32, (tokens, tokens), 1)
    earlier = (src < dst).astype(F32).astype(BF)
    count = mm((first + second).astype(BF), earlier, NN)
    slot0 = jnp.sum(first * count, axis=0, keepdims=True).astype(jnp.int32)
    slot1 = jnp.sum(second * count, axis=0, keepdims=True).astype(jnp.int32)
    return ids_t[0:1] * cap + slot0, ids_t[1:2] * cap + slot1


def slot_cols(ids, owners, cap):
    tokens = ids.shape[0]
    experts = lax.broadcasted_iota(jnp.int32, (tokens, owners), 1)
    first = (experts == ids[:, 0:1]).astype(F32)
    second = (experts == ids[:, 1:2]).astype(F32)
    dst = lax.broadcasted_iota(jnp.int32, (tokens, tokens), 0)
    src = lax.broadcasted_iota(jnp.int32, (tokens, tokens), 1)
    earlier = (src < dst).astype(F32).astype(BF)
    count = mm(earlier, (first + second).astype(BF), NN)
    slot0 = jnp.sum(first * count, axis=1, keepdims=True).astype(jnp.int32)
    slot1 = jnp.sum(second * count, axis=1, keepdims=True).astype(jnp.int32)
    return ids[:, 0:1] * cap + slot0, ids[:, 1:2] * cap + slot1


def one_hot(hit):
    return jnp.where(hit, 1.0, 0.0).astype(BF)


def send_cot_kernel(owners, cap, ids_ref, w_ref, cot_ref, o_ref):
    tokens = cot_ref.shape[0]
    at0, at1 = slot_rows(ids_ref[...], owners, cap)
    rows = lax.broadcasted_iota(jnp.int32, (owners * cap, tokens), 0)
    cot = cot_ref[...].astype(F32)
    o_ref[...] = (
        mm(one_hot(rows == at0), (w_ref[:, 0:1] * cot).astype(BF), NN)
        + mm(one_hot(rows == at1), (w_ref[:, 1:2] * cot).astype(BF), NN)
    ).astype(BF)


def norm_kernel(owners, cap, ids_ref, ctx_ref, resid_ref, gain_ref, stream_ref, o_ref):
    groups, tokens, part = ctx_ref.shape
    width = groups * part
    square = jnp.zeros((tokens, 1), F32)
    for g in range(groups):
        cols = slice(g * part, (g + 1) * part)
        stream = (resid_ref[:, cols].astype(F32) + ctx_ref[g].astype(F32)).astype(BF)
        stream_ref[:, cols] = stream
        stream = stream.astype(F32)
        square = square + jnp.sum(stream * stream, axis=-1, keepdims=True)
    inv_rms = lax.rsqrt(square / width + 1e-05)
    at0, at1 = slot_rows(ids_ref[...], owners, cap)
    rows = lax.broadcasted_iota(jnp.int32, (owners * cap, tokens), 0)
    pick = one_hot((rows == at0) | (rows == at1))
    for g in range(groups):
        cols = slice(g * part, (g + 1) * part)
        normed = ((stream_ref[:, cols].astype(F32) * inv_rms) * gain_ref[:, cols]).astype(BF)
        o_ref[:, cols] = mm(pick, normed, NN).astype(BF)


def fetch(inner, choices, dst, sem):
    if len(choices) == 1:
        pltpu.make_async_copy(choices[0], dst, sem).start()
        return

    @pl.when(inner == 1)
    def _():
        pltpu.make_async_copy(choices[0], dst, sem).start()

    @pl.when(inner == 0)
    def _():
        pltpu.make_async_copy(choices[1], dst, sem).start()


def arrived(choices, dst, sem):
    pltpu.make_async_copy(choices[0], dst, sem).wait()


def regroup(refs, shape):
    refs = list(refs)
    return [[refs.pop(0) for _ in range(size)] for size in shape], refs


def cols_of(place_ref, slot, part):
    return pl.ds(pl.multiple_of(place_ref[1 + slot] * part, part), part)


def up_kernel(shape, place_ref, x_ref, *refs):
    slots = len(shape)
    gate_in, refs = regroup(refs, shape)
    up_in, refs = regroup(refs, shape)
    hidden_ref, to_gate_ref, to_up_ref, gate_w, up_w, sems = refs
    part = gate_w.shape[2]
    inner = place_ref[0]
    for j in range(slots):
        fetch(inner, gate_in[j], gate_w.at[j], sems.at[0, j])
        fetch(inner, up_in[j], up_w.at[j], sems.at[1, j])
    gate = up = None
    for j in range(slots):
        rows = x_ref[:, cols_of(place_ref, j, part)]
        arrived(gate_in[j], gate_w.at[j], sems.at[0, j])
        term = mm(rows, gate_w[j], NT)
        gate = term if gate is None else gate + term
        arrived(up_in[j], up_w.at[j], sems.at[1, j])
        term = mm(rows, up_w[j], NT)
        up = term if up is None else up + term
    sigma = 1.0 / (1.0 + jnp.exp(-gate))
    silu = gate * sigma
    hidden_ref[...] = (silu * up).astype(BF)
    to_gate_ref[...] = up * sigma * (1.0 + gate * (1.0 - sigma))
    to_up_ref[...] = silu


def down_kernel(shape, place_ref, hidden_ref, cot_ref, *refs):
    slots = len(shape)
    down_in, refs = regroup(refs, shape)
    out_ref, d_hidden_ref, down_w, sems = refs
    part = down_w.shape[2]
    inner = place_ref[0]
    for j in range(slots):
        fetch(inner, down_in[j], down_w.at[j], sems.at[j])
    total = None
    for j in range(slots):
        rows = cot_ref[:, cols_of(place_ref, j, part)]
        arrived(down_in[j], down_w.at[j], sems.at[j])
        term = mm(rows, down_w[j], NT)
        total = term if total is None else total + term
        out_ref[:, j * part : (j + 1) * part] = mm(hidden_ref[...], down_w[j], NN).astype(BF)
    d_hidden_ref[...] = total


def grad_kernel(
    shape, place_ref, hidden_ref, cot_ref, d_hidden_ref, to_gate_ref, to_up_ref, *refs
):
    slots = len(shape)
    down_in, refs = regroup(refs, shape[-1:])
    gate_in, refs = regroup(refs, shape)
    up_in, refs = regroup(refs, shape)
    o_ref, down_w, gate_w, up_w, sems = refs
    part = down_w.shape[1]
    inner = place_ref[0]
    fetch(inner, down_in[0], down_w, sems.at[2, 0])
    for j in range(slots):
        fetch(inner, gate_in[j], gate_w.at[j], sems.at[0, j])
        fetch(inner, up_in[j], up_w.at[j], sems.at[1, j])
    rows = cot_ref[:, cols_of(place_ref, slots - 1, part)]
    arrived(down_in[0], down_w, sems.at[2, 0])
    d_hidden = d_hidden_ref[...] + mm(rows, down_w[...], NT)
    d_gate = (d_hidden * to_gate_ref[...]).astype(BF)
    d_up = (d_hidden * to_up_ref[...]).astype(BF)
    o_ref[:, slots * part :] = mm(hidden_ref[...], down_w[...], NN).astype(BF)
    for j in range(slots):
        arrived(gate_in[j], gate_w.at[j], sems.at[0, j])
        arrived(up_in[j], up_w.at[j], sems.at[1, j])
        o_ref[:, j * part : (j + 1) * part] = (
            mm(d_gate, gate_w[j], NN) + mm(d_up, up_w[j], NN)
        ).astype(BF)


def final_kernel(
    owners,
    cap,
    place_ref,
    ids_ref,
    w_ref,
    gain_ref,
    stream_ref,
    cot_ref,
    first_ref,
    last_ref,
    output_ref,
    grad_ref,
    d_normed_ref,
):
    tokens, width = stream_ref.shape
    done = first_ref.shape[1]
    part = width - done
    slots = width // part
    at0, at1 = slot_cols(ids_ref[...], owners, cap)
    rows = lax.broadcasted_iota(jnp.int32, (tokens, owners * cap), 1)
    pick0, pick1 = one_hot(rows == at0), one_hot(rows == at1)
    both = pick0 + pick1
    w0, w1 = w_ref[:, 0:1], w_ref[:, 1:2]
    square = jnp.zeros((tokens, 1), F32)
    dot = jnp.zeros((tokens, 1), F32)
    for j in range(slots):
        cols = cols_of(place_ref, j, part)
        if j < slots - 1:
            pairs = first_ref[:, j * part : (j + 1) * part]
        else:
            pairs = last_ref[:, width : width + part]
        stream = stream_ref[:, cols].astype(F32)
        mixed = w0 * mm(pick0, pairs, NN) + w1 * mm(pick1, pairs, NN)
        output_ref[:, cols] = (stream + mixed).astype(BF)
        gained = mm(both, last_ref[:, j * part : (j + 1) * part], NN) * gain_ref[:, cols]
        d_normed_ref[:, cols] = gained
        square = square + jnp.sum(stream * stream, axis=-1, keepdims=True)
        dot = dot + jnp.sum(gained * stream, axis=-1, keepdims=True)
    inv_rms = lax.rsqrt(square / width + 1e-05)
    mean = dot * inv_rms / width
    unit_rows = stream_ref[...].astype(F32) * inv_rms
    d_stream = inv_rms * (d_normed_ref[...] - unit_rows * mean)
    grad_ref[...] = (cot_ref[...].astype(F32) + d_stream).astype(BF)


def gather_line(shard, groups):
    if groups == 4:
        near = lax.ppermute(shard, "seq", [(0, 1), (1, 0), (2, 3), (3, 2)])
        across = lax.ppermute(shard, "seq", [(1, 2), (2, 1)])
        across_near = lax.ppermute(near, "seq", [(1, 2), (2, 1)])
        far = lax.ppermute(across, "seq", [(1, 0), (2, 3)])
        far_near = lax.ppermute(across_near, "seq", [(1, 0), (2, 3)])
        return [[shard], [near], [across, far], [across_near, far_near]]
    whole = lax.all_gather(shard, "seq", axis=0)
    return [[whole[j]] for j in range(groups)]


def places(groups):
    if groups == 4:
        own = lax.axis_index("seq")
        table = jnp.array(
            [[0, 0, 1, 2, 3], [1, 1, 0, 2, 3], [1, 2, 3, 1, 0], [0, 3, 2, 1, 0]], jnp.int32
        )
        return table[own]
    return jnp.arange(-1, groups, dtype=jnp.int32)


def exchange(rows, owners, axis):
    total, width = rows.shape
    rows = rows.reshape(owners, total // owners, width)
    rows = lax.all_to_all(rows, axis, split_axis=0, concat_axis=0, tiled=True)
    return rows.reshape(total, width)


def flat(slots):
    return [ref for choices in slots for ref in choices]


def per_device(
    queries,
    keys,
    values,
    resid,
    norm_gain,
    w_gate,
    w_up,
    w_down,
    expert_ids,
    route_weights,
    cotangent,
):
    groups = lax.axis_size("seq")
    owners = lax.axis_size("exp")
    tokens, width = queries.shape[1:]
    ffw = w_gate.shape[2]
    part = width // groups
    cap = max(2, tokens * 10 // (4 * owners))
    total = owners * cap
    ids = expert_ids[0]
    ids_t = ids.T
    weights = route_weights[0]
    gain = norm_gain[None]
    cot = cotangent[0]
    place = places(groups)

    packed = pack(queries[0], keys[0], values[0], groups)
    heads = lax.all_to_all(packed, "seq", split_axis=0, concat_axis=0, tiled=True)
    gate_in = gather_line(w_gate[0].T, groups)
    up_in = gather_line(w_up[0].T, groups)
    down_in = gather_line(w_down[0], groups)
    shape = [len(choices) for choices in gate_in]
    ctx = attend(heads)
    ctx = lax.all_to_all(ctx, "seq", split_axis=0, concat_axis=0, tiled=True)

    one = 2 * total * width * ffw
    send_cot = call(
        functools.partial(send_cot_kernel, owners, cap),
        sds((total, width)),
        (ids_t, weights, cot),
        [VMEM] * 3,
        flops=4 * total * tokens * width,
        moved=2 * (total + tokens) * width,
    )
    cot_rows = exchange(send_cot, owners, "exp")
    stream, send_rows = call(
        functools.partial(norm_kernel, owners, cap),
        (sds((tokens, width)), sds((total, width))),
        (ids_t, ctx, resid[0], gain),
        [VMEM] * 4,
        flops=2 * total * tokens * width,
        moved=2 * (total + 3 * tokens) * width,
    )
    rows = exchange(send_rows, owners, "exp")

    full_w = pltpu.VMEM((groups, ffw, part), BF)
    hidden, to_gate, to_up = call(
        functools.partial(up_kernel, shape),
        (sds((total, ffw)), sds((total, ffw), F32), sds((total, ffw), F32)),
        (place, rows, *flat(gate_in), *flat(up_in)),
        [SMEM, VMEM] + [ANY] * (2 * sum(shape)),
        [full_w, full_w, pltpu.SemaphoreType.DMA((2, groups))],
        flops=2 * one,
        moved=4 * width * ffw + 2 * total * width + 10 * total * ffw,
    )
    out_first, d_hidden = call(
        functools.partial(down_kernel, shape[:-1]),
        (sds((total, width - part)), sds((total, ffw), F32)),
        (place, hidden, cot_rows, *flat(down_in[:-1])),
        [SMEM, VMEM, VMEM] + [ANY] * sum(shape[:-1]),
        [
            pltpu.VMEM((groups - 1, ffw, part), BF),
            pltpu.SemaphoreType.DMA((groups - 1,)),
        ],
        flops=2 * one * (groups - 1) // groups,
        moved=2 * width * ffw + 4 * total * width + 6 * total * ffw,
    )
    back_first = exchange(out_first, owners, "exp")
    back = call(
        functools.partial(grad_kernel, shape),
        sds((total, width + part)),
        (
            place,
            hidden,
            cot_rows,
            d_hidden,
            to_gate,
            to_up,
            *flat(down_in[-1:]),
            *flat(gate_in),
            *flat(up_in),
        ),
        [SMEM] + [VMEM] * 5 + [ANY] * (shape[-1] + 2 * sum(shape)),
        [
            pltpu.VMEM((ffw, part), BF),
            full_w,
            full_w,
            pltpu.SemaphoreType.DMA((3, groups)),
        ],
        flops=2 * one + 2 * one // groups,
        moved=4 * width * ffw + 4 * total * width + 14 * total * ffw,
    )
    back_last = exchange(back, owners, "exp")
    output, stream_grad = call(
        functools.partial(final_kernel, owners, cap),
        (sds((tokens, width)), sds((tokens, width))),
        (place, ids, weights, gain, stream, cot, back_first, back_last),
        [SMEM] + [VMEM] * 7,
        [pltpu.VMEM((tokens, width), F32)],
        flops=6 * total * tokens * width,
        moved=4 * total * width + 8 * tokens * width,
    )
    return (output[None], stream_grad[None])


def solution(mesh):
    placed = (
        P("exp", "seq", None),
        P("exp", "seq", None),
        P("exp", "seq", None),
        P("exp", "seq", None),
        P(),
        P("exp", "seq", None),
        P("exp", "seq", None),
        P("exp", None, "seq"),
        P("exp", "seq", None),
        P("exp", "seq", None),
        P("exp", "seq", None),
    )
    return jax.shard_map(
        per_device,
        mesh=mesh,
        in_specs=placed,
        out_specs=(P("exp", "seq", None), P("exp", "seq", None)),
        check_vma=False,
    )
```

time: 305 us -> 250 us (0.82)
  waiting for transfers between devices: 185 us -> 90.6 us
  blocking collectives: 0 us -> 68.6 us
  Pallas kernels: 0 us -> 32.6 us
  matrix products: 25.9 us -> 0 us
  other arithmetic: 15.1 us -> 0 us
  between operations: 14.2 us -> 0.86 us
  local copies, waits for them, and re-layouts: 31.7 us -> 18.5 us
  starting transfers between devices: 31.8 us -> 37.6 us
    all_to_all x8 -> x4, waiting for transfers between devices: 140 us -> 8.68 us  [the longest x1 7.59 us: per_device(): ctx = lax.all_to_all(ctx, 'seq', split_axis=0, concat_axis=0, tiled=True)]
    ppermute x0 -> x15, waiting for transfers between devices: none -> 81.9 us  [the longest x3 32.6 us: gather_line(): far_near = lax.ppermute(across_near, 'seq', [(1, 0), (2, 3)])]
    all_to_all x0 -> x2, blocking collectives: none -> 68.6 us  [the longest x1 43.3 us: per_device(): lax.all_to_all(packed, 'seq', split_axis=0, concat_axis=0, tiled=True)]
    all_gather x3 -> x0, waiting for transfers between devices: 43 us -> none  [the longest x1 43 us: per_device(): lax.all_gather(w_down, 'seq', axis=2, tiled=True)]
    pallas_call x0 -> x8, Pallas kernels: none -> 32.6 us  [the longest x6 21.8 us: call(): pl.pallas_call(kernel, out_shape=outs, in_specs=in_specs, out_specs=jax.t...]
    ppermute x0 -> x15, starting transfers between devices: none -> 22.7 us  [the longest x3 6.69 us: gather_line(): near = lax.ppermute(shard, 'seq', [(0, 1), (1, 0), (2, 3), (3, 2)])]
    dot_general x7 -> x0, matrix products: 22.4 us -> none  [the longest x1 4.17 us: per_device(): jnp.einsum('scf,fd->scd', hidden, down_w, preferred_element_type=jnp.floa...]
    all_to_all x8 -> x4, starting transfers between devices: 31.7 us -> 14.9 us  [the longest x3 11.4 us: exchange(): rows = lax.all_to_all(rows, axis, split_axis=0, concat_axis=0, tiled=True)]
  transfers between devices with their start and end apart: 11 -> 19, of which waited for: 9 -> 11; matrix products, arithmetic and copies ran while one was open for 15% -> 0% of each run, Pallas kernels for 0% -> 8%
where the time goes in v1:
time: 250 us; the launch traced here: 249 us
  waiting for transfers between devices  90.6 us (36%)
  blocking collectives  68.6 us (27%)
  starting transfers between devices  37.6 us (15%)
  Pallas kernels  32.6 us (13%)
  local copies, waits for them, and re-layouts  18.5 us (7%)
    all_to_all x1, blocking collectives, per_device(): lax.all_to_all(packed, 'seq', split_axis=0, concat_axis=0, tiled=True)  43.3 us
    ppermute x3, waiting for transfers between devices, gather_line(): far_near = lax.ppermute(across_near, 'seq', [(1, 0), (2, 3)])  32.6 us
    ppermute x3, waiting for transfers between devices, gather_line(): far = lax.ppermute(across, 'seq', [(1, 0), (2, 3)])  26.9 us
    all_to_all x1, blocking collectives, exchange(): rows = lax.all_to_all(rows, axis, split_axis=0, concat_axis=0, tiled=True)  25.3 us
    ppermute x3, waiting for transfers between devices, gather_line(): near = lax.ppermute(shard, 'seq', [(0, 1), (1, 0), (2, 3), (3, 2)])  22.4 us
    pallas_call x6, Pallas kernels, call(): pl.pallas_call(kernel, out_shape=outs, in_specs=in_specs, out_specs=jax.t...  21.8 us
    unnamed x60, local copies, waits for them, and re-layouts  17.7 us
    all_to_all x3, starting transfers between devices, exchange(): rows = lax.all_to_all(rows, axis, split_axis=0, concat_axis=0, tiled=True)  11.4 us
  transfers between devices with their start and end apart: 19, of which 11 were waited for; matrix products, arithmetic and copies ran while one was open for 0% of the time, Pallas kernels for 8%

profile of v1, /device:TPU:0, one launch (start us, length us, event | category | flops | bytes accessed | tf_op | source)
XLA Modules:
  0.0 248.7 jit_solution(2639069048143137392)
XLA Ops:
  0.6 3.7 %shard_map.131 = bf16[4,384,512]{2,1,0:T(8,128)(2,1)} custom-call(bf16[128,2048]{1,0:T(8,128)(2,1)} %bitcast.58, bf16[128,2048]{1,0:T(8,128)(2,1)} %bitcast.59, bf16[128,2048]{1,0:T(8,128)(2,1)} %bitcast.60), custom_call_target="tpu_custom_call" | custom-call | bytes 3145728 | tf_op jit(solution)/shard_map/pallas_call | solution.py:52
  4.3 43.3 %all_to_all.30.x_ref = bf16[4,384,512]{2,1,0:T(8,128)(2,1)S(1)} all-to-all(bf16[4,384,512]{2,1,0:T(8,128)(2,1)} %shard_map.131), channel_id=1, replica_groups=mesh['seq'=4,'exp'=8] {'seq'}, dimensions={0} | all-to-all | bytes 3145728 | tf_op jit(solution)/shard_map/all_to_all | solution.py:382
  47.6 7.2 %shard_map.132 = bf16[4,128,512]{2,1,0:T(8,128)(2,1)} custom-call(bf16[4,384,512]{2,1,0:T(8,128)(2,1)S(1)} %all_to_all.30.x_ref), custom_call_target="tpu_custom_call" | custom-call | flops 536870912 | bytes 2097152 | tf_op jit(solution)/shard_map/pallas_call | solution.py:98
  54.8 3.5 %all-to-all-start.1 = ((bf16[4,128,512]{2,1,0:T(8,128)(2,1)}), bf16[4,128,512]{2,1,0:T(8,128)(2,1)S(1)}, u32[]{:S(2)}, u32[]{:S(2)}) async-start(bf16[4,128,512]{2,1,0:T(8,128)(2,1)} %shard_map.132), calls=%async_computation.1 | async-start | bytes 1048576 | tf_op jit(solution)/shard_map/all_to_all | solution.py:388
  58.3 2.0 collective-permute-start
  60.2 1.5 collective-permute-start.1
  61.8 3.4 %collective-permute-start.5 = (bf16[704,512]{1,0:T(8,128)(2,1)S(1)}, bf16[704,512]{1,0:T(8,128)(2,1)}, u32[]{:S(2)}, u32[]{:S(2)}) collective-permute-start(bf16[704,512]{1,0:T(8,128)(2,1)S(1)} %bitcast.39), channel_id=1, source_target_pairs={{0,8},{8,0},{16,24},{24,16},{1,9},{9,1},{17,25},{25,17},{2,10},{10... | collective-permute-start | bytes 2162696 | tf_op jit(solution)/shard_map/ppermute | solution.py:323
  65.3 7.6 %all-to-all-done.1.ctx_ref = bf16[4,128,512]{2,1,0:T(8,128)(2,1)S(1)} async-done(((bf16[4,128,512]{2,1,0:T(8,128)(2,1)}), bf16[4,128,512]{2,1,0:T(8,128)(2,1)S(1)}, u32[]{:S(2)}, u32[]{:S(2)}) %all-to-all-start.1) | async-done | bytes 524320 | tf_op jit(solution)/shard_map/all_to_all | solution.py:388
  73.7 1.1 copy-done.11
  75.6 3.9 %all-to-all-start.2 = ((bf16[8,40,2048]{2,1,0:T(8,128)(2,1)}), bf16[8,40,2048]{2,1,0:T(8,128)(2,1)S(1)}, u32[]{:S(2)}, u32[]{:S(2)}) async-start(bf16[8,40,2048]{2,1,0:T(8,128)(2,1)} %bitcast.45), calls=%async_computation.2 | async-start | bytes 2621440 | tf_op jit(solution)/shard_map/all_to_all | solution.py:346
  80.2 1.3 collective-permute-start.10
  81.5 4.2 %collective-permute-done.refs_1_.refs_3_ = bf16[704,512]{1,0:T(8,128)(2,1)} collective-permute-done((bf16[704,512]{1,0:T(8,128)(2,1)S(1)}, bf16[704,512]{1,0:T(8,128)(2,1)}, u32[]{:S(2)}, u32[]{:S(2)}) %collective-permute-start) | collective-permute-done | bytes 720928 | tf_op jit(solution)/shard_map/ppermute | solution.py:323
  85.7 1.5 collective-permute-start.11
  87.2 1.5 collective-permute-start.3
  88.7 12.4 %collective-permute-done.5.refs_7_.refs_9_ = bf16[704,512]{1,0:T(8,128)(2,1)} collective-permute-done((bf16[704,512]{1,0:T(8,128)(2,1)S(1)}, bf16[704,512]{1,0:T(8,128)(2,1)}, u32[]{:S(2)}, u32[]{:S(2)}) %collective-permute-start.5) | collective-permute-done | bytes 720928 | tf_op jit(solution)/shard_map/ppermute | solution.py:323
  101.1 1.5 collective-permute-start.8
  103.5 1.3 collective-permute-start.2
  105.0 1.0 shard_map.135
  106.0 1.1 copy-done.1
  107.1 3.7 %all-to-all-start.3 = ((bf16[8,40,2048]{2,1,0:T(8,128)(2,1)}), bf16[8,40,2048]{2,1,0:T(8,128)(2,1)S(1)}, u32[]{:S(2)}, u32[]{:S(2)}) async-start(bf16[8,40,2048]{2,1,0:T(8,128)(2,1)} %bitcast.33), calls=%async_computation.3 | async-start | bytes 2621440 | tf_op jit(solution)/shard_map/all_to_all | solution.py:346
  110.8 5.8 %collective-permute-done.10.refs_1_ = bf16[704,512]{1,0:T(8,128)(2,1)} collective-permute-done((bf16[704,512]{1,0:T(8,128)(2,1)}, bf16[704,512]{1,0:T(8,128)(2,1)}, u32[]{:S(2)}, u32[]{:S(2)}) %collective-permute-start.10) | collective-permute-done | bytes 720928 | tf_op jit(solution)/shard_map/ppermute | solution.py:323
  116.6 1.3 collective-permute-start.7
  117.9 1.5 collective-permute-start.13
  119.4 1.3 collective-permute-start.4
  120.7 1.3 collective-permute-start.9
  122.0 10.0 %collective-permute-done.2.refs_3_.refs_5_ = bf16[704,512]{1,0:T(8,128)(2,1)} collective-permute-done((bf16[704,512]{1,0:T(8,128)(2,1)}, bf16[704,512]{1,0:T(8,128)(2,1)}, u32[]{:S(2)}, u32[]{:S(2)}) %collective-permute-start.2) | collective-permute-done | bytes 720928 | tf_op jit(solution)/shard_map/ppermute | solution.py:326
  132.0 1.3 collective-permute-start.12
  134.0 1.3 collective-permute-start.14
  135.3 12.2 %collective-permute-done.7.refs_9_.refs_11_ = bf16[704,512]{1,0:T(8,128)(2,1)} collective-permute-done((bf16[704,512]{1,0:T(8,128)(2,1)}, bf16[704,512]{1,0:T(8,128)(2,1)}, u32[]{:S(2)}, u32[]{:S(2)}) %collective-permute-start.7) | collective-permute-done | bytes 720928 | tf_op jit(solution)/shard_map/ppermute | solution.py:326
  147.5 15.4 %collective-permute-done.4.refs_5_.refs_7_ = bf16[704,512]{1,0:T(8,128)(2,1)} collective-permute-done((bf16[704,512]{1,0:T(8,128)(2,1)}, bf16[704,512]{1,0:T(8,128)(2,1)}, u32[]{:S(2)}, u32[]{:S(2)}) %collective-permute-start.4) | collective-permute-done | bytes 720928 | tf_op jit(solution)/shard_map/ppermute | solution.py:327
  162.9 15.4 %collective-permute-done.9.refs_11_.refs_13_ = bf16[704,512]{1,0:T(8,128)(2,1)} collective-permute-done((bf16[704,512]{1,0:T(8,128)(2,1)}, bf16[704,512]{1,0:T(8,128)(2,1)}, u32[]{:S(2)}, u32[]{:S(2)}) %collective-permute-start.9) | collective-permute-done | bytes 720928 | tf_op jit(solution)/shard_map/ppermute | solution.py:327
  178.4 1.1 copy-done.4
  179.5 1.1 copy-done.7
  180.6 5.8 %shard_map.134 = (bf16[320,704]{1,0:T(8,128)(2,1)S(1)}, f32[320,704]{1,0:T(8,128)S(1)}, f32[320,704]{1,0:T(8,128)S(1)}) custom-call(s32[5]{0:T(128)S(1)} %dynamic-slice_bitcast_fusion.place_ref, bf16[320,2048]{1,0:T(8,128)(2,1)S(1)} %bitcast.32, bf16[704,512]{1,0:T(8,128)(2,1)S(1)} %bitcast.37, bf16[704,512]{1,0:T(8,128)(2,1)} %collective-permute-done.refs_1_.refs_3_, ...), custom_call_target="tpu_custom_call" | custom-call | flops 1845493760 | bytes 9330688 | tf_op jit(solution)/shard_map/pallas_call | solution.py:26
  189.2 4.7 %collective-permute-done.12.refs_3_ = bf16[704,512]{1,0:T(8,128)(2,1)} collective-permute-done((bf16[704,512]{1,0:T(8,128)(2,1)}, bf16[704,512]{1,0:T(8,128)(2,1)}, u32[]{:S(2)}, u32[]{:S(2)}) %collective-permute-start.12) | collective-permute-done | bytes 720928 | tf_op jit(solution)/shard_map/ppermute | solution.py:326
  193.8 1.0 copy-done.23
  194.9 1.1 copy-done.26
  196.0 3.8 %shard_map.136 = (bf16[320,1536]{1,0:T(8,128)(2,1)S(1)}, f32[320,704]{1,0:T(8,128)S(1)}) custom-call(s32[5]{0:T(128)S(1)} %dynamic-slice_bitcast_fusion.place_ref, bf16[320,704]{1,0:T(8,128)(2,1)S(1)} %copy-done.23, bf16[320,2048]{1,0:T(8,128)(2,1)S(1)} %bitcast.30, bf16[704,512]{1,0:T(8,128)(2,1)S(1)} %bitcast.56, ...), custom_call_target="tpu_custom_call" | custom-call | flops 1384120320 | bytes 6856704 | tf_op jit(solution)/shard_map/pallas_call | solution.py:26
  201.7 3.9 %all-to-all-start.4 = ((bf16[8,40,1536]{2,1,0:T(8,128)(2,1)}), bf16[8,40,1536]{2,1,0:T(8,128)(2,1)S(1)}, u32[]{:S(2)}, u32[]{:S(2)}) async-start(bf16[8,40,1536]{2,1,0:T(8,128)(2,1)} %bitcast.46), calls=%async_computation.4 | async-start | bytes 1966080 | tf_op jit(solution)/shard_map/all_to_all | solution.py:346
  205.6 1.7 collective-permute-done.14.refs_1_
  207.3 1.2 copy-done.13
  208.5 1.2 copy-done.15
  209.7 1.2 copy-done.17
  210.9 1.0 copy-done.24
  211.9 7.3 %shard_map.137 = bf16[320,2560]{1,0:T(8,128)(2,1)} custom-call(s32[5]{0:T(128)S(1)} %dynamic-slice_bitcast_fusion.place_ref, bf16[320,704]{1,0:T(8,128)(2,1)S(1)} %copy-done.24, bf16[320,2048]{1,0:T(8,128)(2,1)} %bitcast.31, f32[320,704]{1,0:T(8,128)S(1)} %copy-done.17, f32[320,704]{1,0:T(8,128)S(1)} %copy-done.13, f32[320,704]{1,0:T(8,128)S(1)} %copy-done.15, ...), custom_call_target="tpu_custom_call" | custom-call | flops 2306867200 | bytes 11542528 | tf_op jit(solution)/shard_map/pallas_call | solution.py:26
  219.2 1.1 all-to-all-done.4
  220.3 25.3 %all_to_all.31 = bf16[8,40,2560]{2,1,0:T(8,128)(2,1)S(1)} all-to-all(bf16[8,40,2560]{2,1,0:T(8,128)(2,1)} %bitcast.57), channel_id=1, replica_groups=mesh['seq'=4,'exp'=8] {'exp'}, dimensions={0} | all-to-all | bytes 3276800 | tf_op jit(solution)/shard_map/all_to_all | solution.py:346
  245.6 3.1 %shard_map.138 = (bf16[128,2048]{1,0:T(8,128)(2,1)}, bf16[128,2048]{1,0:T(8,128)(2,1)}) custom-call(s32[5]{0:T(128)S(1)} %dynamic-slice_bitcast_fusion.place_ref, s32[128,2]{1,0:T(8,128)S(1)} %bitcast.50, f32[128,2]{1,0:T(8,128)S(1)} %bitcast.48, f32[1,2048]{1,0:T(1,128)S(1)} %bitcast.53, bf16[128,2048]{1,0:T(8,128)(2,1)S(1)} %copy-done.21, ...), custom_call_target="tpu_custom_call" | custom-call | flops 503316480 | bytes 4718592 | tf_op jit(solution)/shard_map/pallas_call | solution.py:26
  (62 shorter events, 8.8 us)
Async XLA Ops:
  47.6 10.7 %copy-start.2 = (bf16[1,512,704]{1,2,0:T(8,128)(2,1)S(1)}, bf16[1,512,704]{1,2,0:T(8,128)(2,1)}, u32[]{:S(2)}) copy-start(bf16[1,512,704]{1,2,0:T(8,128)(2,1)} %param.17) | copy-start | bytes 2162692
  47.6 14.2 %copy-start.3 = (bf16[1,512,704]{1,2,0:T(8,128)(2,1)S(1)}, bf16[1,512,704]{1,2,0:T(8,128)(2,1)}, u32[]{:S(2)}) copy-start(bf16[1,512,704]{1,2,0:T(8,128)(2,1)} %param.18) | copy-start | bytes 2162692
  47.6 17.6 %copy-start.27 = (s32[1,128,2]{1,2,0:T(2,128)S(1)}, s32[1,128,2]{1,2,0:T(2,128)}, u32[]{:S(2)}) copy-start(s32[1,128,2]{1,2,0:T(2,128)} %param.20) | copy-start | bytes 3076
  47.6 25.3 %copy-start.19 = (bf16[1,128,2048]{2,1,0:T(8,128)(2,1)S(1)}, bf16[1,128,2048]{2,1,0:T(8,128)(2,1)}, u32[]{:S(2)}) copy-start(bf16[1,128,2048]{2,1,0:T(8,128)(2,1)} %param.15) | copy-start | bytes 1572868
  47.6 25.3 %copy-start.25 = (f32[2048]{0:T(1024)S(1)}, f32[2048]{0:T(1024)}, u32[]{:S(2)}) copy-start(f32[2048]{0:T(1024)} %param.16) | copy-start | bytes 24580
  54.8 18.1 %all-to-all-start.1 = ((bf16[4,128,512]{2,1,0:T(8,128)(2,1)}), bf16[4,128,512]{2,1,0:T(8,128)(2,1)S(1)}, u32[]{:S(2)}, u32[]{:S(2)}) async-start(bf16[4,128,512]{2,1,0:T(8,128)(2,1)} %shard_map.132), calls=%async_computation.1 | async-start | bytes 1048576 | tf_op jit(solution)/shard_map/all_to_all | solution.py:388
  58.3 27.4 %collective-permute-start = (bf16[704,512]{1,0:T(8,128)(2,1)S(1)}, bf16[704,512]{1,0:T(8,128)(2,1)}, u32[]{:S(2)}, u32[]{:S(2)}) collective-permute-start(bf16[704,512]{1,0:T(8,128)(2,1)S(1)} %bitcast.35), channel_id=1, source_target_pairs={{0,8},{8,0},{16,24},{24,16},{1,9},{9,1},{17,25},{25,17},{2,10},{10... | collective-permute-start | bytes 2162696 | tf_op jit(solution)/shard_map/ppermute | solution.py:323
  60.2 27.0 %collective-permute-start.1 = (bf16[704,512]{1,0:T(8,128)(2,1)S(1)}, bf16[704,512]{1,0:T(8,128)(2,1)}, u32[]{:S(2)}, u32[]{:S(2)}) collective-permute-start(bf16[704,512]{1,0:T(8,128)(2,1)S(1)} %bitcast.36), channel_id=1, source_target_pairs={{8,16},{16,8},{9,17},{17,9},{10,18},{18,10},{11,19},{19,11},{12,20... | collective-permute-start | bytes 2162696 | tf_op jit(solution)/shard_map/ppermute | solution.py:324
  61.8 39.4 %collective-permute-start.5 = (bf16[704,512]{1,0:T(8,128)(2,1)S(1)}, bf16[704,512]{1,0:T(8,128)(2,1)}, u32[]{:S(2)}, u32[]{:S(2)}) collective-permute-start(bf16[704,512]{1,0:T(8,128)(2,1)S(1)} %bitcast.39), channel_id=1, source_target_pairs={{0,8},{8,0},{16,24},{24,16},{1,9},{9,1},{17,25},{25,17},{2,10},{10... | collective-permute-start | bytes 2162696 | tf_op jit(solution)/shard_map/ppermute | solution.py:323
  73.7 1.1 copy-start.11
  74.8 0.8 copy-start.20
  75.6 29.2 %copy-start.28 = (f32[1,128,2]{1,2,0:T(2,128)S(1)}, f32[1,128,2]{1,2,0:T(2,128)}, u32[]{:S(2)}) copy-start(f32[1,128,2]{1,2,0:T(2,128)} %param.21) | copy-start | bytes 3076
  75.6 29.3 %copy-start.9 = (bf16[1,128,2048]{2,1,0:T(8,128)(2,1)S(1)}, bf16[1,128,2048]{2,1,0:T(8,128)(2,1)}, u32[]{:S(2)}) copy-start(bf16[1,128,2048]{2,1,0:T(8,128)(2,1)} %param.22) | copy-start | bytes 1572868
  75.6 31.4 %all-to-all-start.2 = ((bf16[8,40,2048]{2,1,0:T(8,128)(2,1)}), bf16[8,40,2048]{2,1,0:T(8,128)(2,1)S(1)}, u32[]{:S(2)}, u32[]{:S(2)}) async-start(bf16[8,40,2048]{2,1,0:T(8,128)(2,1)} %bitcast.45), calls=%async_computation.2 | async-start | bytes 2621440 | tf_op jit(solution)/shard_map/all_to_all | solution.py:346
  79.5 23.2 %collective-permute-start.6 = (bf16[704,512]{1,0:T(8,128)(2,1)S(1)}, bf16[704,512]{1,0:T(8,128)(2,1)S(1)}, u32[]{:S(2)}, u32[]{:S(2)}) collective-permute-start(bf16[704,512]{1,0:T(8,128)(2,1)S(1)} %bitcast.40), channel_id=1, source_target_pairs={{8,16},{16,8},{9,17},{17,9},{10,18},{18,10},{11,19},{19,11},{12,20... | collective-permute-start | bytes 2162696 | tf_op jit(solution)/shard_map/ppermute | solution.py:324
  80.2 36.4 %collective-permute-start.10 = (bf16[704,512]{1,0:T(8,128)(2,1)}, bf16[704,512]{1,0:T(8,128)(2,1)}, u32[]{:S(2)}, u32[]{:S(2)}) collective-permute-start(bf16[704,512]{1,0:T(8,128)(2,1)} %bitcast.54), channel_id=1, source_target_pairs={{0,8},{8,0},{16,24},{24,16},{1,9},{9,1},{17,25},{25,17},{2,10},{10... | collective-permute-start | bytes 2162696 | tf_op jit(solution)/shard_map/ppermute | solution.py:323
  85.7 32.2 %collective-permute-start.11 = (bf16[704,512]{1,0:T(8,128)(2,1)}, bf16[704,512]{1,0:T(8,128)(2,1)}, u32[]{:S(2)}, u32[]{:S(2)}) collective-permute-start(bf16[704,512]{1,0:T(8,128)(2,1)} %bitcast.55), channel_id=1, source_target_pairs={{8,16},{16,8},{9,17},{17,9},{10,18},{18,10},{11,19},{19,11},{12,20... | collective-permute-start | bytes 2162696 | tf_op jit(solution)/shard_map/ppermute | solution.py:324
  87.2 32.2 %collective-permute-start.3 = (bf16[704,512]{1,0:T(8,128)(2,1)}, bf16[704,512]{1,0:T(8,128)(2,1)}, u32[]{:S(2)}, u32[]{:S(2)}) collective-permute-start(bf16[704,512]{1,0:T(8,128)(2,1)} %collective-permute-done.refs_1_.refs_3_), channel_id=1, source_target_pairs={{8,16},{16,8},{9,17},{17,9},{10,18},{18,10},{11,19},{19,11},{12,20... | collective-permute-start | bytes 2162696 | tf_op jit(solution)/shard_map/ppermute | solution.py:325
  101.1 19.6 %collective-permute-start.8 = (bf16[704,512]{1,0:T(8,128)(2,1)}, bf16[704,512]{1,0:T(8,128)(2,1)}, u32[]{:S(2)}, u32[]{:S(2)}) collective-permute-start(bf16[704,512]{1,0:T(8,128)(2,1)} %collective-permute-done.5.refs_7_.refs_9_), channel_id=1, source_target_pairs={{8,16},{16,8},{9,17},{17,9},{10,18},{18,10},{11,19},{19,11},{12,20... | collective-permute-start | bytes 2162696 | tf_op jit(solution)/shard_map/ppermute | solution.py:325
  102.7 0.9 copy-start.6
  103.5 28.5 %collective-permute-start.2 = (bf16[704,512]{1,0:T(8,128)(2,1)}, bf16[704,512]{1,0:T(8,128)(2,1)}, u32[]{:S(2)}, u32[]{:S(2)}) collective-permute-start(bf16[704,512]{1,0:T(8,128)(2,1)} %collective-permute-done.1.refs_2_.refs_4_), channel_id=1, source_target_pairs={{8,0},{16,24},{9,1},{17,25},{10,2},{18,26},{11,3},{19,27},{12,4},{... | collective-permute-start | bytes 2162696 | tf_op jit(solution)/shard_map/ppermute | solution.py:326
  106.0 1.1 copy-start.1
  107.1 82.1 %all-to-all-start.3 = ((bf16[8,40,2048]{2,1,0:T(8,128)(2,1)}), bf16[8,40,2048]{2,1,0:T(8,128)(2,1)S(1)}, u32[]{:S(2)}, u32[]{:S(2)}) async-start(bf16[8,40,2048]{2,1,0:T(8,128)(2,1)} %bitcast.33), calls=%async_computation.3 | async-start | bytes 2621440 | tf_op jit(solution)/shard_map/all_to_all | solution.py:346
  116.6 30.9 %collective-permute-start.7 = (bf16[704,512]{1,0:T(8,128)(2,1)}, bf16[704,512]{1,0:T(8,128)(2,1)}, u32[]{:S(2)}, u32[]{:S(2)}) collective-permute-start(bf16[704,512]{1,0:T(8,128)(2,1)} %copy-done.6), channel_id=1, source_target_pairs={{8,0},{16,24},{9,1},{17,25},{10,2},{18,26},{11,3},{19,27},{12,4},{... | collective-permute-start | bytes 2162696 | tf_op jit(solution)/shard_map/ppermute | solution.py:326
  117.9 16.1 %collective-permute-start.13 = (bf16[704,512]{1,0:T(8,128)(2,1)}, bf16[704,512]{1,0:T(8,128)(2,1)}, u32[]{:S(2)}, u32[]{:S(2)}) collective-permute-start(bf16[704,512]{1,0:T(8,128)(2,1)} %collective-permute-done.10.refs_1_), channel_id=1, source_target_pairs={{8,16},{16,8},{9,17},{17,9},{10,18},{18,10},{11,19},{19,11},{12,20... | collective-permute-start | bytes 2162696 | tf_op jit(solution)/shard_map/ppermute | solution.py:325
  119.4 43.5 %collective-permute-start.4 = (bf16[704,512]{1,0:T(8,128)(2,1)}, bf16[704,512]{1,0:T(8,128)(2,1)}, u32[]{:S(2)}, u32[]{:S(2)}) collective-permute-start(bf16[704,512]{1,0:T(8,128)(2,1)} %collective-permute-done.3.refs_4_.refs_6_), channel_id=1, source_target_pairs={{8,0},{16,24},{9,1},{17,25},{10,2},{18,26},{11,3},{19,27},{12,4},{... | collective-permute-start | bytes 2162696 | tf_op jit(solution)/shard_map/ppermute | solution.py:327
  120.7 57.7 %collective-permute-start.9 = (bf16[704,512]{1,0:T(8,128)(2,1)}, bf16[704,512]{1,0:T(8,128)(2,1)}, u32[]{:S(2)}, u32[]{:S(2)}) collective-permute-start(bf16[704,512]{1,0:T(8,128)(2,1)} %collective-permute-done.8.refs_10_.refs_12_), channel_id=1, source_target_pairs={{8,0},{16,24},{9,1},{17,25},{10,2},{18,26},{11,3},{19,27},{12,4},{... | collective-permute-start | bytes 2162696 | tf_op jit(solution)/shard_map/ppermute | solution.py:327
  132.0 61.8 %collective-permute-start.12 = (bf16[704,512]{1,0:T(8,128)(2,1)}, bf16[704,512]{1,0:T(8,128)(2,1)}, u32[]{:S(2)}, u32[]{:S(2)}) collective-permute-start(bf16[704,512]{1,0:T(8,128)(2,1)} %collective-permute-done.11.refs_2_), channel_id=1, source_target_pairs={{8,0},{16,24},{9,1},{17,25},{10,2},{18,26},{11,3},{19,27},{12,4},{... | collective-permute-start | bytes 2162696 | tf_op jit(solution)/shard_map/ppermute | solution.py:326
  134.0 73.3 %collective-permute-start.14 = (bf16[704,512]{1,0:T(8,128)(2,1)}, bf16[704,512]{1,0:T(8,128)(2,1)}, u32[]{:S(2)}, u32[]{:S(2)}) collective-permute-start(bf16[704,512]{1,0:T(8,128)(2,1)} %collective-permute-done.13.refs_0_), channel_id=1, source_target_pairs={{8,0},{16,24},{9,1},{17,25},{10,2},{18,26},{11,3},{19,27},{12,4},{... | collective-permute-start | bytes 2162696 | tf_op jit(solution)/shard_map/ppermute | solution.py:327
  178.4 1.1 copy-start.4
  179.5 1.1 copy-start.7
  186.5 1.0 copy-start.12
  187.4 0.9 copy-start.14
  188.4 0.8 copy-start.22
  189.2 10.6 %copy-start = (bf16[8,40,2048]{2,1,0:T(8,128)(2,1)}, bf16[8,40,2048]{2,1,0:T(8,128)(2,1)S(1)}, u32[]{:S(2)}) copy-start(bf16[8,40,2048]{2,1,0:T(8,128)(2,1)S(1)} %all-to-all-done.3) | copy-start | bytes 3932164
  193.8 1.0 copy-start.23
  194.9 1.1 copy-start.26
  199.8 1.0 copy-start.16
  200.8 0.9 copy-start.18
  201.7 5.6 %copy-start.5 = (bf16[1,512,704]{1,2,0:T(8,128)(2,1)S(1)}, bf16[1,512,704]{1,2,0:T(8,128)(2,1)}, u32[]{:S(2)}) copy-start(bf16[1,512,704]{1,2,0:T(8,128)(2,1)} %param.18) | copy-start | bytes 2162692
  201.7 5.6 %copy-start.8 = (bf16[704,512]{1,0:T(8,128)(2,1)S(1)}, bf16[704,512]{1,0:T(8,128)(2,1)}, u32[]{:S(2)}) copy-start(bf16[704,512]{1,0:T(8,128)(2,1)} %copy-done.6) | copy-start | bytes 2162692
  201.7 18.6 %all-to-all-start.4 = ((bf16[8,40,1536]{2,1,0:T(8,128)(2,1)}), bf16[8,40,1536]{2,1,0:T(8,128)(2,1)S(1)}, u32[]{:S(2)}, u32[]{:S(2)}) async-start(bf16[8,40,1536]{2,1,0:T(8,128)(2,1)} %bitcast.46), calls=%async_computation.4 | async-start | bytes 1966080 | tf_op jit(solution)/shard_map/all_to_all | solution.py:346
  207.3 1.2 copy-start.13
  208.5 1.2 copy-start.15
  209.7 1.2 copy-start.17
  210.9 1.0 copy-start.24
  220.3 25.3 %copy-start.10 = (bf16[1,128,2048]{2,1,0:T(8,128)(2,1)S(1)}, bf16[1,128,2048]{2,1,0:T(8,128)(2,1)}, u32[]{:S(2)}) copy-start(bf16[1,128,2048]{2,1,0:T(8,128)(2,1)} %param.22) | copy-start | bytes 1572868
  220.3 25.3 %copy-start.21 = (bf16[128,2048]{1,0:T(8,128)(2,1)S(1)}, bf16[128,2048]{1,0:T(8,128)(2,1)}, u32[]{:S(2)}) copy-start(bf16[128,2048]{1,0:T(8,128)(2,1)} %copy-done.20) | copy-start | bytes 1572868

commit v2 on v1

--- a/solution.py
+++ b/solution.py
@@ -11,7 +11,7 @@
 BF = jnp.bfloat16
 F32 = jnp.float32
 MIB = 1 << 20
-ANY = pl.BlockSpec(memory_space=pl.ANY)
+HBM = pl.BlockSpec(memory_space=pltpu.HBM)
 VMEM = pl.BlockSpec(memory_space=pltpu.VMEM)
 SMEM = pl.BlockSpec(memory_space=pltpu.SMEM)
 NT = (((1,), (1,)), ((), ()))
@@ -22,16 +22,21 @@
     return lax.dot_general(a, b, dims, preferred_element_type=F32)
 
 
-def call(kernel, outs, args, in_specs, scratch=(), flops=0, moved=0, vmem=40):
+def call(kernel, outs, args, in_specs, scratch=(), flops=0, moved=0, vmem=16, after=()):
+    count, extra = len(args), len(after)
+
+    def body(*refs):
+        kernel(*refs[:count], *refs[count + extra :])
+
     return pl.pallas_call(
-        kernel,
+        body,
         out_shape=outs,
-        in_specs=in_specs,
+        in_specs=[*in_specs, *[HBM] * extra],
         out_specs=jax.tree.map(lambda _: VMEM, outs),
         scratch_shapes=list(scratch),
         compiler_params=pltpu.CompilerParams(vmem_limit_bytes=vmem * MIB),
         cost_estimate=pl.CostEstimate(flops=flops, bytes_accessed=moved, transcendentals=0),
-    )(*args)
+    )(*args, *after)
 
 
 def sds(shape, dtype=BF):
@@ -61,17 +66,14 @@
     )(q, k, v)
 
 
-def attend_kernel(x_ref, o_ref):
-    blocks, three, hd = x_ref.shape
-    rows = three // 3
+def attend_head(blocks, query_of, keys, vals, store):
+    rows = keys.shape[0] // blocks
     scale = HD ** (-0.5)
-    keys = x_ref[:, rows : 2 * rows, :].reshape(blocks * rows, hd)
-    vals = x_ref[:, 2 * rows : 3 * rows, :].reshape(blocks * rows, hd)
     row_ids = lax.broadcasted_iota(jnp.int32, (rows, rows), 0)
     col_ids = lax.broadcasted_iota(jnp.int32, (rows, rows), 1)
     keep = col_ids <= row_ids
     for b in range(blocks):
-        query = x_ref[b, 0:rows, :]
+        query = query_of(b)
         end = b * rows
         diag = mm(query, keys[end : end + rows], NT) * scale
         diag = jnp.where(keep, diag, -jnp.inf)
@@ -88,7 +90,23 @@
         ctx = mm((diag * inverse).astype(BF), vals[end : end + rows], NN)
         if b:
             ctx = ctx + mm((early * inverse).astype(BF), vals[:end], NN)
-        o_ref[b] = ctx.astype(BF)
+        store(b, ctx.astype(BF))
+
+
+def attend_kernel(x_ref, o_ref):
+    blocks, three, hd = x_ref.shape
+    rows = three // 3
+
+    def store(b, ctx):
+        o_ref[b] = ctx
+
+    attend_head(
+        blocks,
+        lambda b: x_ref[b, 0:rows, :],
+        x_ref[:, rows : 2 * rows, :].reshape(blocks * rows, hd),
+        x_ref[:, 2 * rows : 3 * rows, :].reshape(blocks * rows, hd),
+        store,
+    )
 
 
 def attend(x):
@@ -110,6 +128,117 @@
     )(x)
 
 
+INNER, COLS, PLANE, ATTEND = 0, 1, 5, 6
+
+
+def halves_kernel(place_ref, q_ref, k_ref, v_ref, first_ref, second_ref):
+    rows, width = q_ref.shape
+    half = width // 2
+
+    def copy(lower, upper):
+        for i, ref in enumerate((q_ref, k_ref, v_ref)):
+            lower[i * rows : (i + 1) * rows] = ref[:, :half]
+            upper[i * rows : (i + 1) * rows] = ref[:, half:]
+
+    @pl.when(place_ref[PLANE] < 2)
+    def _():
+        copy(first_ref, second_ref)
+
+    @pl.when(place_ref[PLANE] >= 2)
+    def _():
+        copy(second_ref, first_ref)
+
+
+def middle_kernel(place_ref, own_in, near_in, mid_in, far_in, *refs):
+    *outs, x_ref, ctx_ref, sems = refs
+    blocks, three, half = x_ref.shape
+    rows = three // 3
+
+    @pl.when(place_ref[INNER] == 1)
+    def _():
+        copies = [
+            pltpu.make_async_copy(ref, x_ref.at[place_ref[ATTEND + i]], sems.at[i])
+            for i, ref in enumerate((own_in, near_in, mid_in, far_in))
+        ]
+        for copy in copies:
+            copy.start()
+        for copy in copies:
+            copy.wait()
+
+        def step(i, carry):
+            for j in range(2):
+                cols = pl.ds(pl.multiple_of((2 * i + j) * HD, HD), HD)
+
+                def store(b, ctx, cols=cols):
+                    ctx_ref[b, :, cols] = ctx
+
+                attend_head(
+                    blocks,
+                    lambda b, cols=cols: x_ref[b, 0:rows, cols],
+                    x_ref[:, rows : 2 * rows, cols].reshape(blocks * rows, HD),
+                    x_ref[:, 2 * rows : 3 * rows, cols].reshape(blocks * rows, HD),
+                    store,
+                )
+            return carry
+
+        lax.fori_loop(0, half // HD // 2, step, 0)
+        for i, out in enumerate(outs):
+            out[...] = ctx_ref[place_ref[ATTEND + i]]
+
+
+def attend_middle(place, queries, keys, values, after):
+    rows, width = queries.shape
+    half = width // 2
+    block = sds((3 * rows, half))
+    first, second = call(
+        halves_kernel,
+        (block, block),
+        (place, queries, keys, values),
+        [SMEM, VMEM, VMEM, VMEM],
+        moved=12 * rows * width,
+    )
+    near = lax.ppermute(first, "seq", [(0, 1), (3, 2)])
+    mid = lax.ppermute(second, "seq", [(1, 2), (2, 1)])
+    far = lax.ppermute(second, "seq", [(0, 2), (3, 1)])
+    piece = sds((rows, half))
+    own, near, mid, far = call(
+        middle_kernel,
+        (piece,) * 4,
+        (place, first, near, mid, far),
+        [SMEM] + [HBM] * 4,
+        [
+            pltpu.VMEM((4, 3 * rows, half), BF),
+            pltpu.VMEM((4, rows, half), BF),
+            pltpu.SemaphoreType.DMA((4,)),
+        ],
+        flops=64 * rows * rows * half,
+        moved=32 * rows * half,
+        after=after,
+    )
+    near = lax.ppermute(near, "seq", [(1, 0), (2, 3)])
+    mid = lax.ppermute(mid, "seq", [(1, 2), (2, 1)])
+    far = lax.ppermute(far, "seq", [(2, 0), (1, 3)])
+    return own, near, mid, far
+
+
+def join_middle(place_ref, pieces, ctx_ref):
+    own, near, mid, far = pieces
+    half = own.shape[1]
+    for plane, (lower, upper) in enumerate(((near, far), (own, mid), (mid, own), (far, near))):
+
+        @pl.when(place_ref[PLANE] == plane)
+        def _(lower=lower, upper=upper):
+            ctx_ref[:, :half] = lower[...]
+            ctx_ref[:, half:] = upper[...]
+
+
+def join_groups(place_ref, pieces, ctx_ref):
+    (ctx,) = pieces
+    groups, _, part = ctx.shape
+    for g in range(groups):
+        ctx_ref[:, g * part : (g + 1) * part] = ctx[g]
+
+
 def slot_rows(ids_t, owners, cap):
     tokens = ids_t.shape[1]
     experts = lax.broadcasted_iota(jnp.int32, (owners, tokens), 0)
@@ -153,24 +282,20 @@
     ).astype(BF)
 
 
-def norm_kernel(owners, cap, ids_ref, ctx_ref, resid_ref, gain_ref, stream_ref, o_ref):
-    groups, tokens, part = ctx_ref.shape
-    width = groups * part
-    square = jnp.zeros((tokens, 1), F32)
-    for g in range(groups):
-        cols = slice(g * part, (g + 1) * part)
-        stream = (resid_ref[:, cols].astype(F32) + ctx_ref[g].astype(F32)).astype(BF)
-        stream_ref[:, cols] = stream
-        stream = stream.astype(F32)
-        square = square + jnp.sum(stream * stream, axis=-1, keepdims=True)
+def norm_kernel(owners, cap, join, place_ref, ids_ref, resid_ref, gain_ref, *refs):
+    *pieces, stream_ref, o_ref, ctx_ref = refs
+    tokens, width = resid_ref.shape
+    join(place_ref, pieces, ctx_ref)
+    stream = (resid_ref[...].astype(F32) + ctx_ref[...].astype(F32)).astype(BF)
+    stream_ref[...] = stream
+    stream = stream.astype(F32)
+    square = jnp.sum(stream * stream, axis=-1, keepdims=True)
     inv_rms = lax.rsqrt(square / width + 1e-05)
     at0, at1 = slot_rows(ids_ref[...], owners, cap)
     rows = lax.broadcasted_iota(jnp.int32, (owners * cap, tokens), 0)
     pick = one_hot((rows == at0) | (rows == at1))
-    for g in range(groups):
-        cols = slice(g * part, (g + 1) * part)
-        normed = ((stream_ref[:, cols].astype(F32) * inv_rms) * gain_ref[:, cols]).astype(BF)
-        o_ref[:, cols] = mm(pick, normed, NN).astype(BF)
+    normed = ((stream_ref[...].astype(F32) * inv_rms) * gain_ref[...]).astype(BF)
+    o_ref[...] = mm(pick, normed, NN).astype(BF)
 
 
 def fetch(inner, choices, dst, sem):
@@ -197,7 +322,7 @@
 
 
 def cols_of(place_ref, slot, part):
-    return pl.ds(pl.multiple_of(place_ref[1 + slot] * part, part), part)
+    return pl.ds(pl.multiple_of(place_ref[COLS + slot] * part, part), part)
 
 
 def up_kernel(shape, place_ref, x_ref, *refs):
@@ -206,7 +331,7 @@
     up_in, refs = regroup(refs, shape)
     hidden_ref, to_gate_ref, to_up_ref, gate_w, up_w, sems = refs
     part = gate_w.shape[2]
-    inner = place_ref[0]
+    inner = place_ref[INNER]
     for j in range(slots):
         fetch(inner, gate_in[j], gate_w.at[j], sems.at[0, j])
         fetch(inner, up_in[j], up_w.at[j], sems.at[1, j])
@@ -231,7 +356,7 @@
     down_in, refs = regroup(refs, shape)
     out_ref, d_hidden_ref, down_w, sems = refs
     part = down_w.shape[2]
-    inner = place_ref[0]
+    inner = place_ref[INNER]
     for j in range(slots):
         fetch(inner, down_in[j], down_w.at[j], sems.at[j])
     total = None
@@ -253,7 +378,7 @@
     up_in, refs = regroup(refs, shape)
     o_ref, down_w, gate_w, up_w, sems = refs
     part = down_w.shape[1]
-    inner = place_ref[0]
+    inner = place_ref[INNER]
     fetch(inner, down_in[0], down_w, sems.at[2, 0])
     for j in range(slots):
         fetch(inner, gate_in[j], gate_w.at[j], sems.at[0, j])
@@ -334,7 +459,13 @@
     if groups == 4:
         own = lax.axis_index("seq")
         table = jnp.array(
-            [[0, 0, 1, 2, 3], [1, 1, 0, 2, 3], [1, 2, 3, 1, 0], [0, 3, 2, 1, 0]], jnp.int32
+            [
+                [0, 0, 1, 2, 3, 0, 0, 0, 0, 0],
+                [1, 1, 0, 2, 3, 1, 1, 0, 2, 3],
+                [1, 2, 3, 1, 0, 2, 2, 3, 1, 0],
+                [0, 3, 2, 1, 0, 3, 0, 0, 0, 0],
+            ],
+            jnp.int32,
         )
         return table[own]
     return jnp.arange(-1, groups, dtype=jnp.int32)
@@ -378,14 +509,23 @@
     cot = cotangent[0]
     place = places(groups)
 
-    packed = pack(queries[0], keys[0], values[0], groups)
-    heads = lax.all_to_all(packed, "seq", split_axis=0, concat_axis=0, tiled=True)
     gate_in = gather_line(w_gate[0].T, groups)
     up_in = gather_line(w_up[0].T, groups)
     down_in = gather_line(w_down[0], groups)
     shape = [len(choices) for choices in gate_in]
-    ctx = attend(heads)
-    ctx = lax.all_to_all(ctx, "seq", split_axis=0, concat_axis=0, tiled=True)
+    if groups == 4:
+        join = join_middle
+        pieces = attend_middle(
+            place, queries[0], keys[0], values[0], (gate_in[1][0], gate_in[2][0])
+        )
+        before_norm = (up_in[1][0], up_in[2][0], down_in[1][0], gate_in[3][0], gate_in[2][1])
+    else:
+        join = join_groups
+        packed = pack(queries[0], keys[0], values[0], groups)
+        heads = lax.all_to_all(packed, "seq", split_axis=0, concat_axis=0, tiled=True)
+        ctx = attend(heads)
+        pieces = (lax.all_to_all(ctx, "seq", split_axis=0, concat_axis=0, tiled=True),)
+        before_norm = ()
 
     one = 2 * total * width * ffw
     send_cot = call(
@@ -398,12 +538,14 @@
     )
     cot_rows = exchange(send_cot, owners, "exp")
     stream, send_rows = call(
-        functools.partial(norm_kernel, owners, cap),
+        functools.partial(norm_kernel, owners, cap, join),
         (sds((tokens, width)), sds((total, width))),
-        (ids_t, ctx, resid[0], gain),
-        [VMEM] * 4,
+        (place, ids_t, resid[0], gain, *pieces),
+        [SMEM] + [VMEM] * (3 + len(pieces)),
+        [pltpu.VMEM((tokens, width), BF)],
         flops=2 * total * tokens * width,
         moved=2 * (total + 3 * tokens) * width,
+        after=before_norm,
     )
     rows = exchange(send_rows, owners, "exp")
 
@@ -412,16 +554,17 @@
         functools.partial(up_kernel, shape),
         (sds((total, ffw)), sds((total, ffw), F32), sds((total, ffw), F32)),
         (place, rows, *flat(gate_in), *flat(up_in)),
-        [SMEM, VMEM] + [ANY] * (2 * sum(shape)),
+        [SMEM, VMEM] + [HBM] * (2 * sum(shape)),
         [full_w, full_w, pltpu.SemaphoreType.DMA((2, groups))],
         flops=2 * one,
         moved=4 * width * ffw + 2 * total * width + 10 * total * ffw,
+        vmem=20,
     )
     out_first, d_hidden = call(
         functools.partial(down_kernel, shape[:-1]),
         (sds((total, width - part)), sds((total, ffw), F32)),
         (place, hidden, cot_rows, *flat(down_in[:-1])),
-        [SMEM, VMEM, VMEM] + [ANY] * sum(shape[:-1]),
+        [SMEM, VMEM, VMEM] + [HBM] * sum(shape[:-1]),
         [
             pltpu.VMEM((groups - 1, ffw, part), BF),
             pltpu.SemaphoreType.DMA((groups - 1,)),
@@ -444,7 +587,7 @@
             *flat(gate_in),
             *flat(up_in),
         ),
-        [SMEM] + [VMEM] * 5 + [ANY] * (shape[-1] + 2 * sum(shape)),
+        [SMEM] + [VMEM] * 5 + [HBM] * (shape[-1] + 2 * sum(shape)),
         [
             pltpu.VMEM((ffw, part), BF),
             full_w,
@@ -453,6 +596,7 @@
         ],
         flops=2 * one + 2 * one // groups,
         moved=4 * width * ffw + 4 * total * width + 14 * total * ffw,
+        vmem=22,
     )
     back_last = exchange(back, owners, "exp")
     output, stream_grad = call(

time: 250 us -> 274 us (1.096)
  blocking collectives: 68.6 us -> 25.5 us
  waiting for transfers between devices: 90.6 us -> 130 us
  local copies, waits for them, and re-layouts: 18.5 us -> 35.4 us
  starting transfers between devices: 37.6 us -> 52.7 us
  Pallas kernels: 32.6 us -> 28.4 us
    all_to_all x1 -> x0, blocking collectives: 43.3 us -> none  [per_device(): lax.all_to_all(packed, 'seq', split_axis=0, concat_axis=0, tiled=True)]
    ppermute x3, waiting for transfers between devices: 22.4 us -> 46.8 us  [gather_line(): near = lax.ppermute(shard, 'seq', [(0, 1), (1, 0), (2, 3), (3, 2)])]
    ppermute x0 -> x6, waiting for transfers between devices: none -> 23.5 us  [the longest x1 10.1 us: attend_middle(): far = lax.ppermute(far, 'seq', [(2, 0), (1, 3)])]
    ppermute x0 -> x6, starting transfers between devices: none -> 19 us  [the longest x1 9.39 us: attend_middle(): far = lax.ppermute(second, 'seq', [(0, 2), (3, 1)])]
    unnamed x60 -> x86, local copies, waits for them, and re-layouts: 17.7 us -> 34.5 us
    ppermute x3, waiting for transfers between devices: 26.9 us -> 15.2 us  [gather_line(): far = lax.ppermute(across, 'seq', [(1, 0), (2, 3)])]
    all_to_all x3, waiting for transfers between devices: 1.08 us -> 11.9 us  [exchange(): rows = lax.all_to_all(rows, axis, split_axis=0, concat_axis=0, tiled=True)]
    all_to_all x1 -> x0, waiting for transfers between devices: 7.59 us -> none  [per_device(): ctx = lax.all_to_all(ctx, 'seq', split_axis=0, concat_axis=0, tiled=True)]
  transfers between devices with their start and end apart: 19 -> 24, of which waited for: 11 -> 12; matrix products, arithmetic and copies ran while one was open for 0% -> 0% of each run, Pallas kernels for 8% -> 8%
where the time goes in v2:
time: 274 us; the launch traced here: 273 us
  waiting for transfers between devices  130 us (47%)
  starting transfers between devices  52.7 us (19%)
  local copies, waits for them, and re-layouts  35.4 us (13%)
  Pallas kernels  28.4 us (10%)
  blocking collectives  25.5 us (9%)
    ppermute x3, waiting for transfers between devices, gather_line(): near = lax.ppermute(shard, 'seq', [(0, 1), (1, 0), (2, 3), (3, 2)])  46.8 us
    unnamed x86, local copies, waits for them, and re-layouts  34.5 us
    ppermute x3, waiting for transfers between devices, gather_line(): far_near = lax.ppermute(across_near, 'seq', [(1, 0), (2, 3)])  32.1 us
    pallas_call x8, Pallas kernels, call(): pl.pallas_call(body, out_shape=outs, in_specs=[*in_specs, *[HBM] * extra]...  28.4 us
    all_to_all x1, blocking collectives, exchange(): rows = lax.all_to_all(rows, axis, split_axis=0, concat_axis=0, tiled=True)  25.5 us
    ppermute x3, waiting for transfers between devices, gather_line(): far = lax.ppermute(across, 'seq', [(1, 0), (2, 3)])  15.2 us
    all_to_all x3, starting transfers between devices, exchange(): rows = lax.all_to_all(rows, axis, split_axis=0, concat_axis=0, tiled=True)  12.9 us
    all_to_all x3, waiting for transfers between devices, exchange(): rows = lax.all_to_all(rows, axis, split_axis=0, concat_axis=0, tiled=True)  11.9 us
  transfers between devices with their start and end apart: 24, of which 12 were waited for; matrix products, arithmetic and copies ran while one was open for 0% of the time, Pallas kernels for 8%

profile of v2, /device:TPU:0, one launch (start us, length us, event | category | flops | bytes accessed | tf_op | source)
XLA Modules:
  0.0 272.5 jit_solution(17514274118288707919)
XLA Ops:
  5.2 5.0 %collective-permute-start = (bf16[384,1024]{1,0:T(8,128)(2,1)S(1)}, bf16[384,1024]{1,0:T(8,128)(2,1)S(1)}, u32[]{:S(2)}, u32[]{:S(2)}) collective-permute-start(bf16[384,1024]{1,0:T(8,128)(2,1)S(1)} %get-tuple-element.17.refs_1_), channel_id=1, source_target_pairs={{0,8},{24,16},{1,9},{25,17},{2,10},{26,18},{3,11},{27,19},{4,12},{... | collective-permute-start | bytes 2359304 | tf_op jit(solution)/shard_map/ppermute | solution.py:200
  11.8 9.4 %collective-permute-start.2 = (bf16[384,1024]{1,0:T(8,128)(2,1)S(1)}, bf16[384,1024]{1,0:T(8,128)(2,1)S(1)}, u32[]{:S(2)}, u32[]{:S(2)}) collective-permute-start(bf16[384,1024]{1,0:T(8,128)(2,1)S(1)} %get-tuple-element.18), channel_id=1, source_target_pairs={{0,16},{24,8},{1,17},{25,9},{2,18},{26,10},{3,19},{27,11},{4,20},{... | collective-permute-start | bytes 2359304 | tf_op jit(solution)/shard_map/ppermute | solution.py:202
  21.2 22.4 %collective-permute-done.3.refs_5_.refs_3_.refs_9_ = bf16[704,512]{1,0:T(8,128)(2,1)S(1)} collective-permute-done((bf16[704,512]{1,0:T(8,128)(2,1)S(1)}, bf16[704,512]{1,0:T(8,128)(2,1)S(1)}, u32[]{:S(2)}, u32[]{:S(2)}) %collective-permute-start.3) | collective-permute-done | bytes 720928 | tf_op jit(solution)/shard_map/ppermute | solution.py:448
  43.6 2.5 collective-permute-start.8
  46.8 2.9 %collective-permute-start.10 = (bf16[704,512]{1,0:T(8,128)(2,1)}, bf16[704,512]{1,0:T(8,128)(2,1)S(1)}, u32[]{:S(2)}, u32[]{:S(2)}) collective-permute-start(bf16[704,512]{1,0:T(8,128)(2,1)} %bitcast.53), channel_id=1, source_target_pairs={{0,8},{8,0},{16,24},{24,16},{1,9},{9,1},{17,25},{25,17},{2,10},{10... | collective-permute-start | bytes 2162696 | tf_op jit(solution)/shard_map/ppermute | solution.py:448
  49.6 1.6 collective-permute-start.11
  51.2 9.3 %collective-permute-done.2.refs_4_ = bf16[384,1024]{1,0:T(8,128)(2,1)S(1)} collective-permute-done((bf16[384,1024]{1,0:T(8,128)(2,1)S(1)}, bf16[384,1024]{1,0:T(8,128)(2,1)S(1)}, u32[]{:S(2)}, u32[]{:S(2)}) %collective-permute-start.2) | collective-permute-done | bytes 786464 | tf_op jit(solution)/shard_map/ppermute | solution.py:202
  60.5 1.3 collective-permute-start.12
  61.7 1.4 shard_map.132
  63.2 12.7 %collective-permute-done.8.refs_8_.refs_9_.refs_15_ = bf16[704,512]{1,0:T(8,128)(2,1)S(1)} collective-permute-done((bf16[704,512]{1,0:T(8,128)(2,1)S(1)}, bf16[704,512]{1,0:T(8,128)(2,1)S(1)}, u32[]{:S(2)}, u32[]{:S(2)}) %collective-permute-start.8) | collective-permute-done | bytes 720928 | tf_op jit(solution)/shard_map/ppermute | solution.py:448
  75.9 1.3 collective-permute-start.5
  77.2 1.4 collective-permute-start.6
  78.6 11.7 %collective-permute-done.10.refs_10_.refs_4_ = bf16[704,512]{1,0:T(8,128)(2,1)S(1)} collective-permute-done((bf16[704,512]{1,0:T(8,128)(2,1)}, bf16[704,512]{1,0:T(8,128)(2,1)S(1)}, u32[]{:S(2)}, u32[]{:S(2)}) %collective-permute-start.10) | collective-permute-done | bytes 720928 | tf_op jit(solution)/shard_map/ppermute | solution.py:448
  91.2 1.3 collective-permute-start.7
  92.7 4.1 %collective-permute-done.5.refs_5_ = bf16[128,1024]{1,0:T(8,128)(2,1)} collective-permute-done((bf16[128,1024]{1,0:T(8,128)(2,1)}, bf16[128,1024]{1,0:T(8,128)(2,1)}, u32[]{:S(2)}, u32[]{:S(2)}) %collective-permute-start.5) | collective-permute-done | bytes 262176 | tf_op jit(solution)/shard_map/ppermute | solution.py:218
  96.8 10.1 %collective-permute-done.7.refs_7_ = bf16[128,1024]{1,0:T(8,128)(2,1)} collective-permute-done((bf16[128,1024]{1,0:T(8,128)(2,1)}, bf16[128,1024]{1,0:T(8,128)(2,1)}, u32[]{:S(2)}, u32[]{:S(2)}) %collective-permute-start.7) | collective-permute-done | bytes 262176 | tf_op jit(solution)/shard_map/ppermute | solution.py:220
  109.1 2.0 shard_map.133
  111.8 1.1 copy-done.19
  112.9 4.4 %all-to-all-start = ((bf16[8,40,2048]{2,1,0:T(8,128)(2,1)}), bf16[8,40,2048]{2,1,0:T(8,128)(2,1)}, u32[]{:S(2)}, u32[]{:S(2)}) async-start(bf16[8,40,2048]{2,1,0:T(8,128)(2,1)} %bitcast.42), calls=%async_computation | async-start | bytes 2621440 | tf_op jit(solution)/shard_map/all_to_all | solution.py:477
  117.4 1.5 collective-permute-start.15
  118.9 1.6 collective-permute-start.17
  123.7 11.9 %all-to-all-done = bf16[8,40,2048]{2,1,0:T(8,128)(2,1)} async-done(((bf16[8,40,2048]{2,1,0:T(8,128)(2,1)}), bf16[8,40,2048]{2,1,0:T(8,128)(2,1)}, u32[]{:S(2)}, u32[]{:S(2)}) %all-to-all-start) | async-done | bytes 1310752 | tf_op jit(solution)/shard_map/all_to_all | solution.py:477
  135.6 4.3 %all-to-all-start.1 = ((bf16[8,40,2048]{2,1,0:T(8,128)(2,1)}), bf16[8,40,2048]{2,1,0:T(8,128)(2,1)}, u32[]{:S(2)}, u32[]{:S(2)}) async-start(bf16[8,40,2048]{2,1,0:T(8,128)(2,1)} %bitcast.31), calls=%async_computation.1 | async-start | bytes 2621440 | tf_op jit(solution)/shard_map/all_to_all | solution.py:477
  139.9 1.5 collective-permute-start.19
  141.4 1.3 collective-permute-start.14
  142.7 1.3 collective-permute-start.13
  144.0 1.3 collective-permute-start.16
  145.3 1.3 collective-permute-start.18
  146.6 1.3 collective-permute-start.20
  147.9 14.3 %collective-permute-done.14.refs_11_.refs_17_ = bf16[704,512]{1,0:T(8,128)(2,1)S(1)} collective-permute-done((bf16[704,512]{1,0:T(8,128)(2,1)S(1)}, bf16[704,512]{1,0:T(8,128)(2,1)S(1)}, u32[]{:S(2)}, u32[]{:S(2)}) %collective-permute-start.14) | collective-permute-done | bytes 720928 | tf_op jit(solution)/shard_map/ppermute | solution.py:451
  162.3 15.4 %collective-permute-done.13.refs_7_.refs_13_ = bf16[704,512]{1,0:T(8,128)(2,1)S(1)} collective-permute-done((bf16[704,512]{1,0:T(8,128)(2,1)}, bf16[704,512]{1,0:T(8,128)(2,1)S(1)}, u32[]{:S(2)}, u32[]{:S(2)}) %collective-permute-start.13) | collective-permute-done | bytes 720928 | tf_op jit(solution)/shard_map/ppermute | solution.py:452
  177.7 15.4 %collective-permute-done.16.refs_13_.refs_19_ = bf16[704,512]{1,0:T(8,128)(2,1)S(1)} collective-permute-done((bf16[704,512]{1,0:T(8,128)(2,1)}, bf16[704,512]{1,0:T(8,128)(2,1)S(1)}, u32[]{:S(2)}, u32[]{:S(2)}) %collective-permute-start.16) | collective-permute-done | bytes 720928 | tf_op jit(solution)/shard_map/ppermute | solution.py:452
  193.2 1.1 copy-done.6
  195.4 7.1 %shard_map.134 = (bf16[320,704]{1,0:T(8,128)(2,1)S(1)}, f32[320,704]{1,0:T(8,128)S(1)}, f32[320,704]{1,0:T(8,128)S(1)}) custom-call(s32[10]{0:T(128)S(1)} %dynamic-slice_bitcast_fusion.refs_0_, bf16[320,2048]{1,0:T(8,128)(2,1)} %bitcast.18.refs_1_, bf16[704,512]{1,0:T(8,128)(2,1)S(1)} %bitcast.34, ...), custom_call_target="tpu_custom_call" | custom-call | flops 1845493760 | bytes 9330688 | tf_op jit(solution)/shard_map/pallas_call | solution.py:31
  208.7 1.1 copy-done.28
  210.8 1.1 copy-done.39
  212.0 5.3 %shard_map.136 = (bf16[320,1536]{1,0:T(8,128)(2,1)}, f32[320,704]{1,0:T(8,128)S(1)}) custom-call(s32[10]{0:T(128)S(1)} %dynamic-slice_bitcast_fusion.refs_0_, bf16[320,704]{1,0:T(8,128)(2,1)S(1)} %copy-done.36, bf16[320,2048]{1,0:T(8,128)(2,1)} %bitcast.20.refs_2_, bf16[704,512]{1,0:T(8,128)(2,1)S(1)} %bitcast.55, bf16[704,512]{1,0:T(8,128)(2,1)S(1)} %copy-done.28, ...), custom_call_target="tpu_custom_call" | custom-call | flops 1384120320 | bytes 6856704 | tf_op jit(solution)/shard_map/pallas_call | solution.py:31
  218.2 4.2 %all-to-all-start.2 = ((bf16[8,40,1536]{2,1,0:T(8,128)(2,1)}), bf16[8,40,1536]{2,1,0:T(8,128)(2,1)}, u32[]{:S(2)}, u32[]{:S(2)}) async-start(bf16[8,40,1536]{2,1,0:T(8,128)(2,1)} %bitcast.21), calls=%async_computation.2 | async-start | bytes 1966080 | tf_op jit(solution)/shard_map/all_to_all | solution.py:477
  222.4 1.2 collective-permute-done.20.refs_7_
  223.6 1.1 copy-done.1
  224.7 1.1 copy-done.3
  225.8 1.1 copy-done.7
  231.4 1.2 copy-done.21
  232.6 1.2 copy-done.23
  233.8 1.2 copy-done.25
  236.0 7.2 %shard_map.137 = bf16[320,2560]{1,0:T(8,128)(2,1)S(1)} custom-call(s32[10]{0:T(128)S(1)} %dynamic-slice_bitcast_fusion.refs_0_, bf16[320,704]{1,0:T(8,128)(2,1)S(1)} %copy-done.37, bf16[320,2048]{1,0:T(8,128)(2,1)} %bitcast.20.refs_2_, f32[320,704]{1,0:T(8,128)S(1)} %copy-done.25, f32[320,704]{1,0:T(8,128)S(1)} %copy-done.21, f32[320,704]{1,0:T(8,128)S(1)} %copy-done.23, ...), custom_call_target="tpu_custom_call" | custom-call | flops 2306867200 | bytes 11542528 | tf_op jit(solution)/shard_map/pallas_call | solution.py:31
  243.2 25.5 %all_to_all.20 = bf16[8,40,2560]{2,1,0:T(8,128)(2,1)S(1)} all-to-all(bf16[8,40,2560]{2,1,0:T(8,128)(2,1)S(1)} %bitcast.29), channel_id=1, replica_groups=mesh['seq'=4,'exp'=8] {'exp'}, dimensions={0} | all-to-all | bytes 3276800 | tf_op jit(solution)/shard_map/all_to_all | solution.py:477
  268.7 3.8 %shard_map.138 = (bf16[128,2048]{1,0:T(8,128)(2,1)}, bf16[128,2048]{1,0:T(8,128)(2,1)}) custom-call(s32[10]{0:T(128)S(1)} %dynamic-slice_bitcast_fusion.refs_0_, s32[128,2]{1,0:T(8,128)S(1)} %bitcast.46, f32[128,2]{1,0:T(8,128)S(1)} %bitcast.44, f32[1,2048]{1,0:T(1,128)S(1)} %bitcast.52, bf16[128,2048]{1,0:T(8,128)(2,1)S(1)} %copy-done.34, ...), custom_call_target="tpu_custom_call" | custom-call | flops 503316480 | bytes 4718592 | tf_op jit(solution)/shard_map/pallas_call | solution.py:31
  (97 shorter events, 28.7 us)
Async XLA Ops:
  0.6 9.6 %copy-start.5 = (bf16[1,512,704]{1,2,0:T(8,128)(2,1)S(1)}, bf16[1,512,704]{1,2,0:T(8,128)(2,1)}, u32[]{:S(2)}) copy-start(bf16[1,512,704]{1,2,0:T(8,128)(2,1)} %param.17) | copy-start | bytes 2162692
  0.6 42.9 %copy-start.8 = (bf16[1,512,704]{1,2,0:T(8,128)(2,1)S(1)}, bf16[1,512,704]{1,2,0:T(8,128)(2,1)}, u32[]{:S(2)}) copy-start(bf16[1,512,704]{1,2,0:T(8,128)(2,1)} %param.18) | copy-start | bytes 2162692
  5.2 41.5 %collective-permute-start = (bf16[384,1024]{1,0:T(8,128)(2,1)S(1)}, bf16[384,1024]{1,0:T(8,128)(2,1)S(1)}, u32[]{:S(2)}, u32[]{:S(2)}) collective-permute-start(bf16[384,1024]{1,0:T(8,128)(2,1)S(1)} %get-tuple-element.17.refs_1_), channel_id=1, source_target_pairs={{0,8},{24,16},{1,9},{25,17},{2,10},{26,18},{3,11},{27,19},{4,12},{... | collective-permute-start | bytes 2359304 | tf_op jit(solution)/shard_map/ppermute | solution.py:200
  10.2 33.3 %collective-permute-start.3 = (bf16[704,512]{1,0:T(8,128)(2,1)S(1)}, bf16[704,512]{1,0:T(8,128)(2,1)S(1)}, u32[]{:S(2)}, u32[]{:S(2)}) collective-permute-start(bf16[704,512]{1,0:T(8,128)(2,1)S(1)} %bitcast.32), channel_id=1, source_target_pairs={{0,8},{8,0},{16,24},{24,16},{1,9},{9,1},{17,25},{25,17},{2,10},{10... | collective-permute-start | bytes 2162696 | tf_op jit(solution)/shard_map/ppermute | solution.py:448
  10.3 35.7 %collective-permute-start.4 = (bf16[704,512]{1,0:T(8,128)(2,1)S(1)}, bf16[704,512]{1,0:T(8,128)(2,1)S(1)}, u32[]{:S(2)}, u32[]{:S(2)}) collective-permute-start(bf16[704,512]{1,0:T(8,128)(2,1)S(1)} %bitcast.33), channel_id=1, source_target_pairs={{8,16},{16,8},{9,17},{17,9},{10,18},{18,10},{11,19},{19,11},{12,20... | collective-permute-start | bytes 2162696 | tf_op jit(solution)/shard_map/ppermute | solution.py:449
  11.0 38.6 %collective-permute-start.1 = (bf16[384,1024]{1,0:T(8,128)(2,1)S(1)}, bf16[384,1024]{1,0:T(8,128)(2,1)S(1)}, u32[]{:S(2)}, u32[]{:S(2)}) collective-permute-start(bf16[384,1024]{1,0:T(8,128)(2,1)S(1)} %get-tuple-element.18), channel_id=1, source_target_pairs={{8,16},{16,8},{9,17},{17,9},{10,18},{18,10},{11,19},{19,11},{12,20... | collective-permute-start | bytes 2359304 | tf_op jit(solution)/shard_map/ppermute | solution.py:201
  11.8 48.7 %collective-permute-start.2 = (bf16[384,1024]{1,0:T(8,128)(2,1)S(1)}, bf16[384,1024]{1,0:T(8,128)(2,1)S(1)}, u32[]{:S(2)}, u32[]{:S(2)}) collective-permute-start(bf16[384,1024]{1,0:T(8,128)(2,1)S(1)} %get-tuple-element.18), channel_id=1, source_target_pairs={{0,16},{24,8},{1,17},{25,9},{2,18},{26,10},{3,19},{27,11},{4,20},{... | collective-permute-start | bytes 2359304 | tf_op jit(solution)/shard_map/ppermute | solution.py:202
  43.6 32.3 %collective-permute-start.8 = (bf16[704,512]{1,0:T(8,128)(2,1)S(1)}, bf16[704,512]{1,0:T(8,128)(2,1)S(1)}, u32[]{:S(2)}, u32[]{:S(2)}) collective-permute-start(bf16[704,512]{1,0:T(8,128)(2,1)S(1)} %bitcast.36), channel_id=1, source_target_pairs={{0,8},{8,0},{16,24},{24,16},{1,9},{9,1},{17,25},{25,17},{2,10},{10... | collective-permute-start | bytes 2162696 | tf_op jit(solution)/shard_map/ppermute | solution.py:448
  46.0 31.1 %collective-permute-start.9 = (bf16[704,512]{1,0:T(8,128)(2,1)S(1)}, bf16[704,512]{1,0:T(8,128)(2,1)S(1)}, u32[]{:S(2)}, u32[]{:S(2)}) collective-permute-start(bf16[704,512]{1,0:T(8,128)(2,1)S(1)} %bitcast.37), channel_id=1, source_target_pairs={{8,16},{16,8},{9,17},{17,9},{10,18},{18,10},{11,19},{19,11},{12,20... | collective-permute-start | bytes 2162696 | tf_op jit(solution)/shard_map/ppermute | solution.py:449
  46.8 45.7 %copy-start.40 = (s32[1,128,2]{1,2,0:T(2,128)S(1)}, s32[1,128,2]{1,2,0:T(2,128)}, u32[]{:S(2)}) copy-start(s32[1,128,2]{1,2,0:T(2,128)} %param.20) | copy-start | bytes 3076
  46.8 60.1 %copy-start.38 = (f32[2048]{0:T(1024)S(1)}, f32[2048]{0:T(1024)}, u32[]{:S(2)}) copy-start(f32[2048]{0:T(1024)} %param.16) | copy-start | bytes 24580
  46.8 43.5 %collective-permute-start.10 = (bf16[704,512]{1,0:T(8,128)(2,1)}, bf16[704,512]{1,0:T(8,128)(2,1)S(1)}, u32[]{:S(2)}, u32[]{:S(2)}) collective-permute-start(bf16[704,512]{1,0:T(8,128)(2,1)} %bitcast.53), channel_id=1, source_target_pairs={{0,8},{8,0},{16,24},{24,16},{1,9},{9,1},{17,25},{25,17},{2,10},{10... | collective-permute-start | bytes 2162696 | tf_op jit(solution)/shard_map/ppermute | solution.py:448
  49.6 57.3 %collective-permute-start.11 = (bf16[704,512]{1,0:T(8,128)(2,1)S(1)}, bf16[704,512]{1,0:T(8,128)(2,1)}, u32[]{:S(2)}, u32[]{:S(2)}) collective-permute-start(bf16[704,512]{1,0:T(8,128)(2,1)S(1)} %collective-permute-done.3.refs_5_.refs_3_.refs_9_), channel_id=1, source_target_pairs={{8,16},{16,8},{9,17},{17,9},{10,18},{18,10},{11,19},{19,11},{12,20... | collective-permute-start | bytes 2162696 | tf_op jit(solution)/shard_map/ppermute | solution.py:450
  60.5 46.5 %collective-permute-start.12 = (bf16[704,512]{1,0:T(8,128)(2,1)S(1)}, bf16[704,512]{1,0:T(8,128)(2,1)}, u32[]{:S(2)}, u32[]{:S(2)}) collective-permute-start(bf16[704,512]{1,0:T(8,128)(2,1)S(1)} %collective-permute-done.4.refs_6_.refs_4_.refs_10_), channel_id=1, source_target_pairs={{8,0},{16,24},{9,1},{17,25},{10,2},{18,26},{11,3},{19,27},{12,4},{... | collective-permute-start | bytes 2162696 | tf_op jit(solution)/shard_map/ppermute | solution.py:451
  75.9 117.2 %copy-start = (bf16[704,512]{1,0:T(8,128)(2,1)}, bf16[704,512]{1,0:T(8,128)(2,1)S(1)}, u32[]{:S(2)}) copy-start(bf16[704,512]{1,0:T(8,128)(2,1)S(1)} %collective-permute-done.8.refs_8_.refs_9_.refs_15_) | copy-start | bytes 2162692
  75.9 20.9 %collective-permute-start.5 = (bf16[128,1024]{1,0:T(8,128)(2,1)}, bf16[128,1024]{1,0:T(8,128)(2,1)}, u32[]{:S(2)}, u32[]{:S(2)}) collective-permute-start(bf16[128,1024]{1,0:T(8,128)(2,1)} %get-tuple-element.20), channel_id=1, source_target_pairs={{8,0},{16,24},{9,1},{17,25},{10,2},{18,26},{11,3},{19,27},{12,4},{... | collective-permute-start | bytes 786440 | tf_op jit(solution)/shard_map/ppermute | solution.py:218
  77.2 116.0 %copy-start.2 = (bf16[704,512]{1,0:T(8,128)(2,1)}, bf16[704,512]{1,0:T(8,128)(2,1)S(1)}, u32[]{:S(2)}) copy-start(bf16[704,512]{1,0:T(8,128)(2,1)S(1)} %collective-permute-done.9.refs_9_.refs_10_.refs_16_) | copy-start | bytes 2162692
  77.2 19.6 %collective-permute-start.6 = (bf16[128,1024]{1,0:T(8,128)(2,1)}, bf16[128,1024]{1,0:T(8,128)(2,1)}, u32[]{:S(2)}, u32[]{:S(2)}) collective-permute-start(bf16[128,1024]{1,0:T(8,128)(2,1)} %get-tuple-element.21), channel_id=1, source_target_pairs={{8,16},{16,8},{9,17},{17,9},{10,18},{18,10},{11,19},{19,11},{12,20... | collective-permute-start | bytes 786440 | tf_op jit(solution)/shard_map/ppermute | solution.py:219
  91.2 15.7 %collective-permute-start.7 = (bf16[128,1024]{1,0:T(8,128)(2,1)}, bf16[128,1024]{1,0:T(8,128)(2,1)}, u32[]{:S(2)}, u32[]{:S(2)}) collective-permute-start(bf16[128,1024]{1,0:T(8,128)(2,1)} %get-tuple-element.22), channel_id=1, source_target_pairs={{16,0},{8,24},{17,1},{9,25},{18,2},{10,26},{19,3},{11,27},{20,4},{... | collective-permute-start | bytes 786440 | tf_op jit(solution)/shard_map/ppermute | solution.py:220
  106.9 1.1 copy-start.27
  111.8 1.1 copy-start.19
  112.9 7.5 %copy-start.41 = (f32[1,128,2]{1,2,0:T(2,128)S(1)}, f32[1,128,2]{1,2,0:T(2,128)}, u32[]{:S(2)}) copy-start(f32[1,128,2]{1,2,0:T(2,128)} %param.21) | copy-start | bytes 3076
  112.9 22.6 %all-to-all-start = ((bf16[8,40,2048]{2,1,0:T(8,128)(2,1)}), bf16[8,40,2048]{2,1,0:T(8,128)(2,1)}, u32[]{:S(2)}, u32[]{:S(2)}) async-start(bf16[8,40,2048]{2,1,0:T(8,128)(2,1)} %bitcast.42), calls=%async_computation | async-start | bytes 2621440 | tf_op jit(solution)/shard_map/all_to_all | solution.py:477
  117.4 26.6 %collective-permute-start.15 = (bf16[704,512]{1,0:T(8,128)(2,1)S(1)}, bf16[704,512]{1,0:T(8,128)(2,1)}, u32[]{:S(2)}, u32[]{:S(2)}) collective-permute-start(bf16[704,512]{1,0:T(8,128)(2,1)S(1)} %collective-permute-done.8.refs_8_.refs_9_.refs_15_), channel_id=1, source_target_pairs={{8,16},{16,8},{9,17},{17,9},{10,18},{18,10},{11,19},{19,11},{12,20... | collective-permute-start | bytes 2162696 | tf_op jit(solution)/shard_map/ppermute | solution.py:450
  118.9 26.4 %collective-permute-start.17 = (bf16[704,512]{1,0:T(8,128)(2,1)}, bf16[704,512]{1,0:T(8,128)(2,1)}, u32[]{:S(2)}, u32[]{:S(2)}) collective-permute-start(bf16[704,512]{1,0:T(8,128)(2,1)} %bitcast.54), channel_id=1, source_target_pairs={{8,16},{16,8},{9,17},{17,9},{10,18},{18,10},{11,19},{19,11},{12,20... | collective-permute-start | bytes 2162696 | tf_op jit(solution)/shard_map/ppermute | solution.py:449
  135.6 72.3 %all-to-all-start.1 = ((bf16[8,40,2048]{2,1,0:T(8,128)(2,1)}), bf16[8,40,2048]{2,1,0:T(8,128)(2,1)}, u32[]{:S(2)}, u32[]{:S(2)}) async-start(bf16[8,40,2048]{2,1,0:T(8,128)(2,1)} %bitcast.31), calls=%async_computation.1 | async-start | bytes 2621440 | tf_op jit(solution)/shard_map/all_to_all | solution.py:477
  139.9 6.7 %collective-permute-start.19 = (bf16[704,512]{1,0:T(8,128)(2,1)}, bf16[704,512]{1,0:T(8,128)(2,1)}, u32[]{:S(2)}, u32[]{:S(2)}) collective-permute-start(bf16[704,512]{1,0:T(8,128)(2,1)} %copy-done.26), channel_id=1, source_target_pairs={{8,16},{16,8},{9,17},{17,9},{10,18},{18,10},{11,19},{19,11},{12,20... | collective-permute-start | bytes 2162696 | tf_op jit(solution)/shard_map/ppermute | solution.py:450
  141.4 20.9 %collective-permute-start.14 = (bf16[704,512]{1,0:T(8,128)(2,1)S(1)}, bf16[704,512]{1,0:T(8,128)(2,1)S(1)}, u32[]{:S(2)}, u32[]{:S(2)}) collective-permute-start(bf16[704,512]{1,0:T(8,128)(2,1)S(1)} %collective-permute-done.9.refs_9_.refs_10_.refs_16_), channel_id=1, source_target_pairs={{8,0},{16,24},{9,1},{17,25},{10,2},{18,26},{11,3},{19,27},{12,4},{... | collective-permute-start | bytes 2162696 | tf_op jit(solution)/shard_map/ppermute | solution.py:451
  142.7 35.0 %collective-permute-start.13 = (bf16[704,512]{1,0:T(8,128)(2,1)}, bf16[704,512]{1,0:T(8,128)(2,1)S(1)}, u32[]{:S(2)}, u32[]{:S(2)}) collective-permute-start(bf16[704,512]{1,0:T(8,128)(2,1)} %collective-permute-done.11.refs_11_.refs_6_.refs_12_), channel_id=1, source_target_pairs={{8,0},{16,24},{9,1},{17,25},{10,2},{18,26},{11,3},{19,27},{12,4},{... | collective-permute-start | bytes 2162696 | tf_op jit(solution)/shard_map/ppermute | solution.py:452
  144.0 49.1 %collective-permute-start.16 = (bf16[704,512]{1,0:T(8,128)(2,1)}, bf16[704,512]{1,0:T(8,128)(2,1)S(1)}, u32[]{:S(2)}, u32[]{:S(2)}) collective-permute-start(bf16[704,512]{1,0:T(8,128)(2,1)} %collective-permute-done.15.refs_12_.refs_18_), channel_id=1, source_target_pairs={{8,0},{16,24},{9,1},{17,25},{10,2},{18,26},{11,3},{19,27},{12,4},{... | collective-permute-start | bytes 2162696 | tf_op jit(solution)/shard_map/ppermute | solution.py:452
  145.3 63.4 %collective-permute-start.18 = (bf16[704,512]{1,0:T(8,128)(2,1)}, bf16[704,512]{1,0:T(8,128)(2,1)}, u32[]{:S(2)}, u32[]{:S(2)}) collective-permute-start(bf16[704,512]{1,0:T(8,128)(2,1)} %collective-permute-done.17.refs_5_), channel_id=1, source_target_pairs={{8,0},{16,24},{9,1},{17,25},{10,2},{18,26},{11,3},{19,27},{12,4},{... | collective-permute-start | bytes 2162696 | tf_op jit(solution)/shard_map/ppermute | solution.py:451
  146.6 77.0 %collective-permute-start.20 = (bf16[704,512]{1,0:T(8,128)(2,1)}, bf16[704,512]{1,0:T(8,128)(2,1)}, u32[]{:S(2)}, u32[]{:S(2)}) collective-permute-start(bf16[704,512]{1,0:T(8,128)(2,1)} %collective-permute-done.19.refs_6_), channel_id=1, source_target_pairs={{8,0},{16,24},{9,1},{17,25},{10,2},{18,26},{11,3},{19,27},{12,4},{... | collective-permute-start | bytes 2162696 | tf_op jit(solution)/shard_map/ppermute | solution.py:452
  193.2 1.1 copy-start.6
  194.3 1.1 copy-start.9
  208.7 1.1 copy-start.28
  210.8 1.1 copy-start.39
  218.2 25.0 %all-to-all-start.2 = ((bf16[8,40,1536]{2,1,0:T(8,128)(2,1)}), bf16[8,40,1536]{2,1,0:T(8,128)(2,1)}, u32[]{:S(2)}, u32[]{:S(2)}) async-start(bf16[8,40,1536]{2,1,0:T(8,128)(2,1)} %bitcast.21), calls=%async_computation.2 | async-start | bytes 1966080 | tf_op jit(solution)/shard_map/all_to_all | solution.py:477
  223.6 1.1 copy-start.1
  224.7 1.1 copy-start.3
  225.8 1.1 copy-start.7
  226.9 1.1 copy-start.10
  228.0 1.1 copy-start.12
  229.1 1.1 copy-start.14
  231.4 1.2 copy-start.21
  232.6 1.2 copy-start.23
  233.8 1.2 copy-start.25
  243.2 25.5 %copy-start.18 = (bf16[1,128,2048]{2,1,0:T(8,128)(2,1)S(1)}, bf16[1,128,2048]{2,1,0:T(8,128)(2,1)}, u32[]{:S(2)}) copy-start(bf16[1,128,2048]{2,1,0:T(8,128)(2,1)} %param.22) | copy-start | bytes 1572868
  243.2 25.5 %copy-start.34 = (bf16[128,2048]{1,0:T(8,128)(2,1)S(1)}, bf16[128,2048]{1,0:T(8,128)(2,1)}, u32[]{:S(2)}) copy-start(bf16[128,2048]{1,0:T(8,128)(2,1)} %copy-done.33) | copy-start | bytes 1572868
  (18 other events, 17.4 us)

commit v3 on v2

--- a/solution.py
+++ b/solution.py
@@ -22,7 +22,11 @@
     return lax.dot_general(a, b, dims, preferred_element_type=F32)
 
 
-def call(kernel, outs, args, in_specs, scratch=(), flops=0, moved=0, vmem=16, after=()):
+def whole(array):
+    return pl.BlockSpec(array.shape, lambda i: (0,) * len(array.shape))
+
+
+def call(kernel, outs, args, in_specs, scratch=(), flops=0, moved=0, vmem=56, after=()):
     count, extra = len(args), len(after)
 
     def body(*refs):
@@ -30,13 +34,21 @@
 
     return pl.pallas_call(
         body,
+        grid=(1,),
         out_shape=outs,
-        in_specs=[*in_specs, *[HBM] * extra],
-        out_specs=jax.tree.map(lambda _: VMEM, outs),
+        in_specs=[
+            *[whole(arg) if spec is VMEM else spec for arg, spec in zip(args, in_specs)],
+            *[HBM] * extra,
+        ],
+        out_specs=jax.tree.map(whole, outs),
         scratch_shapes=list(scratch),
         compiler_params=pltpu.CompilerParams(vmem_limit_bytes=vmem * MIB),
         cost_estimate=pl.CostEstimate(flops=flops, bytes_accessed=moved, transcendentals=0),
     )(*args, *after)
+
+
+def gated(array, *first):
+    return lax.optimization_barrier((array, *first))[0] if first else array
 
 
 def sds(shape, dtype=BF):
@@ -186,7 +198,7 @@
             out[...] = ctx_ref[place_ref[ATTEND + i]]
 
 
-def attend_middle(place, queries, keys, values, after):
+def line_of_four(place, queries, keys, values, gate, up, down):
     rows, width = queries.shape
     half = width // 2
     block = sds((3 * rows, half))
@@ -197,11 +209,13 @@
         [SMEM, VMEM, VMEM, VMEM],
         moved=12 * rows * width,
     )
-    near = lax.ppermute(first, "seq", [(0, 1), (3, 2)])
-    mid = lax.ppermute(second, "seq", [(1, 2), (2, 1)])
-    far = lax.ppermute(second, "seq", [(0, 2), (3, 1)])
+    gate_end = send(gate, OUTWARD)
+    up_end = send(up, OUTWARD)
+    near = send(first, INWARD)
+    mid = send(second, MIDDLE)
+    far = send(second, [(0, 2), (3, 1)])
     piece = sds((rows, half))
-    own, near, mid, far = call(
+    pieces = call(
         middle_kernel,
         (piece,) * 4,
         (place, first, near, mid, far),
@@ -213,12 +227,44 @@
         ],
         flops=64 * rows * rows * half,
         moved=32 * rows * half,
-        after=after,
-    )
-    near = lax.ppermute(near, "seq", [(1, 0), (2, 3)])
-    mid = lax.ppermute(mid, "seq", [(1, 2), (2, 1)])
-    far = lax.ppermute(far, "seq", [(2, 0), (1, 3)])
-    return own, near, mid, far
+        after=(gate_end, up_end),
+    )
+    gate_inner = send(gate, INWARD, near, far)
+    gate_mid = send(gate, MIDDLE, mid, far)
+    down_end = send(down, OUTWARD, gate_end, up_end)
+    own, near, mid, far = lax.optimization_barrier((*pieces, gate_mid, gate_inner, down_end))[:4]
+    near = send(near, OUTWARD)
+    mid = send(mid, MIDDLE)
+    far = send(far, [(2, 0), (1, 3)])
+    gate_mid_near = send(gate_inner, MIDDLE, gate_mid)
+    gate_far = send(gate_mid, OUTWARD, down_end)
+    up_mid = send(up, MIDDLE, gate_mid)
+    up_inner = send(up, INWARD, gate_inner)
+    norm_after = (gate_mid_near, gate_far, up_mid, up_inner)
+    gate_far_near = send(gate_mid_near, OUTWARD, gate_far)
+    up_far = send(up_mid, OUTWARD, gate_far)
+    up_mid_near = send(up_inner, MIDDLE, gate_mid_near)
+    down_mid = send(down, MIDDLE, up_mid)
+    down_inner = send(down, INWARD, up_inner)
+    up_far_near = send(up_mid_near, OUTWARD, gate_far_near)
+    down_far = send(down_mid, OUTWARD, up_far)
+    down_mid_near = send(down_inner, MIDDLE, down_mid)
+    up_after = (down_mid_near,)
+    down_far_near = send(down_mid_near, OUTWARD, up_far_near)
+    gate_in = [
+        [gate],
+        [gate_inner, gate_end],
+        [gate_mid, gate_far],
+        [gate_mid_near, gate_far_near],
+    ]
+    up_in = [[up], [up_inner, up_end], [up_mid, up_far], [up_mid_near, up_far_near]]
+    down_in = [
+        [down],
+        [down_inner, down_end],
+        [down_mid, down_far],
+        [down_mid_near, down_far_near],
+    ]
+    return (own, near, mid, far), gate_in, up_in, down_in, norm_after, up_after
 
 
 def join_middle(place_ref, pieces, ctx_ref):
@@ -443,16 +489,18 @@
     grad_ref[...] = (cot_ref[...].astype(F32) + d_stream).astype(BF)
 
 
-def gather_line(shard, groups):
-    if groups == 4:
-        near = lax.ppermute(shard, "seq", [(0, 1), (1, 0), (2, 3), (3, 2)])
-        across = lax.ppermute(shard, "seq", [(1, 2), (2, 1)])
-        across_near = lax.ppermute(near, "seq", [(1, 2), (2, 1)])
-        far = lax.ppermute(across, "seq", [(1, 0), (2, 3)])
-        far_near = lax.ppermute(across_near, "seq", [(1, 0), (2, 3)])
-        return [[shard], [near], [across, far], [across_near, far_near]]
-    whole = lax.all_gather(shard, "seq", axis=0)
-    return [[whole[j]] for j in range(groups)]
+MIDDLE = [(1, 2), (2, 1)]
+OUTWARD = [(1, 0), (2, 3)]
+INWARD = [(0, 1), (3, 2)]
+
+
+def gather_all(shard, groups):
+    whole_weight = lax.all_gather(shard, "seq", axis=0)
+    return [[whole_weight[j]] for j in range(groups)]
+
+
+def send(array, pairs, *first):
+    return lax.ppermute(gated(array, *first), "seq", pairs)
 
 
 def places(groups):
@@ -509,23 +557,21 @@
     cot = cotangent[0]
     place = places(groups)
 
-    gate_in = gather_line(w_gate[0].T, groups)
-    up_in = gather_line(w_up[0].T, groups)
-    down_in = gather_line(w_down[0], groups)
-    shape = [len(choices) for choices in gate_in]
+    shards = (w_gate[0].T, w_up[0].T, w_down[0])
     if groups == 4:
         join = join_middle
-        pieces = attend_middle(
-            place, queries[0], keys[0], values[0], (gate_in[1][0], gate_in[2][0])
+        pieces, gate_in, up_in, down_in, norm_after, up_after = line_of_four(
+            place, queries[0], keys[0], values[0], *shards
         )
-        before_norm = (up_in[1][0], up_in[2][0], down_in[1][0], gate_in[3][0], gate_in[2][1])
     else:
         join = join_groups
+        gate_in, up_in, down_in = [gather_all(shard, groups) for shard in shards]
         packed = pack(queries[0], keys[0], values[0], groups)
         heads = lax.all_to_all(packed, "seq", split_axis=0, concat_axis=0, tiled=True)
         ctx = attend(heads)
         pieces = (lax.all_to_all(ctx, "seq", split_axis=0, concat_axis=0, tiled=True),)
-        before_norm = ()
+        norm_after = up_after = ()
+    shape = [len(choices) for choices in gate_in]
 
     one = 2 * total * width * ffw
     send_cot = call(
@@ -545,7 +591,7 @@
         [pltpu.VMEM((tokens, width), BF)],
         flops=2 * total * tokens * width,
         moved=2 * (total + 3 * tokens) * width,
-        after=before_norm,
+        after=norm_after,
     )
     rows = exchange(send_rows, owners, "exp")
 
@@ -558,7 +604,8 @@
         [full_w, full_w, pltpu.SemaphoreType.DMA((2, groups))],
         flops=2 * one,
         moved=4 * width * ffw + 2 * total * width + 10 * total * ffw,
-        vmem=20,
+        after=up_after,
+
     )
     out_first, d_hidden = call(
         functools.partial(down_kernel, shape[:-1]),
@@ -596,7 +643,7 @@
         ],
         flops=2 * one + 2 * one // groups,
         moved=4 * width * ffw + 4 * total * width + 14 * total * ffw,
-        vmem=22,
+
     )
     back_last = exchange(back, owners, "exp")
     output, stream_grad = call(

time: 274 us -> 254 us (0.927)
  local copies, waits for them, and re-layouts: 35.4 us -> 7.31 us
  waiting for transfers between devices: 130 us -> 111 us
  starting transfers between devices: 52.7 us -> 69.2 us
  Pallas kernels: 28.4 us -> 37.4 us
    unnamed x86 -> x56, local copies, waits for them, and re-layouts: 34.5 us -> 5.26 us
    ppermute x21 -> x24, starting transfers between devices: 39.8 us -> 56.9 us  [send(): return lax.ppermute(gated(array, *first), 'seq', pairs)]
    all_to_all x3, waiting for transfers between devices: 11.9 us -> 1.66 us  [exchange(): rows = lax.all_to_all(rows, axis, split_axis=0, concat_axis=0, tiled=True)]
    pallas_call x8, Pallas kernels: 28.4 us -> 37.4 us  [call(): pl.pallas_call(body, grid=(1,), out_shape=outs, in_specs=[*[whole(arg) if...]
    ppermute x21 -> x24, waiting for transfers between devices: 118 us -> 110 us  [send(): return lax.ppermute(gated(array, *first), 'seq', pairs)]
  transfers between devices with their start and end apart: 24 -> 27, of which waited for: 12 -> 11; matrix products, arithmetic and copies ran while one was open for 0% -> 1% of each run, Pallas kernels for 8% -> 11%
where the time goes in v3:
time: 254 us; the launch traced here: 253 us
  waiting for transfers between devices  111 us (44%)
  starting transfers between devices  69.2 us (27%)
  Pallas kernels  37.4 us (15%)
  blocking collectives  26 us (10%)
  local copies, waits for them, and re-layouts  7.31 us (3%)
    ppermute x24, waiting for transfers between devices, send(): return lax.ppermute(gated(array, *first), 'seq', pairs)  110 us
    ppermute x24, starting transfers between devices, send(): return lax.ppermute(gated(array, *first), 'seq', pairs)  56.9 us
    pallas_call x8, Pallas kernels, call(): pl.pallas_call(body, grid=(1,), out_shape=outs, in_specs=[*[whole(arg) if...  37.4 us
    all_to_all x1, blocking collectives, exchange(): rows = lax.all_to_all(rows, axis, split_axis=0, concat_axis=0, tiled=True)  26 us
    all_to_all x3, starting transfers between devices, exchange(): rows = lax.all_to_all(rows, axis, split_axis=0, concat_axis=0, tiled=True)  12.3 us
    unnamed x56, local copies, waits for them, and re-layouts  5.26 us
  transfers between devices with their start and end apart: 27, of which 11 were waited for; matrix products, arithmetic and copies ran while one was open for 1% of the time, Pallas kernels for 11%

profile of v3, /device:TPU:0, one launch (start us, length us, event | category | flops | bytes accessed | tf_op | source)
XLA Modules:
  0.0 252.5 jit_solution(4390071201105308853)
XLA Ops:
  0.7 1.4 dynamic-slice_bitcast_fusion.refs_0_
  2.0 2.6 %shard_map.131 = (bf16[384,1024]{1,0:T(8,128)(2,1)}, bf16[384,1024]{1,0:T(8,128)(2,1)}) custom-call(s32[10]{0:T(128)} %dynamic-slice_bitcast_fusion.refs_0_, bf16[128,2048]{1,0:T(8,128)(2,1)} %bitcast.53, bf16[128,2048]{1,0:T(8,128)(2,1)} %bitcast.54, bf16[128,2048]{1,0:T(8,128)(2,1)} %bitcast.55), custom_call_target="tpu_custom_call" | custom-call | bytes 3145728 | tf_op jit(solution)/shard_map/pallas_call | solution.py:35
  5.4 7.6 %collective-permute-start.2 = (bf16[384,1024]{1,0:T(8,128)(2,1)}, bf16[384,1024]{1,0:T(8,128)(2,1)S(1)}, u32[]{:S(2)}, u32[]{:S(2)}) collective-permute-start(bf16[384,1024]{1,0:T(8,128)(2,1)} %get-tuple-element.38), channel_id=1, source_target_pairs={{0,16},{24,8},{1,17},{25,9},{2,18},{26,10},{3,19},{27,11},{4,20},{... | collective-permute-start | bytes 2359304 | tf_op jit(solution)/shard_map/ppermute | solution.py:503
  13.0 1.4 collective-permute-start
  14.5 1.3 collective-permute-start.3
  15.8 1.3 collective-permute-start.4
  17.1 18.4 %collective-permute-done.3.refs_5_.refs_4_.refs_10_ = bf16[704,512]{1,0:T(8,128)(2,1)S(1)} collective-permute-done((bf16[704,512]{1,0:T(8,128)(2,1)S(1)}, bf16[704,512]{1,0:T(8,128)(2,1)S(1)}, u32[]{:S(2)}, u32[]{:S(2)}) %collective-permute-start.3) | collective-permute-done | bytes 720928 | tf_op jit(solution)/shard_map/ppermute | solution.py:503
  35.4 13.7 %collective-permute-done.4.refs_6_.refs_11_.refs_17_ = bf16[704,512]{1,0:T(8,128)(2,1)S(1)} collective-permute-done((bf16[704,512]{1,0:T(8,128)(2,1)}, bf16[704,512]{1,0:T(8,128)(2,1)S(1)}, u32[]{:S(2)}, u32[]{:S(2)}) %collective-permute-start.4) | collective-permute-done | bytes 720928 | tf_op jit(solution)/shard_map/ppermute | solution.py:503
  49.1 1.4 collective-permute-start.7
  50.6 1.5 collective-permute-start.5
  52.1 7.4 %collective-permute-start.6 = (bf16[704,512]{1,0:T(8,128)(2,1)S(1)}, bf16[704,512]{1,0:T(8,128)(2,1)}, u32[]{:S(2)}, u32[]{:S(2)}) collective-permute-start(bf16[704,512]{1,0:T(8,128)(2,1)S(1)} %bitcast.40), channel_id=1, source_target_pairs={{0,8},{24,16},{1,9},{25,17},{2,10},{26,18},{3,11},{27,19},{4,12},{... | collective-permute-start | bytes 2162696 | tf_op jit(solution)/shard_map/ppermute | solution.py:503
  59.5 1.7 shard_map.132
  61.2 6.4 %collective-permute-done.7.refs_5_ = bf16[704,512]{1,0:T(8,128)(2,1)S(1)} collective-permute-done((bf16[704,512]{1,0:T(8,128)(2,1)S(1)}, bf16[704,512]{1,0:T(8,128)(2,1)S(1)}, u32[]{:S(2)}, u32[]{:S(2)}) %collective-permute-start.7) | collective-permute-done | bytes 720928 | tf_op jit(solution)/shard_map/ppermute | solution.py:503
  67.5 4.4 %collective-permute-done.6.refs_3_.refs_9_ = bf16[704,512]{1,0:T(8,128)(2,1)} collective-permute-done((bf16[704,512]{1,0:T(8,128)(2,1)S(1)}, bf16[704,512]{1,0:T(8,128)(2,1)}, u32[]{:S(2)}, u32[]{:S(2)}) %collective-permute-start.6) | collective-permute-done | bytes 720928 | tf_op jit(solution)/shard_map/ppermute | solution.py:503
  72.0 1.3 collective-permute-start.8
  74.0 1.3 collective-permute-start.12
  76.0 9.1 %collective-permute-start.14 = (bf16[704,512]{1,0:T(8,128)(2,1)}, bf16[704,512]{1,0:T(8,128)(2,1)S(1)}, u32[]{:S(2)}, u32[]{:S(2)}) collective-permute-start(bf16[704,512]{1,0:T(8,128)(2,1)} %bitcast.12.refs_9_.refs_15_), channel_id=1, source_target_pairs={{0,8},{24,16},{1,9},{25,17},{2,10},{26,18},{3,11},{27,19},{4,12},{... | collective-permute-start | bytes 2162696 | tf_op jit(solution)/shard_map/ppermute | solution.py:503
  85.8 1.3 collective-permute-start.10
  87.9 32.2 %collective-permute-done.10.refs_7_ = bf16[128,1024]{1,0:T(8,128)(2,1)} collective-permute-done((bf16[128,1024]{1,0:T(8,128)(2,1)}, bf16[128,1024]{1,0:T(8,128)(2,1)}, u32[]{:S(2)}, u32[]{:S(2)}) %collective-permute-start.10) | collective-permute-done | bytes 262176 | tf_op jit(solution)/shard_map/ppermute | solution.py:503
  120.2 0.8 copy-done.3
  121.8 3.3 %shard_map.133 = (bf16[128,2048]{1,0:T(8,128)(2,1)}, bf16[320,2048]{1,0:T(8,128)(2,1)}) custom-call(s32[10]{0:T(128)} %dynamic-slice_bitcast_fusion.refs_0_, s32[2,128]{1,0:T(2,128)} %copy.16.refs_1_.refs_0_, bf16[128,2048]{1,0:T(8,128)(2,1)} %bitcast.56, f32[1,2048]{1,0:T(1,128)} %bitcast.57, bf16[128,1024]{1,0:T(8,128)(2,1)} %get-tuple-element.46.refs_4_, ...), custom_call_target="tpu_custom_call" | custom-call | flops 167772160 | bytes 2883584 | tf_op jit(solution)/shard_map/pallas_call | solution.py:35
  125.1 3.9 %all-to-all-start = ((bf16[8,40,2048]{2,1,0:T(8,128)(2,1)}), bf16[8,40,2048]{2,1,0:T(8,128)(2,1)S(1)}, u32[]{:S(2)}, u32[]{:S(2)}) async-start(bf16[8,40,2048]{2,1,0:T(8,128)(2,1)} %bitcast.43), calls=%async_computation | async-start | bytes 2621440 | tf_op jit(solution)/shard_map/all_to_all | solution.py:525
  128.9 1.3 collective-permute-start.15
  130.2 1.6 collective-permute-start.17
  131.9 9.0 %collective-permute-start.19 = (bf16[704,512]{1,0:T(8,128)(2,1)}, bf16[704,512]{1,0:T(8,128)(2,1)}, u32[]{:S(2)}, u32[]{:S(2)}) collective-permute-start(bf16[704,512]{1,0:T(8,128)(2,1)} %bitcast.45), channel_id=1, source_target_pairs={{0,8},{24,16},{1,9},{25,17},{2,10},{26,18},{3,11},{27,19},{4,12},{... | collective-permute-start | bytes 2162696 | tf_op jit(solution)/shard_map/ppermute | solution.py:503
  140.9 1.5 collective-permute-start.20
  142.4 1.3 collective-permute-start.16
  143.7 0.7 copy.15
  144.4 3.1 %shard_map.135 = bf16[320,2048]{1,0:T(8,128)(2,1)} custom-call(s32[2,128]{1,0:T(2,128)} %copy.16.refs_1_.refs_0_, f32[128,2]{1,0:T(8,128)} %bitcast.49, bf16[128,2048]{1,0:T(8,128)(2,1)} %bitcast.41), custom_call_target="tpu_custom_call" | custom-call | flops 335544320 | bytes 1835008 | tf_op jit(solution)/shard_map/pallas_call | solution.py:35
  147.6 1.1 copy-done.10
  148.7 4.2 %all-to-all-start.1 = ((bf16[8,40,2048]{2,1,0:T(8,128)(2,1)}), bf16[8,40,2048]{2,1,0:T(8,128)(2,1)S(1)}, u32[]{:S(2)}, u32[]{:S(2)}) async-start(bf16[8,40,2048]{2,1,0:T(8,128)(2,1)} %bitcast.34), calls=%async_computation.1 | async-start | bytes 2621440 | tf_op jit(solution)/shard_map/all_to_all | solution.py:525
  152.9 1.3 collective-permute-start.18
  154.2 1.6 collective-permute-done.19.refs_4_
  156.5 8.8 %collective-permute-done.16.refs_13_.refs_19_ = bf16[704,512]{1,0:T(8,128)(2,1)} collective-permute-done((bf16[704,512]{1,0:T(8,128)(2,1)S(1)}, bf16[704,512]{1,0:T(8,128)(2,1)}, u32[]{:S(2)}, u32[]{:S(2)}) %collective-permute-start.16) | collective-permute-done | bytes 720928 | tf_op jit(solution)/shard_map/ppermute | solution.py:503
  165.3 1.3 collective-permute-start.22
  166.6 14.1 %collective-permute-done.18.refs_15_.refs_21_ = bf16[704,512]{1,0:T(8,128)(2,1)S(1)} collective-permute-done((bf16[704,512]{1,0:T(8,128)(2,1)}, bf16[704,512]{1,0:T(8,128)(2,1)S(1)}, u32[]{:S(2)}, u32[]{:S(2)}) %collective-permute-start.18) | collective-permute-done | bytes 720928 | tf_op jit(solution)/shard_map/ppermute | solution.py:503
  180.7 1.3 collective-permute-start.23
  182.0 7.9 %shard_map.134 = (bf16[320,704]{1,0:T(8,128)(2,1)}, f32[320,704]{1,0:T(8,128)}, f32[320,704]{1,0:T(8,128)}) custom-call(s32[10]{0:T(128)} %dynamic-slice_bitcast_fusion.refs_0_, bf16[320,2048]{1,0:T(8,128)(2,1)} %bitcast.33, bf16[704,512]{1,0:T(8,128)(2,1)} %bitcast.36, bf16[704,512]{1,0:T(8,128)(2,1)} %collective-permute-done.6.refs_3_.refs_9_, ...), custom_call_target="tpu_custom_call" | custom-call | flops 1845493760 | bytes 9330688 | tf_op jit(solution)/shard_map/pallas_call | solution.py:35
  189.9 6.2 %collective-permute-done.22.refs_7_ = bf16[704,512]{1,0:T(8,128)(2,1)S(1)} collective-permute-done((bf16[704,512]{1,0:T(8,128)(2,1)}, bf16[704,512]{1,0:T(8,128)(2,1)S(1)}, u32[]{:S(2)}, u32[]{:S(2)}) %collective-permute-start.22) | collective-permute-done | bytes 720928 | tf_op jit(solution)/shard_map/ppermute | solution.py:503
  196.1 0.9 copy-done.20
  197.0 5.9 %shard_map.136 = (bf16[320,1536]{1,0:T(8,128)(2,1)}, f32[320,704]{1,0:T(8,128)}) custom-call(s32[10]{0:T(128)} %dynamic-slice_bitcast_fusion.refs_0_, bf16[320,704]{1,0:T(8,128)(2,1)} %get-tuple-element.63.refs_1_, bf16[320,2048]{1,0:T(8,128)(2,1)} %bitcast.29, bf16[704,512]{1,0:T(8,128)(2,1)} %bitcast.47, bf16[704,512]{1,0:T(8,128)(2,1)} %collective-permute-done.19.refs_4_, ...), custom_call_target="tpu_custom_call" | custom-call | flops 1384120320 | bytes 6856704 | tf_op jit(solution)/shard_map/pallas_call | solution.py:35
  202.9 4.2 %all-to-all-start.2 = ((bf16[8,40,1536]{2,1,0:T(8,128)(2,1)}), bf16[8,40,1536]{2,1,0:T(8,128)(2,1)S(1)}, u32[]{:S(2)}, u32[]{:S(2)}) async-start(bf16[8,40,1536]{2,1,0:T(8,128)(2,1)} %bitcast.44), calls=%async_computation.2 | async-start | bytes 1966080 | tf_op jit(solution)/shard_map/all_to_all | solution.py:525
  207.2 4.0 %collective-permute-done.23.refs_7_ = bf16[704,512]{1,0:T(8,128)(2,1)S(1)} collective-permute-done((bf16[704,512]{1,0:T(8,128)(2,1)S(1)}, bf16[704,512]{1,0:T(8,128)(2,1)S(1)}, u32[]{:S(2)}, u32[]{:S(2)}) %collective-permute-start.23) | collective-permute-done | bytes 720928 | tf_op jit(solution)/shard_map/ppermute | solution.py:503
  211.2 0.9 copy-done.21
  212.0 8.2 %shard_map.137 = bf16[320,2560]{1,0:T(8,128)(2,1)} custom-call(s32[10]{0:T(128)} %dynamic-slice_bitcast_fusion.refs_0_, bf16[320,704]{1,0:T(8,128)(2,1)} %get-tuple-element.63.refs_1_, bf16[320,2048]{1,0:T(8,128)(2,1)} %bitcast.30, f32[320,704]{1,0:T(8,128)} %get-tuple-element.66.refs_3_, f32[320,704]{1,0:T(8,128)} %get-tuple-element.67.refs_4_, ...), custom_call_target="tpu_custom_call" | custom-call | flops 2306867200 | bytes 11542528 | tf_op jit(solution)/shard_map/pallas_call | solution.py:35
  220.2 1.7 all-to-all-done.2
  221.9 26.0 %all_to_all.20 = bf16[8,40,2560]{2,1,0:T(8,128)(2,1)} all-to-all(bf16[8,40,2560]{2,1,0:T(8,128)(2,1)} %bitcast.32), channel_id=1, replica_groups=mesh['seq'=4,'exp'=8] {'exp'}, dimensions={0} | all-to-all | bytes 3276800 | tf_op jit(solution)/shard_map/all_to_all | solution.py:525
  247.9 4.7 %shard_map.138 = (bf16[128,2048]{1,0:T(8,128)(2,1)}, bf16[128,2048]{1,0:T(8,128)(2,1)}) custom-call(s32[10]{0:T(128)} %dynamic-slice_bitcast_fusion.refs_0_, s32[128,2]{1,0:T(8,128)} %bitcast.52, f32[128,2]{1,0:T(8,128)} %bitcast.50, f32[1,2048]{1,0:T(1,128)} %bitcast.58, bf16[128,2048]{1,0:T(8,128)(2,1)} %get-tuple-element.54.refs_4_, ...), custom_call_target="tpu_custom_call" | custom-call | flops 503316480 | bytes 4718592 | tf_op jit(solution)/shard_map/pallas_call | solution.py:35
  (73 shorter events, 5.1 us)
Async XLA Ops:
  0.6 13.8 %copy-start.12 = (bf16[1,512,704]{1,2,0:T(8,128)(2,1)S(1)}, bf16[1,512,704]{1,2,0:T(8,128)(2,1)}, u32[]{:S(2)}) copy-start(bf16[1,512,704]{1,2,0:T(8,128)(2,1)} %param.17) | copy-start | bytes 2162692
  0.6 48.5 %copy-start.18 = (bf16[1,704,512]{2,1,0:T(8,128)(2,1)S(1)}, bf16[1,704,512]{2,1,0:T(8,128)(2,1)}, u32[]{:S(2)}) copy-start(bf16[1,704,512]{2,1,0:T(8,128)(2,1)} %param.19) | copy-start | bytes 2162692
  4.7 45.9 %collective-permute-start.1 = (bf16[384,1024]{1,0:T(8,128)(2,1)}, bf16[384,1024]{1,0:T(8,128)(2,1)S(1)}, u32[]{:S(2)}, u32[]{:S(2)}) collective-permute-start(bf16[384,1024]{1,0:T(8,128)(2,1)} %get-tuple-element.38), channel_id=1, source_target_pairs={{8,16},{16,8},{9,17},{17,9},{10,18},{18,10},{11,19},{19,11},{12,20... | collective-permute-start | bytes 2359304 | tf_op jit(solution)/shard_map/ppermute | solution.py:503
  5.4 45.2 %collective-permute-start.2 = (bf16[384,1024]{1,0:T(8,128)(2,1)}, bf16[384,1024]{1,0:T(8,128)(2,1)S(1)}, u32[]{:S(2)}, u32[]{:S(2)}) collective-permute-start(bf16[384,1024]{1,0:T(8,128)(2,1)} %get-tuple-element.38), channel_id=1, source_target_pairs={{0,16},{24,8},{1,17},{25,9},{2,18},{26,10},{3,19},{27,11},{4,20},{... | collective-permute-start | bytes 2359304 | tf_op jit(solution)/shard_map/ppermute | solution.py:503
  13.0 39.1 %collective-permute-start = (bf16[384,1024]{1,0:T(8,128)(2,1)}, bf16[384,1024]{1,0:T(8,128)(2,1)S(1)}, u32[]{:S(2)}, u32[]{:S(2)}) collective-permute-start(bf16[384,1024]{1,0:T(8,128)(2,1)} %get-tuple-element.37.refs_1_), channel_id=1, source_target_pairs={{0,8},{24,16},{1,9},{25,17},{2,10},{26,18},{3,11},{27,19},{4,12},{... | collective-permute-start | bytes 2359304 | tf_op jit(solution)/shard_map/ppermute | solution.py:503
  14.5 21.0 %collective-permute-start.3 = (bf16[704,512]{1,0:T(8,128)(2,1)S(1)}, bf16[704,512]{1,0:T(8,128)(2,1)S(1)}, u32[]{:S(2)}, u32[]{:S(2)}) collective-permute-start(bf16[704,512]{1,0:T(8,128)(2,1)S(1)} %bitcast.38), channel_id=1, source_target_pairs={{8,0},{16,24},{9,1},{17,25},{10,2},{18,26},{11,3},{19,27},{12,4},{... | collective-permute-start | bytes 2162696 | tf_op jit(solution)/shard_map/ppermute | solution.py:503
  15.8 33.4 %collective-permute-start.4 = (bf16[704,512]{1,0:T(8,128)(2,1)}, bf16[704,512]{1,0:T(8,128)(2,1)S(1)}, u32[]{:S(2)}, u32[]{:S(2)}) collective-permute-start(bf16[704,512]{1,0:T(8,128)(2,1)} %bitcast.12.refs_9_.refs_15_), channel_id=1, source_target_pairs={{8,0},{16,24},{9,1},{17,25},{10,2},{18,26},{11,3},{19,27},{12,4},{... | collective-permute-start | bytes 2162696 | tf_op jit(solution)/shard_map/ppermute | solution.py:503
  35.4 24.1 %copy-start.1 = (bf16[704,512]{1,0:T(8,128)(2,1)}, bf16[704,512]{1,0:T(8,128)(2,1)S(1)}, u32[]{:S(2)}) copy-start(bf16[704,512]{1,0:T(8,128)(2,1)S(1)} %collective-permute-done.3.refs_5_.refs_4_.refs_10_) | copy-start | bytes 2162692
  49.1 10.4 %copy-start.2 = (bf16[704,512]{1,0:T(8,128)(2,1)}, bf16[704,512]{1,0:T(8,128)(2,1)S(1)}, u32[]{:S(2)}) copy-start(bf16[704,512]{1,0:T(8,128)(2,1)S(1)} %collective-permute-done.4.refs_6_.refs_11_.refs_17_) | copy-start | bytes 2162692
  49.1 38.0 %copy-start.25 = (s32[1,128,2]{1,2,0:T(2,128)S(1)}, s32[1,128,2]{1,2,0:T(2,128)}, u32[]{:S(2)}) copy-start(s32[1,128,2]{1,2,0:T(2,128)} %param.20) | copy-start | bytes 3076
  49.1 18.4 %collective-permute-start.7 = (bf16[704,512]{1,0:T(8,128)(2,1)S(1)}, bf16[704,512]{1,0:T(8,128)(2,1)S(1)}, u32[]{:S(2)}, u32[]{:S(2)}) collective-permute-start(bf16[704,512]{1,0:T(8,128)(2,1)S(1)} %bitcast.48), channel_id=1, source_target_pairs={{8,0},{16,24},{9,1},{17,25},{10,2},{18,26},{11,3},{19,27},{12,4},{... | collective-permute-start | bytes 2162696 | tf_op jit(solution)/shard_map/ppermute | solution.py:503
  50.6 8.9 %copy-start.15 = (bf16[384,1024]{1,0:T(8,128)(2,1)}, bf16[384,1024]{1,0:T(8,128)(2,1)S(1)}, u32[]{:S(2)}) copy-start(bf16[384,1024]{1,0:T(8,128)(2,1)S(1)} %collective-permute-done.1.refs_3_) | copy-start | bytes 2359300
  50.6 8.9 %copy-start.16 = (bf16[384,1024]{1,0:T(8,128)(2,1)}, bf16[384,1024]{1,0:T(8,128)(2,1)S(1)}, u32[]{:S(2)}) copy-start(bf16[384,1024]{1,0:T(8,128)(2,1)S(1)} %collective-permute-done.2.refs_4_) | copy-start | bytes 2359300
  50.6 16.9 %collective-permute-start.5 = (bf16[704,512]{1,0:T(8,128)(2,1)S(1)}, bf16[704,512]{1,0:T(8,128)(2,1)}, u32[]{:S(2)}, u32[]{:S(2)}) collective-permute-start(bf16[704,512]{1,0:T(8,128)(2,1)S(1)} %bitcast.39), channel_id=1, source_target_pairs={{8,16},{16,8},{9,17},{17,9},{10,18},{18,10},{11,19},{19,11},{12,20... | collective-permute-start | bytes 2162696 | tf_op jit(solution)/shard_map/ppermute | solution.py:503
  52.1 7.4 %copy-start.17 = (bf16[384,1024]{1,0:T(8,128)(2,1)}, bf16[384,1024]{1,0:T(8,128)(2,1)S(1)}, u32[]{:S(2)}) copy-start(bf16[384,1024]{1,0:T(8,128)(2,1)S(1)} %collective-permute-done.refs_2_) | copy-start | bytes 2359300
  52.1 19.8 %collective-permute-start.6 = (bf16[704,512]{1,0:T(8,128)(2,1)S(1)}, bf16[704,512]{1,0:T(8,128)(2,1)}, u32[]{:S(2)}, u32[]{:S(2)}) collective-permute-start(bf16[704,512]{1,0:T(8,128)(2,1)S(1)} %bitcast.40), channel_id=1, source_target_pairs={{0,8},{24,16},{1,9},{25,17},{2,10},{26,18},{3,11},{27,19},{4,12},{... | collective-permute-start | bytes 2162696 | tf_op jit(solution)/shard_map/ppermute | solution.py:503
  67.5 7.7 %copy-start.19 = (bf16[704,512]{1,0:T(8,128)(2,1)}, bf16[704,512]{1,0:T(8,128)(2,1)S(1)}, u32[]{:S(2)}) copy-start(bf16[704,512]{1,0:T(8,128)(2,1)S(1)} %collective-permute-done.7.refs_5_) | copy-start | bytes 2162692
  72.0 13.1 %collective-permute-start.8 = (bf16[128,1024]{1,0:T(8,128)(2,1)}, bf16[128,1024]{1,0:T(8,128)(2,1)S(1)}, u32[]{:S(2)}, u32[]{:S(2)}) collective-permute-start(bf16[128,1024]{1,0:T(8,128)(2,1)} %get-tuple-element.47), channel_id=1, source_target_pairs={{8,0},{16,24},{9,1},{17,25},{10,2},{18,26},{11,3},{19,27},{12,4},{... | collective-permute-start | bytes 786440 | tf_op jit(solution)/shard_map/ppermute | solution.py:503
  73.3 46.9 %collective-permute-start.11 = (bf16[704,512]{1,0:T(8,128)(2,1)}, bf16[704,512]{1,0:T(8,128)(2,1)S(1)}, u32[]{:S(2)}, u32[]{:S(2)}) collective-permute-start(bf16[704,512]{1,0:T(8,128)(2,1)} %collective-permute-done.6.refs_3_.refs_9_), channel_id=1, source_target_pairs={{8,16},{16,8},{9,17},{17,9},{10,18},{18,10},{11,19},{19,11},{12,20... | collective-permute-start | bytes 2162696 | tf_op jit(solution)/shard_map/ppermute | solution.py:503
  74.0 46.2 %collective-permute-start.12 = (bf16[704,512]{1,0:T(8,128)(2,1)}, bf16[704,512]{1,0:T(8,128)(2,1)S(1)}, u32[]{:S(2)}, u32[]{:S(2)}) collective-permute-start(bf16[704,512]{1,0:T(8,128)(2,1)} %collective-permute-done.5.refs_5_.refs_11_), channel_id=1, source_target_pairs={{8,0},{16,24},{9,1},{17,25},{10,2},{18,26},{11,3},{19,27},{12,4},{... | collective-permute-start | bytes 2162696 | tf_op jit(solution)/shard_map/ppermute | solution.py:503
  75.3 44.9 %collective-permute-start.13 = (bf16[704,512]{1,0:T(8,128)(2,1)}, bf16[704,512]{1,0:T(8,128)(2,1)S(1)}, u32[]{:S(2)}, u32[]{:S(2)}) collective-permute-start(bf16[704,512]{1,0:T(8,128)(2,1)} %bitcast.12.refs_9_.refs_15_), channel_id=1, source_target_pairs={{8,16},{16,8},{9,17},{17,9},{10,18},{18,10},{11,19},{19,11},{12,20... | collective-permute-start | bytes 2162696 | tf_op jit(solution)/shard_map/ppermute | solution.py:503
  76.0 44.2 %collective-permute-start.14 = (bf16[704,512]{1,0:T(8,128)(2,1)}, bf16[704,512]{1,0:T(8,128)(2,1)S(1)}, u32[]{:S(2)}, u32[]{:S(2)}) collective-permute-start(bf16[704,512]{1,0:T(8,128)(2,1)} %bitcast.12.refs_9_.refs_15_), channel_id=1, source_target_pairs={{0,8},{24,16},{1,9},{25,17},{2,10},{26,18},{3,11},{27,19},{4,12},{... | collective-permute-start | bytes 2162696 | tf_op jit(solution)/shard_map/ppermute | solution.py:503
  85.1 35.1 %copy-start.23 = (bf16[128,1024]{1,0:T(8,128)(2,1)}, bf16[128,1024]{1,0:T(8,128)(2,1)S(1)}, u32[]{:S(2)}) copy-start(bf16[128,1024]{1,0:T(8,128)(2,1)S(1)} %collective-permute-done.8.refs_5_) | copy-start | bytes 786436
  85.1 0.7 collective-permute-start.9
  85.8 34.4 %copy-start.24 = (bf16[128,1024]{1,0:T(8,128)(2,1)}, bf16[128,1024]{1,0:T(8,128)(2,1)S(1)}, u32[]{:S(2)}) copy-start(bf16[128,1024]{1,0:T(8,128)(2,1)S(1)} %collective-permute-done.9.refs_6_) | copy-start | bytes 786436
  85.8 34.3 %collective-permute-start.10 = (bf16[128,1024]{1,0:T(8,128)(2,1)}, bf16[128,1024]{1,0:T(8,128)(2,1)}, u32[]{:S(2)}, u32[]{:S(2)}) collective-permute-start(bf16[128,1024]{1,0:T(8,128)(2,1)} %get-tuple-element.49), channel_id=1, source_target_pairs={{16,0},{8,24},{17,1},{9,25},{18,2},{10,26},{19,3},{11,27},{20,4},{... | collective-permute-start | bytes 786440 | tf_op jit(solution)/shard_map/ppermute | solution.py:503
  87.2 37.8 %copy-start.22 = (s32[1,128,2]{2,1,0:T(8,128)}, s32[1,128,2]{2,1,0:T(8,128)S(1)}, u32[]{:S(2)}) copy-start(s32[1,128,2]{2,1,0:T(8,128)S(1)} %copy.14) | copy-start | bytes 3076
  120.2 1.3 copy-start.6
  120.2 1.5 copy-start.8
  125.0 3.9 %copy-start.4 = (bf16[704,512]{1,0:T(8,128)(2,1)S(1)}, bf16[704,512]{1,0:T(8,128)(2,1)}, u32[]{:S(2)}) copy-start(bf16[704,512]{1,0:T(8,128)(2,1)} %copy-done.3) | copy-start | bytes 2162692
  125.0 5.2 %copy-start.9 = (bf16[704,512]{1,0:T(8,128)(2,1)S(1)}, bf16[704,512]{1,0:T(8,128)(2,1)}, u32[]{:S(2)}) copy-start(bf16[704,512]{1,0:T(8,128)(2,1)} %copy-done.8) | copy-start | bytes 2162692
  125.0 17.4 %copy-start.7 = (bf16[704,512]{1,0:T(8,128)(2,1)S(1)}, bf16[704,512]{1,0:T(8,128)(2,1)}, u32[]{:S(2)}) copy-start(bf16[704,512]{1,0:T(8,128)(2,1)} %copy-done.6) | copy-start | bytes 2162692
  125.0 18.6 %copy-start.26 = (f32[1,128,2]{1,2,0:T(2,128)S(1)}, f32[1,128,2]{1,2,0:T(2,128)}, u32[]{:S(2)}) copy-start(f32[1,128,2]{1,2,0:T(2,128)} %param.21) | copy-start | bytes 3076
  125.1 22.5 %all-to-all-start = ((bf16[8,40,2048]{2,1,0:T(8,128)(2,1)}), bf16[8,40,2048]{2,1,0:T(8,128)(2,1)S(1)}, u32[]{:S(2)}, u32[]{:S(2)}) async-start(bf16[8,40,2048]{2,1,0:T(8,128)(2,1)} %bitcast.43), calls=%async_computation | async-start | bytes 2621440 | tf_op jit(solution)/shard_map/all_to_all | solution.py:525
  128.9 23.9 %collective-permute-start.15 = (bf16[704,512]{1,0:T(8,128)(2,1)S(1)}, bf16[704,512]{1,0:T(8,128)(2,1)}, u32[]{:S(2)}, u32[]{:S(2)}) collective-permute-start(bf16[704,512]{1,0:T(8,128)(2,1)S(1)} %copy-done.4), channel_id=1, source_target_pairs={{8,0},{16,24},{9,1},{17,25},{10,2},{18,26},{11,3},{19,27},{12,4},{... | collective-permute-start | bytes 2162696 | tf_op jit(solution)/shard_map/ppermute | solution.py:503
  130.2 22.6 %collective-permute-start.17 = (bf16[704,512]{1,0:T(8,128)(2,1)S(1)}, bf16[704,512]{1,0:T(8,128)(2,1)}, u32[]{:S(2)}, u32[]{:S(2)}) collective-permute-start(bf16[704,512]{1,0:T(8,128)(2,1)S(1)} %copy-done.9), channel_id=1, source_target_pairs={{8,16},{16,8},{9,17},{17,9},{10,18},{18,10},{11,19},{19,11},{12,20... | collective-permute-start | bytes 2162696 | tf_op jit(solution)/shard_map/ppermute | solution.py:503
  131.9 23.9 %collective-permute-start.19 = (bf16[704,512]{1,0:T(8,128)(2,1)}, bf16[704,512]{1,0:T(8,128)(2,1)}, u32[]{:S(2)}, u32[]{:S(2)}) collective-permute-start(bf16[704,512]{1,0:T(8,128)(2,1)} %bitcast.45), channel_id=1, source_target_pairs={{0,8},{24,16},{1,9},{25,17},{2,10},{26,18},{3,11},{27,19},{4,12},{... | collective-permute-start | bytes 2162696 | tf_op jit(solution)/shard_map/ppermute | solution.py:503
  140.9 14.9 %collective-permute-start.20 = (bf16[704,512]{1,0:T(8,128)(2,1)}, bf16[704,512]{1,0:T(8,128)(2,1)}, u32[]{:S(2)}, u32[]{:S(2)}) collective-permute-start(bf16[704,512]{1,0:T(8,128)(2,1)} %bitcast.46), channel_id=1, source_target_pairs={{8,16},{16,8},{9,17},{17,9},{10,18},{18,10},{11,19},{19,11},{12,20... | collective-permute-start | bytes 2162696 | tf_op jit(solution)/shard_map/ppermute | solution.py:503
  142.4 22.9 %collective-permute-start.16 = (bf16[704,512]{1,0:T(8,128)(2,1)S(1)}, bf16[704,512]{1,0:T(8,128)(2,1)}, u32[]{:S(2)}, u32[]{:S(2)}) collective-permute-start(bf16[704,512]{1,0:T(8,128)(2,1)S(1)} %copy-done.7), channel_id=1, source_target_pairs={{8,0},{16,24},{9,1},{17,25},{10,2},{18,26},{11,3},{19,27},{12,4},{... | collective-permute-start | bytes 2162696 | tf_op jit(solution)/shard_map/ppermute | solution.py:503
  148.7 41.3 %all-to-all-start.1 = ((bf16[8,40,2048]{2,1,0:T(8,128)(2,1)}), bf16[8,40,2048]{2,1,0:T(8,128)(2,1)S(1)}, u32[]{:S(2)}, u32[]{:S(2)}) async-start(bf16[8,40,2048]{2,1,0:T(8,128)(2,1)} %bitcast.34), calls=%async_computation.1 | async-start | bytes 2621440 | tf_op jit(solution)/shard_map/all_to_all | solution.py:525
  152.9 27.8 %collective-permute-start.18 = (bf16[704,512]{1,0:T(8,128)(2,1)}, bf16[704,512]{1,0:T(8,128)(2,1)S(1)}, u32[]{:S(2)}, u32[]{:S(2)}) collective-permute-start(bf16[704,512]{1,0:T(8,128)(2,1)} %collective-permute-done.17.refs_14_.refs_20_), channel_id=1, source_target_pairs={{8,0},{16,24},{9,1},{17,25},{10,2},{18,26},{11,3},{19,27},{12,4},{... | collective-permute-start | bytes 2162696 | tf_op jit(solution)/shard_map/ppermute | solution.py:503
  155.8 24.9 %collective-permute-start.21 = (bf16[704,512]{1,0:T(8,128)(2,1)}, bf16[704,512]{1,0:T(8,128)(2,1)S(1)}, u32[]{:S(2)}, u32[]{:S(2)}) collective-permute-start(bf16[704,512]{1,0:T(8,128)(2,1)} %collective-permute-done.19.refs_4_), channel_id=1, source_target_pairs={{8,16},{16,8},{9,17},{17,9},{10,18},{18,10},{11,19},{19,11},{12,20... | collective-permute-start | bytes 2162696 | tf_op jit(solution)/shard_map/ppermute | solution.py:503
  165.3 30.8 %collective-permute-start.22 = (bf16[704,512]{1,0:T(8,128)(2,1)}, bf16[704,512]{1,0:T(8,128)(2,1)S(1)}, u32[]{:S(2)}, u32[]{:S(2)}) collective-permute-start(bf16[704,512]{1,0:T(8,128)(2,1)} %collective-permute-done.20.refs_6_), channel_id=1, source_target_pairs={{8,0},{16,24},{9,1},{17,25},{10,2},{18,26},{11,3},{19,27},{12,4},{... | collective-permute-start | bytes 2162696 | tf_op jit(solution)/shard_map/ppermute | solution.py:503
  180.7 1.3 copy-start.14
  180.7 30.5 %collective-permute-start.23 = (bf16[704,512]{1,0:T(8,128)(2,1)S(1)}, bf16[704,512]{1,0:T(8,128)(2,1)S(1)}, u32[]{:S(2)}, u32[]{:S(2)}) collective-permute-start(bf16[704,512]{1,0:T(8,128)(2,1)S(1)} %collective-permute-done.21.refs_16_.refs_6_), channel_id=1, source_target_pairs={{8,0},{16,24},{9,1},{17,25},{10,2},{18,26},{11,3},{19,27},{12,4},{... | collective-permute-start | bytes 2162696 | tf_op jit(solution)/shard_map/ppermute | solution.py:503
  189.9 6.2 %copy-start = (bf16[8,40,2048]{2,1,0:T(8,128)(2,1)}, bf16[8,40,2048]{2,1,0:T(8,128)(2,1)S(1)}, u32[]{:S(2)}) copy-start(bf16[8,40,2048]{2,1,0:T(8,128)(2,1)S(1)} %all-to-all-done.1) | copy-start | bytes 3932164
  202.9 19.0 %all-to-all-start.2 = ((bf16[8,40,1536]{2,1,0:T(8,128)(2,1)}), bf16[8,40,1536]{2,1,0:T(8,128)(2,1)S(1)}, u32[]{:S(2)}, u32[]{:S(2)}) async-start(bf16[8,40,1536]{2,1,0:T(8,128)(2,1)} %bitcast.44), calls=%async_computation.2 | async-start | bytes 1966080 | tf_op jit(solution)/shard_map/all_to_all | solution.py:525
  221.9 26.0 %copy-start.11 = (bf16[8,40,1536]{2,1,0:T(8,128)(2,1)}, bf16[8,40,1536]{2,1,0:T(8,128)(2,1)S(1)}, u32[]{:S(2)}) copy-start(bf16[8,40,1536]{2,1,0:T(8,128)(2,1)S(1)} %all-to-all-done.2) | copy-start | bytes 2949124
  (6 other events, 6.1 us)

commit v4 on v3

--- a/solution.py
+++ b/solution.py
@@ -26,7 +26,7 @@
     return pl.BlockSpec(array.shape, lambda i: (0,) * len(array.shape))
 
 
-def call(kernel, outs, args, in_specs, scratch=(), flops=0, moved=0, vmem=56, after=()):
+def call(kernel, outs, args, in_specs, scratch=(), flops=0, moved=0, vmem=56, after=(), held=False):
     count, extra = len(args), len(after)
 
     def body(*refs):
@@ -34,13 +34,16 @@
 
     return pl.pallas_call(
         body,
-        grid=(1,),
+        grid=() if held else (1,),
         out_shape=outs,
         in_specs=[
-            *[whole(arg) if spec is VMEM else spec for arg, spec in zip(args, in_specs)],
+            *[
+                whole(arg) if spec is VMEM and not held else spec
+                for arg, spec in zip(args, in_specs)
+            ],
             *[HBM] * extra,
         ],
-        out_specs=jax.tree.map(whole, outs),
+        out_specs=jax.tree.map(lambda out: VMEM if held else whole(out), outs),
         scratch_shapes=list(scratch),
         compiler_params=pltpu.CompilerParams(vmem_limit_bytes=vmem * MIB),
         cost_estimate=pl.CostEstimate(flops=flops, bytes_accessed=moved, transcendentals=0),
@@ -198,7 +201,7 @@
             out[...] = ctx_ref[place_ref[ATTEND + i]]
 
 
-def line_of_four(place, queries, keys, values, gate, up, down):
+def line_of_four(place, queries, keys, values, gate, up, down, send_cot):
     rows, width = queries.shape
     half = width // 2
     block = sds((3 * rows, half))
@@ -227,28 +230,28 @@
         ],
         flops=64 * rows * rows * half,
         moved=32 * rows * half,
-        after=(gate_end, up_end),
+        after=(gate_end, up_end, send_cot),
     )
     gate_inner = send(gate, INWARD, near, far)
-    gate_mid = send(gate, MIDDLE, mid, far)
-    down_end = send(down, OUTWARD, gate_end, up_end)
+    gate_mid = send(gate, MIDDLE, near, mid, far)
+    down_end = send(down, OUTWARD)
     own, near, mid, far = lax.optimization_barrier((*pieces, gate_mid, gate_inner, down_end))[:4]
     near = send(near, OUTWARD)
     mid = send(mid, MIDDLE)
     far = send(far, [(2, 0), (1, 3)])
-    gate_mid_near = send(gate_inner, MIDDLE, gate_mid)
+    gate_mid_near = send(gate_inner, MIDDLE, mid, far)
     gate_far = send(gate_mid, OUTWARD, down_end)
     up_mid = send(up, MIDDLE, gate_mid)
     up_inner = send(up, INWARD, gate_inner)
-    norm_after = (gate_mid_near, gate_far, up_mid, up_inner)
-    gate_far_near = send(gate_mid_near, OUTWARD, gate_far)
-    up_far = send(up_mid, OUTWARD, gate_far)
-    up_mid_near = send(up_inner, MIDDLE, gate_mid_near)
-    down_mid = send(down, MIDDLE, up_mid)
+    norm_after = (gate_far, up_mid)
+    gate_far_near = send(gate_mid_near, OUTWARD)
+    up_far = send(up_mid, OUTWARD)
+    up_mid_near = send(up_inner, MIDDLE, up_mid)
+    down_mid = send(down, MIDDLE, gate_mid_near)
     down_inner = send(down, INWARD, up_inner)
-    up_far_near = send(up_mid_near, OUTWARD, gate_far_near)
-    down_far = send(down_mid, OUTWARD, up_far)
-    down_mid_near = send(down_inner, MIDDLE, down_mid)
+    up_far_near = send(up_mid_near, OUTWARD, up_far)
+    down_far = send(down_mid, OUTWARD, gate_far_near)
+    down_mid_near = send(down_inner, MIDDLE, up_mid_near)
     up_after = (down_mid_near,)
     down_far_near = send(down_mid_near, OUTWARD, up_far_near)
     gate_in = [
@@ -416,30 +419,65 @@
 
 
 def grad_kernel(
-    shape, place_ref, hidden_ref, cot_ref, d_hidden_ref, to_gate_ref, to_up_ref, *refs
+    shape, place_ref, hidden_in, cot_in, d_hidden_in, to_gate_in, to_up_in, *refs
 ):
-    slots = len(shape)
+    slots = len(shape) - 1
     down_in, refs = regroup(refs, shape[-1:])
-    gate_in, refs = regroup(refs, shape)
-    up_in, refs = regroup(refs, shape)
-    o_ref, down_w, gate_w, up_w, sems = refs
+    gate_in, refs = regroup(refs, shape[:-1])
+    up_in, refs = regroup(refs, shape[:-1])
+    (o_ref, d_gate_ref, d_up_ref, down_w, gate_w, up_w, sems) = refs[:7]
+    hidden_ref, cot_ref, d_hidden_ref, to_gate_ref, to_up_ref = refs[7:]
     part = down_w.shape[1]
     inner = place_ref[INNER]
+    last = place_ref[COLS + cot_in.shape[1] // part - 1]
+    pairs = [
+        (cot_in.at[:, pl.ds(pl.multiple_of(last * part, part), part)], cot_ref),
+        (d_hidden_in, d_hidden_ref),
+        (to_gate_in, to_gate_ref),
+        (to_up_in, to_up_ref),
+        (hidden_in, hidden_ref),
+    ]
     fetch(inner, down_in[0], down_w, sems.at[2, 0])
+    copies = [
+        pltpu.make_async_copy(src, dst, sems.at[3 + i, 0]) for i, (src, dst) in enumerate(pairs)
+    ]
+    for copy in copies:
+        copy.start()
     for j in range(slots):
         fetch(inner, gate_in[j], gate_w.at[j], sems.at[0, j])
         fetch(inner, up_in[j], up_w.at[j], sems.at[1, j])
-    rows = cot_ref[:, cols_of(place_ref, slots - 1, part)]
     arrived(down_in[0], down_w, sems.at[2, 0])
-    d_hidden = d_hidden_ref[...] + mm(rows, down_w[...], NT)
+    for copy in copies:
+        copy.wait()
+    d_hidden = d_hidden_ref[...] + mm(cot_ref[...], down_w[...], NT)
     d_gate = (d_hidden * to_gate_ref[...]).astype(BF)
     d_up = (d_hidden * to_up_ref[...]).astype(BF)
+    d_gate_ref[...] = d_gate
+    d_up_ref[...] = d_up
     o_ref[:, slots * part :] = mm(hidden_ref[...], down_w[...], NN).astype(BF)
     for j in range(slots):
         arrived(gate_in[j], gate_w.at[j], sems.at[0, j])
         arrived(up_in[j], up_w.at[j], sems.at[1, j])
         o_ref[:, j * part : (j + 1) * part] = (
             mm(d_gate, gate_w[j], NN) + mm(d_up, up_w[j], NN)
+        ).astype(BF)
+
+
+def rest_kernel(shape, place_ref, d_gate_ref, d_up_ref, *refs):
+    slots = len(shape)
+    gate_in, refs = regroup(refs, shape)
+    up_in, refs = regroup(refs, shape)
+    o_ref, gate_w, up_w, sems = refs
+    part = gate_w.shape[2]
+    inner = place_ref[INNER]
+    for j in range(slots):
+        fetch(inner, gate_in[j], gate_w.at[j], sems.at[0, j])
+        fetch(inner, up_in[j], up_w.at[j], sems.at[1, j])
+    for j in range(slots):
+        arrived(gate_in[j], gate_w.at[j], sems.at[0, j])
+        arrived(up_in[j], up_w.at[j], sems.at[1, j])
+        o_ref[:, j * part : (j + 1) * part] = (
+            mm(d_gate_ref[...], gate_w[j], NN) + mm(d_up_ref[...], up_w[j], NN)
         ).astype(BF)
 
 
@@ -453,7 +491,8 @@
     stream_ref,
     cot_ref,
     first_ref,
-    last_ref,
+    early_ref,
+    late_ref,
     output_ref,
     grad_ref,
     d_normed_ref,
@@ -474,11 +513,15 @@
         if j < slots - 1:
             pairs = first_ref[:, j * part : (j + 1) * part]
         else:
-            pairs = last_ref[:, width : width + part]
+            pairs = early_ref[:, slots // 2 * part :]
         stream = stream_ref[:, cols].astype(F32)
         mixed = w0 * mm(pick0, pairs, NN) + w1 * mm(pick1, pairs, NN)
         output_ref[:, cols] = (stream + mixed).astype(BF)
-        gained = mm(both, last_ref[:, j * part : (j + 1) * part], NN) * gain_ref[:, cols]
+        if j < slots // 2:
+            grads = early_ref[:, j * part : (j + 1) * part]
+        else:
+            grads = late_ref[:, (j - slots // 2) * part : (j - slots // 2 + 1) * part]
+        gained = mm(both, grads, NN) * gain_ref[:, cols]
         d_normed_ref[:, cols] = gained
         square = square + jnp.sum(stream * stream, axis=-1, keepdims=True)
         dot = dot + jnp.sum(gained * stream, axis=-1, keepdims=True)
@@ -557,11 +600,21 @@
     cot = cotangent[0]
     place = places(groups)
 
+    one = 2 * total * width * ffw
+    send_cot = call(
+        functools.partial(send_cot_kernel, owners, cap),
+        sds((total, width)),
+        (ids_t, weights, cot),
+        [VMEM] * 3,
+        flops=4 * total * tokens * width,
+        moved=2 * (total + tokens) * width,
+    )
+    cot_rows = exchange(send_cot, owners, "exp")
     shards = (w_gate[0].T, w_up[0].T, w_down[0])
     if groups == 4:
         join = join_middle
         pieces, gate_in, up_in, down_in, norm_after, up_after = line_of_four(
-            place, queries[0], keys[0], values[0], *shards
+            place, queries[0], keys[0], values[0], *shards, send_cot
         )
     else:
         join = join_groups
@@ -573,16 +626,6 @@
         norm_after = up_after = ()
     shape = [len(choices) for choices in gate_in]
 
-    one = 2 * total * width * ffw
-    send_cot = call(
-        functools.partial(send_cot_kernel, owners, cap),
-        sds((total, width)),
-        (ids_t, weights, cot),
-        [VMEM] * 3,
-        flops=4 * total * tokens * width,
-        moved=2 * (total + tokens) * width,
-    )
-    cot_rows = exchange(send_cot, owners, "exp")
     stream, send_rows = call(
         functools.partial(norm_kernel, owners, cap, join),
         (sds((tokens, width)), sds((total, width))),
@@ -591,7 +634,7 @@
         [pltpu.VMEM((tokens, width), BF)],
         flops=2 * total * tokens * width,
         moved=2 * (total + 3 * tokens) * width,
-        after=norm_after,
+        after=(*norm_after, cot_rows),
     )
     rows = exchange(send_rows, owners, "exp")
 
@@ -620,9 +663,13 @@
         moved=2 * width * ffw + 4 * total * width + 6 * total * ffw,
     )
     back_first = exchange(out_first, owners, "exp")
-    back = call(
-        functools.partial(grad_kernel, shape),
-        sds((total, width + part)),
+    early = groups // 2
+    shape_early = [*shape[:early], shape[-1]]
+    half_w = pltpu.VMEM((early, ffw, part), BF)
+    late_w = pltpu.VMEM((groups - early, ffw, part), BF)
+    back, d_gate, d_up = call(
+        functools.partial(grad_kernel, shape_early),
+        (sds((total, (early + 1) * part)), sds((total, ffw)), sds((total, ffw))),
         (
             place,
             hidden,
@@ -631,29 +678,45 @@
             to_gate,
             to_up,
             *flat(down_in[-1:]),
-            *flat(gate_in),
-            *flat(up_in),
+            *flat(gate_in[:early]),
+            *flat(up_in[:early]),
         ),
-        [SMEM] + [VMEM] * 5 + [HBM] * (shape[-1] + 2 * sum(shape)),
+        [SMEM] + [HBM] * (5 + shape[-1] + 2 * sum(shape[:early])),
         [
             pltpu.VMEM((ffw, part), BF),
-            full_w,
-            full_w,
-            pltpu.SemaphoreType.DMA((3, groups)),
+            half_w,
+            half_w,
+            pltpu.SemaphoreType.DMA((8, groups)),
+            pltpu.VMEM((total, ffw), BF),
+            pltpu.VMEM((total, part), BF),
+            pltpu.VMEM((total, ffw), F32),
+            pltpu.VMEM((total, ffw), F32),
+            pltpu.VMEM((total, ffw), F32),
         ],
-        flops=2 * one + 2 * one // groups,
-        moved=4 * width * ffw + 4 * total * width + 14 * total * ffw,
-
-    )
-    back_last = exchange(back, owners, "exp")
+        flops=one + 2 * one // groups,
+        moved=2 * width * ffw + 2 * total * width + 18 * total * ffw,
+    )
+    back_early = exchange(back, owners, "exp")
+    rest = call(
+        functools.partial(rest_kernel, shape[early:]),
+        sds((total, width - early * part)),
+        (place, d_gate, d_up, *flat(gate_in[early:]), *flat(up_in[early:])),
+        [SMEM, VMEM, VMEM] + [HBM] * (2 * sum(shape[early:])),
+        [late_w, late_w, pltpu.SemaphoreType.DMA((2, groups))],
+        flops=one,
+        moved=2 * width * ffw + 2 * total * width + 4 * total * ffw,
+    )
+    back_late = exchange(rest, owners, "exp")
     output, stream_grad = call(
         functools.partial(final_kernel, owners, cap),
         (sds((tokens, width)), sds((tokens, width))),
-        (place, ids, weights, gain, stream, cot, back_first, back_last),
-        [SMEM] + [VMEM] * 7,
+        (place, ids, weights, gain, stream, cot, back_first, back_early, back_late),
+        [SMEM] + [VMEM] * 8,
         [pltpu.VMEM((tokens, width), F32)],
         flops=6 * total * tokens * width,
         moved=4 * total * width + 8 * tokens * width,
+        vmem=16,
+        held=True,
     )
     return (output[None], stream_grad[None])
 

time: 254 us -> 241 us (0.949)
  waiting for transfers between devices: 111 us -> 76.2 us
  starting transfers between devices: 69.2 us -> 84.2 us
  blocking collectives: 26 us -> 31.9 us
    ppermute x24, waiting for transfers between devices: 110 us -> 75.8 us  [send(): return lax.ppermute(gated(array, *first), 'seq', pairs)]
    ppermute x24, starting transfers between devices: 56.9 us -> 73.1 us  [send(): return lax.ppermute(gated(array, *first), 'seq', pairs)]
    all_to_all x1 -> x2, blocking collectives: 26 us -> 31.9 us  [exchange(): rows = lax.all_to_all(rows, axis, split_axis=0, concat_axis=0, tiled=True)]
    pallas_call x8 -> x9, Pallas kernels: 37.4 us -> 38.8 us  [call(): pl.pallas_call(body, grid=() if held else (1,), out_shape=outs, in_specs=...]
    unnamed x56 -> x50, local copies, waits for them, and re-layouts: 5.26 us -> 5.7 us
  transfers between devices with their start and end apart: 27 -> 27, of which waited for: 11 -> 11; matrix products, arithmetic and copies ran while one was open for 1% -> 1% of each run, Pallas kernels for 11% -> 14%
where the time goes in v4:
time: 241 us; the launch traced here: 240 us
  starting transfers between devices  84.2 us (35%)
  waiting for transfers between devices  76.2 us (32%)
  Pallas kernels  38.8 us (16%)
  blocking collectives  31.9 us (13%)
  local copies, waits for them, and re-layouts  7.63 us (3%)
    ppermute x24, waiting for transfers between devices, send(): return lax.ppermute(gated(array, *first), 'seq', pairs)  75.8 us
    ppermute x24, starting transfers between devices, send(): return lax.ppermute(gated(array, *first), 'seq', pairs)  73.1 us
    pallas_call x9, Pallas kernels, call(): pl.pallas_call(body, grid=() if held else (1,), out_shape=outs, in_specs=...  38.8 us
    all_to_all x2, blocking collectives, exchange(): rows = lax.all_to_all(rows, axis, split_axis=0, concat_axis=0, tiled=True)  31.9 us
    all_to_all x3, starting transfers between devices, exchange(): rows = lax.all_to_all(rows, axis, split_axis=0, concat_axis=0, tiled=True)  11.1 us
    unnamed x50, local copies, waits for them, and re-layouts  5.7 us
  transfers between devices with their start and end apart: 27, of which 11 were waited for; matrix products, arithmetic and copies ran while one was open for 1% of the time, Pallas kernels for 14%

profile of v4, /device:TPU:0, one launch (start us, length us, event | category | flops | bytes accessed | tf_op | source)
XLA Modules:
  0.0 239.8 jit_solution(9444226793818619356)
XLA Ops:
  0.7 1.3 dynamic-slice_bitcast_fusion.refs_0_
  1.9 2.6 %shard_map.131 = (bf16[384,1024]{1,0:T(8,128)(2,1)}, bf16[384,1024]{1,0:T(8,128)(2,1)}) custom-call(s32[10]{0:T(128)} %dynamic-slice_bitcast_fusion.refs_0_, bf16[128,2048]{1,0:T(8,128)(2,1)} %bitcast.56, bf16[128,2048]{1,0:T(8,128)(2,1)} %bitcast.57, bf16[128,2048]{1,0:T(8,128)(2,1)} %bitcast.58), custom_call_target="tpu_custom_call" | custom-call | bytes 3145728 | tf_op jit(solution)/shard_map/pallas_call | solution.py:35
  4.6 5.0 %collective-permute-start = (bf16[384,1024]{1,0:T(8,128)(2,1)}, bf16[384,1024]{1,0:T(8,128)(2,1)S(1)}, u32[]{:S(2)}, u32[]{:S(2)}) collective-permute-start(bf16[384,1024]{1,0:T(8,128)(2,1)} %get-tuple-element.37.refs_1_), channel_id=1, source_target_pairs={{0,8},{24,16},{1,9},{25,17},{2,10},{26,18},{3,11},{27,19},{4,12},{... | collective-permute-start | bytes 2359304 | tf_op jit(solution)/shard_map/ppermute | solution.py:546
  10.3 4.0 %collective-permute-start.2 = (bf16[384,1024]{1,0:T(8,128)(2,1)}, bf16[384,1024]{1,0:T(8,128)(2,1)S(1)}, u32[]{:S(2)}, u32[]{:S(2)}) collective-permute-start(bf16[384,1024]{1,0:T(8,128)(2,1)} %get-tuple-element.38), channel_id=1, source_target_pairs={{0,16},{24,8},{1,17},{25,9},{2,18},{26,10},{3,19},{27,11},{4,20},{... | collective-permute-start | bytes 2359304 | tf_op jit(solution)/shard_map/ppermute | solution.py:546
  14.2 1.3 collective-permute-start.3
  15.5 1.3 collective-permute-start.4
  16.8 10.9 %collective-permute-done.refs_2_ = bf16[384,1024]{1,0:T(8,128)(2,1)S(1)} collective-permute-done((bf16[384,1024]{1,0:T(8,128)(2,1)}, bf16[384,1024]{1,0:T(8,128)(2,1)S(1)}, u32[]{:S(2)}, u32[]{:S(2)}) %collective-permute-start) | collective-permute-done | bytes 786464 | tf_op jit(solution)/shard_map/ppermute | solution.py:546
  27.7 1.3 collective-permute-start.7
  29.0 14.4 %collective-permute-done.2.refs_4_ = bf16[384,1024]{1,0:T(8,128)(2,1)S(1)} collective-permute-done((bf16[384,1024]{1,0:T(8,128)(2,1)}, bf16[384,1024]{1,0:T(8,128)(2,1)S(1)}, u32[]{:S(2)}, u32[]{:S(2)}) %collective-permute-start.2) | collective-permute-done | bytes 786464 | tf_op jit(solution)/shard_map/ppermute | solution.py:546
  44.4 9.0 %collective-permute-start.6 = (bf16[704,512]{1,0:T(8,128)(2,1)S(1)}, bf16[704,512]{1,0:T(8,128)(2,1)}, u32[]{:S(2)}, u32[]{:S(2)}) collective-permute-start(bf16[704,512]{1,0:T(8,128)(2,1)S(1)} %bitcast.50), channel_id=1, source_target_pairs={{0,8},{24,16},{1,9},{25,17},{2,10},{26,18},{3,11},{27,19},{4,12},{... | collective-permute-start | bytes 2162696 | tf_op jit(solution)/shard_map/ppermute | solution.py:546
  54.9 3.2 %shard_map.132.refs_7_ = bf16[320,2048]{1,0:T(8,128)(2,1)} custom-call(s32[2,128]{1,0:T(2,128)} %copy.17.refs_0_.refs_1_, f32[128,2]{1,0:T(8,128)} %bitcast.36, bf16[128,2048]{1,0:T(8,128)(2,1)} %bitcast.34), custom_call_target="tpu_custom_call" | custom-call | flops 335544320 | bytes 1835008 | tf_op jit(solution)/shard_map/pallas_call | solution.py:35
  58.1 0.9 copy-done.8
  59.0 0.9 copy-done.9
  59.9 1.7 shard_map.133
  61.6 2.9 %collective-permute-done.7.refs_5_ = bf16[704,512]{1,0:T(8,128)(2,1)} collective-permute-done((bf16[704,512]{1,0:T(8,128)(2,1)}, bf16[704,512]{1,0:T(8,128)(2,1)}, u32[]{:S(2)}, u32[]{:S(2)}) %collective-permute-start.7) | collective-permute-done | bytes 720928 | tf_op jit(solution)/shard_map/ppermute | solution.py:546
  64.4 2.3 collective-permute-done.6.refs_3_.refs_9_
  67.5 1.3 collective-permute-start.10
  68.8 3.7 %all-to-all-start = ((bf16[8,40,2048]{2,1,0:T(8,128)(2,1)}), bf16[8,40,2048]{2,1,0:T(8,128)(2,1)S(1)}, u32[]{:S(2)}, u32[]{:S(2)}) async-start(bf16[8,40,2048]{2,1,0:T(8,128)(2,1)} %bitcast.17), calls=%async_computation | async-start | bytes 2621440 | tf_op jit(solution)/shard_map/all_to_all | solution.py:568
  73.2 14.3 %collective-permute-start.15 = (bf16[704,512]{1,0:T(8,128)(2,1)}, bf16[704,512]{1,0:T(8,128)(2,1)}, u32[]{:S(2)}, u32[]{:S(2)}) collective-permute-start(bf16[704,512]{1,0:T(8,128)(2,1)} %bitcast.12.refs_9_.refs_11_), channel_id=1, source_target_pairs={{0,8},{24,16},{1,9},{25,17},{2,10},{26,18},{3,11},{27,19},{4,12},{... | collective-permute-start | bytes 2162696 | tf_op jit(solution)/shard_map/ppermute | solution.py:546
  87.5 2.3 collective-permute-done.10.refs_7_
  90.5 1.5 collective-permute-start.13
  92.0 1.3 collective-permute-start.11
  93.3 1.3 collective-permute-start.8
  94.6 8.1 %collective-permute-done.15.refs_10_.refs_12_ = bf16[704,512]{1,0:T(8,128)(2,1)} collective-permute-done((bf16[704,512]{1,0:T(8,128)(2,1)}, bf16[704,512]{1,0:T(8,128)(2,1)}, u32[]{:S(2)}, u32[]{:S(2)}) %collective-permute-start.15) | collective-permute-done | bytes 720928 | tf_op jit(solution)/shard_map/ppermute | solution.py:546
  102.7 1.3 collective-permute-start.16
  104.0 1.6 collective-permute-start.17
  105.6 18.6 %collective-permute-start.19 = (bf16[704,512]{1,0:T(8,128)(2,1)}, bf16[704,512]{1,0:T(8,128)(2,1)}, u32[]{:S(2)}, u32[]{:S(2)}) collective-permute-start(bf16[704,512]{1,0:T(8,128)(2,1)} %bitcast.15.refs_3_), channel_id=1, source_target_pairs={{0,8},{24,16},{1,9},{25,17},{2,10},{26,18},{3,11},{27,19},{4,12},{... | collective-permute-start | bytes 2162696 | tf_op jit(solution)/shard_map/ppermute | solution.py:546
  124.1 1.3 collective-permute-start.14
  125.4 1.6 collective-permute-start.21
  127.0 1.1 copy-done.5
  128.1 3.3 %shard_map.134 = (bf16[128,2048]{1,0:T(8,128)(2,1)}, bf16[320,2048]{1,0:T(8,128)(2,1)}) custom-call(s32[10]{0:T(128)} %dynamic-slice_bitcast_fusion.refs_0_, s32[2,128]{1,0:T(2,128)} %copy.17.refs_0_.refs_1_, bf16[128,2048]{1,0:T(8,128)(2,1)} %bitcast.55, f32[1,2048]{1,0:T(1,128)} %bitcast.40, bf16[128,1024]{1,0:T(8,128)(2,1)} %get-tuple-element.45.refs_4_, ...), custom_call_target="tpu_custom_call" | custom-call | flops 167772160 | bytes 2883584 | tf_op jit(solution)/shard_map/pallas_call | solution.py:35
  131.4 3.6 %all-to-all-start.1 = ((bf16[8,40,2048]{2,1,0:T(8,128)(2,1)}), bf16[8,40,2048]{2,1,0:T(8,128)(2,1)S(1)}, u32[]{:S(2)}, u32[]{:S(2)}) async-start(bf16[8,40,2048]{2,1,0:T(8,128)(2,1)} %bitcast.52), calls=%async_computation.1 | async-start | bytes 2621440 | tf_op jit(solution)/shard_map/all_to_all | solution.py:568
  135.0 1.3 collective-permute-start.18
  137.0 12.5 %collective-permute-done.14.refs_8_.refs_6_ = bf16[704,512]{1,0:T(8,128)(2,1)} collective-permute-done((bf16[704,512]{1,0:T(8,128)(2,1)}, bf16[704,512]{1,0:T(8,128)(2,1)}, u32[]{:S(2)}, u32[]{:S(2)}) %collective-permute-start.14) | collective-permute-done | bytes 720928 | tf_op jit(solution)/shard_map/ppermute | solution.py:546
  149.6 1.3 collective-permute-start.22
  150.8 14.1 %collective-permute-done.18.refs_15_.refs_10_ = bf16[704,512]{1,0:T(8,128)(2,1)S(1)} collective-permute-done((bf16[704,512]{1,0:T(8,128)(2,1)}, bf16[704,512]{1,0:T(8,128)(2,1)S(1)}, u32[]{:S(2)}, u32[]{:S(2)}) %collective-permute-start.18) | collective-permute-done | bytes 720928 | tf_op jit(solution)/shard_map/ppermute | solution.py:546
  164.9 1.3 collective-permute-start.23
  166.2 1.0 copy-done.10
  167.3 8.0 %shard_map.135 = (bf16[320,704]{1,0:T(8,128)(2,1)}, f32[320,704]{1,0:T(8,128)}, f32[320,704]{1,0:T(8,128)}) custom-call(s32[10]{0:T(128)} %dynamic-slice_bitcast_fusion.refs_0_, bf16[320,2048]{1,0:T(8,128)(2,1)} %bitcast.45, bf16[704,512]{1,0:T(8,128)(2,1)} %bitcast.46, bf16[704,512]{1,0:T(8,128)(2,1)} %collective-permute-done.6.refs_3_.refs_9_, ...), custom_call_target="tpu_custom_call" | custom-call | flops 1845493760 | bytes 9330688 | tf_op jit(solution)/shard_map/pallas_call | solution.py:35
  175.2 5.2 %collective-permute-done.22.refs_7_ = bf16[704,512]{1,0:T(8,128)(2,1)} collective-permute-done((bf16[704,512]{1,0:T(8,128)(2,1)}, bf16[704,512]{1,0:T(8,128)(2,1)}, u32[]{:S(2)}, u32[]{:S(2)}) %collective-permute-start.22) | collective-permute-done | bytes 720928 | tf_op jit(solution)/shard_map/ppermute | solution.py:546
  180.5 5.9 %shard_map.136 = (bf16[320,1536]{1,0:T(8,128)(2,1)}, f32[320,704]{1,0:T(8,128)}) custom-call(s32[10]{0:T(128)} %dynamic-slice_bitcast_fusion.refs_0_, bf16[320,704]{1,0:T(8,128)(2,1)} %get-tuple-element.59.refs_1_, bf16[320,2048]{1,0:T(8,128)(2,1)} %bitcast.43, bf16[704,512]{1,0:T(8,128)(2,1)} %bitcast.15.refs_3_, ...), custom_call_target="tpu_custom_call" | custom-call | flops 1384120320 | bytes 6856704 | tf_op jit(solution)/shard_map/pallas_call | solution.py:35
  186.4 3.7 %all-to-all-start.2 = ((bf16[8,40,1536]{2,1,0:T(8,128)(2,1)}), bf16[8,40,1536]{2,1,0:T(8,128)(2,1)S(1)}, u32[]{:S(2)}, u32[]{:S(2)}) async-start(bf16[8,40,1536]{2,1,0:T(8,128)(2,1)} %bitcast.53), calls=%async_computation.2 | async-start | bytes 1966080 | tf_op jit(solution)/shard_map/all_to_all | solution.py:568
  190.1 3.1 %collective-permute-done.23.refs_7_ = bf16[704,512]{1,0:T(8,128)(2,1)} collective-permute-done((bf16[704,512]{1,0:T(8,128)(2,1)S(1)}, bf16[704,512]{1,0:T(8,128)(2,1)}, u32[]{:S(2)}, u32[]{:S(2)}) %collective-permute-start.23) | collective-permute-done | bytes 720928 | tf_op jit(solution)/shard_map/ppermute | solution.py:546
  193.2 6.2 %shard_map.137 = (bf16[320,1536]{1,0:T(8,128)(2,1)}, bf16[320,704]{1,0:T(8,128)(2,1)}, bf16[320,704]{1,0:T(8,128)(2,1)}) custom-call(s32[10]{0:T(128)} %dynamic-slice_bitcast_fusion.refs_0_, bf16[320,704]{1,0:T(8,128)(2,1)} %get-tuple-element.59.refs_1_, bf16[320,2048]{1,0:T(8,128)(2,1)} %bitcast.44, f32[320,704]{1,0:T(8,128)} %get-tuple-element.63.refs_3_, ...), custom_call_target="tpu_custom_call" | custom-call | flops 1384120320 | bytes 8249344 | tf_op jit(solution)/shard_map/pallas_call | solution.py:35
  199.5 4.8 %shard_map.138 = bf16[320,1024]{1,0:T(8,128)(2,1)} custom-call(s32[10]{0:T(128)} %dynamic-slice_bitcast_fusion.refs_0_, bf16[320,704]{1,0:T(8,128)(2,1)} %get-tuple-element.68.refs_1_, bf16[320,704]{1,0:T(8,128)(2,1)} %get-tuple-element.69.refs_2_, bf16[704,512]{1,0:T(8,128)(2,1)} %copy-done.11, bf16[704,512]{1,0:T(8,128)(2,1)} %copy-done.7, ...), custom_call_target="tpu_custom_call" | custom-call | flops 922746880 | bytes 5095424 | tf_op jit(solution)/shard_map/pallas_call | solution.py:35
  204.7 14.7 %all_to_all.25 = bf16[8,40,1024]{2,1,0:T(8,128)(2,1)S(1)} all-to-all(bf16[8,40,1024]{2,1,0:T(8,128)(2,1)} %bitcast.51), channel_id=1, replica_groups=mesh['seq'=4,'exp'=8] {'exp'}, dimensions={0} | all-to-all | bytes 1310720 | tf_op jit(solution)/shard_map/all_to_all | solution.py:568
  219.5 17.2 %all_to_all.26 = bf16[8,40,1536]{2,1,0:T(8,128)(2,1)S(1)} all-to-all(bf16[8,40,1536]{2,1,0:T(8,128)(2,1)S(1)} %bitcast.54), channel_id=1, replica_groups=mesh['seq'=4,'exp'=8] {'exp'}, dimensions={0} | all-to-all | bytes 1966080 | tf_op jit(solution)/shard_map/all_to_all | solution.py:568
  236.7 3.1 %shard_map.139 = (bf16[128,2048]{1,0:T(8,128)(2,1)}, bf16[128,2048]{1,0:T(8,128)(2,1)}) custom-call(s32[10]{0:T(128)S(1)} %copy-done.4, s32[128,2]{1,0:T(8,128)S(1)} %bitcast.39, f32[128,2]{1,0:T(8,128)S(1)} %bitcast.37, f32[1,2048]{1,0:T(1,128)S(1)} %bitcast.41, bf16[128,2048]{1,0:T(8,128)(2,1)S(1)} %copy-done.2, bf16[128,2048]{1,0:T(8,128)(2,1)S(1)} %bitcast.35, ...), custom_call_target="tpu_custom_call" | custom-call | flops 503316480 | bytes 4718592 | tf_op jit(solution)/shard_map/pallas_call | solution.py:35
  (69 shorter events, 6.4 us)
Async XLA Ops:
  0.6 13.6 %copy-start.13 = (bf16[1,512,704]{1,2,0:T(8,128)(2,1)S(1)}, bf16[1,512,704]{1,2,0:T(8,128)(2,1)}, u32[]{:S(2)}) copy-start(bf16[1,512,704]{1,2,0:T(8,128)(2,1)} %param.17) | copy-start | bytes 2162692
  0.6 52.8 %copy-start.22 = (s32[1,128,2]{1,2,0:T(2,128)S(1)}, s32[1,128,2]{1,2,0:T(2,128)}, u32[]{:S(2)}) copy-start(s32[1,128,2]{1,2,0:T(2,128)} %param.20) | copy-start | bytes 3076
  0.7 52.9 %copy-start.23 = (f32[1,128,2]{1,2,0:T(2,128)S(1)}, f32[1,128,2]{1,2,0:T(2,128)}, u32[]{:S(2)}) copy-start(f32[1,128,2]{1,2,0:T(2,128)} %param.21) | copy-start | bytes 3076
  4.6 23.2 %collective-permute-start = (bf16[384,1024]{1,0:T(8,128)(2,1)}, bf16[384,1024]{1,0:T(8,128)(2,1)S(1)}, u32[]{:S(2)}, u32[]{:S(2)}) collective-permute-start(bf16[384,1024]{1,0:T(8,128)(2,1)} %get-tuple-element.37.refs_1_), channel_id=1, source_target_pairs={{0,8},{24,16},{1,9},{25,17},{2,10},{26,18},{3,11},{27,19},{4,12},{... | collective-permute-start | bytes 2359304 | tf_op jit(solution)/shard_map/ppermute | solution.py:546
  9.5 19.5 %collective-permute-start.1 = (bf16[384,1024]{1,0:T(8,128)(2,1)}, bf16[384,1024]{1,0:T(8,128)(2,1)S(1)}, u32[]{:S(2)}, u32[]{:S(2)}) collective-permute-start(bf16[384,1024]{1,0:T(8,128)(2,1)} %get-tuple-element.38), channel_id=1, source_target_pairs={{8,16},{16,8},{9,17},{17,9},{10,18},{18,10},{11,19},{19,11},{12,20... | collective-permute-start | bytes 2359304 | tf_op jit(solution)/shard_map/ppermute | solution.py:546
  10.3 33.2 %collective-permute-start.2 = (bf16[384,1024]{1,0:T(8,128)(2,1)}, bf16[384,1024]{1,0:T(8,128)(2,1)S(1)}, u32[]{:S(2)}, u32[]{:S(2)}) collective-permute-start(bf16[384,1024]{1,0:T(8,128)(2,1)} %get-tuple-element.38), channel_id=1, source_target_pairs={{0,16},{24,8},{1,17},{25,9},{2,18},{26,10},{3,19},{27,11},{4,20},{... | collective-permute-start | bytes 2359304 | tf_op jit(solution)/shard_map/ppermute | solution.py:546
  14.2 43.9 %collective-permute-start.3 = (bf16[704,512]{1,0:T(8,128)(2,1)S(1)}, bf16[704,512]{1,0:T(8,128)(2,1)S(1)}, u32[]{:S(2)}, u32[]{:S(2)}) collective-permute-start(bf16[704,512]{1,0:T(8,128)(2,1)S(1)} %bitcast.48), channel_id=1, source_target_pairs={{8,0},{16,24},{9,1},{17,25},{10,2},{18,26},{11,3},{19,27},{12,4},{... | collective-permute-start | bytes 2162696 | tf_op jit(solution)/shard_map/ppermute | solution.py:546
  15.5 42.6 %collective-permute-start.4 = (bf16[704,512]{1,0:T(8,128)(2,1)}, bf16[704,512]{1,0:T(8,128)(2,1)S(1)}, u32[]{:S(2)}, u32[]{:S(2)}) collective-permute-start(bf16[704,512]{1,0:T(8,128)(2,1)} %bitcast.12.refs_9_.refs_11_), channel_id=1, source_target_pairs={{8,0},{16,24},{9,1},{17,25},{10,2},{18,26},{11,3},{19,27},{12,4},{... | collective-permute-start | bytes 2162696 | tf_op jit(solution)/shard_map/ppermute | solution.py:546
  27.7 16.5 %copy-start.16 = (bf16[384,1024]{1,0:T(8,128)(2,1)}, bf16[384,1024]{1,0:T(8,128)(2,1)S(1)}, u32[]{:S(2)}) copy-start(bf16[384,1024]{1,0:T(8,128)(2,1)S(1)} %collective-permute-done.refs_2_) | copy-start | bytes 2359300
  27.7 36.7 %collective-permute-start.7 = (bf16[704,512]{1,0:T(8,128)(2,1)}, bf16[704,512]{1,0:T(8,128)(2,1)}, u32[]{:S(2)}, u32[]{:S(2)}) collective-permute-start(bf16[704,512]{1,0:T(8,128)(2,1)} %bitcast.15.refs_3_), channel_id=1, source_target_pairs={{8,0},{16,24},{9,1},{17,25},{10,2},{18,26},{11,3},{19,27},{12,4},{... | collective-permute-start | bytes 2162696 | tf_op jit(solution)/shard_map/ppermute | solution.py:546
  29.0 15.2 %copy-start.17 = (bf16[384,1024]{1,0:T(8,128)(2,1)}, bf16[384,1024]{1,0:T(8,128)(2,1)S(1)}, u32[]{:S(2)}) copy-start(bf16[384,1024]{1,0:T(8,128)(2,1)S(1)} %collective-permute-done.1.refs_3_) | copy-start | bytes 2359300
  43.5 21.0 %collective-permute-start.5 = (bf16[704,512]{1,0:T(8,128)(2,1)S(1)}, bf16[704,512]{1,0:T(8,128)(2,1)S(1)}, u32[]{:S(2)}, u32[]{:S(2)}) collective-permute-start(bf16[704,512]{1,0:T(8,128)(2,1)S(1)} %bitcast.49), channel_id=1, source_target_pairs={{8,16},{16,8},{9,17},{17,9},{10,18},{18,10},{11,19},{19,11},{12,20... | collective-permute-start | bytes 2162696 | tf_op jit(solution)/shard_map/ppermute | solution.py:546
  44.4 22.4 %collective-permute-start.6 = (bf16[704,512]{1,0:T(8,128)(2,1)S(1)}, bf16[704,512]{1,0:T(8,128)(2,1)}, u32[]{:S(2)}, u32[]{:S(2)}) collective-permute-start(bf16[704,512]{1,0:T(8,128)(2,1)S(1)} %bitcast.50), channel_id=1, source_target_pairs={{0,8},{24,16},{1,9},{25,17},{2,10},{26,18},{3,11},{27,19},{4,12},{... | collective-permute-start | bytes 2162696 | tf_op jit(solution)/shard_map/ppermute | solution.py:546
  58.1 0.9 copy-start.8
  64.4 66.9 %copy-start.11 = (bf16[704,512]{1,0:T(8,128)(2,1)}, bf16[704,512]{1,0:T(8,128)(2,1)S(1)}, u32[]{:S(2)}) copy-start(bf16[704,512]{1,0:T(8,128)(2,1)S(1)} %collective-permute-done.5.refs_5_.refs_3_) | copy-start | bytes 2162692
  66.8 20.7 %collective-permute-start.9 = (bf16[128,1024]{1,0:T(8,128)(2,1)}, bf16[128,1024]{1,0:T(8,128)(2,1)S(1)}, u32[]{:S(2)}, u32[]{:S(2)}) collective-permute-start(bf16[128,1024]{1,0:T(8,128)(2,1)} %get-tuple-element.47), channel_id=1, source_target_pairs={{8,16},{16,8},{9,17},{17,9},{10,18},{18,10},{11,19},{19,11},{12,20... | collective-permute-start | bytes 786440 | tf_op jit(solution)/shard_map/ppermute | solution.py:546
  67.5 22.3 %collective-permute-start.10 = (bf16[128,1024]{1,0:T(8,128)(2,1)}, bf16[128,1024]{1,0:T(8,128)(2,1)S(1)}, u32[]{:S(2)}, u32[]{:S(2)}) collective-permute-start(bf16[128,1024]{1,0:T(8,128)(2,1)} %get-tuple-element.48), channel_id=1, source_target_pairs={{16,0},{8,24},{17,1},{9,25},{18,2},{10,26},{19,3},{11,27},{20,4},{... | collective-permute-start | bytes 786440 | tf_op jit(solution)/shard_map/ppermute | solution.py:546
  68.8 58.2 %all-to-all-start = ((bf16[8,40,2048]{2,1,0:T(8,128)(2,1)}), bf16[8,40,2048]{2,1,0:T(8,128)(2,1)S(1)}, u32[]{:S(2)}, u32[]{:S(2)}) async-start(bf16[8,40,2048]{2,1,0:T(8,128)(2,1)} %bitcast.17), calls=%async_computation | async-start | bytes 2621440 | tf_op jit(solution)/shard_map/all_to_all | solution.py:568
  72.5 22.1 %collective-permute-start.12 = (bf16[704,512]{1,0:T(8,128)(2,1)}, bf16[704,512]{1,0:T(8,128)(2,1)S(1)}, u32[]{:S(2)}, u32[]{:S(2)}) collective-permute-start(bf16[704,512]{1,0:T(8,128)(2,1)} %bitcast.12.refs_9_.refs_11_), channel_id=1, source_target_pairs={{8,16},{16,8},{9,17},{17,9},{10,18},{18,10},{11,19},{19,11},{12,20... | collective-permute-start | bytes 2162696 | tf_op jit(solution)/shard_map/ppermute | solution.py:546
  73.2 29.5 %collective-permute-start.15 = (bf16[704,512]{1,0:T(8,128)(2,1)}, bf16[704,512]{1,0:T(8,128)(2,1)}, u32[]{:S(2)}, u32[]{:S(2)}) collective-permute-start(bf16[704,512]{1,0:T(8,128)(2,1)} %bitcast.12.refs_9_.refs_11_), channel_id=1, source_target_pairs={{0,8},{24,16},{1,9},{25,17},{2,10},{26,18},{3,11},{27,19},{4,12},{... | collective-permute-start | bytes 2162696 | tf_op jit(solution)/shard_map/ppermute | solution.py:546
  87.5 2.3 copy-start.19
  90.5 15.1 %collective-permute-start.13 = (bf16[704,512]{1,0:T(8,128)(2,1)}, bf16[704,512]{1,0:T(8,128)(2,1)}, u32[]{:S(2)}, u32[]{:S(2)}) collective-permute-start(bf16[704,512]{1,0:T(8,128)(2,1)} %collective-permute-done.6.refs_3_.refs_9_), channel_id=1, source_target_pairs={{8,16},{16,8},{9,17},{17,9},{10,18},{18,10},{11,19},{19,11},{12,20... | collective-permute-start | bytes 2162696 | tf_op jit(solution)/shard_map/ppermute | solution.py:546
  92.0 33.4 %collective-permute-start.11 = (bf16[704,512]{1,0:T(8,128)(2,1)S(1)}, bf16[704,512]{1,0:T(8,128)(2,1)S(1)}, u32[]{:S(2)}, u32[]{:S(2)}) collective-permute-start(bf16[704,512]{1,0:T(8,128)(2,1)S(1)} %collective-permute-done.5.refs_5_.refs_3_), channel_id=1, source_target_pairs={{8,0},{16,24},{9,1},{17,25},{10,2},{18,26},{11,3},{19,27},{12,4},{... | collective-permute-start | bytes 2162696 | tf_op jit(solution)/shard_map/ppermute | solution.py:546
  93.3 30.9 %collective-permute-start.8 = (bf16[128,1024]{1,0:T(8,128)(2,1)}, bf16[128,1024]{1,0:T(8,128)(2,1)S(1)}, u32[]{:S(2)}, u32[]{:S(2)}) collective-permute-start(bf16[128,1024]{1,0:T(8,128)(2,1)} %get-tuple-element.46), channel_id=1, source_target_pairs={{8,0},{16,24},{9,1},{17,25},{10,2},{18,26},{11,3},{19,27},{12,4},{... | collective-permute-start | bytes 786440 | tf_op jit(solution)/shard_map/ppermute | solution.py:546
  94.6 32.4 %copy-start.6 = (bf16[704,512]{1,0:T(8,128)(2,1)}, bf16[704,512]{1,0:T(8,128)(2,1)S(1)}, u32[]{:S(2)}) copy-start(bf16[704,512]{1,0:T(8,128)(2,1)S(1)} %collective-permute-done.12.refs_9_.refs_12_.refs_7_) | copy-start | bytes 2162692
  102.7 32.3 %collective-permute-start.16 = (bf16[704,512]{1,0:T(8,128)(2,1)S(1)}, bf16[704,512]{1,0:T(8,128)(2,1)}, u32[]{:S(2)}, u32[]{:S(2)}) collective-permute-start(bf16[704,512]{1,0:T(8,128)(2,1)S(1)} %collective-permute-done.12.refs_9_.refs_12_.refs_7_), channel_id=1, source_target_pairs={{8,0},{16,24},{9,1},{17,25},{10,2},{18,26},{11,3},{19,27},{12,4},{... | collective-permute-start | bytes 2162696 | tf_op jit(solution)/shard_map/ppermute | solution.py:546
  104.0 31.0 %collective-permute-start.17 = (bf16[704,512]{1,0:T(8,128)(2,1)}, bf16[704,512]{1,0:T(8,128)(2,1)}, u32[]{:S(2)}, u32[]{:S(2)}) collective-permute-start(bf16[704,512]{1,0:T(8,128)(2,1)} %collective-permute-done.15.refs_10_.refs_12_), channel_id=1, source_target_pairs={{8,16},{16,8},{9,17},{17,9},{10,18},{18,10},{11,19},{19,11},{12,20... | collective-permute-start | bytes 2162696 | tf_op jit(solution)/shard_map/ppermute | solution.py:546
  105.6 30.8 %collective-permute-start.19 = (bf16[704,512]{1,0:T(8,128)(2,1)}, bf16[704,512]{1,0:T(8,128)(2,1)}, u32[]{:S(2)}, u32[]{:S(2)}) collective-permute-start(bf16[704,512]{1,0:T(8,128)(2,1)} %bitcast.15.refs_3_), channel_id=1, source_target_pairs={{0,8},{24,16},{1,9},{25,17},{2,10},{26,18},{3,11},{27,19},{4,12},{... | collective-permute-start | bytes 2162696 | tf_op jit(solution)/shard_map/ppermute | solution.py:546
  124.1 1.3 copy-start.21
  124.1 25.4 %collective-permute-start.14 = (bf16[704,512]{1,0:T(8,128)(2,1)}, bf16[704,512]{1,0:T(8,128)(2,1)}, u32[]{:S(2)}, u32[]{:S(2)}) collective-permute-start(bf16[704,512]{1,0:T(8,128)(2,1)} %collective-permute-done.13.refs_7_.refs_5_), channel_id=1, source_target_pairs={{8,0},{16,24},{9,1},{17,25},{10,2},{18,26},{11,3},{19,27},{12,4},{... | collective-permute-start | bytes 2162696 | tf_op jit(solution)/shard_map/ppermute | solution.py:546
  125.4 1.6 copy-start.7
  125.4 24.1 %collective-permute-start.21 = (bf16[704,512]{1,0:T(8,128)(2,1)}, bf16[704,512]{1,0:T(8,128)(2,1)}, u32[]{:S(2)}, u32[]{:S(2)}) collective-permute-start(bf16[704,512]{1,0:T(8,128)(2,1)} %bitcast.15.refs_3_), channel_id=1, source_target_pairs={{8,16},{16,8},{9,17},{17,9},{10,18},{18,10},{11,19},{19,11},{12,20... | collective-permute-start | bytes 2162696 | tf_op jit(solution)/shard_map/ppermute | solution.py:546
  127.0 1.1 copy-start.5
  131.4 34.8 %all-to-all-start.1 = ((bf16[8,40,2048]{2,1,0:T(8,128)(2,1)}), bf16[8,40,2048]{2,1,0:T(8,128)(2,1)S(1)}, u32[]{:S(2)}, u32[]{:S(2)}) async-start(bf16[8,40,2048]{2,1,0:T(8,128)(2,1)} %bitcast.52), calls=%async_computation.1 | async-start | bytes 2621440 | tf_op jit(solution)/shard_map/all_to_all | solution.py:568
  135.0 29.9 %collective-permute-start.18 = (bf16[704,512]{1,0:T(8,128)(2,1)}, bf16[704,512]{1,0:T(8,128)(2,1)S(1)}, u32[]{:S(2)}, u32[]{:S(2)}) collective-permute-start(bf16[704,512]{1,0:T(8,128)(2,1)} %collective-permute-done.17.refs_14_.refs_9_), channel_id=1, source_target_pairs={{8,0},{16,24},{9,1},{17,25},{10,2},{18,26},{11,3},{19,27},{12,4},{... | collective-permute-start | bytes 2162696 | tf_op jit(solution)/shard_map/ppermute | solution.py:546
  136.3 28.6 %collective-permute-start.20 = (bf16[704,512]{1,0:T(8,128)(2,1)}, bf16[704,512]{1,0:T(8,128)(2,1)S(1)}, u32[]{:S(2)}, u32[]{:S(2)}) collective-permute-start(bf16[704,512]{1,0:T(8,128)(2,1)} %collective-permute-done.19.refs_4_), channel_id=1, source_target_pairs={{8,16},{16,8},{9,17},{17,9},{10,18},{18,10},{11,19},{19,11},{12,20... | collective-permute-start | bytes 2162696 | tf_op jit(solution)/shard_map/ppermute | solution.py:546
  149.6 30.9 %collective-permute-start.22 = (bf16[704,512]{1,0:T(8,128)(2,1)}, bf16[704,512]{1,0:T(8,128)(2,1)}, u32[]{:S(2)}, u32[]{:S(2)}) collective-permute-start(bf16[704,512]{1,0:T(8,128)(2,1)} %collective-permute-done.21.refs_6_), channel_id=1, source_target_pairs={{8,0},{16,24},{9,1},{17,25},{10,2},{18,26},{11,3},{19,27},{12,4},{... | collective-permute-start | bytes 2162696 | tf_op jit(solution)/shard_map/ppermute | solution.py:546
  164.9 1.3 copy-start.12
  164.9 1.3 copy-start.14
  164.9 28.3 %collective-permute-start.23 = (bf16[704,512]{1,0:T(8,128)(2,1)S(1)}, bf16[704,512]{1,0:T(8,128)(2,1)}, u32[]{:S(2)}, u32[]{:S(2)}) collective-permute-start(bf16[704,512]{1,0:T(8,128)(2,1)S(1)} %collective-permute-done.20.refs_16_.refs_6_), channel_id=1, source_target_pairs={{8,0},{16,24},{9,1},{17,25},{10,2},{18,26},{11,3},{19,27},{12,4},{... | collective-permute-start | bytes 2162696 | tf_op jit(solution)/shard_map/ppermute | solution.py:546
  166.2 1.1 copy-start.10
  186.4 18.3 %all-to-all-start.2 = ((bf16[8,40,1536]{2,1,0:T(8,128)(2,1)}), bf16[8,40,1536]{2,1,0:T(8,128)(2,1)S(1)}, u32[]{:S(2)}, u32[]{:S(2)}) async-start(bf16[8,40,1536]{2,1,0:T(8,128)(2,1)} %bitcast.53), calls=%async_computation.2 | async-start | bytes 1966080 | tf_op jit(solution)/shard_map/all_to_all | solution.py:568
  204.3 15.2 %copy-start.15 = (bf16[320,1536]{1,0:T(8,128)(2,1)S(1)}, bf16[320,1536]{1,0:T(8,128)(2,1)}, u32[]{:S(2)}) copy-start(bf16[320,1536]{1,0:T(8,128)(2,1)} %get-tuple-element.67) | copy-start | bytes 2949124
  219.4 17.2 %copy-start = (bf16[1,128,2048]{2,1,0:T(8,128)(2,1)S(1)}, bf16[1,128,2048]{2,1,0:T(8,128)(2,1)}, u32[]{:S(2)}) copy-start(bf16[1,128,2048]{2,1,0:T(8,128)(2,1)} %param.22) | copy-start | bytes 1572868
  219.4 17.2 %copy-start.1 = (f32[1,128,2]{2,1,0:T(8,128)S(1)}, f32[1,128,2]{2,1,0:T(8,128)}, u32[]{:S(2)}) copy-start(f32[1,128,2]{2,1,0:T(8,128)} %copy.15) | copy-start | bytes 3076
  219.4 17.2 %copy-start.2 = (bf16[128,2048]{1,0:T(8,128)(2,1)S(1)}, bf16[128,2048]{1,0:T(8,128)(2,1)}, u32[]{:S(2)}) copy-start(bf16[128,2048]{1,0:T(8,128)(2,1)} %get-tuple-element.51.refs_4_) | copy-start | bytes 1572868
  219.4 17.2 %copy-start.3 = (f32[2048]{0:T(1024)S(1)}, f32[2048]{0:T(1024)}, u32[]{:S(2)}) copy-start(f32[2048]{0:T(1024)} %param.16) | copy-start | bytes 24580
  219.5 17.2 %copy-start.4 = (s32[10]{0:T(128)S(1)}, s32[10]{0:T(128)}, u32[]{:S(2)}) copy-start(s32[10]{0:T(128)} %dynamic-slice_bitcast_fusion.refs_0_) | copy-start | bytes 124
  (3 other events, 2.4 us)

commit v5 on v4

--- a/solution.py
+++ b/solution.py
@@ -201,7 +201,7 @@
             out[...] = ctx_ref[place_ref[ATTEND + i]]
 
 
-def line_of_four(place, queries, keys, values, gate, up, down, send_cot):
+def line_of_four(place, queries, keys, values, gate, up, down, cot_rows):
     rows, width = queries.shape
     half = width // 2
     block = sds((3 * rows, half))
@@ -230,30 +230,30 @@
         ],
         flops=64 * rows * rows * half,
         moved=32 * rows * half,
-        after=(gate_end, up_end, send_cot),
-    )
+        after=(gate_end, up_end, cot_rows),
+    )
+    gate_mid = send(gate, MIDDLE, near, mid, far)
     gate_inner = send(gate, INWARD, near, far)
-    gate_mid = send(gate, MIDDLE, near, mid, far)
     down_end = send(down, OUTWARD)
-    own, near, mid, far = lax.optimization_barrier((*pieces, gate_mid, gate_inner, down_end))[:4]
+    gate_far = send(gate_mid, OUTWARD, down_end, *pieces)
+    up_mid = send(up, MIDDLE, gate_mid)
+    up_inner = send(up, INWARD, gate_inner)
+    own, near, mid, far = lax.optimization_barrier((*pieces, gate_far, up_mid))[:4]
     near = send(near, OUTWARD)
     mid = send(mid, MIDDLE)
     far = send(far, [(2, 0), (1, 3)])
-    gate_mid_near = send(gate_inner, MIDDLE, mid, far)
-    gate_far = send(gate_mid, OUTWARD, down_end)
-    up_mid = send(up, MIDDLE, gate_mid)
-    up_inner = send(up, INWARD, gate_inner)
-    norm_after = (gate_far, up_mid)
-    gate_far_near = send(gate_mid_near, OUTWARD)
-    up_far = send(up_mid, OUTWARD)
-    up_mid_near = send(up_inner, MIDDLE, up_mid)
+    gate_mid_near = send(gate_inner, MIDDLE, up_mid, gate_far)
+    up_far = send(up_mid, OUTWARD, gate_far)
+    up_mid_near = send(up_inner, MIDDLE, mid, far)
+    down_inner = send(down, INWARD, up_inner, up_mid)
+    gate_far_near = send(gate_mid_near, OUTWARD, up_far)
     down_mid = send(down, MIDDLE, gate_mid_near)
-    down_inner = send(down, INWARD, up_inner)
     up_far_near = send(up_mid_near, OUTWARD, up_far)
+    down_mid_near = send(down_inner, MIDDLE, up_mid_near)
     down_far = send(down_mid, OUTWARD, gate_far_near)
-    down_mid_near = send(down_inner, MIDDLE, up_mid_near)
+    down_far_near = send(down_mid_near, OUTWARD, up_far_near)
+    norm_after = ()
     up_after = (down_mid_near,)
-    down_far_near = send(down_mid_near, OUTWARD, up_far_near)
     gate_in = [
         [gate],
         [gate_inner, gate_end],
@@ -425,8 +425,8 @@
     down_in, refs = regroup(refs, shape[-1:])
     gate_in, refs = regroup(refs, shape[:-1])
     up_in, refs = regroup(refs, shape[:-1])
-    (o_ref, d_gate_ref, d_up_ref, down_w, gate_w, up_w, sems) = refs[:7]
-    hidden_ref, cot_ref, d_hidden_ref, to_gate_ref, to_up_ref = refs[7:]
+    o_ref, down_w, gate_w, up_w, sems = refs[:5]
+    hidden_ref, cot_ref, d_hidden_ref, to_gate_ref, to_up_ref = refs[5:]
     part = down_w.shape[1]
     inner = place_ref[INNER]
     last = place_ref[COLS + cot_in.shape[1] // part - 1]
@@ -452,32 +452,12 @@
     d_hidden = d_hidden_ref[...] + mm(cot_ref[...], down_w[...], NT)
     d_gate = (d_hidden * to_gate_ref[...]).astype(BF)
     d_up = (d_hidden * to_up_ref[...]).astype(BF)
-    d_gate_ref[...] = d_gate
-    d_up_ref[...] = d_up
     o_ref[:, slots * part :] = mm(hidden_ref[...], down_w[...], NN).astype(BF)
     for j in range(slots):
         arrived(gate_in[j], gate_w.at[j], sems.at[0, j])
         arrived(up_in[j], up_w.at[j], sems.at[1, j])
         o_ref[:, j * part : (j + 1) * part] = (
             mm(d_gate, gate_w[j], NN) + mm(d_up, up_w[j], NN)
-        ).astype(BF)
-
-
-def rest_kernel(shape, place_ref, d_gate_ref, d_up_ref, *refs):
-    slots = len(shape)
-    gate_in, refs = regroup(refs, shape)
-    up_in, refs = regroup(refs, shape)
-    o_ref, gate_w, up_w, sems = refs
-    part = gate_w.shape[2]
-    inner = place_ref[INNER]
-    for j in range(slots):
-        fetch(inner, gate_in[j], gate_w.at[j], sems.at[0, j])
-        fetch(inner, up_in[j], up_w.at[j], sems.at[1, j])
-    for j in range(slots):
-        arrived(gate_in[j], gate_w.at[j], sems.at[0, j])
-        arrived(up_in[j], up_w.at[j], sems.at[1, j])
-        o_ref[:, j * part : (j + 1) * part] = (
-            mm(d_gate_ref[...], gate_w[j], NN) + mm(d_up_ref[...], up_w[j], NN)
         ).astype(BF)
 
 
@@ -491,8 +471,7 @@
     stream_ref,
     cot_ref,
     first_ref,
-    early_ref,
-    late_ref,
+    last_ref,
     output_ref,
     grad_ref,
     d_normed_ref,
@@ -513,14 +492,11 @@
         if j < slots - 1:
             pairs = first_ref[:, j * part : (j + 1) * part]
         else:
-            pairs = early_ref[:, slots // 2 * part :]
+            pairs = last_ref[:, width:]
         stream = stream_ref[:, cols].astype(F32)
         mixed = w0 * mm(pick0, pairs, NN) + w1 * mm(pick1, pairs, NN)
         output_ref[:, cols] = (stream + mixed).astype(BF)
-        if j < slots // 2:
-            grads = early_ref[:, j * part : (j + 1) * part]
-        else:
-            grads = late_ref[:, (j - slots // 2) * part : (j - slots // 2 + 1) * part]
+        grads = last_ref[:, j * part : (j + 1) * part]
         gained = mm(both, grads, NN) * gain_ref[:, cols]
         d_normed_ref[:, cols] = gained
         square = square + jnp.sum(stream * stream, axis=-1, keepdims=True)
@@ -614,7 +590,7 @@
     if groups == 4:
         join = join_middle
         pieces, gate_in, up_in, down_in, norm_after, up_after = line_of_four(
-            place, queries[0], keys[0], values[0], *shards, send_cot
+            place, queries[0], keys[0], values[0], *shards, cot_rows
         )
     else:
         join = join_groups
@@ -634,7 +610,7 @@
         [pltpu.VMEM((tokens, width), BF)],
         flops=2 * total * tokens * width,
         moved=2 * (total + 3 * tokens) * width,
-        after=(*norm_after, cot_rows),
+        after=norm_after,
     )
     rows = exchange(send_rows, owners, "exp")
 
@@ -663,13 +639,9 @@
         moved=2 * width * ffw + 4 * total * width + 6 * total * ffw,
     )
     back_first = exchange(out_first, owners, "exp")
-    early = groups // 2
-    shape_early = [*shape[:early], shape[-1]]
-    half_w = pltpu.VMEM((early, ffw, part), BF)
-    late_w = pltpu.VMEM((groups - early, ffw, part), BF)
-    back, d_gate, d_up = call(
-        functools.partial(grad_kernel, shape_early),
-        (sds((total, (early + 1) * part)), sds((total, ffw)), sds((total, ffw))),
+    back = call(
+        functools.partial(grad_kernel, [*shape, shape[-1]]),
+        sds((total, width + part)),
         (
             place,
             hidden,
@@ -678,14 +650,14 @@
             to_gate,
             to_up,
             *flat(down_in[-1:]),
-            *flat(gate_in[:early]),
-            *flat(up_in[:early]),
+            *flat(gate_in),
+            *flat(up_in),
         ),
-        [SMEM] + [HBM] * (5 + shape[-1] + 2 * sum(shape[:early])),
+        [SMEM] + [HBM] * (5 + shape[-1] + 2 * sum(shape)),
         [
             pltpu.VMEM((ffw, part), BF),
-            half_w,
-            half_w,
+            full_w,
+            full_w,
             pltpu.SemaphoreType.DMA((8, groups)),
             pltpu.VMEM((total, ffw), BF),
             pltpu.VMEM((total, part), BF),
@@ -693,25 +665,15 @@
             pltpu.VMEM((total, ffw), F32),
             pltpu.VMEM((total, ffw), F32),
         ],
-        flops=one + 2 * one // groups,
-        moved=2 * width * ffw + 2 * total * width + 18 * total * ffw,
-    )
-    back_early = exchange(back, owners, "exp")
-    rest = call(
-        functools.partial(rest_kernel, shape[early:]),
-        sds((total, width - early * part)),
-        (place, d_gate, d_up, *flat(gate_in[early:]), *flat(up_in[early:])),
-        [SMEM, VMEM, VMEM] + [HBM] * (2 * sum(shape[early:])),
-        [late_w, late_w, pltpu.SemaphoreType.DMA((2, groups))],
-        flops=one,
-        moved=2 * width * ffw + 2 * total * width + 4 * total * ffw,
-    )
-    back_late = exchange(rest, owners, "exp")
+        flops=2 * one + 2 * one // groups,
+        moved=4 * width * ffw + 4 * total * width + 14 * total * ffw,
+    )
+    back_last = exchange(back, owners, "exp")
     output, stream_grad = call(
         functools.partial(final_kernel, owners, cap),
         (sds((tokens, width)), sds((tokens, width))),
-        (place, ids, weights, gain, stream, cot, back_first, back_early, back_late),
-        [SMEM] + [VMEM] * 8,
+        (place, ids, weights, gain, stream, cot, back_first, back_last),
+        [SMEM] + [VMEM] * 7,
         [pltpu.VMEM((tokens, width), F32)],
         flops=6 * total * tokens * width,
         moved=4 * total * width + 8 * tokens * width,

time: 241 us -> 243 us (level)
  waiting for transfers between devices: 76.2 us -> 109 us
  starting transfers between devices: 84.2 us -> 63.8 us
  blocking collectives: 31.9 us -> 25.3 us
  Pallas kernels: 38.8 us -> 35.6 us
    ppermute x24, waiting for transfers between devices: 75.8 us -> 106 us  [send(): return lax.ppermute(gated(array, *first), 'seq', pairs)]
    ppermute x24, starting transfers between devices: 73.1 us -> 52.2 us  [send(): return lax.ppermute(gated(array, *first), 'seq', pairs)]
    all_to_all x2 -> x1, blocking collectives: 31.9 us -> 25.3 us  [exchange(): rows = lax.all_to_all(rows, axis, split_axis=0, concat_axis=0, tiled=True)]
    pallas_call x9 -> x8, Pallas kernels: 38.8 us -> 35.6 us  [call(): pl.pallas_call(body, grid=() if held else (1,), out_shape=outs, in_specs=...]
    all_to_all x3, waiting for transfers between devices: 0.4 us -> 2.83 us  [exchange(): rows = lax.all_to_all(rows, axis, split_axis=0, concat_axis=0, tiled=True)]
    unnamed x50 -> x48, local copies, waits for them, and re-layouts: 5.7 us -> 5.73 us
  transfers between devices with their start and end apart: 27 -> 27, of which waited for: 11 -> 12; matrix products, arithmetic and copies ran while one was open for 1% -> 1% of each run, Pallas kernels for 14% -> 12%
where the time goes in v5:
time: 243 us; the launch traced here: 242 us
  waiting for transfers between devices  109 us (45%)
  starting transfers between devices  63.8 us (26%)
  Pallas kernels  35.6 us (15%)
  blocking collectives  25.3 us (10%)
  local copies, waits for them, and re-layouts  7.57 us (3%)
    ppermute x24, waiting for transfers between devices, send(): return lax.ppermute(gated(array, *first), 'seq', pairs)  106 us
    ppermute x24, starting transfers between devices, send(): return lax.ppermute(gated(array, *first), 'seq', pairs)  52.2 us
    pallas_call x8, Pallas kernels, call(): pl.pallas_call(body, grid=() if held else (1,), out_shape=outs, in_specs=...  35.6 us
    all_to_all x1, blocking collectives, exchange(): rows = lax.all_to_all(rows, axis, split_axis=0, concat_axis=0, tiled=True)  25.3 us
    all_to_all x3, starting transfers between devices, exchange(): rows = lax.all_to_all(rows, axis, split_axis=0, concat_axis=0, tiled=True)  11.6 us
    unnamed x48, local copies, waits for them, and re-layouts  5.73 us
  transfers between devices with their start and end apart: 27, of which 12 were waited for; matrix products, arithmetic and copies ran while one was open for 1% of the time, Pallas kernels for 12%

profile of v5, /device:TPU:0, one launch (start us, length us, event | category | flops | bytes accessed | tf_op | source)
XLA Modules:
  0.0 242.1 jit_solution(8384460685309521268)
XLA Ops:
  0.7 1.2 dynamic-slice_bitcast_fusion.refs_0_
  1.9 2.6 %shard_map.131 = (bf16[384,1024]{1,0:T(8,128)(2,1)}, bf16[384,1024]{1,0:T(8,128)(2,1)}) custom-call(s32[10]{0:T(128)} %dynamic-slice_bitcast_fusion.refs_0_, bf16[128,2048]{1,0:T(8,128)(2,1)} %bitcast.58, bf16[128,2048]{1,0:T(8,128)(2,1)} %bitcast.59, bf16[128,2048]{1,0:T(8,128)(2,1)} %bitcast.60), custom_call_target="tpu_custom_call" | custom-call | bytes 3145728 | tf_op jit(solution)/shard_map/pallas_call | solution.py:35
  4.5 5.8 %collective-permute-start = (bf16[384,1024]{1,0:T(8,128)(2,1)}, bf16[384,1024]{1,0:T(8,128)(2,1)}, u32[]{:S(2)}, u32[]{:S(2)}) collective-permute-start(bf16[384,1024]{1,0:T(8,128)(2,1)} %get-tuple-element.36.refs_1_), channel_id=1, source_target_pairs={{0,8},{24,16},{1,9},{25,17},{2,10},{26,18},{3,11},{27,19},{4,12},{... | collective-permute-start | bytes 2359304 | tf_op jit(solution)/shard_map/ppermute | solution.py:522
  10.3 1.5 collective-permute-start.1
  11.9 3.2 %collective-permute-start.2 = (bf16[384,1024]{1,0:T(8,128)(2,1)}, bf16[384,1024]{1,0:T(8,128)(2,1)}, u32[]{:S(2)}, u32[]{:S(2)}) collective-permute-start(bf16[384,1024]{1,0:T(8,128)(2,1)} %get-tuple-element.37), channel_id=1, source_target_pairs={{0,16},{24,8},{1,17},{25,9},{2,18},{26,10},{3,19},{27,11},{4,20},{... | collective-permute-start | bytes 2359304 | tf_op jit(solution)/shard_map/ppermute | solution.py:522
  16.6 3.2 %shard_map.132 = bf16[320,2048]{1,0:T(8,128)(2,1)} custom-call(s32[2,128]{1,0:T(2,128)} %copy.17.refs_0_.refs_1_, f32[128,2]{1,0:T(8,128)} %bitcast.33, bf16[128,2048]{1,0:T(8,128)(2,1)} %bitcast.31), custom_call_target="tpu_custom_call" | custom-call | flops 335544320 | bytes 1835008 | tf_op jit(solution)/shard_map/pallas_call | solution.py:35
  19.7 3.9 %all-to-all-start = ((bf16[8,40,2048]{2,1,0:T(8,128)(2,1)}), bf16[8,40,2048]{2,1,0:T(8,128)(2,1)S(1)}, u32[]{:S(2)}, u32[]{:S(2)}) async-start(bf16[8,40,2048]{2,1,0:T(8,128)(2,1)} %bitcast.44), calls=%async_computation | async-start | bytes 2621440 | tf_op jit(solution)/shard_map/all_to_all | solution.py:544
  23.6 1.3 collective-permute-start.3
  24.9 1.3 collective-permute-start.4
  26.2 1.5 collective-permute-done.refs_2_
  27.7 1.3 collective-permute-start.6
  29.0 14.5 %collective-permute-done.2.refs_4_ = bf16[384,1024]{1,0:T(8,128)(2,1)} collective-permute-done((bf16[384,1024]{1,0:T(8,128)(2,1)}, bf16[384,1024]{1,0:T(8,128)(2,1)}, u32[]{:S(2)}, u32[]{:S(2)}) %collective-permute-start.2) | collective-permute-done | bytes 786464 | tf_op jit(solution)/shard_map/ppermute | solution.py:522
  43.5 1.5 collective-permute-start.5
  45.0 8.5 %collective-permute-start.12 = (bf16[704,512]{1,0:T(8,128)(2,1)S(1)}, bf16[704,512]{1,0:T(8,128)(2,1)}, u32[]{:S(2)}, u32[]{:S(2)}) collective-permute-start(bf16[704,512]{1,0:T(8,128)(2,1)S(1)} %bitcast.49), channel_id=1, source_target_pairs={{0,8},{24,16},{1,9},{25,17},{2,10},{26,18},{3,11},{27,19},{4,12},{... | collective-permute-start | bytes 2162696 | tf_op jit(solution)/shard_map/ppermute | solution.py:522
  53.5 6.4 %collective-permute-done.4.refs_6_.refs_11_.refs_17_ = bf16[704,512]{1,0:T(8,128)(2,1)S(1)} collective-permute-done((bf16[704,512]{1,0:T(8,128)(2,1)}, bf16[704,512]{1,0:T(8,128)(2,1)S(1)}, u32[]{:S(2)}, u32[]{:S(2)}) %collective-permute-start.4) | collective-permute-done | bytes 720928 | tf_op jit(solution)/shard_map/ppermute | solution.py:522
  61.2 1.8 shard_map.133
  63.0 12.0 %collective-permute-done.6.refs_5_ = bf16[704,512]{1,0:T(8,128)(2,1)} collective-permute-done((bf16[704,512]{1,0:T(8,128)(2,1)}, bf16[704,512]{1,0:T(8,128)(2,1)}, u32[]{:S(2)}, u32[]{:S(2)}) %collective-permute-start.6) | collective-permute-done | bytes 720928 | tf_op jit(solution)/shard_map/ppermute | solution.py:522
  75.0 1.3 collective-permute-start.7
  77.0 7.4 %collective-permute-start.16 = (bf16[704,512]{1,0:T(8,128)(2,1)S(1)}, bf16[704,512]{1,0:T(8,128)(2,1)S(1)}, u32[]{:S(2)}, u32[]{:S(2)}) collective-permute-start(bf16[704,512]{1,0:T(8,128)(2,1)S(1)} %bitcast.54), channel_id=1, source_target_pairs={{0,8},{24,16},{1,9},{25,17},{2,10},{26,18},{3,11},{27,19},{4,12},{... | collective-permute-start | bytes 2162696 | tf_op jit(solution)/shard_map/ppermute | solution.py:522
  84.5 10.4 %collective-permute-done.7.refs_6_.refs_12_ = bf16[704,512]{1,0:T(8,128)(2,1)S(1)} collective-permute-done((bf16[704,512]{1,0:T(8,128)(2,1)}, bf16[704,512]{1,0:T(8,128)(2,1)S(1)}, u32[]{:S(2)}, u32[]{:S(2)}) %collective-permute-start.7) | collective-permute-done | bytes 720928 | tf_op jit(solution)/shard_map/ppermute | solution.py:522
  94.9 1.6 collective-permute-start.13
  96.4 1.3 collective-permute-start.14
  98.4 1.3 collective-permute-start.11
  99.7 27.9 %collective-permute-done.11.refs_7_ = bf16[128,1024]{1,0:T(8,128)(2,1)S(1)} collective-permute-done((bf16[128,1024]{1,0:T(8,128)(2,1)}, bf16[128,1024]{1,0:T(8,128)(2,1)S(1)}, u32[]{:S(2)}, u32[]{:S(2)}) %collective-permute-start.11) | collective-permute-done | bytes 262176 | tf_op jit(solution)/shard_map/ppermute | solution.py:522
  127.7 1.6 collective-permute-start.17
  129.3 3.3 %collective-permute-start.19 = (bf16[704,512]{1,0:T(8,128)(2,1)}, bf16[704,512]{1,0:T(8,128)(2,1)}, u32[]{:S(2)}, u32[]{:S(2)}) collective-permute-start(bf16[704,512]{1,0:T(8,128)(2,1)} %bitcast.17.refs_3_), channel_id=1, source_target_pairs={{0,8},{24,16},{1,9},{25,17},{2,10},{26,18},{3,11},{27,19},{4,12},{... | collective-permute-start | bytes 2162696 | tf_op jit(solution)/shard_map/ppermute | solution.py:522
  132.6 1.3 collective-permute-start.9
  133.9 0.9 copy-done.14
  134.8 1.3 collective-permute-start.15
  136.1 1.6 collective-permute-start.21
  137.7 6.3 %collective-permute-done.9.refs_5_ = bf16[128,1024]{1,0:T(8,128)(2,1)S(1)} collective-permute-done((bf16[128,1024]{1,0:T(8,128)(2,1)}, bf16[128,1024]{1,0:T(8,128)(2,1)S(1)}, u32[]{:S(2)}, u32[]{:S(2)}) %collective-permute-start.9) | collective-permute-done | bytes 262176 | tf_op jit(solution)/shard_map/ppermute | solution.py:522
  144.6 3.3 %shard_map.134 = (bf16[128,2048]{1,0:T(8,128)(2,1)}, bf16[320,2048]{1,0:T(8,128)(2,1)}) custom-call(s32[10]{0:T(128)} %dynamic-slice_bitcast_fusion.refs_0_, s32[2,128]{1,0:T(2,128)} %copy.17.refs_0_.refs_1_, bf16[128,2048]{1,0:T(8,128)(2,1)} %bitcast.57, f32[1,2048]{1,0:T(1,128)} %bitcast.37, bf16[128,1024]{1,0:T(8,128)(2,1)} %get-tuple-element.45.refs_4_, ...), custom_call_target="tpu_custom_call" | custom-call | flops 167772160 | bytes 2883584 | tf_op jit(solution)/shard_map/pallas_call | solution.py:35
  147.9 3.6 %all-to-all-start.1 = ((bf16[8,40,2048]{2,1,0:T(8,128)(2,1)}), bf16[8,40,2048]{2,1,0:T(8,128)(2,1)S(1)}, u32[]{:S(2)}, u32[]{:S(2)}) async-start(bf16[8,40,2048]{2,1,0:T(8,128)(2,1)} %bitcast.55), calls=%async_computation.1 | async-start | bytes 2621440 | tf_op jit(solution)/shard_map/all_to_all | solution.py:544
  151.5 1.3 collective-permute-start.18
  153.6 1.9 collective-permute-done.15.refs_8_.refs_14_
  155.5 1.3 collective-permute-start.22
  156.8 15.8 %collective-permute-done.18.refs_15_.refs_21_ = bf16[704,512]{1,0:T(8,128)(2,1)S(1)} collective-permute-done((bf16[704,512]{1,0:T(8,128)(2,1)}, bf16[704,512]{1,0:T(8,128)(2,1)S(1)}, u32[]{:S(2)}, u32[]{:S(2)}) %collective-permute-start.18) | collective-permute-done | bytes 720928 | tf_op jit(solution)/shard_map/ppermute | solution.py:522
  172.6 1.3 collective-permute-start.23
  174.0 1.1 copy-done.8
  175.0 7.9 %shard_map.135 = (bf16[320,704]{1,0:T(8,128)(2,1)}, f32[320,704]{1,0:T(8,128)}, f32[320,704]{1,0:T(8,128)}) custom-call(s32[10]{0:T(128)} %dynamic-slice_bitcast_fusion.refs_0_, bf16[320,2048]{1,0:T(8,128)(2,1)} %bitcast.43, bf16[704,512]{1,0:T(8,128)(2,1)} %bitcast.45, bf16[704,512]{1,0:T(8,128)(2,1)} %collective-permute-done.12.refs_3_.refs_9_, ...), custom_call_target="tpu_custom_call" | custom-call | flops 1845493760 | bytes 9330688 | tf_op jit(solution)/shard_map/pallas_call | solution.py:35
  182.9 5.1 %collective-permute-done.22.refs_7_ = bf16[704,512]{1,0:T(8,128)(2,1)S(1)} collective-permute-done((bf16[704,512]{1,0:T(8,128)(2,1)}, bf16[704,512]{1,0:T(8,128)(2,1)S(1)}, u32[]{:S(2)}, u32[]{:S(2)}) %collective-permute-start.22) | collective-permute-done | bytes 720928 | tf_op jit(solution)/shard_map/ppermute | solution.py:522
  188.9 5.9 %shard_map.136 = (bf16[320,1536]{1,0:T(8,128)(2,1)}, f32[320,704]{1,0:T(8,128)}) custom-call(s32[10]{0:T(128)} %dynamic-slice_bitcast_fusion.refs_0_, bf16[320,704]{1,0:T(8,128)(2,1)} %get-tuple-element.60.refs_1_, bf16[320,2048]{1,0:T(8,128)(2,1)} %bitcast.40, bf16[704,512]{1,0:T(8,128)(2,1)} %bitcast.17.refs_3_, ...), custom_call_target="tpu_custom_call" | custom-call | flops 1384120320 | bytes 6856704 | tf_op jit(solution)/shard_map/pallas_call | solution.py:35
  194.9 4.1 %all-to-all-start.2 = ((bf16[8,40,1536]{2,1,0:T(8,128)(2,1)}), bf16[8,40,1536]{2,1,0:T(8,128)(2,1)S(1)}, u32[]{:S(2)}, u32[]{:S(2)}) async-start(bf16[8,40,1536]{2,1,0:T(8,128)(2,1)} %bitcast.56), calls=%async_computation.2 | async-start | bytes 1966080 | tf_op jit(solution)/shard_map/all_to_all | solution.py:544
  199.0 4.1 %collective-permute-done.23.refs_7_ = bf16[704,512]{1,0:T(8,128)(2,1)} collective-permute-done((bf16[704,512]{1,0:T(8,128)(2,1)S(1)}, bf16[704,512]{1,0:T(8,128)(2,1)}, u32[]{:S(2)}, u32[]{:S(2)}) %collective-permute-start.23) | collective-permute-done | bytes 720928 | tf_op jit(solution)/shard_map/ppermute | solution.py:522
  203.1 7.8 %shard_map.137 = bf16[320,2560]{1,0:T(8,128)(2,1)} custom-call(s32[10]{0:T(128)} %dynamic-slice_bitcast_fusion.refs_0_, bf16[320,704]{1,0:T(8,128)(2,1)} %get-tuple-element.60.refs_1_, bf16[320,2048]{1,0:T(8,128)(2,1)} %bitcast.41, f32[320,704]{1,0:T(8,128)} %get-tuple-element.64.refs_3_, f32[320,704]{1,0:T(8,128)} %get-tuple-element.65.refs_4_, ...), custom_call_target="tpu_custom_call" | custom-call | flops 2306867200 | bytes 11542528 | tf_op jit(solution)/shard_map/pallas_call | solution.py:35
  210.9 2.8 %all-to-all-done.2 = bf16[8,40,1536]{2,1,0:T(8,128)(2,1)S(1)} async-done(((bf16[8,40,1536]{2,1,0:T(8,128)(2,1)}), bf16[8,40,1536]{2,1,0:T(8,128)(2,1)S(1)}, u32[]{:S(2)}, u32[]{:S(2)}) %all-to-all-start.2) | async-done | bytes 983072 | tf_op jit(solution)/shard_map/all_to_all | solution.py:544
  213.7 25.3 %all_to_all.20 = bf16[8,40,2560]{2,1,0:T(8,128)(2,1)S(1)} all-to-all(bf16[8,40,2560]{2,1,0:T(8,128)(2,1)} %bitcast.42), channel_id=1, replica_groups=mesh['seq'=4,'exp'=8] {'exp'}, dimensions={0} | all-to-all | bytes 3276800 | tf_op jit(solution)/shard_map/all_to_all | solution.py:544
  239.1 3.1 %shard_map.138 = (bf16[128,2048]{1,0:T(8,128)(2,1)}, bf16[128,2048]{1,0:T(8,128)(2,1)}) custom-call(s32[10]{0:T(128)S(1)} %copy-done.4, s32[128,2]{1,0:T(8,128)S(1)} %bitcast.36, f32[128,2]{1,0:T(8,128)S(1)} %bitcast.34, f32[1,2048]{1,0:T(1,128)S(1)} %bitcast.38, bf16[128,2048]{1,0:T(8,128)(2,1)S(1)} %copy-done.2, bf16[128,2048]{1,0:T(8,128)(2,1)S(1)} %bitcast.32, ...), custom_call_target="tpu_custom_call" | custom-call | flops 503316480 | bytes 4718592 | tf_op jit(solution)/shard_map/pallas_call | solution.py:35
  (65 shorter events, 6.5 us)
Async XLA Ops:
  0.6 14.5 %copy-start.21 = (s32[1,128,2]{1,2,0:T(2,128)S(1)}, s32[1,128,2]{1,2,0:T(2,128)}, u32[]{:S(2)}) copy-start(s32[1,128,2]{1,2,0:T(2,128)} %param.20) | copy-start | bytes 3076
  0.6 14.6 %copy-start.22 = (f32[1,128,2]{1,2,0:T(2,128)S(1)}, f32[1,128,2]{1,2,0:T(2,128)}, u32[]{:S(2)}) copy-start(f32[1,128,2]{1,2,0:T(2,128)} %param.21) | copy-start | bytes 3076
  4.5 23.2 %collective-permute-start = (bf16[384,1024]{1,0:T(8,128)(2,1)}, bf16[384,1024]{1,0:T(8,128)(2,1)}, u32[]{:S(2)}, u32[]{:S(2)}) collective-permute-start(bf16[384,1024]{1,0:T(8,128)(2,1)} %get-tuple-element.36.refs_1_), channel_id=1, source_target_pairs={{0,8},{24,16},{1,9},{25,17},{2,10},{26,18},{3,11},{27,19},{4,12},{... | collective-permute-start | bytes 2359304 | tf_op jit(solution)/shard_map/ppermute | solution.py:522
  10.3 18.7 %collective-permute-start.1 = (bf16[384,1024]{1,0:T(8,128)(2,1)}, bf16[384,1024]{1,0:T(8,128)(2,1)}, u32[]{:S(2)}, u32[]{:S(2)}) collective-permute-start(bf16[384,1024]{1,0:T(8,128)(2,1)} %get-tuple-element.37), channel_id=1, source_target_pairs={{8,16},{16,8},{9,17},{17,9},{10,18},{18,10},{11,19},{19,11},{12,20... | collective-permute-start | bytes 2359304 | tf_op jit(solution)/shard_map/ppermute | solution.py:522
  11.9 31.6 %collective-permute-start.2 = (bf16[384,1024]{1,0:T(8,128)(2,1)}, bf16[384,1024]{1,0:T(8,128)(2,1)}, u32[]{:S(2)}, u32[]{:S(2)}) collective-permute-start(bf16[384,1024]{1,0:T(8,128)(2,1)} %get-tuple-element.37), channel_id=1, source_target_pairs={{0,16},{24,8},{1,17},{25,9},{2,18},{26,10},{3,19},{27,11},{4,20},{... | collective-permute-start | bytes 2359304 | tf_op jit(solution)/shard_map/ppermute | solution.py:522
  19.7 3.9 %copy-start.9 = (bf16[1,512,704]{1,2,0:T(8,128)(2,1)S(1)}, bf16[1,512,704]{1,2,0:T(8,128)(2,1)}, u32[]{:S(2)}) copy-start(bf16[1,512,704]{1,2,0:T(8,128)(2,1)} %param.17) | copy-start | bytes 2162692
  19.7 40.1 %all-to-all-start = ((bf16[8,40,2048]{2,1,0:T(8,128)(2,1)}), bf16[8,40,2048]{2,1,0:T(8,128)(2,1)S(1)}, u32[]{:S(2)}, u32[]{:S(2)}) async-start(bf16[8,40,2048]{2,1,0:T(8,128)(2,1)} %bitcast.44), calls=%async_computation | async-start | bytes 2621440 | tf_op jit(solution)/shard_map/all_to_all | solution.py:544
  23.6 29.9 %collective-permute-start.3 = (bf16[704,512]{1,0:T(8,128)(2,1)S(1)}, bf16[704,512]{1,0:T(8,128)(2,1)S(1)}, u32[]{:S(2)}, u32[]{:S(2)}) collective-permute-start(bf16[704,512]{1,0:T(8,128)(2,1)S(1)} %bitcast.47), channel_id=1, source_target_pairs={{8,0},{16,24},{9,1},{17,25},{10,2},{18,26},{11,3},{19,27},{12,4},{... | collective-permute-start | bytes 2162696 | tf_op jit(solution)/shard_map/ppermute | solution.py:522
  24.9 35.0 %collective-permute-start.4 = (bf16[704,512]{1,0:T(8,128)(2,1)}, bf16[704,512]{1,0:T(8,128)(2,1)S(1)}, u32[]{:S(2)}, u32[]{:S(2)}) collective-permute-start(bf16[704,512]{1,0:T(8,128)(2,1)} %bitcast.50), channel_id=1, source_target_pairs={{8,0},{16,24},{9,1},{17,25},{10,2},{18,26},{11,3},{19,27},{12,4},{... | collective-permute-start | bytes 2162696 | tf_op jit(solution)/shard_map/ppermute | solution.py:522
  27.7 47.3 %collective-permute-start.6 = (bf16[704,512]{1,0:T(8,128)(2,1)}, bf16[704,512]{1,0:T(8,128)(2,1)}, u32[]{:S(2)}, u32[]{:S(2)}) collective-permute-start(bf16[704,512]{1,0:T(8,128)(2,1)} %bitcast.17.refs_3_), channel_id=1, source_target_pairs={{8,0},{16,24},{9,1},{17,25},{10,2},{18,26},{11,3},{19,27},{12,4},{... | collective-permute-start | bytes 2162696 | tf_op jit(solution)/shard_map/ppermute | solution.py:522
  43.5 31.6 %collective-permute-start.5 = (bf16[704,512]{1,0:T(8,128)(2,1)S(1)}, bf16[704,512]{1,0:T(8,128)(2,1)}, u32[]{:S(2)}, u32[]{:S(2)}) collective-permute-start(bf16[704,512]{1,0:T(8,128)(2,1)S(1)} %bitcast.48), channel_id=1, source_target_pairs={{8,16},{16,8},{9,17},{17,9},{10,18},{18,10},{11,19},{19,11},{12,20... | collective-permute-start | bytes 2162696 | tf_op jit(solution)/shard_map/ppermute | solution.py:522
  45.0 32.1 %collective-permute-start.12 = (bf16[704,512]{1,0:T(8,128)(2,1)S(1)}, bf16[704,512]{1,0:T(8,128)(2,1)}, u32[]{:S(2)}, u32[]{:S(2)}) collective-permute-start(bf16[704,512]{1,0:T(8,128)(2,1)S(1)} %bitcast.49), channel_id=1, source_target_pairs={{0,8},{24,16},{1,9},{25,17},{2,10},{26,18},{3,11},{27,19},{4,12},{... | collective-permute-start | bytes 2162696 | tf_op jit(solution)/shard_map/ppermute | solution.py:522
  53.5 6.4 %copy-start.6 = (bf16[704,512]{1,0:T(8,128)(2,1)}, bf16[704,512]{1,0:T(8,128)(2,1)S(1)}, u32[]{:S(2)}) copy-start(bf16[704,512]{1,0:T(8,128)(2,1)S(1)} %collective-permute-done.3.refs_5_.refs_4_.refs_10_) | copy-start | bytes 2162692
  59.9 0.9 copy-start.7
  59.9 1.3 copy-start.5
  61.2 15.1 %copy-start.10 = (bf16[1,512,704]{1,2,0:T(8,128)(2,1)S(1)}, bf16[1,512,704]{1,2,0:T(8,128)(2,1)}, u32[]{:S(2)}) copy-start(bf16[1,512,704]{1,2,0:T(8,128)(2,1)} %param.18) | copy-start | bytes 2162692
  75.0 19.8 %collective-permute-start.7 = (bf16[704,512]{1,0:T(8,128)(2,1)}, bf16[704,512]{1,0:T(8,128)(2,1)S(1)}, u32[]{:S(2)}, u32[]{:S(2)}) collective-permute-start(bf16[704,512]{1,0:T(8,128)(2,1)} %collective-permute-done.5.refs_5_.refs_11_), channel_id=1, source_target_pairs={{8,0},{16,24},{9,1},{17,25},{10,2},{18,26},{11,3},{19,27},{12,4},{... | collective-permute-start | bytes 2162696 | tf_op jit(solution)/shard_map/ppermute | solution.py:522
  76.3 18.6 %collective-permute-start.8 = (bf16[704,512]{1,0:T(8,128)(2,1)S(1)}, bf16[704,512]{1,0:T(8,128)(2,1)S(1)}, u32[]{:S(2)}, u32[]{:S(2)}) collective-permute-start(bf16[704,512]{1,0:T(8,128)(2,1)S(1)} %bitcast.53), channel_id=1, source_target_pairs={{8,16},{16,8},{9,17},{17,9},{10,18},{18,10},{11,19},{19,11},{12,20... | collective-permute-start | bytes 2162696 | tf_op jit(solution)/shard_map/ppermute | solution.py:522
  77.0 22.7 %collective-permute-start.16 = (bf16[704,512]{1,0:T(8,128)(2,1)S(1)}, bf16[704,512]{1,0:T(8,128)(2,1)S(1)}, u32[]{:S(2)}, u32[]{:S(2)}) collective-permute-start(bf16[704,512]{1,0:T(8,128)(2,1)S(1)} %bitcast.54), channel_id=1, source_target_pairs={{0,8},{24,16},{1,9},{25,17},{2,10},{26,18},{3,11},{27,19},{4,12},{... | collective-permute-start | bytes 2162696 | tf_op jit(solution)/shard_map/ppermute | solution.py:522
  94.9 53.1 %copy-start.11 = (bf16[704,512]{1,0:T(8,128)(2,1)}, bf16[704,512]{1,0:T(8,128)(2,1)S(1)}, u32[]{:S(2)}) copy-start(bf16[704,512]{1,0:T(8,128)(2,1)S(1)} %collective-permute-done.7.refs_6_.refs_12_) | copy-start | bytes 2162692
  94.9 53.1 %copy-start.12 = (bf16[704,512]{1,0:T(8,128)(2,1)}, bf16[704,512]{1,0:T(8,128)(2,1)S(1)}, u32[]{:S(2)}) copy-start(bf16[704,512]{1,0:T(8,128)(2,1)S(1)} %collective-permute-done.8.refs_12_.refs_18_) | copy-start | bytes 2162692
  94.9 39.0 %collective-permute-start.13 = (bf16[704,512]{1,0:T(8,128)(2,1)}, bf16[704,512]{1,0:T(8,128)(2,1)}, u32[]{:S(2)}, u32[]{:S(2)}) collective-permute-start(bf16[704,512]{1,0:T(8,128)(2,1)} %collective-permute-done.12.refs_3_.refs_9_), channel_id=1, source_target_pairs={{8,16},{16,8},{9,17},{17,9},{10,18},{18,10},{11,19},{19,11},{12,20... | collective-permute-start | bytes 2162696 | tf_op jit(solution)/shard_map/ppermute | solution.py:522
  96.4 37.5 %collective-permute-start.14 = (bf16[704,512]{1,0:T(8,128)(2,1)S(1)}, bf16[704,512]{1,0:T(8,128)(2,1)S(1)}, u32[]{:S(2)}, u32[]{:S(2)}) collective-permute-start(bf16[704,512]{1,0:T(8,128)(2,1)S(1)} %collective-permute-done.8.refs_12_.refs_18_), channel_id=1, source_target_pairs={{8,0},{16,24},{9,1},{17,25},{10,2},{18,26},{11,3},{19,27},{12,4},{... | collective-permute-start | bytes 2162696 | tf_op jit(solution)/shard_map/ppermute | solution.py:522
  97.7 2.0 collective-permute-start.10
  98.4 29.3 %collective-permute-start.11 = (bf16[128,1024]{1,0:T(8,128)(2,1)}, bf16[128,1024]{1,0:T(8,128)(2,1)S(1)}, u32[]{:S(2)}, u32[]{:S(2)}) collective-permute-start(bf16[128,1024]{1,0:T(8,128)(2,1)} %get-tuple-element.48), channel_id=1, source_target_pairs={{16,0},{8,24},{17,1},{9,25},{18,2},{10,26},{19,3},{11,27},{20,4},{... | collective-permute-start | bytes 786440 | tf_op jit(solution)/shard_map/ppermute | solution.py:522
  99.7 48.2 %copy-start.13 = (bf16[704,512]{1,0:T(8,128)(2,1)}, bf16[704,512]{1,0:T(8,128)(2,1)S(1)}, u32[]{:S(2)}) copy-start(bf16[704,512]{1,0:T(8,128)(2,1)S(1)} %collective-permute-done.16.refs_10_.refs_16_) | copy-start | bytes 2162692
  99.7 44.2 %copy-start.18 = (bf16[128,1024]{1,0:T(8,128)(2,1)}, bf16[128,1024]{1,0:T(8,128)(2,1)S(1)}, u32[]{:S(2)}) copy-start(bf16[128,1024]{1,0:T(8,128)(2,1)S(1)} %collective-permute-done.10.refs_6_) | copy-start | bytes 786436
  127.7 16.3 %copy-start.19 = (bf16[128,1024]{1,0:T(8,128)(2,1)}, bf16[128,1024]{1,0:T(8,128)(2,1)S(1)}, u32[]{:S(2)}) copy-start(bf16[128,1024]{1,0:T(8,128)(2,1)S(1)} %collective-permute-done.11.refs_7_) | copy-start | bytes 786436
  127.7 23.8 %collective-permute-start.17 = (bf16[704,512]{1,0:T(8,128)(2,1)S(1)}, bf16[704,512]{1,0:T(8,128)(2,1)}, u32[]{:S(2)}, u32[]{:S(2)}) collective-permute-start(bf16[704,512]{1,0:T(8,128)(2,1)S(1)} %collective-permute-done.16.refs_10_.refs_16_), channel_id=1, source_target_pairs={{8,16},{16,8},{9,17},{17,9},{10,18},{18,10},{11,19},{19,11},{12,20... | collective-permute-start | bytes 2162696 | tf_op jit(solution)/shard_map/ppermute | solution.py:522
  129.3 23.6 %collective-permute-start.19 = (bf16[704,512]{1,0:T(8,128)(2,1)}, bf16[704,512]{1,0:T(8,128)(2,1)}, u32[]{:S(2)}, u32[]{:S(2)}) collective-permute-start(bf16[704,512]{1,0:T(8,128)(2,1)} %bitcast.17.refs_3_), channel_id=1, source_target_pairs={{0,8},{24,16},{1,9},{25,17},{2,10},{26,18},{3,11},{27,19},{4,12},{... | collective-permute-start | bytes 2162696 | tf_op jit(solution)/shard_map/ppermute | solution.py:522
  132.6 11.3 %collective-permute-start.9 = (bf16[128,1024]{1,0:T(8,128)(2,1)}, bf16[128,1024]{1,0:T(8,128)(2,1)S(1)}, u32[]{:S(2)}, u32[]{:S(2)}) collective-permute-start(bf16[128,1024]{1,0:T(8,128)(2,1)} %get-tuple-element.46), channel_id=1, source_target_pairs={{8,0},{16,24},{9,1},{17,25},{10,2},{18,26},{11,3},{19,27},{12,4},{... | collective-permute-start | bytes 786440 | tf_op jit(solution)/shard_map/ppermute | solution.py:522
  133.9 0.9 copy-start.14
  134.8 20.7 %collective-permute-start.15 = (bf16[704,512]{1,0:T(8,128)(2,1)}, bf16[704,512]{1,0:T(8,128)(2,1)}, u32[]{:S(2)}, u32[]{:S(2)}) collective-permute-start(bf16[704,512]{1,0:T(8,128)(2,1)} %collective-permute-done.13.refs_7_.refs_13_), channel_id=1, source_target_pairs={{8,0},{16,24},{9,1},{17,25},{10,2},{18,26},{11,3},{19,27},{12,4},{... | collective-permute-start | bytes 2162696 | tf_op jit(solution)/shard_map/ppermute | solution.py:522
  136.1 19.4 %collective-permute-start.21 = (bf16[704,512]{1,0:T(8,128)(2,1)}, bf16[704,512]{1,0:T(8,128)(2,1)}, u32[]{:S(2)}, u32[]{:S(2)}) collective-permute-start(bf16[704,512]{1,0:T(8,128)(2,1)} %bitcast.17.refs_3_), channel_id=1, source_target_pairs={{8,16},{16,8},{9,17},{17,9},{10,18},{18,10},{11,19},{19,11},{12,20... | collective-permute-start | bytes 2162696 | tf_op jit(solution)/shard_map/ppermute | solution.py:522
  147.9 26.0 %all-to-all-start.1 = ((bf16[8,40,2048]{2,1,0:T(8,128)(2,1)}), bf16[8,40,2048]{2,1,0:T(8,128)(2,1)S(1)}, u32[]{:S(2)}, u32[]{:S(2)}) async-start(bf16[8,40,2048]{2,1,0:T(8,128)(2,1)} %bitcast.55), calls=%async_computation.1 | async-start | bytes 2621440 | tf_op jit(solution)/shard_map/all_to_all | solution.py:544
  151.5 21.1 %collective-permute-start.18 = (bf16[704,512]{1,0:T(8,128)(2,1)}, bf16[704,512]{1,0:T(8,128)(2,1)S(1)}, u32[]{:S(2)}, u32[]{:S(2)}) collective-permute-start(bf16[704,512]{1,0:T(8,128)(2,1)} %collective-permute-done.17.refs_14_.refs_20_), channel_id=1, source_target_pairs={{8,0},{16,24},{9,1},{17,25},{10,2},{18,26},{11,3},{19,27},{12,4},{... | collective-permute-start | bytes 2162696 | tf_op jit(solution)/shard_map/ppermute | solution.py:522
  152.8 19.8 %collective-permute-start.20 = (bf16[704,512]{1,0:T(8,128)(2,1)}, bf16[704,512]{1,0:T(8,128)(2,1)S(1)}, u32[]{:S(2)}, u32[]{:S(2)}) collective-permute-start(bf16[704,512]{1,0:T(8,128)(2,1)} %collective-permute-done.19.refs_4_), channel_id=1, source_target_pairs={{8,16},{16,8},{9,17},{17,9},{10,18},{18,10},{11,19},{19,11},{12,20... | collective-permute-start | bytes 2162696 | tf_op jit(solution)/shard_map/ppermute | solution.py:522
  155.5 32.6 %collective-permute-start.22 = (bf16[704,512]{1,0:T(8,128)(2,1)}, bf16[704,512]{1,0:T(8,128)(2,1)S(1)}, u32[]{:S(2)}, u32[]{:S(2)}) collective-permute-start(bf16[704,512]{1,0:T(8,128)(2,1)} %collective-permute-done.21.refs_6_), channel_id=1, source_target_pairs={{8,0},{16,24},{9,1},{17,25},{10,2},{18,26},{11,3},{19,27},{12,4},{... | collective-permute-start | bytes 2162696 | tf_op jit(solution)/shard_map/ppermute | solution.py:522
  172.6 1.3 copy-start.15
  172.6 1.3 copy-start.16
  172.6 30.4 %collective-permute-start.23 = (bf16[704,512]{1,0:T(8,128)(2,1)S(1)}, bf16[704,512]{1,0:T(8,128)(2,1)}, u32[]{:S(2)}, u32[]{:S(2)}) collective-permute-start(bf16[704,512]{1,0:T(8,128)(2,1)S(1)} %collective-permute-done.20.refs_16_.refs_6_), channel_id=1, source_target_pairs={{8,0},{16,24},{9,1},{17,25},{10,2},{18,26},{11,3},{19,27},{12,4},{... | collective-permute-start | bytes 2162696 | tf_op jit(solution)/shard_map/ppermute | solution.py:522
  173.9 1.1 copy-start.8
  194.9 18.8 %all-to-all-start.2 = ((bf16[8,40,1536]{2,1,0:T(8,128)(2,1)}), bf16[8,40,1536]{2,1,0:T(8,128)(2,1)S(1)}, u32[]{:S(2)}, u32[]{:S(2)}) async-start(bf16[8,40,1536]{2,1,0:T(8,128)(2,1)} %bitcast.56), calls=%async_computation.2 | async-start | bytes 1966080 | tf_op jit(solution)/shard_map/all_to_all | solution.py:544
  213.7 25.3 %copy-start = (bf16[1,128,2048]{2,1,0:T(8,128)(2,1)S(1)}, bf16[1,128,2048]{2,1,0:T(8,128)(2,1)}, u32[]{:S(2)}) copy-start(bf16[1,128,2048]{2,1,0:T(8,128)(2,1)} %param.22) | copy-start | bytes 1572868
  213.7 25.3 %copy-start.1 = (f32[1,128,2]{2,1,0:T(8,128)S(1)}, f32[1,128,2]{2,1,0:T(8,128)}, u32[]{:S(2)}) copy-start(f32[1,128,2]{2,1,0:T(8,128)} %copy.15) | copy-start | bytes 3076
  213.7 25.3 %copy-start.2 = (bf16[128,2048]{1,0:T(8,128)(2,1)S(1)}, bf16[128,2048]{1,0:T(8,128)(2,1)}, u32[]{:S(2)}) copy-start(bf16[128,2048]{1,0:T(8,128)(2,1)} %get-tuple-element.49.refs_4_) | copy-start | bytes 1572868
  213.7 25.3 %copy-start.3 = (f32[2048]{0:T(1024)S(1)}, f32[2048]{0:T(1024)}, u32[]{:S(2)}) copy-start(f32[2048]{0:T(1024)} %param.16) | copy-start | bytes 24580
  213.7 25.3 %copy-start.4 = (s32[10]{0:T(128)S(1)}, s32[10]{0:T(128)}, u32[]{:S(2)}) copy-start(s32[10]{0:T(128)} %dynamic-slice_bitcast_fusion.refs_0_) | copy-start | bytes 124
  (2 other events, 1.6 us)

commit v6 on v5

--- a/solution.py
+++ b/solution.py
@@ -214,6 +214,7 @@
     )
     gate_end = send(gate, OUTWARD)
     up_end = send(up, OUTWARD)
+    down_end = send(down, OUTWARD, gate_end)
     near = send(first, INWARD)
     mid = send(second, MIDDLE)
     far = send(second, [(0, 2), (3, 1)])
@@ -233,26 +234,25 @@
         after=(gate_end, up_end, cot_rows),
     )
     gate_mid = send(gate, MIDDLE, near, mid, far)
+    up_mid = send(up, MIDDLE, near, mid, far)
+    down_mid = send(down, MIDDLE, gate_mid)
     gate_inner = send(gate, INWARD, near, far)
-    down_end = send(down, OUTWARD)
-    gate_far = send(gate_mid, OUTWARD, down_end, *pieces)
-    up_mid = send(up, MIDDLE, gate_mid)
     up_inner = send(up, INWARD, gate_inner)
-    own, near, mid, far = lax.optimization_barrier((*pieces, gate_far, up_mid))[:4]
+    down_inner = send(down, INWARD, up_inner)
+    own, near, mid, far = lax.optimization_barrier((*pieces, gate_mid, gate_inner, down_end))[:4]
     near = send(near, OUTWARD)
     mid = send(mid, MIDDLE)
     far = send(far, [(2, 0), (1, 3)])
-    gate_mid_near = send(gate_inner, MIDDLE, up_mid, gate_far)
-    up_far = send(up_mid, OUTWARD, gate_far)
-    up_mid_near = send(up_inner, MIDDLE, mid, far)
-    down_inner = send(down, INWARD, up_inner, up_mid)
-    gate_far_near = send(gate_mid_near, OUTWARD, up_far)
-    down_mid = send(down, MIDDLE, gate_mid_near)
-    up_far_near = send(up_mid_near, OUTWARD, up_far)
-    down_mid_near = send(down_inner, MIDDLE, up_mid_near)
+    gate_mid_near = send(gate_inner, MIDDLE)
+    gate_far = send(gate_mid, OUTWARD)
+    up_far = send(up_mid, OUTWARD)
+    up_mid_near = send(up_inner, MIDDLE, gate_far)
+    down_mid_near = send(down_inner, MIDDLE, up_far)
+    gate_far_near = send(gate_mid_near, OUTWARD)
+    up_far_near = send(up_mid_near, OUTWARD, gate_far_near)
     down_far = send(down_mid, OUTWARD, gate_far_near)
     down_far_near = send(down_mid_near, OUTWARD, up_far_near)
-    norm_after = ()
+    norm_after = (down_mid, gate_mid_near, gate_far, up_far)
     up_after = (down_mid_near,)
     gate_in = [
         [gate],

time: 243 us -> 238 us (0.979)
  starting transfers between devices: 63.8 us -> 61.2 us
    ppermute x24, waiting for transfers between devices: 106 us -> 101 us  [send(): return lax.ppermute(gated(array, *first), 'seq', pairs)]
    all_to_all x3, waiting for transfers between devices: 2.83 us -> 5.48 us  [exchange(): rows = lax.all_to_all(rows, axis, split_axis=0, concat_axis=0, tiled=True)]
    unnamed x48 -> x44, local copies, waits for them, and re-layouts: 5.73 us -> 4.79 us
  transfers between devices with their start and end apart: 27 -> 27, of which waited for: 12 -> 13; matrix products, arithmetic and copies ran while one was open for 1% -> 1% of each run, Pallas kernels for 12% -> 13%
where the time goes in v6:
time: 238 us; the launch traced here: 237 us
  waiting for transfers between devices  107 us (45%)
  starting transfers between devices  61.2 us (26%)
  Pallas kernels  35.6 us (15%)
  blocking collectives  25.3 us (11%)
  local copies, waits for them, and re-layouts  6.79 us (3%)
    ppermute x24, waiting for transfers between devices, send(): return lax.ppermute(gated(array, *first), 'seq', pairs)  101 us
    ppermute x24, starting transfers between devices, send(): return lax.ppermute(gated(array, *first), 'seq', pairs)  49.9 us
    pallas_call x8, Pallas kernels, call(): pl.pallas_call(body, grid=() if held else (1,), out_shape=outs, in_specs=...  35.6 us
    all_to_all x1, blocking collectives, exchange(): rows = lax.all_to_all(rows, axis, split_axis=0, concat_axis=0, tiled=True)  25.3 us
    all_to_all x3, starting transfers between devices, exchange(): rows = lax.all_to_all(rows, axis, split_axis=0, concat_axis=0, tiled=True)  11.3 us
    all_to_all x3, waiting for transfers between devices, exchange(): rows = lax.all_to_all(rows, axis, split_axis=0, concat_axis=0, tiled=True)  5.48 us
    unnamed x44, local copies, waits for them, and re-layouts  4.79 us
  transfers between devices with their start and end apart: 27, of which 13 were waited for; matrix products, arithmetic and copies ran while one was open for 1% of the time, Pallas kernels for 13%

profile of v6, /device:TPU:0, one launch (start us, length us, event | category | flops | bytes accessed | tf_op | source)
XLA Modules:
  0.0 236.8 jit_solution(12563391464627366175)
XLA Ops:
  0.7 1.3 dynamic-slice_bitcast_fusion.refs_0_
  2.0 2.7 %shard_map.131 = (bf16[384,1024]{1,0:T(8,128)(2,1)}, bf16[384,1024]{1,0:T(8,128)(2,1)}) custom-call(s32[10]{0:T(128)} %dynamic-slice_bitcast_fusion.refs_0_, bf16[128,2048]{1,0:T(8,128)(2,1)} %bitcast.57, bf16[128,2048]{1,0:T(8,128)(2,1)} %bitcast.58, bf16[128,2048]{1,0:T(8,128)(2,1)} %bitcast.59), custom_call_target="tpu_custom_call" | custom-call | bytes 3145728 | tf_op jit(solution)/shard_map/pallas_call | solution.py:35
  4.7 5.8 %collective-permute-start = (bf16[384,1024]{1,0:T(8,128)(2,1)}, bf16[384,1024]{1,0:T(8,128)(2,1)}, u32[]{:S(2)}, u32[]{:S(2)}) collective-permute-start(bf16[384,1024]{1,0:T(8,128)(2,1)} %get-tuple-element.33.refs_1_), channel_id=1, source_target_pairs={{0,8},{24,16},{1,9},{25,17},{2,10},{26,18},{3,11},{27,19},{4,12},{... | collective-permute-start | bytes 2359304 | tf_op jit(solution)/shard_map/ppermute | solution.py:522
  10.6 1.5 collective-permute-start.1
  12.1 3.1 %collective-permute-start.2 = (bf16[384,1024]{1,0:T(8,128)(2,1)}, bf16[384,1024]{1,0:T(8,128)(2,1)}, u32[]{:S(2)}, u32[]{:S(2)}) collective-permute-start(bf16[384,1024]{1,0:T(8,128)(2,1)} %get-tuple-element.34), channel_id=1, source_target_pairs={{0,16},{24,8},{1,17},{25,9},{2,18},{26,10},{3,19},{27,11},{4,20},{... | collective-permute-start | bytes 2359304 | tf_op jit(solution)/shard_map/ppermute | solution.py:522
  15.3 1.3 collective-permute-start.3
  18.1 3.1 %shard_map.132 = bf16[320,2048]{1,0:T(8,128)(2,1)} custom-call(s32[2,128]{1,0:T(2,128)} %copy.17.refs_0_.refs_1_, f32[128,2]{1,0:T(8,128)} %bitcast.33, bf16[128,2048]{1,0:T(8,128)(2,1)} %bitcast.31), custom_call_target="tpu_custom_call" | custom-call | flops 335544320 | bytes 1835008 | tf_op jit(solution)/shard_map/pallas_call | solution.py:35
  21.2 3.7 %all-to-all-start = ((bf16[8,40,2048]{2,1,0:T(8,128)(2,1)}), bf16[8,40,2048]{2,1,0:T(8,128)(2,1)S(1)}, u32[]{:S(2)}, u32[]{:S(2)}) async-start(bf16[8,40,2048]{2,1,0:T(8,128)(2,1)} %bitcast.44), calls=%async_computation | async-start | bytes 2621440 | tf_op jit(solution)/shard_map/all_to_all | solution.py:544
  25.0 2.9 %collective-permute-done.refs_2_ = bf16[384,1024]{1,0:T(8,128)(2,1)} collective-permute-done((bf16[384,1024]{1,0:T(8,128)(2,1)}, bf16[384,1024]{1,0:T(8,128)(2,1)}, u32[]{:S(2)}, u32[]{:S(2)}) %collective-permute-start) | collective-permute-done | bytes 786464 | tf_op jit(solution)/shard_map/ppermute | solution.py:522
  27.9 15.7 %collective-permute-done.2.refs_4_ = bf16[384,1024]{1,0:T(8,128)(2,1)} collective-permute-done((bf16[384,1024]{1,0:T(8,128)(2,1)}, bf16[384,1024]{1,0:T(8,128)(2,1)}, u32[]{:S(2)}, u32[]{:S(2)}) %collective-permute-start.2) | collective-permute-done | bytes 786464 | tf_op jit(solution)/shard_map/ppermute | solution.py:522
  43.7 1.5 collective-permute-start.5
  45.2 8.5 %collective-permute-start.6 = (bf16[704,512]{1,0:T(8,128)(2,1)S(1)}, bf16[704,512]{1,0:T(8,128)(2,1)}, u32[]{:S(2)}, u32[]{:S(2)}) collective-permute-start(bf16[704,512]{1,0:T(8,128)(2,1)S(1)} %bitcast.49), channel_id=1, source_target_pairs={{0,8},{24,16},{1,9},{25,17},{2,10},{26,18},{3,11},{27,19},{4,12},{... | collective-permute-start | bytes 2162696 | tf_op jit(solution)/shard_map/ppermute | solution.py:522
  53.7 1.3 collective-permute-start.4
  55.0 1.3 collective-permute-start.7
  56.3 1.6 collective-permute-start.14
  57.9 1.3 collective-permute-start.13
  59.1 7.9 %collective-permute-done.6.refs_3_.refs_9_ = bf16[704,512]{1,0:T(8,128)(2,1)} collective-permute-done((bf16[704,512]{1,0:T(8,128)(2,1)S(1)}, bf16[704,512]{1,0:T(8,128)(2,1)}, u32[]{:S(2)}, u32[]{:S(2)}) %collective-permute-start.6) | collective-permute-done | bytes 720928 | tf_op jit(solution)/shard_map/ppermute | solution.py:522
  67.0 6.4 %collective-permute-start.17 = (bf16[704,512]{1,0:T(8,128)(2,1)}, bf16[704,512]{1,0:T(8,128)(2,1)}, u32[]{:S(2)}, u32[]{:S(2)}) collective-permute-start(bf16[704,512]{1,0:T(8,128)(2,1)} %bitcast.52), channel_id=1, source_target_pairs={{0,8},{24,16},{1,9},{25,17},{2,10},{26,18},{3,11},{27,19},{4,12},{... | collective-permute-start | bytes 2162696 | tf_op jit(solution)/shard_map/ppermute | solution.py:522
  73.4 1.4 collective-permute-done.4.refs_6_.refs_11_.refs_17_
  74.8 1.5 collective-permute-start.12
  76.4 1.1 copy-done.5
  77.4 1.7 shard_map.133
  79.1 11.3 %collective-permute-done.7.refs_5_ = bf16[704,512]{1,0:T(8,128)(2,1)} collective-permute-done((bf16[704,512]{1,0:T(8,128)(2,1)}, bf16[704,512]{1,0:T(8,128)(2,1)}, u32[]{:S(2)}, u32[]{:S(2)}) %collective-permute-start.7) | collective-permute-done | bytes 720928 | tf_op jit(solution)/shard_map/ppermute | solution.py:522
  90.4 1.3 collective-permute-start.8
  92.4 16.3 %collective-permute-done.8.refs_5_ = bf16[128,1024]{1,0:T(8,128)(2,1)S(1)} collective-permute-done((bf16[128,1024]{1,0:T(8,128)(2,1)}, bf16[128,1024]{1,0:T(8,128)(2,1)S(1)}, u32[]{:S(2)}, u32[]{:S(2)}) %collective-permute-start.8) | collective-permute-done | bytes 262176 | tf_op jit(solution)/shard_map/ppermute | solution.py:522
  108.7 1.3 collective-permute-start.15
  110.7 1.3 collective-permute-start.10
  112.0 1.3 collective-permute-start.16
  114.1 15.1 %collective-permute-done.10.refs_7_ = bf16[128,1024]{1,0:T(8,128)(2,1)S(1)} collective-permute-done((bf16[128,1024]{1,0:T(8,128)(2,1)}, bf16[128,1024]{1,0:T(8,128)(2,1)S(1)}, u32[]{:S(2)}, u32[]{:S(2)}) %collective-permute-start.10) | collective-permute-done | bytes 262176 | tf_op jit(solution)/shard_map/ppermute | solution.py:522
  129.2 2.2 collective-permute-start.20
  131.3 4.2 %collective-permute-done.15.refs_11_.refs_13_.refs_19_ = bf16[704,512]{1,0:T(8,128)(2,1)S(1)} collective-permute-done((bf16[704,512]{1,0:T(8,128)(2,1)}, bf16[704,512]{1,0:T(8,128)(2,1)S(1)}, u32[]{:S(2)}, u32[]{:S(2)}) %collective-permute-start.15) | collective-permute-done | bytes 720928 | tf_op jit(solution)/shard_map/ppermute | solution.py:522
  136.4 3.3 %shard_map.134 = (bf16[128,2048]{1,0:T(8,128)(2,1)}, bf16[320,2048]{1,0:T(8,128)(2,1)}) custom-call(s32[10]{0:T(128)} %dynamic-slice_bitcast_fusion.refs_0_, s32[2,128]{1,0:T(2,128)} %copy.17.refs_0_.refs_1_, bf16[128,2048]{1,0:T(8,128)(2,1)} %bitcast.60, f32[1,2048]{1,0:T(1,128)} %bitcast.37, bf16[128,1024]{1,0:T(8,128)(2,1)} %get-tuple-element.42.refs_4_, ...), custom_call_target="tpu_custom_call" | custom-call | flops 167772160 | bytes 2883584 | tf_op jit(solution)/shard_map/pallas_call | solution.py:35
  139.7 3.9 %all-to-all-start.1 = ((bf16[8,40,2048]{2,1,0:T(8,128)(2,1)}), bf16[8,40,2048]{2,1,0:T(8,128)(2,1)S(1)}, u32[]{:S(2)}, u32[]{:S(2)}) async-start(bf16[8,40,2048]{2,1,0:T(8,128)(2,1)} %bitcast.55), calls=%async_computation.1 | async-start | bytes 2621440 | tf_op jit(solution)/shard_map/all_to_all | solution.py:544
  143.6 3.8 %collective-permute-done.16.refs_8_.refs_14_ = bf16[704,512]{1,0:T(8,128)(2,1)S(1)} collective-permute-done((bf16[704,512]{1,0:T(8,128)(2,1)}, bf16[704,512]{1,0:T(8,128)(2,1)S(1)}, u32[]{:S(2)}, u32[]{:S(2)}) %collective-permute-start.16) | collective-permute-done | bytes 720928 | tf_op jit(solution)/shard_map/ppermute | solution.py:522
  147.4 1.3 collective-permute-start.19
  148.7 1.5 collective-permute-start.21
  150.3 1.3 collective-permute-start.22
  151.6 16.8 %collective-permute-done.19.refs_15_.refs_21_ = bf16[704,512]{1,0:T(8,128)(2,1)S(1)} collective-permute-done((bf16[704,512]{1,0:T(8,128)(2,1)S(1)}, bf16[704,512]{1,0:T(8,128)(2,1)S(1)}, u32[]{:S(2)}, u32[]{:S(2)}) %collective-permute-start.19) | collective-permute-done | bytes 720928 | tf_op jit(solution)/shard_map/ppermute | solution.py:522
  169.2 1.3 collective-permute-start.23
  171.6 7.9 %shard_map.135 = (bf16[320,704]{1,0:T(8,128)(2,1)}, f32[320,704]{1,0:T(8,128)}, f32[320,704]{1,0:T(8,128)}) custom-call(s32[10]{0:T(128)} %dynamic-slice_bitcast_fusion.refs_0_, bf16[320,2048]{1,0:T(8,128)(2,1)} %bitcast.43, bf16[704,512]{1,0:T(8,128)(2,1)} %bitcast.45, bf16[704,512]{1,0:T(8,128)(2,1)} %collective-permute-done.6.refs_3_.refs_9_, ...), custom_call_target="tpu_custom_call" | custom-call | flops 1845493760 | bytes 9330688 | tf_op jit(solution)/shard_map/pallas_call | solution.py:35
  179.5 4.4 %collective-permute-done.22.refs_7_ = bf16[704,512]{1,0:T(8,128)(2,1)} collective-permute-done((bf16[704,512]{1,0:T(8,128)(2,1)S(1)}, bf16[704,512]{1,0:T(8,128)(2,1)}, u32[]{:S(2)}, u32[]{:S(2)}) %collective-permute-start.22) | collective-permute-done | bytes 720928 | tf_op jit(solution)/shard_map/ppermute | solution.py:522
  183.9 5.9 %shard_map.136 = (bf16[320,1536]{1,0:T(8,128)(2,1)}, f32[320,704]{1,0:T(8,128)}) custom-call(s32[10]{0:T(128)} %dynamic-slice_bitcast_fusion.refs_0_, bf16[320,704]{1,0:T(8,128)(2,1)} %get-tuple-element.55.refs_1_, bf16[320,2048]{1,0:T(8,128)(2,1)} %bitcast.40, bf16[704,512]{1,0:T(8,128)(2,1)} %bitcast.17.refs_3_, ...), custom_call_target="tpu_custom_call" | custom-call | flops 1384120320 | bytes 6856704 | tf_op jit(solution)/shard_map/pallas_call | solution.py:35
  189.9 3.7 %all-to-all-start.2 = ((bf16[8,40,1536]{2,1,0:T(8,128)(2,1)}), bf16[8,40,1536]{2,1,0:T(8,128)(2,1)S(1)}, u32[]{:S(2)}, u32[]{:S(2)}) async-start(bf16[8,40,1536]{2,1,0:T(8,128)(2,1)} %bitcast.56), calls=%async_computation.2 | async-start | bytes 1966080 | tf_op jit(solution)/shard_map/all_to_all | solution.py:544
  193.6 1.4 collective-permute-done.23.refs_7_
  195.1 7.8 %shard_map.137 = bf16[320,2560]{1,0:T(8,128)(2,1)} custom-call(s32[10]{0:T(128)} %dynamic-slice_bitcast_fusion.refs_0_, bf16[320,704]{1,0:T(8,128)(2,1)} %get-tuple-element.55.refs_1_, bf16[320,2048]{1,0:T(8,128)(2,1)} %bitcast.41, f32[320,704]{1,0:T(8,128)} %get-tuple-element.58.refs_3_, f32[320,704]{1,0:T(8,128)} %get-tuple-element.59.refs_4_, ...), custom_call_target="tpu_custom_call" | custom-call | flops 2306867200 | bytes 11542528 | tf_op jit(solution)/shard_map/pallas_call | solution.py:35
  202.9 5.5 %all-to-all-done.2 = bf16[8,40,1536]{2,1,0:T(8,128)(2,1)S(1)} async-done(((bf16[8,40,1536]{2,1,0:T(8,128)(2,1)}), bf16[8,40,1536]{2,1,0:T(8,128)(2,1)S(1)}, u32[]{:S(2)}, u32[]{:S(2)}) %all-to-all-start.2) | async-done | bytes 983072 | tf_op jit(solution)/shard_map/all_to_all | solution.py:544
  208.4 25.3 %all_to_all.20 = bf16[8,40,2560]{2,1,0:T(8,128)(2,1)S(1)} all-to-all(bf16[8,40,2560]{2,1,0:T(8,128)(2,1)} %bitcast.42), channel_id=1, replica_groups=mesh['seq'=4,'exp'=8] {'exp'}, dimensions={0} | all-to-all | bytes 3276800 | tf_op jit(solution)/shard_map/all_to_all | solution.py:544
  233.7 3.1 %shard_map.138 = (bf16[128,2048]{1,0:T(8,128)(2,1)}, bf16[128,2048]{1,0:T(8,128)(2,1)}) custom-call(s32[10]{0:T(128)S(1)} %copy-done.4, s32[128,2]{1,0:T(8,128)S(1)} %bitcast.36, f32[128,2]{1,0:T(8,128)S(1)} %bitcast.34, f32[1,2048]{1,0:T(1,128)S(1)} %bitcast.38, bf16[128,2048]{1,0:T(8,128)(2,1)S(1)} %copy-done.2, bf16[128,2048]{1,0:T(8,128)(2,1)S(1)} %bitcast.32, ...), custom_call_target="tpu_custom_call" | custom-call | flops 503316480 | bytes 4718592 | tf_op jit(solution)/shard_map/pallas_call | solution.py:35
  (61 shorter events, 6.5 us)
Async XLA Ops:
  0.6 14.6 %copy-start.12 = (bf16[1,512,704]{1,2,0:T(8,128)(2,1)S(1)}, bf16[1,512,704]{1,2,0:T(8,128)(2,1)}, u32[]{:S(2)}) copy-start(bf16[1,512,704]{1,2,0:T(8,128)(2,1)} %param.17) | copy-start | bytes 2162692
  0.6 15.9 %copy-start.19 = (s32[1,128,2]{1,2,0:T(2,128)S(1)}, s32[1,128,2]{1,2,0:T(2,128)}, u32[]{:S(2)}) copy-start(s32[1,128,2]{1,2,0:T(2,128)} %param.20) | copy-start | bytes 3076
  0.7 16.0 %copy-start.20 = (f32[1,128,2]{1,2,0:T(2,128)S(1)}, f32[1,128,2]{1,2,0:T(2,128)}, u32[]{:S(2)}) copy-start(f32[1,128,2]{1,2,0:T(2,128)} %param.21) | copy-start | bytes 3076
  4.7 23.2 %collective-permute-start = (bf16[384,1024]{1,0:T(8,128)(2,1)}, bf16[384,1024]{1,0:T(8,128)(2,1)}, u32[]{:S(2)}, u32[]{:S(2)}) collective-permute-start(bf16[384,1024]{1,0:T(8,128)(2,1)} %get-tuple-element.33.refs_1_), channel_id=1, source_target_pairs={{0,8},{24,16},{1,9},{25,17},{2,10},{26,18},{3,11},{27,19},{4,12},{... | collective-permute-start | bytes 2359304 | tf_op jit(solution)/shard_map/ppermute | solution.py:522
  10.6 17.3 %collective-permute-start.1 = (bf16[384,1024]{1,0:T(8,128)(2,1)}, bf16[384,1024]{1,0:T(8,128)(2,1)}, u32[]{:S(2)}, u32[]{:S(2)}) collective-permute-start(bf16[384,1024]{1,0:T(8,128)(2,1)} %get-tuple-element.34), channel_id=1, source_target_pairs={{8,16},{16,8},{9,17},{17,9},{10,18},{18,10},{11,19},{19,11},{12,20... | collective-permute-start | bytes 2359304 | tf_op jit(solution)/shard_map/ppermute | solution.py:522
  12.1 31.5 %collective-permute-start.2 = (bf16[384,1024]{1,0:T(8,128)(2,1)}, bf16[384,1024]{1,0:T(8,128)(2,1)}, u32[]{:S(2)}, u32[]{:S(2)}) collective-permute-start(bf16[384,1024]{1,0:T(8,128)(2,1)} %get-tuple-element.34), channel_id=1, source_target_pairs={{0,16},{24,8},{1,17},{25,9},{2,18},{26,10},{3,19},{27,11},{4,20},{... | collective-permute-start | bytes 2359304 | tf_op jit(solution)/shard_map/ppermute | solution.py:522
  15.3 39.7 %collective-permute-start.3 = (bf16[704,512]{1,0:T(8,128)(2,1)S(1)}, bf16[704,512]{1,0:T(8,128)(2,1)S(1)}, u32[]{:S(2)}, u32[]{:S(2)}) collective-permute-start(bf16[704,512]{1,0:T(8,128)(2,1)S(1)} %bitcast.47), channel_id=1, source_target_pairs={{8,0},{16,24},{9,1},{17,25},{10,2},{18,26},{11,3},{19,27},{12,4},{... | collective-permute-start | bytes 2162696 | tf_op jit(solution)/shard_map/ppermute | solution.py:522
  21.2 55.1 %all-to-all-start = ((bf16[8,40,2048]{2,1,0:T(8,128)(2,1)}), bf16[8,40,2048]{2,1,0:T(8,128)(2,1)S(1)}, u32[]{:S(2)}, u32[]{:S(2)}) async-start(bf16[8,40,2048]{2,1,0:T(8,128)(2,1)} %bitcast.44), calls=%async_computation | async-start | bytes 2621440 | tf_op jit(solution)/shard_map/all_to_all | solution.py:544
  43.7 14.2 %collective-permute-start.5 = (bf16[704,512]{1,0:T(8,128)(2,1)S(1)}, bf16[704,512]{1,0:T(8,128)(2,1)}, u32[]{:S(2)}, u32[]{:S(2)}) collective-permute-start(bf16[704,512]{1,0:T(8,128)(2,1)S(1)} %bitcast.48), channel_id=1, source_target_pairs={{8,16},{16,8},{9,17},{17,9},{10,18},{18,10},{11,19},{19,11},{12,20... | collective-permute-start | bytes 2162696 | tf_op jit(solution)/shard_map/ppermute | solution.py:522
  45.2 21.8 %collective-permute-start.6 = (bf16[704,512]{1,0:T(8,128)(2,1)S(1)}, bf16[704,512]{1,0:T(8,128)(2,1)}, u32[]{:S(2)}, u32[]{:S(2)}) collective-permute-start(bf16[704,512]{1,0:T(8,128)(2,1)S(1)} %bitcast.49), channel_id=1, source_target_pairs={{0,8},{24,16},{1,9},{25,17},{2,10},{26,18},{3,11},{27,19},{4,12},{... | collective-permute-start | bytes 2162696 | tf_op jit(solution)/shard_map/ppermute | solution.py:522
  53.7 21.2 %collective-permute-start.4 = (bf16[704,512]{1,0:T(8,128)(2,1)}, bf16[704,512]{1,0:T(8,128)(2,1)S(1)}, u32[]{:S(2)}, u32[]{:S(2)}) collective-permute-start(bf16[704,512]{1,0:T(8,128)(2,1)} %bitcast.50), channel_id=1, source_target_pairs={{8,0},{16,24},{9,1},{17,25},{10,2},{18,26},{11,3},{19,27},{12,4},{... | collective-permute-start | bytes 2162696 | tf_op jit(solution)/shard_map/ppermute | solution.py:522
  55.0 21.4 %copy-start.6 = (bf16[704,512]{1,0:T(8,128)(2,1)}, bf16[704,512]{1,0:T(8,128)(2,1)S(1)}, u32[]{:S(2)}) copy-start(bf16[704,512]{1,0:T(8,128)(2,1)S(1)} %collective-permute-done.3.refs_5_.refs_4_.refs_10_) | copy-start | bytes 2162692
  55.0 35.4 %collective-permute-start.7 = (bf16[704,512]{1,0:T(8,128)(2,1)}, bf16[704,512]{1,0:T(8,128)(2,1)}, u32[]{:S(2)}, u32[]{:S(2)}) collective-permute-start(bf16[704,512]{1,0:T(8,128)(2,1)} %bitcast.17.refs_3_), channel_id=1, source_target_pairs={{8,0},{16,24},{9,1},{17,25},{10,2},{18,26},{11,3},{19,27},{12,4},{... | collective-permute-start | bytes 2162696 | tf_op jit(solution)/shard_map/ppermute | solution.py:522
  56.3 35.4 %collective-permute-start.14 = (bf16[704,512]{1,0:T(8,128)(2,1)}, bf16[704,512]{1,0:T(8,128)(2,1)}, u32[]{:S(2)}, u32[]{:S(2)}) collective-permute-start(bf16[704,512]{1,0:T(8,128)(2,1)} %bitcast.51), channel_id=1, source_target_pairs={{8,16},{16,8},{9,17},{17,9},{10,18},{18,10},{11,19},{19,11},{12,20... | collective-permute-start | bytes 2162696 | tf_op jit(solution)/shard_map/ppermute | solution.py:522
  57.9 52.2 %collective-permute-start.13 = (bf16[704,512]{1,0:T(8,128)(2,1)}, bf16[704,512]{1,0:T(8,128)(2,1)}, u32[]{:S(2)}, u32[]{:S(2)}) collective-permute-start(bf16[704,512]{1,0:T(8,128)(2,1)} %collective-permute-done.5.refs_5_.refs_11_), channel_id=1, source_target_pairs={{8,0},{16,24},{9,1},{17,25},{10,2},{18,26},{11,3},{19,27},{12,4},{... | collective-permute-start | bytes 2162696 | tf_op jit(solution)/shard_map/ppermute | solution.py:522
  67.0 43.7 %collective-permute-start.17 = (bf16[704,512]{1,0:T(8,128)(2,1)}, bf16[704,512]{1,0:T(8,128)(2,1)}, u32[]{:S(2)}, u32[]{:S(2)}) collective-permute-start(bf16[704,512]{1,0:T(8,128)(2,1)} %bitcast.52), channel_id=1, source_target_pairs={{0,8},{24,16},{1,9},{25,17},{2,10},{26,18},{3,11},{27,19},{4,12},{... | collective-permute-start | bytes 2162696 | tf_op jit(solution)/shard_map/ppermute | solution.py:522
  74.8 1.5 copy-start.7
  74.8 37.2 %collective-permute-start.12 = (bf16[704,512]{1,0:T(8,128)(2,1)}, bf16[704,512]{1,0:T(8,128)(2,1)}, u32[]{:S(2)}, u32[]{:S(2)}) collective-permute-start(bf16[704,512]{1,0:T(8,128)(2,1)} %collective-permute-done.6.refs_3_.refs_9_), channel_id=1, source_target_pairs={{8,16},{16,8},{9,17},{17,9},{10,18},{18,10},{11,19},{19,11},{12,20... | collective-permute-start | bytes 2162696 | tf_op jit(solution)/shard_map/ppermute | solution.py:522
  76.4 1.1 copy-start.5
  90.4 18.3 %collective-permute-start.8 = (bf16[128,1024]{1,0:T(8,128)(2,1)}, bf16[128,1024]{1,0:T(8,128)(2,1)S(1)}, u32[]{:S(2)}, u32[]{:S(2)}) collective-permute-start(bf16[128,1024]{1,0:T(8,128)(2,1)} %get-tuple-element.43), channel_id=1, source_target_pairs={{8,0},{16,24},{9,1},{17,25},{10,2},{18,26},{11,3},{19,27},{12,4},{... | collective-permute-start | bytes 786440 | tf_op jit(solution)/shard_map/ppermute | solution.py:522
  91.7 39.7 %collective-permute-start.11 = (bf16[704,512]{1,0:T(8,128)(2,1)}, bf16[704,512]{1,0:T(8,128)(2,1)S(1)}, u32[]{:S(2)}, u32[]{:S(2)}) collective-permute-start(bf16[704,512]{1,0:T(8,128)(2,1)} %bitcast.17.refs_3_), channel_id=1, source_target_pairs={{8,16},{16,8},{9,17},{17,9},{10,18},{18,10},{11,19},{19,11},{12,20... | collective-permute-start | bytes 2162696 | tf_op jit(solution)/shard_map/ppermute | solution.py:522
  108.7 26.8 %copy-start.16 = (bf16[128,1024]{1,0:T(8,128)(2,1)}, bf16[128,1024]{1,0:T(8,128)(2,1)S(1)}, u32[]{:S(2)}) copy-start(bf16[128,1024]{1,0:T(8,128)(2,1)S(1)} %collective-permute-done.8.refs_5_) | copy-start | bytes 786436
  108.7 26.8 %collective-permute-start.15 = (bf16[704,512]{1,0:T(8,128)(2,1)}, bf16[704,512]{1,0:T(8,128)(2,1)S(1)}, u32[]{:S(2)}, u32[]{:S(2)}) collective-permute-start(bf16[704,512]{1,0:T(8,128)(2,1)} %collective-permute-done.14.refs_12_.refs_18_), channel_id=1, source_target_pairs={{8,0},{16,24},{9,1},{17,25},{10,2},{18,26},{11,3},{19,27},{12,4},{... | collective-permute-start | bytes 2162696 | tf_op jit(solution)/shard_map/ppermute | solution.py:522
  110.0 3.3 %collective-permute-start.9 = (bf16[128,1024]{1,0:T(8,128)(2,1)}, bf16[128,1024]{1,0:T(8,128)(2,1)S(1)}, u32[]{:S(2)}, u32[]{:S(2)}) collective-permute-start(bf16[128,1024]{1,0:T(8,128)(2,1)} %get-tuple-element.44), channel_id=1, source_target_pairs={{8,16},{16,8},{9,17},{17,9},{10,18},{18,10},{11,19},{19,11},{12,20... | collective-permute-start | bytes 786440 | tf_op jit(solution)/shard_map/ppermute | solution.py:522
  110.7 18.4 %collective-permute-start.10 = (bf16[128,1024]{1,0:T(8,128)(2,1)}, bf16[128,1024]{1,0:T(8,128)(2,1)S(1)}, u32[]{:S(2)}, u32[]{:S(2)}) collective-permute-start(bf16[128,1024]{1,0:T(8,128)(2,1)} %get-tuple-element.45), channel_id=1, source_target_pairs={{16,0},{8,24},{17,1},{9,25},{18,2},{10,26},{19,3},{11,27},{20,4},{... | collective-permute-start | bytes 786440 | tf_op jit(solution)/shard_map/ppermute | solution.py:522
  112.0 35.4 %collective-permute-start.16 = (bf16[704,512]{1,0:T(8,128)(2,1)}, bf16[704,512]{1,0:T(8,128)(2,1)S(1)}, u32[]{:S(2)}, u32[]{:S(2)}) collective-permute-start(bf16[704,512]{1,0:T(8,128)(2,1)} %collective-permute-done.12.refs_9_.refs_7_.refs_13_), channel_id=1, source_target_pairs={{8,0},{16,24},{9,1},{17,25},{10,2},{18,26},{11,3},{19,27},{12,4},{... | collective-permute-start | bytes 2162696 | tf_op jit(solution)/shard_map/ppermute | solution.py:522
  113.3 22.2 %copy-start.17 = (bf16[128,1024]{1,0:T(8,128)(2,1)}, bf16[128,1024]{1,0:T(8,128)(2,1)S(1)}, u32[]{:S(2)}) copy-start(bf16[128,1024]{1,0:T(8,128)(2,1)S(1)} %collective-permute-done.9.refs_6_) | copy-start | bytes 786436
  113.4 34.1 %collective-permute-start.18 = (bf16[704,512]{1,0:T(8,128)(2,1)}, bf16[704,512]{1,0:T(8,128)(2,1)S(1)}, u32[]{:S(2)}, u32[]{:S(2)}) collective-permute-start(bf16[704,512]{1,0:T(8,128)(2,1)} %collective-permute-done.17.refs_10_.refs_16_), channel_id=1, source_target_pairs={{8,16},{16,8},{9,17},{17,9},{10,18},{18,10},{11,19},{19,11},{12,20... | collective-permute-start | bytes 2162696 | tf_op jit(solution)/shard_map/ppermute | solution.py:522
  129.2 6.4 %copy-start.18 = (bf16[128,1024]{1,0:T(8,128)(2,1)}, bf16[128,1024]{1,0:T(8,128)(2,1)S(1)}, u32[]{:S(2)}) copy-start(bf16[128,1024]{1,0:T(8,128)(2,1)S(1)} %collective-permute-done.10.refs_7_) | copy-start | bytes 786436
  129.2 19.6 %collective-permute-start.20 = (bf16[704,512]{1,0:T(8,128)(2,1)}, bf16[704,512]{1,0:T(8,128)(2,1)}, u32[]{:S(2)}, u32[]{:S(2)}) collective-permute-start(bf16[704,512]{1,0:T(8,128)(2,1)} %bitcast.17.refs_3_), channel_id=1, source_target_pairs={{0,8},{24,16},{1,9},{25,17},{2,10},{26,18},{3,11},{27,19},{4,12},{... | collective-permute-start | bytes 2162696 | tf_op jit(solution)/shard_map/ppermute | solution.py:522
  131.3 4.2 %copy-start.10 = (bf16[704,512]{1,0:T(8,128)(2,1)}, bf16[704,512]{1,0:T(8,128)(2,1)S(1)}, u32[]{:S(2)}) copy-start(bf16[704,512]{1,0:T(8,128)(2,1)S(1)} %collective-permute-done.11.refs_8_.refs_6_) | copy-start | bytes 2162692
  135.5 0.9 copy-start.8
  139.7 10.5 %copy-start.11 = (bf16[704,512]{1,0:T(8,128)(2,1)S(1)}, bf16[704,512]{1,0:T(8,128)(2,1)}, u32[]{:S(2)}) copy-start(bf16[704,512]{1,0:T(8,128)(2,1)} %copy-done.10) | copy-start | bytes 2162692
  139.7 30.8 %all-to-all-start.1 = ((bf16[8,40,2048]{2,1,0:T(8,128)(2,1)}), bf16[8,40,2048]{2,1,0:T(8,128)(2,1)S(1)}, u32[]{:S(2)}, u32[]{:S(2)}) async-start(bf16[8,40,2048]{2,1,0:T(8,128)(2,1)} %bitcast.55), calls=%async_computation.1 | async-start | bytes 2621440 | tf_op jit(solution)/shard_map/all_to_all | solution.py:544
  147.4 23.1 %copy-start.13 = (bf16[704,512]{1,0:T(8,128)(2,1)}, bf16[704,512]{1,0:T(8,128)(2,1)S(1)}, u32[]{:S(2)}) copy-start(bf16[704,512]{1,0:T(8,128)(2,1)S(1)} %collective-permute-done.16.refs_8_.refs_14_) | copy-start | bytes 2162692
  147.4 23.1 %copy-start.14 = (bf16[704,512]{1,0:T(8,128)(2,1)}, bf16[704,512]{1,0:T(8,128)(2,1)S(1)}, u32[]{:S(2)}) copy-start(bf16[704,512]{1,0:T(8,128)(2,1)S(1)} %collective-permute-done.18.refs_14_.refs_20_) | copy-start | bytes 2162692
  147.4 21.0 %collective-permute-start.19 = (bf16[704,512]{1,0:T(8,128)(2,1)S(1)}, bf16[704,512]{1,0:T(8,128)(2,1)S(1)}, u32[]{:S(2)}, u32[]{:S(2)}) collective-permute-start(bf16[704,512]{1,0:T(8,128)(2,1)S(1)} %collective-permute-done.18.refs_14_.refs_20_), channel_id=1, source_target_pairs={{8,0},{16,24},{9,1},{17,25},{10,2},{18,26},{11,3},{19,27},{12,4},{... | collective-permute-start | bytes 2162696 | tf_op jit(solution)/shard_map/ppermute | solution.py:522
  148.7 19.7 %collective-permute-start.21 = (bf16[704,512]{1,0:T(8,128)(2,1)}, bf16[704,512]{1,0:T(8,128)(2,1)}, u32[]{:S(2)}, u32[]{:S(2)}) collective-permute-start(bf16[704,512]{1,0:T(8,128)(2,1)} %collective-permute-done.20.refs_4_), channel_id=1, source_target_pairs={{8,16},{16,8},{9,17},{17,9},{10,18},{18,10},{11,19},{19,11},{12,20... | collective-permute-start | bytes 2162696 | tf_op jit(solution)/shard_map/ppermute | solution.py:522
  150.3 33.7 %collective-permute-start.22 = (bf16[704,512]{1,0:T(8,128)(2,1)S(1)}, bf16[704,512]{1,0:T(8,128)(2,1)}, u32[]{:S(2)}, u32[]{:S(2)}) collective-permute-start(bf16[704,512]{1,0:T(8,128)(2,1)S(1)} %copy-done.11), channel_id=1, source_target_pairs={{8,0},{16,24},{9,1},{17,25},{10,2},{18,26},{11,3},{19,27},{12,4},{... | collective-permute-start | bytes 2162696 | tf_op jit(solution)/shard_map/ppermute | solution.py:522
  168.4 0.8 copy-start.15
  169.2 25.8 %collective-permute-start.23 = (bf16[704,512]{1,0:T(8,128)(2,1)}, bf16[704,512]{1,0:T(8,128)(2,1)}, u32[]{:S(2)}, u32[]{:S(2)}) collective-permute-start(bf16[704,512]{1,0:T(8,128)(2,1)} %collective-permute-done.21.refs_16_.refs_6_), channel_id=1, source_target_pairs={{8,0},{16,24},{9,1},{17,25},{10,2},{18,26},{11,3},{19,27},{12,4},{... | collective-permute-start | bytes 2162696 | tf_op jit(solution)/shard_map/ppermute | solution.py:522
  170.5 1.1 copy-start.9
  189.9 18.5 %all-to-all-start.2 = ((bf16[8,40,1536]{2,1,0:T(8,128)(2,1)}), bf16[8,40,1536]{2,1,0:T(8,128)(2,1)S(1)}, u32[]{:S(2)}, u32[]{:S(2)}) async-start(bf16[8,40,1536]{2,1,0:T(8,128)(2,1)} %bitcast.56), calls=%async_computation.2 | async-start | bytes 1966080 | tf_op jit(solution)/shard_map/all_to_all | solution.py:544
  208.3 25.3 %copy-start = (bf16[1,128,2048]{2,1,0:T(8,128)(2,1)S(1)}, bf16[1,128,2048]{2,1,0:T(8,128)(2,1)}, u32[]{:S(2)}) copy-start(bf16[1,128,2048]{2,1,0:T(8,128)(2,1)} %param.22) | copy-start | bytes 1572868
  208.3 25.3 %copy-start.1 = (f32[1,128,2]{2,1,0:T(8,128)S(1)}, f32[1,128,2]{2,1,0:T(8,128)}, u32[]{:S(2)}) copy-start(f32[1,128,2]{2,1,0:T(8,128)} %copy.15) | copy-start | bytes 3076
  208.3 25.3 %copy-start.2 = (bf16[128,2048]{1,0:T(8,128)(2,1)S(1)}, bf16[128,2048]{1,0:T(8,128)(2,1)}, u32[]{:S(2)}) copy-start(bf16[128,2048]{1,0:T(8,128)(2,1)} %get-tuple-element.48.refs_4_) | copy-start | bytes 1572868
  208.3 25.3 %copy-start.3 = (f32[2048]{0:T(1024)S(1)}, f32[2048]{0:T(1024)}, u32[]{:S(2)}) copy-start(f32[2048]{0:T(1024)} %param.16) | copy-start | bytes 24580
  208.3 25.3 %copy-start.4 = (s32[10]{0:T(128)S(1)}, s32[10]{0:T(128)}, u32[]{:S(2)}) copy-start(s32[10]{0:T(128)} %dynamic-slice_bitcast_fusion.refs_0_) | copy-start | bytes 124

commit v7 on v6

--- a/solution.py
+++ b/solution.py
@@ -236,23 +236,23 @@
     gate_mid = send(gate, MIDDLE, near, mid, far)
     up_mid = send(up, MIDDLE, near, mid, far)
     down_mid = send(down, MIDDLE, gate_mid)
-    gate_inner = send(gate, INWARD, near, far)
-    up_inner = send(up, INWARD, gate_inner)
+    gate_inner = send(gate, INWARD, near, far, gate_end, up_end)
+    up_inner = send(up, INWARD, gate_inner, down_end)
     down_inner = send(down, INWARD, up_inner)
-    own, near, mid, far = lax.optimization_barrier((*pieces, gate_mid, gate_inner, down_end))[:4]
-    near = send(near, OUTWARD)
+    own, near, mid, far = lax.optimization_barrier((*pieces, gate_inner))[:4]
     mid = send(mid, MIDDLE)
     far = send(far, [(2, 0), (1, 3)])
+    up_far = send(up_mid, OUTWARD, own)
+    near = send(near, OUTWARD, up_far)
     gate_mid_near = send(gate_inner, MIDDLE)
-    gate_far = send(gate_mid, OUTWARD)
-    up_far = send(up_mid, OUTWARD)
+    gate_far = send(gate_mid, OUTWARD, own)
     up_mid_near = send(up_inner, MIDDLE, gate_far)
     down_mid_near = send(down_inner, MIDDLE, up_far)
     gate_far_near = send(gate_mid_near, OUTWARD)
     up_far_near = send(up_mid_near, OUTWARD, gate_far_near)
     down_far = send(down_mid, OUTWARD, gate_far_near)
     down_far_near = send(down_mid_near, OUTWARD, up_far_near)
-    norm_after = (down_mid, gate_mid_near, gate_far, up_far)
+    norm_after = (down_mid, gate_mid_near, gate_far)
     up_after = (down_mid_near,)
     gate_in = [
         [gate],
@@ -374,30 +374,42 @@
     return pl.ds(pl.multiple_of(place_ref[COLS + slot] * part, part), part)
 
 
-def up_kernel(shape, place_ref, x_ref, *refs):
+def gate_kernel(shape, place_ref, x_ref, *refs):
     slots = len(shape)
     gate_in, refs = regroup(refs, shape)
-    up_in, refs = regroup(refs, shape)
-    hidden_ref, to_gate_ref, to_up_ref, gate_w, up_w, sems = refs
-    part = gate_w.shape[2]
+    o_ref, gate_w, sems = refs
     inner = place_ref[INNER]
     for j in range(slots):
-        fetch(inner, gate_in[j], gate_w.at[j], sems.at[0, j])
-        fetch(inner, up_in[j], up_w.at[j], sems.at[1, j])
-    gate = up = None
+        fetch(inner, gate_in[j], gate_w.at[j], sems.at[j])
+    o_ref[...] = by_slots(place_ref, x_ref, gate_in, gate_w, sems)
+
+
+def by_slots(place_ref, x_ref, weight_in, weight, sems):
+    slots, _, part = weight.shape
+    total = None
     for j in range(slots):
         rows = x_ref[:, cols_of(place_ref, j, part)]
-        arrived(gate_in[j], gate_w.at[j], sems.at[0, j])
-        term = mm(rows, gate_w[j], NT)
-        gate = term if gate is None else gate + term
-        arrived(up_in[j], up_w.at[j], sems.at[1, j])
-        term = mm(rows, up_w[j], NT)
-        up = term if up is None else up + term
+        arrived(weight_in[j], weight.at[j], sems.at[j])
+        term = mm(rows, weight[j], NT)
+        total = term if total is None else total + term
+    return total
+
+
+def up_kernel(shape, place_ref, x_ref, gate_ref, *refs):
+    slots = len(shape)
+    up_in, refs = regroup(refs, shape)
+    hidden_ref, to_gate_ref, to_up_ref, up_w, sems = refs
+    inner = place_ref[INNER]
+    for j in range(slots):
+        fetch(inner, up_in[j], up_w.at[j], sems.at[j])
+    gate = gate_ref[...]
     sigma = 1.0 / (1.0 + jnp.exp(-gate))
     silu = gate * sigma
-    hidden_ref[...] = (silu * up).astype(BF)
-    to_gate_ref[...] = up * sigma * (1.0 + gate * (1.0 - sigma))
     to_up_ref[...] = silu
+    to_gate_ref[...] = sigma * (1.0 + gate * (1.0 - sigma))
+    up = by_slots(place_ref, x_ref, up_in, up_w, sems)
+    hidden_ref[...] = (to_up_ref[...] * up).astype(BF)
+    to_gate_ref[...] = up * to_gate_ref[...]
 
 
 def down_kernel(shape, place_ref, hidden_ref, cot_ref, *refs):
@@ -615,16 +627,24 @@
     rows = exchange(send_rows, owners, "exp")
 
     full_w = pltpu.VMEM((groups, ffw, part), BF)
+    gate_pre = call(
+        functools.partial(gate_kernel, shape),
+        sds((total, ffw), F32),
+        (place, rows, *flat(gate_in)),
+        [SMEM, VMEM] + [HBM] * sum(shape),
+        [full_w, pltpu.SemaphoreType.DMA((groups,))],
+        flops=one,
+        moved=2 * width * ffw + 2 * total * width + 4 * total * ffw,
+    )
     hidden, to_gate, to_up = call(
         functools.partial(up_kernel, shape),
         (sds((total, ffw)), sds((total, ffw), F32), sds((total, ffw), F32)),
-        (place, rows, *flat(gate_in), *flat(up_in)),
-        [SMEM, VMEM] + [HBM] * (2 * sum(shape)),
-        [full_w, full_w, pltpu.SemaphoreType.DMA((2, groups))],
-        flops=2 * one,
-        moved=4 * width * ffw + 2 * total * width + 10 * total * ffw,
+        (place, rows, gate_pre, *flat(up_in)),
+        [SMEM, VMEM, VMEM] + [HBM] * sum(shape),
+        [full_w, pltpu.SemaphoreType.DMA((groups,))],
+        flops=one,
+        moved=2 * width * ffw + 2 * total * width + 14 * total * ffw,
         after=up_after,
-
     )
     out_first, d_hidden = call(
         functools.partial(down_kernel, shape[:-1]),

time: 238 us -> 236 us (level)
  waiting for transfers between devices: 107 us -> 99.9 us
  Pallas kernels: 35.6 us -> 38.7 us
    ppermute x24, waiting for transfers between devices: 101 us -> 84.6 us  [send(): return lax.ppermute(gated(array, *first), 'seq', pairs)]
    all_to_all x3, waiting for transfers between devices: 5.48 us -> 15.3 us  [exchange(): rows = lax.all_to_all(rows, axis, split_axis=0, concat_axis=0, tiled=True)]
    pallas_call x8 -> x9, Pallas kernels: 35.6 us -> 38.7 us  [call(): pl.pallas_call(body, grid=() if held else (1,), out_shape=outs, in_specs=...]
    unnamed x44 -> x48, local copies, waits for them, and re-layouts: 4.79 us -> 4.89 us
  transfers between devices with their start and end apart: 27 -> 27, of which waited for: 13 -> 11; matrix products, arithmetic and copies ran while one was open for 1% -> 1% of each run, Pallas kernels for 13% -> 14%
where the time goes in v7:
time: 236 us; the launch traced here: 235 us
  waiting for transfers between devices  99.9 us (42%)
  starting transfers between devices  63.2 us (27%)
  Pallas kernels  38.7 us (16%)
  blocking collectives  25.3 us (11%)
  local copies, waits for them, and re-layouts  6.79 us (3%)
    ppermute x24, waiting for transfers between devices, send(): return lax.ppermute(gated(array, *first), 'seq', pairs)  84.6 us
    ppermute x24, starting transfers between devices, send(): return lax.ppermute(gated(array, *first), 'seq', pairs)  51.4 us
    pallas_call x9, Pallas kernels, call(): pl.pallas_call(body, grid=() if held else (1,), out_shape=outs, in_specs=...  38.7 us
    all_to_all x1, blocking collectives, exchange(): rows = lax.all_to_all(rows, axis, split_axis=0, concat_axis=0, tiled=True)  25.3 us
    all_to_all x3, waiting for transfers between devices, exchange(): rows = lax.all_to_all(rows, axis, split_axis=0, concat_axis=0, tiled=True)  15.3 us
    all_to_all x3, starting transfers between devices, exchange(): rows = lax.all_to_all(rows, axis, split_axis=0, concat_axis=0, tiled=True)  11.8 us
    unnamed x48, local copies, waits for them, and re-layouts  4.89 us
  transfers between devices with their start and end apart: 27, of which 11 were waited for; matrix products, arithmetic and copies ran while one was open for 1% of the time, Pallas kernels for 14%

profile of v7, /device:TPU:0, one launch (start us, length us, event | category | flops | bytes accessed | tf_op | source)
XLA Modules:
  0.0 235.0 jit_solution(12689876292264640290)
XLA Ops:
  0.7 1.3 dynamic-slice_bitcast_fusion.refs_0_
  2.0 2.6 %shard_map.131 = (bf16[384,1024]{1,0:T(8,128)(2,1)}, bf16[384,1024]{1,0:T(8,128)(2,1)}) custom-call(s32[10]{0:T(128)} %dynamic-slice_bitcast_fusion.refs_0_, bf16[128,2048]{1,0:T(8,128)(2,1)} %bitcast.53, bf16[128,2048]{1,0:T(8,128)(2,1)} %bitcast.54, bf16[128,2048]{1,0:T(8,128)(2,1)} %bitcast.55), custom_call_target="tpu_custom_call" | custom-call | bytes 3145728 | tf_op jit(solution)/shard_map/pallas_call | solution.py:35
  4.6 5.8 %collective-permute-start = (bf16[384,1024]{1,0:T(8,128)(2,1)}, bf16[384,1024]{1,0:T(8,128)(2,1)}, u32[]{:S(2)}, u32[]{:S(2)}) collective-permute-start(bf16[384,1024]{1,0:T(8,128)(2,1)} %get-tuple-element.36.refs_1_), channel_id=1, source_target_pairs={{0,8},{24,16},{1,9},{25,17},{2,10},{26,18},{3,11},{27,19},{4,12},{... | collective-permute-start | bytes 2359304 | tf_op jit(solution)/shard_map/ppermute | solution.py:534
  10.4 2.4 %collective-permute-start.2 = (bf16[384,1024]{1,0:T(8,128)(2,1)}, bf16[384,1024]{1,0:T(8,128)(2,1)}, u32[]{:S(2)}, u32[]{:S(2)}) collective-permute-start(bf16[384,1024]{1,0:T(8,128)(2,1)} %get-tuple-element.37), channel_id=1, source_target_pairs={{0,16},{24,8},{1,17},{25,9},{2,18},{26,10},{3,19},{27,11},{4,20},{... | collective-permute-start | bytes 2359304 | tf_op jit(solution)/shard_map/ppermute | solution.py:534
  12.8 1.5 collective-permute-start.1
  14.3 1.3 collective-permute-start.3
  15.6 1.3 collective-permute-start.4
  18.4 3.2 %shard_map.132 = bf16[320,2048]{1,0:T(8,128)(2,1)} custom-call(s32[2,128]{1,0:T(2,128)} %copy.17.refs_0_.refs_1_, f32[128,2]{1,0:T(8,128)} %bitcast.33, bf16[128,2048]{1,0:T(8,128)(2,1)} %bitcast.31), custom_call_target="tpu_custom_call" | custom-call | flops 335544320 | bytes 1835008 | tf_op jit(solution)/shard_map/pallas_call | solution.py:35
  21.6 3.7 %all-to-all-start = ((bf16[8,40,2048]{2,1,0:T(8,128)(2,1)}), bf16[8,40,2048]{2,1,0:T(8,128)(2,1)S(1)}, u32[]{:S(2)}, u32[]{:S(2)}) async-start(bf16[8,40,2048]{2,1,0:T(8,128)(2,1)} %bitcast.45), calls=%async_computation | async-start | bytes 2621440 | tf_op jit(solution)/shard_map/all_to_all | solution.py:556
  25.3 10.0 %collective-permute-done.3.refs_5_.refs_4_.refs_10_ = bf16[704,512]{1,0:T(8,128)(2,1)S(1)} collective-permute-done((bf16[704,512]{1,0:T(8,128)(2,1)S(1)}, bf16[704,512]{1,0:T(8,128)(2,1)S(1)}, u32[]{:S(2)}, u32[]{:S(2)}) %collective-permute-start.3) | collective-permute-done | bytes 720928 | tf_op jit(solution)/shard_map/ppermute | solution.py:534
  35.3 14.0 %collective-permute-done.4.refs_6_.refs_5_.refs_17_ = bf16[704,512]{1,0:T(8,128)(2,1)S(1)} collective-permute-done((bf16[704,512]{1,0:T(8,128)(2,1)}, bf16[704,512]{1,0:T(8,128)(2,1)S(1)}, u32[]{:S(2)}, u32[]{:S(2)}) %collective-permute-start.4) | collective-permute-done | bytes 720928 | tf_op jit(solution)/shard_map/ppermute | solution.py:534
  49.3 2.4 %collective-permute-start.5 = (bf16[704,512]{1,0:T(8,128)(2,1)S(1)}, bf16[704,512]{1,0:T(8,128)(2,1)}, u32[]{:S(2)}, u32[]{:S(2)}) collective-permute-start(bf16[704,512]{1,0:T(8,128)(2,1)S(1)} %bitcast.49), channel_id=1, source_target_pairs={{0,8},{24,16},{1,9},{25,17},{2,10},{26,18},{3,11},{27,19},{4,12},{... | collective-permute-start | bytes 2162696 | tf_op jit(solution)/shard_map/ppermute | solution.py:534
  51.7 1.5 collective-permute-start.6
  53.2 1.5 collective-permute-start.11
  54.7 1.3 collective-permute-start.16
  56.1 1.1 copy-done.5
  57.1 1.7 shard_map.133
  58.8 6.2 %collective-permute-done.5.refs_3_.refs_9_ = bf16[704,512]{1,0:T(8,128)(2,1)} collective-permute-done((bf16[704,512]{1,0:T(8,128)(2,1)S(1)}, bf16[704,512]{1,0:T(8,128)(2,1)}, u32[]{:S(2)}, u32[]{:S(2)}) %collective-permute-start.5) | collective-permute-done | bytes 720928 | tf_op jit(solution)/shard_map/ppermute | solution.py:534
  65.0 1.3 collective-permute-start.7
  66.3 1.3 collective-permute-start.14
  67.6 5.7 %collective-permute-done.16.refs_5_ = bf16[704,512]{1,0:T(8,128)(2,1)} collective-permute-done((bf16[704,512]{1,0:T(8,128)(2,1)}, bf16[704,512]{1,0:T(8,128)(2,1)}, u32[]{:S(2)}, u32[]{:S(2)}) %collective-permute-start.16) | collective-permute-done | bytes 720928 | tf_op jit(solution)/shard_map/ppermute | solution.py:534
  73.4 14.5 %collective-permute-start.17 = (bf16[704,512]{1,0:T(8,128)(2,1)}, bf16[704,512]{1,0:T(8,128)(2,1)S(1)}, u32[]{:S(2)}, u32[]{:S(2)}) collective-permute-start(bf16[704,512]{1,0:T(8,128)(2,1)} %bitcast.12.refs_3_.refs_15_), channel_id=1, source_target_pairs={{0,8},{24,16},{1,9},{25,17},{2,10},{26,18},{3,11},{27,19},{4,12},{... | collective-permute-start | bytes 2162696 | tf_op jit(solution)/shard_map/ppermute | solution.py:534
  89.3 5.2 %collective-permute-done.7.refs_7_.refs_19_ = bf16[704,512]{1,0:T(8,128)(2,1)S(1)} collective-permute-done((bf16[704,512]{1,0:T(8,128)(2,1)}, bf16[704,512]{1,0:T(8,128)(2,1)S(1)}, u32[]{:S(2)}, u32[]{:S(2)}) %collective-permute-start.7) | collective-permute-done | bytes 720928 | tf_op jit(solution)/shard_map/ppermute | solution.py:534
  95.2 12.1 %collective-permute-done.14.refs_10_.refs_6_.refs_12_ = bf16[704,512]{1,0:T(8,128)(2,1)S(1)} collective-permute-done((bf16[704,512]{1,0:T(8,128)(2,1)}, bf16[704,512]{1,0:T(8,128)(2,1)S(1)}, u32[]{:S(2)}, u32[]{:S(2)}) %collective-permute-start.14) | collective-permute-done | bytes 720928 | tf_op jit(solution)/shard_map/ppermute | solution.py:534
  107.3 1.3 collective-permute-start.10
  108.6 1.3 collective-permute-start.8
  110.0 1.3 collective-permute-start.15
  111.3 1.5 collective-permute-start.18
  112.8 21.7 %collective-permute-done.10.refs_7_ = bf16[128,1024]{1,0:T(8,128)(2,1)S(1)} collective-permute-done((bf16[128,1024]{1,0:T(8,128)(2,1)}, bf16[128,1024]{1,0:T(8,128)(2,1)S(1)}, u32[]{:S(2)}, u32[]{:S(2)}) %collective-permute-start.10) | collective-permute-done | bytes 262176 | tf_op jit(solution)/shard_map/ppermute | solution.py:534
  134.5 2.4 %collective-permute-start.20 = (bf16[704,512]{1,0:T(8,128)(2,1)}, bf16[704,512]{1,0:T(8,128)(2,1)}, u32[]{:S(2)}, u32[]{:S(2)}) collective-permute-start(bf16[704,512]{1,0:T(8,128)(2,1)} %bitcast.18.refs_3_), channel_id=1, source_target_pairs={{0,8},{24,16},{1,9},{25,17},{2,10},{26,18},{3,11},{27,19},{4,12},{... | collective-permute-start | bytes 2162696 | tf_op jit(solution)/shard_map/ppermute | solution.py:534
  137.9 3.3 %shard_map.134 = (bf16[128,2048]{1,0:T(8,128)(2,1)}, bf16[320,2048]{1,0:T(8,128)(2,1)}) custom-call(s32[10]{0:T(128)} %dynamic-slice_bitcast_fusion.refs_0_, s32[2,128]{1,0:T(2,128)} %copy.17.refs_0_.refs_1_, bf16[128,2048]{1,0:T(8,128)(2,1)} %bitcast.56, f32[1,2048]{1,0:T(1,128)} %bitcast.37, bf16[128,1024]{1,0:T(8,128)(2,1)} %get-tuple-element.43.refs_4_, ...), custom_call_target="tpu_custom_call" | custom-call | flops 167772160 | bytes 2883584 | tf_op jit(solution)/shard_map/pallas_call | solution.py:35
  141.2 3.9 %all-to-all-start.1 = ((bf16[8,40,2048]{2,1,0:T(8,128)(2,1)}), bf16[8,40,2048]{2,1,0:T(8,128)(2,1)S(1)}, u32[]{:S(2)}, u32[]{:S(2)}) async-start(bf16[8,40,2048]{2,1,0:T(8,128)(2,1)} %bitcast.51), calls=%async_computation.1 | async-start | bytes 2621440 | tf_op jit(solution)/shard_map/all_to_all | solution.py:556
  145.1 1.3 collective-permute-start.19
  146.4 1.5 collective-permute-start.21
  148.0 1.3 collective-permute-start.22
  149.2 14.1 %all-to-all-done.1 = bf16[8,40,2048]{2,1,0:T(8,128)(2,1)S(1)} async-done(((bf16[8,40,2048]{2,1,0:T(8,128)(2,1)}), bf16[8,40,2048]{2,1,0:T(8,128)(2,1)S(1)}, u32[]{:S(2)}, u32[]{:S(2)}) %all-to-all-start.1) | async-done | bytes 1310752 | tf_op jit(solution)/shard_map/all_to_all | solution.py:556
  163.3 1.1 copy-done.6
  164.4 5.2 %shard_map.135.refs_2_ = f32[320,704]{1,0:T(8,128)} custom-call(s32[10]{0:T(128)} %dynamic-slice_bitcast_fusion.refs_0_, bf16[320,2048]{1,0:T(8,128)(2,1)} %bitcast.42, bf16[704,512]{1,0:T(8,128)(2,1)} %bitcast.46, bf16[704,512]{1,0:T(8,128)(2,1)} %collective-permute-done.5.refs_3_.refs_9_, bf16[704,512]{1,0:T(8,128)(2,1)} %copy-done.7, ...), custom_call_target="tpu_custom_call" | custom-call | flops 922746880 | bytes 5095424 | tf_op jit(solution)/shard_map/pallas_call | solution.py:35
  169.6 1.3 collective-permute-start.23
  170.9 6.0 %shard_map.136 = (bf16[320,704]{1,0:T(8,128)(2,1)}, f32[320,704]{1,0:T(8,128)}, f32[320,704]{1,0:T(8,128)}) custom-call(s32[10]{0:T(128)} %dynamic-slice_bitcast_fusion.refs_0_, bf16[320,2048]{1,0:T(8,128)(2,1)} %bitcast.43, f32[320,704]{1,0:T(8,128)} %shard_map.135.refs_2_, bf16[704,512]{1,0:T(8,128)(2,1)} %bitcast.12.refs_3_.refs_15_, ...), custom_call_target="tpu_custom_call" | custom-call | flops 922746880 | bytes 7348224 | tf_op jit(solution)/shard_map/pallas_call | solution.py:35
  176.9 4.8 %collective-permute-done.22.refs_7_ = bf16[704,512]{1,0:T(8,128)(2,1)} collective-permute-done((bf16[704,512]{1,0:T(8,128)(2,1)S(1)}, bf16[704,512]{1,0:T(8,128)(2,1)}, u32[]{:S(2)}, u32[]{:S(2)}) %collective-permute-start.22) | collective-permute-done | bytes 720928 | tf_op jit(solution)/shard_map/ppermute | solution.py:534
  181.7 5.9 %shard_map.137 = (bf16[320,1536]{1,0:T(8,128)(2,1)}, f32[320,704]{1,0:T(8,128)}) custom-call(s32[10]{0:T(128)} %dynamic-slice_bitcast_fusion.refs_0_, bf16[320,704]{1,0:T(8,128)(2,1)} %get-tuple-element.61.refs_1_, bf16[320,2048]{1,0:T(8,128)(2,1)} %bitcast.40, bf16[704,512]{1,0:T(8,128)(2,1)} %bitcast.18.refs_3_, ...), custom_call_target="tpu_custom_call" | custom-call | flops 1384120320 | bytes 6856704 | tf_op jit(solution)/shard_map/pallas_call | solution.py:35
  187.6 4.2 %all-to-all-start.2 = ((bf16[8,40,1536]{2,1,0:T(8,128)(2,1)}), bf16[8,40,1536]{2,1,0:T(8,128)(2,1)S(1)}, u32[]{:S(2)}, u32[]{:S(2)}) async-start(bf16[8,40,1536]{2,1,0:T(8,128)(2,1)} %bitcast.52), calls=%async_computation.2 | async-start | bytes 1966080 | tf_op jit(solution)/shard_map/all_to_all | solution.py:556
  191.9 4.8 %collective-permute-done.23.refs_7_ = bf16[704,512]{1,0:T(8,128)(2,1)S(1)} collective-permute-done((bf16[704,512]{1,0:T(8,128)(2,1)}, bf16[704,512]{1,0:T(8,128)(2,1)S(1)}, u32[]{:S(2)}, u32[]{:S(2)}) %collective-permute-start.23) | collective-permute-done | bytes 720928 | tf_op jit(solution)/shard_map/ppermute | solution.py:534
  197.5 7.8 %shard_map.138 = bf16[320,2560]{1,0:T(8,128)(2,1)} custom-call(s32[10]{0:T(128)} %dynamic-slice_bitcast_fusion.refs_0_, bf16[320,704]{1,0:T(8,128)(2,1)} %get-tuple-element.61.refs_1_, bf16[320,2048]{1,0:T(8,128)(2,1)} %bitcast.41, f32[320,704]{1,0:T(8,128)} %get-tuple-element.64.refs_3_, f32[320,704]{1,0:T(8,128)} %get-tuple-element.65.refs_4_, ...), custom_call_target="tpu_custom_call" | custom-call | flops 2306867200 | bytes 11542528 | tf_op jit(solution)/shard_map/pallas_call | solution.py:35
  205.3 1.2 all-to-all-done.2
  206.6 25.3 %all_to_all.20 = bf16[8,40,2560]{2,1,0:T(8,128)(2,1)S(1)} all-to-all(bf16[8,40,2560]{2,1,0:T(8,128)(2,1)} %bitcast.44), channel_id=1, replica_groups=mesh['seq'=4,'exp'=8] {'exp'}, dimensions={0} | all-to-all | bytes 3276800 | tf_op jit(solution)/shard_map/all_to_all | solution.py:556
  231.9 3.1 %shard_map.139 = (bf16[128,2048]{1,0:T(8,128)(2,1)}, bf16[128,2048]{1,0:T(8,128)(2,1)}) custom-call(s32[10]{0:T(128)S(1)} %copy-done.4, s32[128,2]{1,0:T(8,128)S(1)} %bitcast.36, f32[128,2]{1,0:T(8,128)S(1)} %bitcast.34, f32[1,2048]{1,0:T(1,128)S(1)} %bitcast.38, bf16[128,2048]{1,0:T(8,128)(2,1)S(1)} %copy-done.2, bf16[128,2048]{1,0:T(8,128)(2,1)S(1)} %bitcast.32, ...), custom_call_target="tpu_custom_call" | custom-call | flops 503316480 | bytes 4718592 | tf_op jit(solution)/shard_map/pallas_call | solution.py:35
  (66 shorter events, 5.5 us)
Async XLA Ops:
  0.6 13.7 %copy-start.13 = (bf16[1,512,704]{1,2,0:T(8,128)(2,1)S(1)}, bf16[1,512,704]{1,2,0:T(8,128)(2,1)}, u32[]{:S(2)}) copy-start(bf16[1,512,704]{1,2,0:T(8,128)(2,1)} %param.17) | copy-start | bytes 2162692
  0.6 16.3 %copy-start.21 = (s32[1,128,2]{1,2,0:T(2,128)S(1)}, s32[1,128,2]{1,2,0:T(2,128)}, u32[]{:S(2)}) copy-start(s32[1,128,2]{1,2,0:T(2,128)} %param.20) | copy-start | bytes 3076
  0.7 16.4 %copy-start.22 = (f32[1,128,2]{1,2,0:T(2,128)S(1)}, f32[1,128,2]{1,2,0:T(2,128)}, u32[]{:S(2)}) copy-start(f32[1,128,2]{1,2,0:T(2,128)} %param.21) | copy-start | bytes 3076
  4.6 44.7 %collective-permute-start = (bf16[384,1024]{1,0:T(8,128)(2,1)}, bf16[384,1024]{1,0:T(8,128)(2,1)}, u32[]{:S(2)}, u32[]{:S(2)}) collective-permute-start(bf16[384,1024]{1,0:T(8,128)(2,1)} %get-tuple-element.36.refs_1_), channel_id=1, source_target_pairs={{0,8},{24,16},{1,9},{25,17},{2,10},{26,18},{3,11},{27,19},{4,12},{... | collective-permute-start | bytes 2359304 | tf_op jit(solution)/shard_map/ppermute | solution.py:534
  10.4 38.9 %collective-permute-start.2 = (bf16[384,1024]{1,0:T(8,128)(2,1)}, bf16[384,1024]{1,0:T(8,128)(2,1)}, u32[]{:S(2)}, u32[]{:S(2)}) collective-permute-start(bf16[384,1024]{1,0:T(8,128)(2,1)} %get-tuple-element.37), channel_id=1, source_target_pairs={{0,16},{24,8},{1,17},{25,9},{2,18},{26,10},{3,19},{27,11},{4,20},{... | collective-permute-start | bytes 2359304 | tf_op jit(solution)/shard_map/ppermute | solution.py:534
  12.8 38.9 %collective-permute-start.1 = (bf16[384,1024]{1,0:T(8,128)(2,1)}, bf16[384,1024]{1,0:T(8,128)(2,1)}, u32[]{:S(2)}, u32[]{:S(2)}) collective-permute-start(bf16[384,1024]{1,0:T(8,128)(2,1)} %get-tuple-element.37), channel_id=1, source_target_pairs={{8,16},{16,8},{9,17},{17,9},{10,18},{18,10},{11,19},{19,11},{12,20... | collective-permute-start | bytes 2359304 | tf_op jit(solution)/shard_map/ppermute | solution.py:534
  14.3 20.9 %collective-permute-start.3 = (bf16[704,512]{1,0:T(8,128)(2,1)S(1)}, bf16[704,512]{1,0:T(8,128)(2,1)S(1)}, u32[]{:S(2)}, u32[]{:S(2)}) collective-permute-start(bf16[704,512]{1,0:T(8,128)(2,1)S(1)} %bitcast.48), channel_id=1, source_target_pairs={{8,0},{16,24},{9,1},{17,25},{10,2},{18,26},{11,3},{19,27},{12,4},{... | collective-permute-start | bytes 2162696 | tf_op jit(solution)/shard_map/ppermute | solution.py:534
  15.6 33.6 %collective-permute-start.4 = (bf16[704,512]{1,0:T(8,128)(2,1)}, bf16[704,512]{1,0:T(8,128)(2,1)S(1)}, u32[]{:S(2)}, u32[]{:S(2)}) collective-permute-start(bf16[704,512]{1,0:T(8,128)(2,1)} %bitcast.12.refs_3_.refs_15_), channel_id=1, source_target_pairs={{8,0},{16,24},{9,1},{17,25},{10,2},{18,26},{11,3},{19,27},{12,4},{... | collective-permute-start | bytes 2162696 | tf_op jit(solution)/shard_map/ppermute | solution.py:534
  21.6 34.5 %all-to-all-start = ((bf16[8,40,2048]{2,1,0:T(8,128)(2,1)}), bf16[8,40,2048]{2,1,0:T(8,128)(2,1)S(1)}, u32[]{:S(2)}, u32[]{:S(2)}) async-start(bf16[8,40,2048]{2,1,0:T(8,128)(2,1)} %bitcast.45), calls=%async_computation | async-start | bytes 2621440 | tf_op jit(solution)/shard_map/all_to_all | solution.py:556
  35.3 20.8 %copy-start.7 = (bf16[704,512]{1,0:T(8,128)(2,1)}, bf16[704,512]{1,0:T(8,128)(2,1)S(1)}, u32[]{:S(2)}) copy-start(bf16[704,512]{1,0:T(8,128)(2,1)S(1)} %collective-permute-done.3.refs_5_.refs_4_.refs_10_) | copy-start | bytes 2162692
  49.3 6.8 %copy-start.8 = (bf16[704,512]{1,0:T(8,128)(2,1)}, bf16[704,512]{1,0:T(8,128)(2,1)S(1)}, u32[]{:S(2)}) copy-start(bf16[704,512]{1,0:T(8,128)(2,1)S(1)} %collective-permute-done.4.refs_6_.refs_5_.refs_17_) | copy-start | bytes 2162692
  49.3 15.8 %collective-permute-start.5 = (bf16[704,512]{1,0:T(8,128)(2,1)S(1)}, bf16[704,512]{1,0:T(8,128)(2,1)}, u32[]{:S(2)}, u32[]{:S(2)}) collective-permute-start(bf16[704,512]{1,0:T(8,128)(2,1)S(1)} %bitcast.49), channel_id=1, source_target_pairs={{0,8},{24,16},{1,9},{25,17},{2,10},{26,18},{3,11},{27,19},{4,12},{... | collective-permute-start | bytes 2162696 | tf_op jit(solution)/shard_map/ppermute | solution.py:534
  51.7 13.3 %collective-permute-start.6 = (bf16[704,512]{1,0:T(8,128)(2,1)}, bf16[704,512]{1,0:T(8,128)(2,1)}, u32[]{:S(2)}, u32[]{:S(2)}) collective-permute-start(bf16[704,512]{1,0:T(8,128)(2,1)} %bitcast.12.refs_3_.refs_15_), channel_id=1, source_target_pairs={{8,16},{16,8},{9,17},{17,9},{10,18},{18,10},{11,19},{19,11},{12,20... | collective-permute-start | bytes 2162696 | tf_op jit(solution)/shard_map/ppermute | solution.py:534
  53.2 13.1 %collective-permute-start.11 = (bf16[704,512]{1,0:T(8,128)(2,1)S(1)}, bf16[704,512]{1,0:T(8,128)(2,1)}, u32[]{:S(2)}, u32[]{:S(2)}) collective-permute-start(bf16[704,512]{1,0:T(8,128)(2,1)S(1)} %bitcast.50), channel_id=1, source_target_pairs={{8,16},{16,8},{9,17},{17,9},{10,18},{18,10},{11,19},{19,11},{12,20... | collective-permute-start | bytes 2162696 | tf_op jit(solution)/shard_map/ppermute | solution.py:534
  54.7 18.6 %collective-permute-start.16 = (bf16[704,512]{1,0:T(8,128)(2,1)}, bf16[704,512]{1,0:T(8,128)(2,1)}, u32[]{:S(2)}, u32[]{:S(2)}) collective-permute-start(bf16[704,512]{1,0:T(8,128)(2,1)} %bitcast.18.refs_3_), channel_id=1, source_target_pairs={{8,0},{16,24},{9,1},{17,25},{10,2},{18,26},{11,3},{19,27},{12,4},{... | collective-permute-start | bytes 2162696 | tf_op jit(solution)/shard_map/ppermute | solution.py:534
  56.0 1.1 copy-start.5
  65.0 29.5 %collective-permute-start.7 = (bf16[704,512]{1,0:T(8,128)(2,1)}, bf16[704,512]{1,0:T(8,128)(2,1)S(1)}, u32[]{:S(2)}, u32[]{:S(2)}) collective-permute-start(bf16[704,512]{1,0:T(8,128)(2,1)} %collective-permute-done.6.refs_6_.refs_18_), channel_id=1, source_target_pairs={{8,0},{16,24},{9,1},{17,25},{10,2},{18,26},{11,3},{19,27},{12,4},{... | collective-permute-start | bytes 2162696 | tf_op jit(solution)/shard_map/ppermute | solution.py:534
  66.3 41.0 %collective-permute-start.14 = (bf16[704,512]{1,0:T(8,128)(2,1)}, bf16[704,512]{1,0:T(8,128)(2,1)S(1)}, u32[]{:S(2)}, u32[]{:S(2)}) collective-permute-start(bf16[704,512]{1,0:T(8,128)(2,1)} %collective-permute-done.11.refs_5_.refs_11_), channel_id=1, source_target_pairs={{8,0},{16,24},{9,1},{17,25},{10,2},{18,26},{11,3},{19,27},{12,4},{... | collective-permute-start | bytes 2162696 | tf_op jit(solution)/shard_map/ppermute | solution.py:534
  73.4 35.3 %collective-permute-start.17 = (bf16[704,512]{1,0:T(8,128)(2,1)}, bf16[704,512]{1,0:T(8,128)(2,1)S(1)}, u32[]{:S(2)}, u32[]{:S(2)}) collective-permute-start(bf16[704,512]{1,0:T(8,128)(2,1)} %bitcast.12.refs_3_.refs_15_), channel_id=1, source_target_pairs={{0,8},{24,16},{1,9},{25,17},{2,10},{26,18},{3,11},{27,19},{4,12},{... | collective-permute-start | bytes 2162696 | tf_op jit(solution)/shard_map/ppermute | solution.py:534
  87.9 22.1 %collective-permute-start.13 = (bf16[704,512]{1,0:T(8,128)(2,1)}, bf16[704,512]{1,0:T(8,128)(2,1)S(1)}, u32[]{:S(2)}, u32[]{:S(2)}) collective-permute-start(bf16[704,512]{1,0:T(8,128)(2,1)} %collective-permute-done.5.refs_3_.refs_9_), channel_id=1, source_target_pairs={{8,16},{16,8},{9,17},{17,9},{10,18},{18,10},{11,19},{19,11},{12,20... | collective-permute-start | bytes 2162696 | tf_op jit(solution)/shard_map/ppermute | solution.py:534
  88.6 48.3 %collective-permute-start.12 = (bf16[704,512]{1,0:T(8,128)(2,1)}, bf16[704,512]{1,0:T(8,128)(2,1)S(1)}, u32[]{:S(2)}, u32[]{:S(2)}) collective-permute-start(bf16[704,512]{1,0:T(8,128)(2,1)} %bitcast.18.refs_3_), channel_id=1, source_target_pairs={{8,16},{16,8},{9,17},{17,9},{10,18},{18,10},{11,19},{19,11},{12,20... | collective-permute-start | bytes 2162696 | tf_op jit(solution)/shard_map/ppermute | solution.py:534
  94.5 46.7 %copy-start.14 = (bf16[704,512]{1,0:T(8,128)(2,1)}, bf16[704,512]{1,0:T(8,128)(2,1)S(1)}, u32[]{:S(2)}) copy-start(bf16[704,512]{1,0:T(8,128)(2,1)S(1)} %collective-permute-done.7.refs_7_.refs_19_) | copy-start | bytes 2162692
  94.5 16.7 %collective-permute-start.9 = (bf16[128,1024]{1,0:T(8,128)(2,1)}, bf16[128,1024]{1,0:T(8,128)(2,1)S(1)}, u32[]{:S(2)}, u32[]{:S(2)}) collective-permute-start(bf16[128,1024]{1,0:T(8,128)(2,1)} %get-tuple-element.48), channel_id=1, source_target_pairs={{8,16},{16,8},{9,17},{17,9},{10,18},{18,10},{11,19},{19,11},{12,20... | collective-permute-start | bytes 786440 | tf_op jit(solution)/shard_map/ppermute | solution.py:534
  107.3 29.6 %copy-start.9 = (bf16[704,512]{1,0:T(8,128)(2,1)}, bf16[704,512]{1,0:T(8,128)(2,1)S(1)}, u32[]{:S(2)}) copy-start(bf16[704,512]{1,0:T(8,128)(2,1)S(1)} %collective-permute-done.14.refs_10_.refs_6_.refs_12_) | copy-start | bytes 2162692
  107.3 27.2 %collective-permute-start.10 = (bf16[128,1024]{1,0:T(8,128)(2,1)}, bf16[128,1024]{1,0:T(8,128)(2,1)S(1)}, u32[]{:S(2)}, u32[]{:S(2)}) collective-permute-start(bf16[128,1024]{1,0:T(8,128)(2,1)} %get-tuple-element.49), channel_id=1, source_target_pairs={{16,0},{8,24},{17,1},{9,25},{18,2},{10,26},{19,3},{11,27},{20,4},{... | collective-permute-start | bytes 786440 | tf_op jit(solution)/shard_map/ppermute | solution.py:534
  108.6 61.0 %copy-start.15 = (bf16[704,512]{1,0:T(8,128)(2,1)}, bf16[704,512]{1,0:T(8,128)(2,1)S(1)}, u32[]{:S(2)}) copy-start(bf16[704,512]{1,0:T(8,128)(2,1)S(1)} %collective-permute-done.17.refs_4_.refs_16_) | copy-start | bytes 2162692
  108.6 28.3 %collective-permute-start.8 = (bf16[128,1024]{1,0:T(8,128)(2,1)}, bf16[128,1024]{1,0:T(8,128)(2,1)S(1)}, u32[]{:S(2)}, u32[]{:S(2)}) collective-permute-start(bf16[128,1024]{1,0:T(8,128)(2,1)} %get-tuple-element.47), channel_id=1, source_target_pairs={{8,0},{16,24},{9,1},{17,25},{10,2},{18,26},{11,3},{19,27},{12,4},{... | collective-permute-start | bytes 786440 | tf_op jit(solution)/shard_map/ppermute | solution.py:534
  109.9 27.0 %copy-start.10 = (bf16[704,512]{1,0:T(8,128)(2,1)}, bf16[704,512]{1,0:T(8,128)(2,1)S(1)}, u32[]{:S(2)}) copy-start(bf16[704,512]{1,0:T(8,128)(2,1)S(1)} %collective-permute-done.13.refs_9_.refs_7_.refs_13_) | copy-start | bytes 2162692
  110.0 35.1 %collective-permute-start.15 = (bf16[704,512]{1,0:T(8,128)(2,1)S(1)}, bf16[704,512]{1,0:T(8,128)(2,1)}, u32[]{:S(2)}, u32[]{:S(2)}) collective-permute-start(bf16[704,512]{1,0:T(8,128)(2,1)S(1)} %collective-permute-done.13.refs_9_.refs_7_.refs_13_), channel_id=1, source_target_pairs={{8,0},{16,24},{9,1},{17,25},{10,2},{18,26},{11,3},{19,27},{12,4},{... | collective-permute-start | bytes 2162696 | tf_op jit(solution)/shard_map/ppermute | solution.py:534
  111.3 25.7 %copy-start.18 = (bf16[128,1024]{1,0:T(8,128)(2,1)}, bf16[128,1024]{1,0:T(8,128)(2,1)S(1)}, u32[]{:S(2)}) copy-start(bf16[128,1024]{1,0:T(8,128)(2,1)S(1)} %collective-permute-done.9.refs_6_) | copy-start | bytes 786436
  111.3 33.8 %collective-permute-start.18 = (bf16[704,512]{1,0:T(8,128)(2,1)S(1)}, bf16[704,512]{1,0:T(8,128)(2,1)}, u32[]{:S(2)}, u32[]{:S(2)}) collective-permute-start(bf16[704,512]{1,0:T(8,128)(2,1)S(1)} %collective-permute-done.17.refs_4_.refs_16_), channel_id=1, source_target_pairs={{8,16},{16,8},{9,17},{17,9},{10,18},{18,10},{11,19},{19,11},{12,20... | collective-permute-start | bytes 2162696 | tf_op jit(solution)/shard_map/ppermute | solution.py:534
  134.5 2.5 %copy-start.19 = (bf16[128,1024]{1,0:T(8,128)(2,1)}, bf16[128,1024]{1,0:T(8,128)(2,1)S(1)}, u32[]{:S(2)}) copy-start(bf16[128,1024]{1,0:T(8,128)(2,1)S(1)} %collective-permute-done.10.refs_7_) | copy-start | bytes 786436
  134.5 11.9 %collective-permute-start.20 = (bf16[704,512]{1,0:T(8,128)(2,1)}, bf16[704,512]{1,0:T(8,128)(2,1)}, u32[]{:S(2)}, u32[]{:S(2)}) collective-permute-start(bf16[704,512]{1,0:T(8,128)(2,1)} %bitcast.18.refs_3_), channel_id=1, source_target_pairs={{0,8},{24,16},{1,9},{25,17},{2,10},{26,18},{3,11},{27,19},{4,12},{... | collective-permute-start | bytes 2162696 | tf_op jit(solution)/shard_map/ppermute | solution.py:534
  136.9 1.0 copy-start.20
  141.2 6.7 %copy-start.12 = (bf16[704,512]{1,0:T(8,128)(2,1)S(1)}, bf16[704,512]{1,0:T(8,128)(2,1)}, u32[]{:S(2)}) copy-start(bf16[704,512]{1,0:T(8,128)(2,1)} %copy-done.11) | copy-start | bytes 2162692
  141.2 22.1 %all-to-all-start.1 = ((bf16[8,40,2048]{2,1,0:T(8,128)(2,1)}), bf16[8,40,2048]{2,1,0:T(8,128)(2,1)S(1)}, u32[]{:S(2)}, u32[]{:S(2)}) async-start(bf16[8,40,2048]{2,1,0:T(8,128)(2,1)} %bitcast.51), calls=%async_computation.1 | async-start | bytes 2621440 | tf_op jit(solution)/shard_map/all_to_all | solution.py:556
  145.1 24.5 %collective-permute-start.19 = (bf16[704,512]{1,0:T(8,128)(2,1)}, bf16[704,512]{1,0:T(8,128)(2,1)S(1)}, u32[]{:S(2)}, u32[]{:S(2)}) collective-permute-start(bf16[704,512]{1,0:T(8,128)(2,1)} %collective-permute-done.18.refs_8_.refs_20_), channel_id=1, source_target_pairs={{8,0},{16,24},{9,1},{17,25},{10,2},{18,26},{11,3},{19,27},{12,4},{... | collective-permute-start | bytes 2162696 | tf_op jit(solution)/shard_map/ppermute | solution.py:534
  146.4 23.2 %collective-permute-start.21 = (bf16[704,512]{1,0:T(8,128)(2,1)}, bf16[704,512]{1,0:T(8,128)(2,1)}, u32[]{:S(2)}, u32[]{:S(2)}) collective-permute-start(bf16[704,512]{1,0:T(8,128)(2,1)} %collective-permute-done.20.refs_4_), channel_id=1, source_target_pairs={{8,16},{16,8},{9,17},{17,9},{10,18},{18,10},{11,19},{19,11},{12,20... | collective-permute-start | bytes 2162696 | tf_op jit(solution)/shard_map/ppermute | solution.py:534
  148.0 33.7 %collective-permute-start.22 = (bf16[704,512]{1,0:T(8,128)(2,1)S(1)}, bf16[704,512]{1,0:T(8,128)(2,1)}, u32[]{:S(2)}, u32[]{:S(2)}) collective-permute-start(bf16[704,512]{1,0:T(8,128)(2,1)S(1)} %copy-done.12), channel_id=1, source_target_pairs={{8,0},{16,24},{9,1},{17,25},{10,2},{18,26},{11,3},{19,27},{12,4},{... | collective-permute-start | bytes 2162696 | tf_op jit(solution)/shard_map/ppermute | solution.py:534
  163.3 1.1 copy-start.6
  169.6 1.3 copy-start.16
  169.6 27.0 %collective-permute-start.23 = (bf16[704,512]{1,0:T(8,128)(2,1)}, bf16[704,512]{1,0:T(8,128)(2,1)S(1)}, u32[]{:S(2)}, u32[]{:S(2)}) collective-permute-start(bf16[704,512]{1,0:T(8,128)(2,1)} %collective-permute-done.21.refs_10_.refs_6_), channel_id=1, source_target_pairs={{8,0},{16,24},{9,1},{17,25},{10,2},{18,26},{11,3},{19,27},{12,4},{... | collective-permute-start | bytes 2162696 | tf_op jit(solution)/shard_map/ppermute | solution.py:534
  187.6 19.0 %all-to-all-start.2 = ((bf16[8,40,1536]{2,1,0:T(8,128)(2,1)}), bf16[8,40,1536]{2,1,0:T(8,128)(2,1)S(1)}, u32[]{:S(2)}, u32[]{:S(2)}) async-start(bf16[8,40,1536]{2,1,0:T(8,128)(2,1)} %bitcast.52), calls=%async_computation.2 | async-start | bytes 1966080 | tf_op jit(solution)/shard_map/all_to_all | solution.py:556
  206.6 25.3 %copy-start = (bf16[1,128,2048]{2,1,0:T(8,128)(2,1)S(1)}, bf16[1,128,2048]{2,1,0:T(8,128)(2,1)}, u32[]{:S(2)}) copy-start(bf16[1,128,2048]{2,1,0:T(8,128)(2,1)} %param.22) | copy-start | bytes 1572868
  206.6 25.3 %copy-start.1 = (f32[1,128,2]{2,1,0:T(8,128)S(1)}, f32[1,128,2]{2,1,0:T(8,128)}, u32[]{:S(2)}) copy-start(f32[1,128,2]{2,1,0:T(8,128)} %copy.15) | copy-start | bytes 3076
  206.6 25.3 %copy-start.2 = (bf16[128,2048]{1,0:T(8,128)(2,1)S(1)}, bf16[128,2048]{1,0:T(8,128)(2,1)}, u32[]{:S(2)}) copy-start(bf16[128,2048]{1,0:T(8,128)(2,1)} %get-tuple-element.53.refs_4_) | copy-start | bytes 1572868
  206.6 25.3 %copy-start.3 = (f32[2048]{0:T(1024)S(1)}, f32[2048]{0:T(1024)}, u32[]{:S(2)}) copy-start(f32[2048]{0:T(1024)} %param.16) | copy-start | bytes 24580
  206.6 25.3 %copy-start.4 = (s32[10]{0:T(128)S(1)}, s32[10]{0:T(128)}, u32[]{:S(2)}) copy-start(s32[10]{0:T(128)} %dynamic-slice_bitcast_fusion.refs_0_) | copy-start | bytes 124
  (2 other events, 1.8 us)

commit v8 on v7

--- a/solution.py
+++ b/solution.py
@@ -81,47 +81,39 @@
     )(q, k, v)
 
 
-def attend_head(blocks, query_of, keys, vals, store):
-    rows = keys.shape[0] // blocks
+def attend_head(query, keys, vals, store):
+    length = keys.shape[0]
+    block = min(512, length)
     scale = HD ** (-0.5)
-    row_ids = lax.broadcasted_iota(jnp.int32, (rows, rows), 0)
-    col_ids = lax.broadcasted_iota(jnp.int32, (rows, rows), 1)
+    row_ids = lax.broadcasted_iota(jnp.int32, (block, block), 0)
+    col_ids = lax.broadcasted_iota(jnp.int32, (block, block), 1)
     keep = col_ids <= row_ids
-    for b in range(blocks):
-        query = query_of(b)
-        end = b * rows
-        diag = mm(query, keys[end : end + rows], NT) * scale
-        diag = jnp.where(keep, diag, -jnp.inf)
-        top = jnp.max(diag, axis=-1, keepdims=True)
-        if b:
-            early = mm(query, keys[:end], NT) * scale
-            top = jnp.maximum(top, jnp.max(early, axis=-1, keepdims=True))
-        diag = jnp.exp(diag - top)
-        total = jnp.sum(diag, axis=-1, keepdims=True)
-        if b:
-            early = jnp.exp(early - top)
-            total = total + jnp.sum(early, axis=-1, keepdims=True)
-        inverse = 1.0 / total
-        ctx = mm((diag * inverse).astype(BF), vals[end : end + rows], NN)
-        if b:
-            ctx = ctx + mm((early * inverse).astype(BF), vals[:end], NN)
-        store(b, ctx.astype(BF))
+    for start in range(0, length, block):
+        end = start + block
+        scores = mm(query[start:end], keys[:end], NT) * scale
+        diag = jnp.where(keep, scores[:, start:], -jnp.inf)
+        scores = jnp.concatenate([scores[:, :start], diag], axis=1) if start else diag
+        exps = jnp.exp(scores - jnp.max(scores, axis=-1, keepdims=True))
+        inverse = 1.0 / jnp.sum(exps, axis=-1, keepdims=True)
+        store(start, end, mm((exps * inverse).astype(BF), vals[:end], NN).astype(BF))
+
+
+def attend_columns(x_ref, cols, o_ref):
+    blocks, three, _ = x_ref.shape
+    rows = three // 3
+    query, keys, vals = [
+        x_ref[:, i * rows : (i + 1) * rows, cols].reshape(blocks * rows, HD) for i in range(3)
+    ]
+
+    def store(start, end, ctx):
+        first, last = start // rows, end // rows
+        o_ref[first:last, :, cols] = ctx.reshape(last - first, rows, HD)
+
+    attend_head(query, keys, vals, store)
 
 
 def attend_kernel(x_ref, o_ref):
-    blocks, three, hd = x_ref.shape
-    rows = three // 3
-
-    def store(b, ctx):
-        o_ref[b] = ctx
-
-    attend_head(
-        blocks,
-        lambda b: x_ref[b, 0:rows, :],
-        x_ref[:, rows : 2 * rows, :].reshape(blocks * rows, hd),
-        x_ref[:, 2 * rows : 3 * rows, :].reshape(blocks * rows, hd),
-        store,
-    )
+    attend_columns(x_ref, slice(0, HD), o_ref)
 
 
 def attend(x):
@@ -183,17 +175,7 @@
         def step(i, carry):
             for j in range(2):
                 cols = pl.ds(pl.multiple_of((2 * i + j) * HD, HD), HD)
-
-                def store(b, ctx, cols=cols):
-                    ctx_ref[b, :, cols] = ctx
-
-                attend_head(
-                    blocks,
-                    lambda b, cols=cols: x_ref[b, 0:rows, cols],
-                    x_ref[:, rows : 2 * rows, cols].reshape(blocks * rows, HD),
-                    x_ref[:, 2 * rows : 3 * rows, cols].reshape(blocks * rows, HD),
-                    store,
-                )
+                attend_columns(x_ref, cols, ctx_ref)
             return carry
 
         lax.fori_loop(0, half // HD // 2, step, 0)
@@ -235,24 +217,24 @@
     )
     gate_mid = send(gate, MIDDLE, near, mid, far)
     up_mid = send(up, MIDDLE, near, mid, far)
-    down_mid = send(down, MIDDLE, gate_mid)
     gate_inner = send(gate, INWARD, near, far, gate_end, up_end)
-    up_inner = send(up, INWARD, gate_inner, down_end)
-    down_inner = send(down, INWARD, up_inner)
-    own, near, mid, far = lax.optimization_barrier((*pieces, gate_inner))[:4]
+    up_inner = send(up, INWARD, near, far, gate_end, up_end)
+    down_inner = send(down, INWARD, gate_inner)
+    own, near, mid, far = lax.optimization_barrier((*pieces, gate_inner, up_inner, down_end))[:4]
     mid = send(mid, MIDDLE)
     far = send(far, [(2, 0), (1, 3)])
     up_far = send(up_mid, OUTWARD, own)
     near = send(near, OUTWARD, up_far)
     gate_mid_near = send(gate_inner, MIDDLE)
     gate_far = send(gate_mid, OUTWARD, own)
-    up_mid_near = send(up_inner, MIDDLE, gate_far)
-    down_mid_near = send(down_inner, MIDDLE, up_far)
+    up_mid_near = send(up_inner, MIDDLE, own)
+    down_mid = send(down, MIDDLE, gate_mid_near)
+    down_mid_near = send(down_inner, MIDDLE, up_mid_near)
     gate_far_near = send(gate_mid_near, OUTWARD)
     up_far_near = send(up_mid_near, OUTWARD, gate_far_near)
     down_far = send(down_mid, OUTWARD, gate_far_near)
     down_far_near = send(down_mid_near, OUTWARD, up_far_near)
-    norm_after = (down_mid, gate_mid_near, gate_far)
+    norm_after = (gate_mid_near, gate_far)
     up_after = (down_mid_near,)
     gate_in = [
         [gate],

time: 236 us -> 230 us (0.975)
  starting transfers between devices: 63.2 us -> 50.3 us
  waiting for transfers between devices: 99.9 us -> 107 us
    ppermute x24, starting transfers between devices: 51.4 us -> 39.1 us  [send(): return lax.ppermute(gated(array, *first), 'seq', pairs)]
    ppermute x24, waiting for transfers between devices: 84.6 us -> 91.7 us  [send(): return lax.ppermute(gated(array, *first), 'seq', pairs)]
    unnamed x48 -> x44, local copies, waits for them, and re-layouts: 4.89 us -> 4.66 us
  transfers between devices with their start and end apart: 27 -> 27, of which waited for: 11 -> 14; matrix products, arithmetic and copies ran while one was open for 1% -> 1% of each run, Pallas kernels for 14% -> 14%
where the time goes in v8:
time: 230 us; the launch traced here: 229 us
  waiting for transfers between devices  107 us (47%)
  starting transfers between devices  50.3 us (22%)
  Pallas kernels  38.8 us (17%)
  blocking collectives  25.3 us (11%)
  local copies, waits for them, and re-layouts  6.66 us (3%)
    ppermute x24, waiting for transfers between devices, send(): return lax.ppermute(gated(array, *first), 'seq', pairs)  91.7 us
    ppermute x24, starting transfers between devices, send(): return lax.ppermute(gated(array, *first), 'seq', pairs)  39.1 us
    pallas_call x9, Pallas kernels, call(): pl.pallas_call(body, grid=() if held else (1,), out_shape=outs, in_specs=...  38.8 us
    all_to_all x1, blocking collectives, exchange(): rows = lax.all_to_all(rows, axis, split_axis=0, concat_axis=0, tiled=True)  25.3 us
    all_to_all x3, waiting for transfers between devices, exchange(): rows = lax.all_to_all(rows, axis, split_axis=0, concat_axis=0, tiled=True)  15 us
    all_to_all x3, starting transfers between devices, exchange(): rows = lax.all_to_all(rows, axis, split_axis=0, concat_axis=0, tiled=True)  11.2 us
    unnamed x44, local copies, waits for them, and re-layouts  4.66 us
  transfers between devices with their start and end apart: 27, of which 14 were waited for; matrix products, arithmetic and copies ran while one was open for 1% of the time, Pallas kernels for 14%

profile of v8, /device:TPU:0, one launch (start us, length us, event | category | flops | bytes accessed | tf_op | source)
XLA Modules:
  0.0 228.8 jit_solution(14637171698984858287)
XLA Ops:
  0.7 1.3 dynamic-slice_bitcast_fusion.refs_0_
  2.0 2.6 %shard_map.131 = (bf16[384,1024]{1,0:T(8,128)(2,1)}, bf16[384,1024]{1,0:T(8,128)(2,1)}) custom-call(s32[10]{0:T(128)} %dynamic-slice_bitcast_fusion.refs_0_, bf16[128,2048]{1,0:T(8,128)(2,1)} %bitcast.53, bf16[128,2048]{1,0:T(8,128)(2,1)} %bitcast.54, bf16[128,2048]{1,0:T(8,128)(2,1)} %bitcast.55), custom_call_target="tpu_custom_call" | custom-call | bytes 3145728 | tf_op jit(solution)/shard_map/pallas_call | solution.py:35
  4.6 5.9 %collective-permute-start = (bf16[384,1024]{1,0:T(8,128)(2,1)}, bf16[384,1024]{1,0:T(8,128)(2,1)}, u32[]{:S(2)}, u32[]{:S(2)}) collective-permute-start(bf16[384,1024]{1,0:T(8,128)(2,1)} %get-tuple-element.36.refs_1_), channel_id=1, source_target_pairs={{0,8},{24,16},{1,9},{25,17},{2,10},{26,18},{3,11},{27,19},{4,12},{... | collective-permute-start | bytes 2359304 | tf_op jit(solution)/shard_map/ppermute | solution.py:516
  10.5 2.3 collective-permute-start.2
  12.8 1.6 collective-permute-start.1
  14.4 1.3 collective-permute-start.3
  15.7 1.3 collective-permute-start.4
  18.5 3.2 %shard_map.132 = bf16[320,2048]{1,0:T(8,128)(2,1)} custom-call(s32[2,128]{1,0:T(2,128)} %copy.17.refs_0_.refs_1_, f32[128,2]{1,0:T(8,128)} %bitcast.33, bf16[128,2048]{1,0:T(8,128)(2,1)} %bitcast.31), custom_call_target="tpu_custom_call" | custom-call | flops 335544320 | bytes 1835008 | tf_op jit(solution)/shard_map/pallas_call | solution.py:35
  21.7 3.7 %all-to-all-start = ((bf16[8,40,2048]{2,1,0:T(8,128)(2,1)}), bf16[8,40,2048]{2,1,0:T(8,128)(2,1)S(1)}, u32[]{:S(2)}, u32[]{:S(2)}) async-start(bf16[8,40,2048]{2,1,0:T(8,128)(2,1)} %bitcast.45), calls=%async_computation | async-start | bytes 2621440 | tf_op jit(solution)/shard_map/all_to_all | solution.py:538
  25.4 9.9 %collective-permute-done.3.refs_5_.refs_4_.refs_10_ = bf16[704,512]{1,0:T(8,128)(2,1)S(1)} collective-permute-done((bf16[704,512]{1,0:T(8,128)(2,1)S(1)}, bf16[704,512]{1,0:T(8,128)(2,1)S(1)}, u32[]{:S(2)}, u32[]{:S(2)}) %collective-permute-start.3) | collective-permute-done | bytes 720928 | tf_op jit(solution)/shard_map/ppermute | solution.py:516
  35.3 1.3 collective-permute-start.7
  36.6 14.2 %collective-permute-done.4.refs_6_.refs_5_.refs_17_ = bf16[704,512]{1,0:T(8,128)(2,1)S(1)} collective-permute-done((bf16[704,512]{1,0:T(8,128)(2,1)}, bf16[704,512]{1,0:T(8,128)(2,1)S(1)}, u32[]{:S(2)}, u32[]{:S(2)}) %collective-permute-start.4) | collective-permute-done | bytes 720928 | tf_op jit(solution)/shard_map/ppermute | solution.py:516
  50.8 2.4 %collective-permute-start.5 = (bf16[704,512]{1,0:T(8,128)(2,1)S(1)}, bf16[704,512]{1,0:T(8,128)(2,1)}, u32[]{:S(2)}, u32[]{:S(2)}) collective-permute-start(bf16[704,512]{1,0:T(8,128)(2,1)S(1)} %bitcast.49), channel_id=1, source_target_pairs={{0,8},{24,16},{1,9},{25,17},{2,10},{26,18},{3,11},{27,19},{4,12},{... | collective-permute-start | bytes 2162696 | tf_op jit(solution)/shard_map/ppermute | solution.py:516
  53.2 2.2 collective-permute-start.6
  55.4 1.5 collective-permute-start.8
  56.9 1.5 collective-permute-start.14
  59.5 1.7 shard_map.133
  61.2 3.7 %collective-permute-done.7.refs_5_ = bf16[704,512]{1,0:T(8,128)(2,1)} collective-permute-done((bf16[704,512]{1,0:T(8,128)(2,1)}, bf16[704,512]{1,0:T(8,128)(2,1)}, u32[]{:S(2)}, u32[]{:S(2)}) %collective-permute-start.7) | collective-permute-done | bytes 720928 | tf_op jit(solution)/shard_map/ppermute | solution.py:516
  64.9 4.1 %collective-permute-done.5.refs_3_.refs_9_ = bf16[704,512]{1,0:T(8,128)(2,1)} collective-permute-done((bf16[704,512]{1,0:T(8,128)(2,1)S(1)}, bf16[704,512]{1,0:T(8,128)(2,1)}, u32[]{:S(2)}, u32[]{:S(2)}) %collective-permute-start.5) | collective-permute-done | bytes 720928 | tf_op jit(solution)/shard_map/ppermute | solution.py:516
  68.9 11.7 %collective-permute-done.6.refs_4_.refs_16_ = bf16[704,512]{1,0:T(8,128)(2,1)} collective-permute-done((bf16[704,512]{1,0:T(8,128)(2,1)}, bf16[704,512]{1,0:T(8,128)(2,1)}, u32[]{:S(2)}, u32[]{:S(2)}) %collective-permute-start.6) | collective-permute-done | bytes 720928 | tf_op jit(solution)/shard_map/ppermute | solution.py:516
  80.6 1.3 collective-permute-start.9
  82.7 1.3 collective-permute-start.15
  84.6 1.3 collective-permute-start.12
  85.9 15.9 %collective-permute-done.9.refs_7_.refs_19_ = bf16[704,512]{1,0:T(8,128)(2,1)S(1)} collective-permute-done((bf16[704,512]{1,0:T(8,128)(2,1)}, bf16[704,512]{1,0:T(8,128)(2,1)S(1)}, u32[]{:S(2)}, u32[]{:S(2)}) %collective-permute-start.9) | collective-permute-done | bytes 720928 | tf_op jit(solution)/shard_map/ppermute | solution.py:516
  101.8 1.3 collective-permute-start.10
  103.8 12.6 %collective-permute-done.12.refs_7_ = bf16[128,1024]{1,0:T(8,128)(2,1)S(1)} collective-permute-done((bf16[128,1024]{1,0:T(8,128)(2,1)}, bf16[128,1024]{1,0:T(8,128)(2,1)S(1)}, u32[]{:S(2)}, u32[]{:S(2)}) %collective-permute-start.12) | collective-permute-done | bytes 262176 | tf_op jit(solution)/shard_map/ppermute | solution.py:516
  116.5 2.5 %collective-permute-start.19 = (bf16[704,512]{1,0:T(8,128)(2,1)}, bf16[704,512]{1,0:T(8,128)(2,1)}, u32[]{:S(2)}, u32[]{:S(2)}) collective-permute-start(bf16[704,512]{1,0:T(8,128)(2,1)} %bitcast.18.refs_3_), channel_id=1, source_target_pairs={{0,8},{24,16},{1,9},{25,17},{2,10},{26,18},{3,11},{27,19},{4,12},{... | collective-permute-start | bytes 2162696 | tf_op jit(solution)/shard_map/ppermute | solution.py:516
  118.9 1.3 collective-permute-start.16
  120.2 2.6 %collective-permute-done.15.refs_9_.refs_6_.refs_12_ = bf16[704,512]{1,0:T(8,128)(2,1)S(1)} collective-permute-done((bf16[704,512]{1,0:T(8,128)(2,1)}, bf16[704,512]{1,0:T(8,128)(2,1)S(1)}, u32[]{:S(2)}, u32[]{:S(2)}) %collective-permute-start.15) | collective-permute-done | bytes 720928 | tf_op jit(solution)/shard_map/ppermute | solution.py:516
  122.9 1.5 collective-permute-start.21
  124.4 4.1 %collective-permute-done.10.refs_5_ = bf16[128,1024]{1,0:T(8,128)(2,1)S(1)} collective-permute-done((bf16[128,1024]{1,0:T(8,128)(2,1)}, bf16[128,1024]{1,0:T(8,128)(2,1)S(1)}, u32[]{:S(2)}, u32[]{:S(2)}) %collective-permute-start.10) | collective-permute-done | bytes 262176 | tf_op jit(solution)/shard_map/ppermute | solution.py:516
  129.2 3.3 %shard_map.134 = (bf16[128,2048]{1,0:T(8,128)(2,1)}, bf16[320,2048]{1,0:T(8,128)(2,1)}) custom-call(s32[10]{0:T(128)} %dynamic-slice_bitcast_fusion.refs_0_, s32[2,128]{1,0:T(2,128)} %copy.17.refs_0_.refs_1_, bf16[128,2048]{1,0:T(8,128)(2,1)} %bitcast.56, f32[1,2048]{1,0:T(1,128)} %bitcast.37, bf16[128,1024]{1,0:T(8,128)(2,1)} %get-tuple-element.45.refs_4_, ...), custom_call_target="tpu_custom_call" | custom-call | flops 167772160 | bytes 2883584 | tf_op jit(solution)/shard_map/pallas_call | solution.py:35
  132.5 3.7 %all-to-all-start.1 = ((bf16[8,40,2048]{2,1,0:T(8,128)(2,1)}), bf16[8,40,2048]{2,1,0:T(8,128)(2,1)S(1)}, u32[]{:S(2)}, u32[]{:S(2)}) async-start(bf16[8,40,2048]{2,1,0:T(8,128)(2,1)} %bitcast.51), calls=%async_computation.1 | async-start | bytes 2621440 | tf_op jit(solution)/shard_map/all_to_all | solution.py:538
  136.3 1.5 collective-permute-start.20
  137.8 1.6 collective-permute-done.16.refs_8_.refs_14_
  140.7 1.3 collective-permute-start.22
  142.0 12.5 %all-to-all-done.1 = bf16[8,40,2048]{2,1,0:T(8,128)(2,1)S(1)} async-done(((bf16[8,40,2048]{2,1,0:T(8,128)(2,1)}), bf16[8,40,2048]{2,1,0:T(8,128)(2,1)S(1)}, u32[]{:S(2)}, u32[]{:S(2)}) %all-to-all-start.1) | async-done | bytes 1310752 | tf_op jit(solution)/shard_map/all_to_all | solution.py:538
  155.5 5.2 %shard_map.135.refs_2_ = f32[320,704]{1,0:T(8,128)} custom-call(s32[10]{0:T(128)} %dynamic-slice_bitcast_fusion.refs_0_, bf16[320,2048]{1,0:T(8,128)(2,1)} %bitcast.42, bf16[704,512]{1,0:T(8,128)(2,1)} %bitcast.46, bf16[704,512]{1,0:T(8,128)(2,1)} %collective-permute-done.5.refs_3_.refs_9_, bf16[704,512]{1,0:T(8,128)(2,1)} %copy-done.7, ...), custom_call_target="tpu_custom_call" | custom-call | flops 922746880 | bytes 5095424 | tf_op jit(solution)/shard_map/pallas_call | solution.py:35
  160.8 1.3 collective-permute-start.23
  162.1 6.0 %shard_map.136 = (bf16[320,704]{1,0:T(8,128)(2,1)}, f32[320,704]{1,0:T(8,128)}, f32[320,704]{1,0:T(8,128)}) custom-call(s32[10]{0:T(128)} %dynamic-slice_bitcast_fusion.refs_0_, bf16[320,2048]{1,0:T(8,128)(2,1)} %bitcast.43, f32[320,704]{1,0:T(8,128)} %shard_map.135.refs_2_, bf16[704,512]{1,0:T(8,128)(2,1)} %bitcast.12.refs_3_.refs_15_, ...), custom_call_target="tpu_custom_call" | custom-call | flops 922746880 | bytes 7348224 | tf_op jit(solution)/shard_map/pallas_call | solution.py:35
  168.1 7.8 %collective-permute-done.22.refs_7_ = bf16[704,512]{1,0:T(8,128)(2,1)} collective-permute-done((bf16[704,512]{1,0:T(8,128)(2,1)}, bf16[704,512]{1,0:T(8,128)(2,1)}, u32[]{:S(2)}, u32[]{:S(2)}) %collective-permute-start.22) | collective-permute-done | bytes 720928 | tf_op jit(solution)/shard_map/ppermute | solution.py:516
  175.9 6.0 %shard_map.137 = (bf16[320,1536]{1,0:T(8,128)(2,1)}, f32[320,704]{1,0:T(8,128)}) custom-call(s32[10]{0:T(128)} %dynamic-slice_bitcast_fusion.refs_0_, bf16[320,704]{1,0:T(8,128)(2,1)} %get-tuple-element.60.refs_1_, bf16[320,2048]{1,0:T(8,128)(2,1)} %bitcast.40, bf16[704,512]{1,0:T(8,128)(2,1)} %bitcast.18.refs_3_, ...), custom_call_target="tpu_custom_call" | custom-call | flops 1384120320 | bytes 6856704 | tf_op jit(solution)/shard_map/pallas_call | solution.py:35
  181.9 3.7 %all-to-all-start.2 = ((bf16[8,40,1536]{2,1,0:T(8,128)(2,1)}), bf16[8,40,1536]{2,1,0:T(8,128)(2,1)S(1)}, u32[]{:S(2)}, u32[]{:S(2)}) async-start(bf16[8,40,1536]{2,1,0:T(8,128)(2,1)} %bitcast.52), calls=%async_computation.2 | async-start | bytes 1966080 | tf_op jit(solution)/shard_map/all_to_all | solution.py:538
  185.7 3.5 %collective-permute-done.23.refs_7_ = bf16[704,512]{1,0:T(8,128)(2,1)S(1)} collective-permute-done((bf16[704,512]{1,0:T(8,128)(2,1)}, bf16[704,512]{1,0:T(8,128)(2,1)S(1)}, u32[]{:S(2)}, u32[]{:S(2)}) %collective-permute-start.23) | collective-permute-done | bytes 720928 | tf_op jit(solution)/shard_map/ppermute | solution.py:516
  190.0 7.8 %shard_map.138 = bf16[320,2560]{1,0:T(8,128)(2,1)} custom-call(s32[10]{0:T(128)} %dynamic-slice_bitcast_fusion.refs_0_, bf16[320,704]{1,0:T(8,128)(2,1)} %get-tuple-element.60.refs_1_, bf16[320,2048]{1,0:T(8,128)(2,1)} %bitcast.41, f32[320,704]{1,0:T(8,128)} %get-tuple-element.64.refs_3_, f32[320,704]{1,0:T(8,128)} %get-tuple-element.65.refs_4_, ...), custom_call_target="tpu_custom_call" | custom-call | flops 2306867200 | bytes 11542528 | tf_op jit(solution)/shard_map/pallas_call | solution.py:35
  197.8 2.5 %all-to-all-done.2 = bf16[8,40,1536]{2,1,0:T(8,128)(2,1)S(1)} async-done(((bf16[8,40,1536]{2,1,0:T(8,128)(2,1)}), bf16[8,40,1536]{2,1,0:T(8,128)(2,1)S(1)}, u32[]{:S(2)}, u32[]{:S(2)}) %all-to-all-start.2) | async-done | bytes 983072 | tf_op jit(solution)/shard_map/all_to_all | solution.py:538
  200.4 25.3 %all_to_all.20 = bf16[8,40,2560]{2,1,0:T(8,128)(2,1)S(1)} all-to-all(bf16[8,40,2560]{2,1,0:T(8,128)(2,1)} %bitcast.44), channel_id=1, replica_groups=mesh['seq'=4,'exp'=8] {'exp'}, dimensions={0} | all-to-all | bytes 3276800 | tf_op jit(solution)/shard_map/all_to_all | solution.py:538
  225.7 3.1 %shard_map.139 = (bf16[128,2048]{1,0:T(8,128)(2,1)}, bf16[128,2048]{1,0:T(8,128)(2,1)}) custom-call(s32[10]{0:T(128)S(1)} %copy-done.4, s32[128,2]{1,0:T(8,128)S(1)} %bitcast.36, f32[128,2]{1,0:T(8,128)S(1)} %bitcast.34, f32[1,2048]{1,0:T(1,128)S(1)} %bitcast.38, bf16[128,2048]{1,0:T(8,128)(2,1)S(1)} %copy-done.2, bf16[128,2048]{1,0:T(8,128)(2,1)S(1)} %bitcast.32, ...), custom_call_target="tpu_custom_call" | custom-call | flops 503316480 | bytes 4718592 | tf_op jit(solution)/shard_map/pallas_call | solution.py:35
  (62 shorter events, 8.7 us)
Async XLA Ops:
  0.6 13.7 %copy-start.11 = (bf16[1,512,704]{1,2,0:T(8,128)(2,1)S(1)}, bf16[1,512,704]{1,2,0:T(8,128)(2,1)}, u32[]{:S(2)}) copy-start(bf16[1,512,704]{1,2,0:T(8,128)(2,1)} %param.17) | copy-start | bytes 2162692
  0.6 16.3 %copy-start.19 = (s32[1,128,2]{1,2,0:T(2,128)S(1)}, s32[1,128,2]{1,2,0:T(2,128)}, u32[]{:S(2)}) copy-start(s32[1,128,2]{1,2,0:T(2,128)} %param.20) | copy-start | bytes 3076
  0.7 16.4 %copy-start.20 = (f32[1,128,2]{1,2,0:T(2,128)S(1)}, f32[1,128,2]{1,2,0:T(2,128)}, u32[]{:S(2)}) copy-start(f32[1,128,2]{1,2,0:T(2,128)} %param.21) | copy-start | bytes 3076
  4.6 46.1 %collective-permute-start = (bf16[384,1024]{1,0:T(8,128)(2,1)}, bf16[384,1024]{1,0:T(8,128)(2,1)}, u32[]{:S(2)}, u32[]{:S(2)}) collective-permute-start(bf16[384,1024]{1,0:T(8,128)(2,1)} %get-tuple-element.36.refs_1_), channel_id=1, source_target_pairs={{0,8},{24,16},{1,9},{25,17},{2,10},{26,18},{3,11},{27,19},{4,12},{... | collective-permute-start | bytes 2359304 | tf_op jit(solution)/shard_map/ppermute | solution.py:516
  10.5 40.3 %collective-permute-start.2 = (bf16[384,1024]{1,0:T(8,128)(2,1)}, bf16[384,1024]{1,0:T(8,128)(2,1)}, u32[]{:S(2)}, u32[]{:S(2)}) collective-permute-start(bf16[384,1024]{1,0:T(8,128)(2,1)} %get-tuple-element.37), channel_id=1, source_target_pairs={{0,16},{24,8},{1,17},{25,9},{2,18},{26,10},{3,19},{27,11},{4,20},{... | collective-permute-start | bytes 2359304 | tf_op jit(solution)/shard_map/ppermute | solution.py:516
  12.8 42.6 %collective-permute-start.1 = (bf16[384,1024]{1,0:T(8,128)(2,1)}, bf16[384,1024]{1,0:T(8,128)(2,1)}, u32[]{:S(2)}, u32[]{:S(2)}) collective-permute-start(bf16[384,1024]{1,0:T(8,128)(2,1)} %get-tuple-element.37), channel_id=1, source_target_pairs={{8,16},{16,8},{9,17},{17,9},{10,18},{18,10},{11,19},{19,11},{12,20... | collective-permute-start | bytes 2359304 | tf_op jit(solution)/shard_map/ppermute | solution.py:516
  14.4 20.9 %collective-permute-start.3 = (bf16[704,512]{1,0:T(8,128)(2,1)S(1)}, bf16[704,512]{1,0:T(8,128)(2,1)S(1)}, u32[]{:S(2)}, u32[]{:S(2)}) collective-permute-start(bf16[704,512]{1,0:T(8,128)(2,1)S(1)} %bitcast.48), channel_id=1, source_target_pairs={{8,0},{16,24},{9,1},{17,25},{10,2},{18,26},{11,3},{19,27},{12,4},{... | collective-permute-start | bytes 2162696 | tf_op jit(solution)/shard_map/ppermute | solution.py:516
  15.7 35.1 %collective-permute-start.4 = (bf16[704,512]{1,0:T(8,128)(2,1)}, bf16[704,512]{1,0:T(8,128)(2,1)S(1)}, u32[]{:S(2)}, u32[]{:S(2)}) collective-permute-start(bf16[704,512]{1,0:T(8,128)(2,1)} %bitcast.12.refs_3_.refs_15_), channel_id=1, source_target_pairs={{8,0},{16,24},{9,1},{17,25},{10,2},{18,26},{11,3},{19,27},{12,4},{... | collective-permute-start | bytes 2162696 | tf_op jit(solution)/shard_map/ppermute | solution.py:516
  21.7 36.7 %all-to-all-start = ((bf16[8,40,2048]{2,1,0:T(8,128)(2,1)}), bf16[8,40,2048]{2,1,0:T(8,128)(2,1)S(1)}, u32[]{:S(2)}, u32[]{:S(2)}) async-start(bf16[8,40,2048]{2,1,0:T(8,128)(2,1)} %bitcast.45), calls=%async_computation | async-start | bytes 2621440 | tf_op jit(solution)/shard_map/all_to_all | solution.py:538
  35.3 23.1 %copy-start.7 = (bf16[704,512]{1,0:T(8,128)(2,1)}, bf16[704,512]{1,0:T(8,128)(2,1)S(1)}, u32[]{:S(2)}) copy-start(bf16[704,512]{1,0:T(8,128)(2,1)S(1)} %collective-permute-done.3.refs_5_.refs_4_.refs_10_) | copy-start | bytes 2162692
  35.3 29.5 %collective-permute-start.7 = (bf16[704,512]{1,0:T(8,128)(2,1)}, bf16[704,512]{1,0:T(8,128)(2,1)}, u32[]{:S(2)}, u32[]{:S(2)}) collective-permute-start(bf16[704,512]{1,0:T(8,128)(2,1)} %bitcast.18.refs_3_), channel_id=1, source_target_pairs={{8,0},{16,24},{9,1},{17,25},{10,2},{18,26},{11,3},{19,27},{12,4},{... | collective-permute-start | bytes 2162696 | tf_op jit(solution)/shard_map/ppermute | solution.py:516
  50.8 7.6 %copy-start.8 = (bf16[704,512]{1,0:T(8,128)(2,1)}, bf16[704,512]{1,0:T(8,128)(2,1)S(1)}, u32[]{:S(2)}) copy-start(bf16[704,512]{1,0:T(8,128)(2,1)S(1)} %collective-permute-done.4.refs_6_.refs_5_.refs_17_) | copy-start | bytes 2162692
  50.8 18.1 %collective-permute-start.5 = (bf16[704,512]{1,0:T(8,128)(2,1)S(1)}, bf16[704,512]{1,0:T(8,128)(2,1)}, u32[]{:S(2)}, u32[]{:S(2)}) collective-permute-start(bf16[704,512]{1,0:T(8,128)(2,1)S(1)} %bitcast.49), channel_id=1, source_target_pairs={{0,8},{24,16},{1,9},{25,17},{2,10},{26,18},{3,11},{27,19},{4,12},{... | collective-permute-start | bytes 2162696 | tf_op jit(solution)/shard_map/ppermute | solution.py:516
  53.2 27.4 %collective-permute-start.6 = (bf16[704,512]{1,0:T(8,128)(2,1)}, bf16[704,512]{1,0:T(8,128)(2,1)}, u32[]{:S(2)}, u32[]{:S(2)}) collective-permute-start(bf16[704,512]{1,0:T(8,128)(2,1)} %bitcast.12.refs_3_.refs_15_), channel_id=1, source_target_pairs={{0,8},{24,16},{1,9},{25,17},{2,10},{26,18},{3,11},{27,19},{4,12},{... | collective-permute-start | bytes 2162696 | tf_op jit(solution)/shard_map/ppermute | solution.py:516
  55.4 25.3 %collective-permute-start.8 = (bf16[704,512]{1,0:T(8,128)(2,1)}, bf16[704,512]{1,0:T(8,128)(2,1)}, u32[]{:S(2)}, u32[]{:S(2)}) collective-permute-start(bf16[704,512]{1,0:T(8,128)(2,1)} %bitcast.12.refs_3_.refs_15_), channel_id=1, source_target_pairs={{8,16},{16,8},{9,17},{17,9},{10,18},{18,10},{11,19},{19,11},{12,20... | collective-permute-start | bytes 2162696 | tf_op jit(solution)/shard_map/ppermute | solution.py:516
  56.9 25.8 %collective-permute-start.14 = (bf16[704,512]{1,0:T(8,128)(2,1)S(1)}, bf16[704,512]{1,0:T(8,128)(2,1)}, u32[]{:S(2)}, u32[]{:S(2)}) collective-permute-start(bf16[704,512]{1,0:T(8,128)(2,1)S(1)} %bitcast.50), channel_id=1, source_target_pairs={{8,16},{16,8},{9,17},{17,9},{10,18},{18,10},{11,19},{19,11},{12,20... | collective-permute-start | bytes 2162696 | tf_op jit(solution)/shard_map/ppermute | solution.py:516
  58.4 1.1 copy-start.5
  80.6 21.2 %collective-permute-start.9 = (bf16[704,512]{1,0:T(8,128)(2,1)}, bf16[704,512]{1,0:T(8,128)(2,1)S(1)}, u32[]{:S(2)}, u32[]{:S(2)}) collective-permute-start(bf16[704,512]{1,0:T(8,128)(2,1)} %collective-permute-done.8.refs_6_.refs_18_), channel_id=1, source_target_pairs={{8,0},{16,24},{9,1},{17,25},{10,2},{18,26},{11,3},{19,27},{12,4},{... | collective-permute-start | bytes 2162696 | tf_op jit(solution)/shard_map/ppermute | solution.py:516
  81.9 37.0 %collective-permute-start.13 = (bf16[704,512]{1,0:T(8,128)(2,1)}, bf16[704,512]{1,0:T(8,128)(2,1)S(1)}, u32[]{:S(2)}, u32[]{:S(2)}) collective-permute-start(bf16[704,512]{1,0:T(8,128)(2,1)} %collective-permute-done.5.refs_3_.refs_9_), channel_id=1, source_target_pairs={{8,16},{16,8},{9,17},{17,9},{10,18},{18,10},{11,19},{19,11},{12,20... | collective-permute-start | bytes 2162696 | tf_op jit(solution)/shard_map/ppermute | solution.py:516
  82.7 40.2 %collective-permute-start.15 = (bf16[704,512]{1,0:T(8,128)(2,1)}, bf16[704,512]{1,0:T(8,128)(2,1)S(1)}, u32[]{:S(2)}, u32[]{:S(2)}) collective-permute-start(bf16[704,512]{1,0:T(8,128)(2,1)} %collective-permute-done.14.refs_5_.refs_11_), channel_id=1, source_target_pairs={{8,0},{16,24},{9,1},{17,25},{10,2},{18,26},{11,3},{19,27},{12,4},{... | collective-permute-start | bytes 2162696 | tf_op jit(solution)/shard_map/ppermute | solution.py:516
  84.0 19.2 %collective-permute-start.11 = (bf16[128,1024]{1,0:T(8,128)(2,1)}, bf16[128,1024]{1,0:T(8,128)(2,1)S(1)}, u32[]{:S(2)}, u32[]{:S(2)}) collective-permute-start(bf16[128,1024]{1,0:T(8,128)(2,1)} %get-tuple-element.50), channel_id=1, source_target_pairs={{8,16},{16,8},{9,17},{17,9},{10,18},{18,10},{11,19},{19,11},{12,20... | collective-permute-start | bytes 786440 | tf_op jit(solution)/shard_map/ppermute | solution.py:516
  84.6 31.8 %collective-permute-start.12 = (bf16[128,1024]{1,0:T(8,128)(2,1)}, bf16[128,1024]{1,0:T(8,128)(2,1)S(1)}, u32[]{:S(2)}, u32[]{:S(2)}) collective-permute-start(bf16[128,1024]{1,0:T(8,128)(2,1)} %get-tuple-element.51), channel_id=1, source_target_pairs={{16,0},{8,24},{17,1},{9,25},{18,2},{10,26},{19,3},{11,27},{20,4},{... | collective-permute-start | bytes 786440 | tf_op jit(solution)/shard_map/ppermute | solution.py:516
  101.8 58.9 %copy-start.12 = (bf16[704,512]{1,0:T(8,128)(2,1)}, bf16[704,512]{1,0:T(8,128)(2,1)S(1)}, u32[]{:S(2)}) copy-start(bf16[704,512]{1,0:T(8,128)(2,1)S(1)} %collective-permute-done.9.refs_7_.refs_19_) | copy-start | bytes 2162692
  101.8 26.7 %collective-permute-start.10 = (bf16[128,1024]{1,0:T(8,128)(2,1)}, bf16[128,1024]{1,0:T(8,128)(2,1)S(1)}, u32[]{:S(2)}, u32[]{:S(2)}) collective-permute-start(bf16[128,1024]{1,0:T(8,128)(2,1)} %get-tuple-element.49), channel_id=1, source_target_pairs={{8,0},{16,24},{9,1},{17,25},{10,2},{18,26},{11,3},{19,27},{12,4},{... | collective-permute-start | bytes 786440 | tf_op jit(solution)/shard_map/ppermute | solution.py:516
  103.1 25.4 %copy-start.16 = (bf16[128,1024]{1,0:T(8,128)(2,1)}, bf16[128,1024]{1,0:T(8,128)(2,1)S(1)}, u32[]{:S(2)}) copy-start(bf16[128,1024]{1,0:T(8,128)(2,1)S(1)} %collective-permute-done.11.refs_6_) | copy-start | bytes 786436
  103.1 33.1 %collective-permute-start.17 = (bf16[704,512]{1,0:T(8,128)(2,1)}, bf16[704,512]{1,0:T(8,128)(2,1)S(1)}, u32[]{:S(2)}, u32[]{:S(2)}) collective-permute-start(bf16[704,512]{1,0:T(8,128)(2,1)} %collective-permute-done.6.refs_4_.refs_16_), channel_id=1, source_target_pairs={{8,16},{16,8},{9,17},{17,9},{10,18},{18,10},{11,19},{19,11},{12,20... | collective-permute-start | bytes 2162696 | tf_op jit(solution)/shard_map/ppermute | solution.py:516
  116.5 12.0 %copy-start.17 = (bf16[128,1024]{1,0:T(8,128)(2,1)}, bf16[128,1024]{1,0:T(8,128)(2,1)S(1)}, u32[]{:S(2)}) copy-start(bf16[128,1024]{1,0:T(8,128)(2,1)S(1)} %collective-permute-done.12.refs_7_) | copy-start | bytes 786436
  116.5 19.8 %collective-permute-start.19 = (bf16[704,512]{1,0:T(8,128)(2,1)}, bf16[704,512]{1,0:T(8,128)(2,1)}, u32[]{:S(2)}, u32[]{:S(2)}) collective-permute-start(bf16[704,512]{1,0:T(8,128)(2,1)} %bitcast.18.refs_3_), channel_id=1, source_target_pairs={{0,8},{24,16},{1,9},{25,17},{2,10},{26,18},{3,11},{27,19},{4,12},{... | collective-permute-start | bytes 2162696 | tf_op jit(solution)/shard_map/ppermute | solution.py:516
  118.9 9.6 %copy-start.9 = (bf16[704,512]{1,0:T(8,128)(2,1)}, bf16[704,512]{1,0:T(8,128)(2,1)S(1)}, u32[]{:S(2)}) copy-start(bf16[704,512]{1,0:T(8,128)(2,1)S(1)} %collective-permute-done.13.refs_8_.refs_7_.refs_13_) | copy-start | bytes 2162692
  118.9 20.5 %collective-permute-start.16 = (bf16[704,512]{1,0:T(8,128)(2,1)S(1)}, bf16[704,512]{1,0:T(8,128)(2,1)}, u32[]{:S(2)}, u32[]{:S(2)}) collective-permute-start(bf16[704,512]{1,0:T(8,128)(2,1)S(1)} %collective-permute-done.13.refs_8_.refs_7_.refs_13_), channel_id=1, source_target_pairs={{8,0},{16,24},{9,1},{17,25},{10,2},{18,26},{11,3},{19,27},{12,4},{... | collective-permute-start | bytes 2162696 | tf_op jit(solution)/shard_map/ppermute | solution.py:516
  122.9 5.6 %copy-start.10 = (bf16[704,512]{1,0:T(8,128)(2,1)}, bf16[704,512]{1,0:T(8,128)(2,1)S(1)}, u32[]{:S(2)}) copy-start(bf16[704,512]{1,0:T(8,128)(2,1)S(1)} %collective-permute-done.15.refs_9_.refs_6_.refs_12_) | copy-start | bytes 2162692
  122.9 17.8 %collective-permute-start.21 = (bf16[704,512]{1,0:T(8,128)(2,1)}, bf16[704,512]{1,0:T(8,128)(2,1)}, u32[]{:S(2)}, u32[]{:S(2)}) collective-permute-start(bf16[704,512]{1,0:T(8,128)(2,1)} %bitcast.18.refs_3_), channel_id=1, source_target_pairs={{8,16},{16,8},{9,17},{17,9},{10,18},{18,10},{11,19},{19,11},{12,20... | collective-permute-start | bytes 2162696 | tf_op jit(solution)/shard_map/ppermute | solution.py:516
  128.5 0.7 copy-start.18
  132.5 21.9 %all-to-all-start.1 = ((bf16[8,40,2048]{2,1,0:T(8,128)(2,1)}), bf16[8,40,2048]{2,1,0:T(8,128)(2,1)S(1)}, u32[]{:S(2)}, u32[]{:S(2)}) async-start(bf16[8,40,2048]{2,1,0:T(8,128)(2,1)} %bitcast.51), calls=%async_computation.1 | async-start | bytes 2621440 | tf_op jit(solution)/shard_map/all_to_all | solution.py:538
  136.2 25.8 %copy-start.13 = (bf16[704,512]{1,0:T(8,128)(2,1)}, bf16[704,512]{1,0:T(8,128)(2,1)S(1)}, u32[]{:S(2)}) copy-start(bf16[704,512]{1,0:T(8,128)(2,1)S(1)} %collective-permute-done.17.refs_8_.refs_20_) | copy-start | bytes 2162692
  136.3 24.5 %collective-permute-start.20 = (bf16[704,512]{1,0:T(8,128)(2,1)}, bf16[704,512]{1,0:T(8,128)(2,1)}, u32[]{:S(2)}, u32[]{:S(2)}) collective-permute-start(bf16[704,512]{1,0:T(8,128)(2,1)} %collective-permute-done.19.refs_4_), channel_id=1, source_target_pairs={{8,16},{16,8},{9,17},{17,9},{10,18},{18,10},{11,19},{19,11},{12,20... | collective-permute-start | bytes 2162696 | tf_op jit(solution)/shard_map/ppermute | solution.py:516
  139.4 21.3 %collective-permute-start.18 = (bf16[704,512]{1,0:T(8,128)(2,1)S(1)}, bf16[704,512]{1,0:T(8,128)(2,1)S(1)}, u32[]{:S(2)}, u32[]{:S(2)}) collective-permute-start(bf16[704,512]{1,0:T(8,128)(2,1)S(1)} %collective-permute-done.17.refs_8_.refs_20_), channel_id=1, source_target_pairs={{8,0},{16,24},{9,1},{17,25},{10,2},{18,26},{11,3},{19,27},{12,4},{... | collective-permute-start | bytes 2162696 | tf_op jit(solution)/shard_map/ppermute | solution.py:516
  140.7 35.2 %collective-permute-start.22 = (bf16[704,512]{1,0:T(8,128)(2,1)}, bf16[704,512]{1,0:T(8,128)(2,1)}, u32[]{:S(2)}, u32[]{:S(2)}) collective-permute-start(bf16[704,512]{1,0:T(8,128)(2,1)} %collective-permute-done.21.refs_6_), channel_id=1, source_target_pairs={{8,0},{16,24},{9,1},{17,25},{10,2},{18,26},{11,3},{19,27},{12,4},{... | collective-permute-start | bytes 2162696 | tf_op jit(solution)/shard_map/ppermute | solution.py:516
  154.5 1.1 copy-start.6
  160.8 1.3 copy-start.14
  160.8 28.4 %collective-permute-start.23 = (bf16[704,512]{1,0:T(8,128)(2,1)}, bf16[704,512]{1,0:T(8,128)(2,1)S(1)}, u32[]{:S(2)}, u32[]{:S(2)}) collective-permute-start(bf16[704,512]{1,0:T(8,128)(2,1)} %collective-permute-done.20.refs_10_.refs_6_), channel_id=1, source_target_pairs={{8,0},{16,24},{9,1},{17,25},{10,2},{18,26},{11,3},{19,27},{12,4},{... | collective-permute-start | bytes 2162696 | tf_op jit(solution)/shard_map/ppermute | solution.py:516
  181.9 18.4 %all-to-all-start.2 = ((bf16[8,40,1536]{2,1,0:T(8,128)(2,1)}), bf16[8,40,1536]{2,1,0:T(8,128)(2,1)S(1)}, u32[]{:S(2)}, u32[]{:S(2)}) async-start(bf16[8,40,1536]{2,1,0:T(8,128)(2,1)} %bitcast.52), calls=%async_computation.2 | async-start | bytes 1966080 | tf_op jit(solution)/shard_map/all_to_all | solution.py:538
  189.1 0.9 copy-start.15
  200.4 25.3 %copy-start = (bf16[1,128,2048]{2,1,0:T(8,128)(2,1)S(1)}, bf16[1,128,2048]{2,1,0:T(8,128)(2,1)}, u32[]{:S(2)}) copy-start(bf16[1,128,2048]{2,1,0:T(8,128)(2,1)} %param.22) | copy-start | bytes 1572868
  200.4 25.3 %copy-start.1 = (f32[1,128,2]{2,1,0:T(8,128)S(1)}, f32[1,128,2]{2,1,0:T(8,128)}, u32[]{:S(2)}) copy-start(f32[1,128,2]{2,1,0:T(8,128)} %copy.15) | copy-start | bytes 3076
  200.4 25.3 %copy-start.2 = (bf16[128,2048]{1,0:T(8,128)(2,1)S(1)}, bf16[128,2048]{1,0:T(8,128)(2,1)}, u32[]{:S(2)}) copy-start(bf16[128,2048]{1,0:T(8,128)(2,1)} %get-tuple-element.54.refs_4_) | copy-start | bytes 1572868
  200.4 25.3 %copy-start.3 = (f32[2048]{0:T(1024)S(1)}, f32[2048]{0:T(1024)}, u32[]{:S(2)}) copy-start(f32[2048]{0:T(1024)} %param.16) | copy-start | bytes 24580
  200.4 25.3 %copy-start.4 = (s32[10]{0:T(128)S(1)}, s32[10]{0:T(128)}, u32[]{:S(2)}) copy-start(s32[10]{0:T(128)} %dynamic-slice_bitcast_fusion.refs_0_) | copy-start | bytes 124

commit v9 on v8

--- a/solution.py
+++ b/solution.py
@@ -197,9 +197,11 @@
     gate_end = send(gate, OUTWARD)
     up_end = send(up, OUTWARD)
     down_end = send(down, OUTWARD, gate_end)
-    near = send(first, INWARD)
-    mid = send(second, MIDDLE)
-    far = send(second, [(0, 2), (3, 1)])
+    gate_mid = send(gate, MIDDLE)
+    gate_far = send(gate_mid, OUTWARD)
+    near = send(first, INWARD, gate_mid, gate_end)
+    mid = send(second, MIDDLE, gate_mid, gate_end)
+    far = send(second, [(0, 2), (3, 1)], gate_mid, gate_end)
     piece = sds((rows, half))
     pieces = call(
         middle_kernel,
@@ -213,28 +215,26 @@
         ],
         flops=64 * rows * rows * half,
         moved=32 * rows * half,
-        after=(gate_end, up_end, cot_rows),
-    )
-    gate_mid = send(gate, MIDDLE, near, mid, far)
+        after=(gate_end, up_end, gate_far, cot_rows),
+    )
     up_mid = send(up, MIDDLE, near, mid, far)
     gate_inner = send(gate, INWARD, near, far, gate_end, up_end)
     up_inner = send(up, INWARD, near, far, gate_end, up_end)
     down_inner = send(down, INWARD, gate_inner)
-    own, near, mid, far = lax.optimization_barrier((*pieces, gate_inner, up_inner, down_end))[:4]
+    own, near, mid, far = lax.optimization_barrier((*pieces, gate_inner, down_end))[:4]
     mid = send(mid, MIDDLE)
     far = send(far, [(2, 0), (1, 3)])
-    up_far = send(up_mid, OUTWARD, own)
+    up_far = send(up_mid, OUTWARD, pieces[0])
     near = send(near, OUTWARD, up_far)
     gate_mid_near = send(gate_inner, MIDDLE)
-    gate_far = send(gate_mid, OUTWARD, own)
-    up_mid_near = send(up_inner, MIDDLE, own)
+    up_mid_near = send(up_inner, MIDDLE, pieces[0])
     down_mid = send(down, MIDDLE, gate_mid_near)
     down_mid_near = send(down_inner, MIDDLE, up_mid_near)
     gate_far_near = send(gate_mid_near, OUTWARD)
     up_far_near = send(up_mid_near, OUTWARD, gate_far_near)
     down_far = send(down_mid, OUTWARD, gate_far_near)
     down_far_near = send(down_mid_near, OUTWARD, up_far_near)
-    norm_after = (gate_mid_near, gate_far)
+    norm_after = (gate_mid_near,)
     up_after = (down_mid_near,)
     gate_in = [
         [gate],

time: 230 us -> 225 us (0.978)
  waiting for transfers between devices: 107 us -> 78.9 us
  starting transfers between devices: 50.3 us -> 73.3 us
    ppermute x24, waiting for transfers between devices: 91.7 us -> 60.8 us  [send(): return lax.ppermute(gated(array, *first), 'seq', pairs)]
    ppermute x24, starting transfers between devices: 39.1 us -> 61.9 us  [send(): return lax.ppermute(gated(array, *first), 'seq', pairs)]
    all_to_all x3, waiting for transfers between devices: 15 us -> 18.1 us  [exchange(): rows = lax.all_to_all(rows, axis, split_axis=0, concat_axis=0, tiled=True)]
    unnamed x44 -> x46, local copies, waits for them, and re-layouts: 4.66 us -> 4.85 us
  transfers between devices with their start and end apart: 27 -> 27, of which waited for: 14 -> 12; matrix products, arithmetic and copies ran while one was open for 1% -> 1% of each run, Pallas kernels for 14% -> 16%
where the time goes in v9:
time: 225 us; the launch traced here: 224 us
  waiting for transfers between devices  78.9 us (35%)
  starting transfers between devices  73.3 us (33%)
  Pallas kernels  38.7 us (17%)
  blocking collectives  25.3 us (11%)
  local copies, waits for them, and re-layouts  6.72 us (3%)
    ppermute x24, starting transfers between devices, send(): return lax.ppermute(gated(array, *first), 'seq', pairs)  61.9 us
    ppermute x24, waiting for transfers between devices, send(): return lax.ppermute(gated(array, *first), 'seq', pairs)  60.8 us
    pallas_call x9, Pallas kernels, call(): pl.pallas_call(body, grid=() if held else (1,), out_shape=outs, in_specs=...  38.7 us
    all_to_all x1, blocking collectives, exchange(): rows = lax.all_to_all(rows, axis, split_axis=0, concat_axis=0, tiled=True)  25.3 us
    all_to_all x3, waiting for transfers between devices, exchange(): rows = lax.all_to_all(rows, axis, split_axis=0, concat_axis=0, tiled=True)  18.1 us
    all_to_all x3, starting transfers between devices, exchange(): rows = lax.all_to_all(rows, axis, split_axis=0, concat_axis=0, tiled=True)  11.3 us
    unnamed x46, local copies, waits for them, and re-layouts  4.85 us
  transfers between devices with their start and end apart: 27, of which 12 were waited for; matrix products, arithmetic and copies ran while one was open for 1% of the time, Pallas kernels for 16%

profile of v9, /device:TPU:0, one launch (start us, length us, event | category | flops | bytes accessed | tf_op | source)
XLA Modules:
  0.0 224.0 jit_solution(4300325375078161303)
XLA Ops:
  1.5 1.3 collective-permute-start.1
  2.8 1.3 dynamic-slice_bitcast_fusion.refs_0_
  4.1 2.6 %shard_map.131 = (bf16[384,1024]{1,0:T(8,128)(2,1)}, bf16[384,1024]{1,0:T(8,128)(2,1)}) custom-call(s32[10]{0:T(128)} %dynamic-slice_bitcast_fusion.refs_0_, bf16[128,2048]{1,0:T(8,128)(2,1)} %bitcast.53, bf16[128,2048]{1,0:T(8,128)(2,1)} %bitcast.54, bf16[128,2048]{1,0:T(8,128)(2,1)} %bitcast.55), custom_call_target="tpu_custom_call" | custom-call | bytes 3145728 | tf_op jit(solution)/shard_map/pallas_call | solution.py:35
  6.7 17.9 %collective-permute-done.1.refs_5_.refs_4_.refs_10_ = bf16[704,512]{1,0:T(8,128)(2,1)S(1)} collective-permute-done((bf16[704,512]{1,0:T(8,128)(2,1)}, bf16[704,512]{1,0:T(8,128)(2,1)S(1)}, u32[]{:S(2)}, u32[]{:S(2)}) %collective-permute-start.1) | collective-permute-done | bytes 720928 | tf_op jit(solution)/shard_map/ppermute | solution.py:516
  24.6 2.4 %collective-permute-start.2 = (bf16[384,1024]{1,0:T(8,128)(2,1)}, bf16[384,1024]{1,0:T(8,128)(2,1)}, u32[]{:S(2)}, u32[]{:S(2)}) collective-permute-start(bf16[384,1024]{1,0:T(8,128)(2,1)} %get-tuple-element.37.refs_1_), channel_id=1, source_target_pairs={{0,8},{24,16},{1,9},{25,17},{2,10},{26,18},{3,11},{27,19},{4,12},{... | collective-permute-start | bytes 2359304 | tf_op jit(solution)/shard_map/ppermute | solution.py:516
  27.1 1.6 collective-permute-start.3
  28.7 3.1 %collective-permute-start.4 = (bf16[384,1024]{1,0:T(8,128)(2,1)}, bf16[384,1024]{1,0:T(8,128)(2,1)}, u32[]{:S(2)}, u32[]{:S(2)}) collective-permute-start(bf16[384,1024]{1,0:T(8,128)(2,1)} %get-tuple-element.39), channel_id=1, source_target_pairs={{0,16},{24,8},{1,17},{25,9},{2,18},{26,10},{3,19},{27,11},{4,20},{... | collective-permute-start | bytes 2359304 | tf_op jit(solution)/shard_map/ppermute | solution.py:516
  31.8 1.3 collective-permute-start.5
  34.6 3.2 %shard_map.132 = bf16[320,2048]{1,0:T(8,128)(2,1)} custom-call(s32[2,128]{1,0:T(2,128)} %copy.17.refs_0_.refs_1_, f32[128,2]{1,0:T(8,128)} %bitcast.33, bf16[128,2048]{1,0:T(8,128)(2,1)} %bitcast.31), custom_call_target="tpu_custom_call" | custom-call | flops 335544320 | bytes 1835008 | tf_op jit(solution)/shard_map/pallas_call | solution.py:35
  37.7 3.9 %all-to-all-start = ((bf16[8,40,2048]{2,1,0:T(8,128)(2,1)}), bf16[8,40,2048]{2,1,0:T(8,128)(2,1)S(1)}, u32[]{:S(2)}, u32[]{:S(2)}) async-start(bf16[8,40,2048]{2,1,0:T(8,128)(2,1)} %bitcast.45), calls=%async_computation | async-start | bytes 2621440 | tf_op jit(solution)/shard_map/all_to_all | solution.py:538
  41.6 1.3 collective-permute-start.6
  42.9 1.6 collective-permute-done.2.refs_2_
  44.5 14.8 %collective-permute-done.4.refs_4_ = bf16[384,1024]{1,0:T(8,128)(2,1)} collective-permute-done((bf16[384,1024]{1,0:T(8,128)(2,1)}, bf16[384,1024]{1,0:T(8,128)(2,1)}, u32[]{:S(2)}, u32[]{:S(2)}) %collective-permute-start.4) | collective-permute-done | bytes 786464 | tf_op jit(solution)/shard_map/ppermute | solution.py:516
  59.3 1.5 collective-permute-start.9
  60.8 8.0 %collective-permute-start.7 = (bf16[704,512]{1,0:T(8,128)(2,1)S(1)}, bf16[704,512]{1,0:T(8,128)(2,1)}, u32[]{:S(2)}, u32[]{:S(2)}) collective-permute-start(bf16[704,512]{1,0:T(8,128)(2,1)S(1)} %bitcast.50), channel_id=1, source_target_pairs={{0,8},{24,16},{1,9},{25,17},{2,10},{26,18},{3,11},{27,19},{4,12},{... | collective-permute-start | bytes 2162696 | tf_op jit(solution)/shard_map/ppermute | solution.py:516
  68.9 1.3 collective-permute-start.8
  70.2 1.1 copy-done.5
  71.5 1.7 shard_map.133
  73.2 1.3 collective-permute-start.10
  74.5 13.2 %collective-permute-start.16 = (bf16[704,512]{1,0:T(8,128)(2,1)}, bf16[704,512]{1,0:T(8,128)(2,1)}, u32[]{:S(2)}, u32[]{:S(2)}) collective-permute-start(bf16[704,512]{1,0:T(8,128)(2,1)} %bitcast.13.refs_3_.refs_15_), channel_id=1, source_target_pairs={{0,8},{24,16},{1,9},{25,17},{2,10},{26,18},{3,11},{27,19},{4,12},{... | collective-permute-start | bytes 2162696 | tf_op jit(solution)/shard_map/ppermute | solution.py:516
  89.7 1.3 collective-permute-start.13
  91.0 10.1 %collective-permute-done.10.refs_7_.refs_19_ = bf16[704,512]{1,0:T(8,128)(2,1)S(1)} collective-permute-done((bf16[704,512]{1,0:T(8,128)(2,1)}, bf16[704,512]{1,0:T(8,128)(2,1)S(1)}, u32[]{:S(2)}, u32[]{:S(2)}) %collective-permute-start.10) | collective-permute-done | bytes 720928 | tf_op jit(solution)/shard_map/ppermute | solution.py:516
  101.1 1.3 collective-permute-start.11
  102.4 1.6 collective-permute-start.17
  104.0 11.0 %collective-permute-start.19 = (bf16[704,512]{1,0:T(8,128)(2,1)}, bf16[704,512]{1,0:T(8,128)(2,1)S(1)}, u32[]{:S(2)}, u32[]{:S(2)}) collective-permute-start(bf16[704,512]{1,0:T(8,128)(2,1)} %bitcast.17.refs_3_), channel_id=1, source_target_pairs={{0,8},{24,16},{1,9},{25,17},{2,10},{26,18},{3,11},{27,19},{4,12},{... | collective-permute-start | bytes 2162696 | tf_op jit(solution)/shard_map/ppermute | solution.py:516
  115.0 1.3 collective-permute-start.15
  116.3 1.8 collective-permute-done.13.refs_7_
  118.1 1.5 collective-permute-start.21
  120.3 3.3 %shard_map.134 = (bf16[128,2048]{1,0:T(8,128)(2,1)}, bf16[320,2048]{1,0:T(8,128)(2,1)}) custom-call(s32[10]{0:T(128)} %dynamic-slice_bitcast_fusion.refs_0_, s32[2,128]{1,0:T(2,128)} %copy.17.refs_0_.refs_1_, bf16[128,2048]{1,0:T(8,128)(2,1)} %bitcast.56, f32[1,2048]{1,0:T(1,128)} %bitcast.37, bf16[128,1024]{1,0:T(8,128)(2,1)} %get-tuple-element.46.refs_4_, ...), custom_call_target="tpu_custom_call" | custom-call | flops 167772160 | bytes 2883584 | tf_op jit(solution)/shard_map/pallas_call | solution.py:35
  123.7 3.7 %all-to-all-start.1 = ((bf16[8,40,2048]{2,1,0:T(8,128)(2,1)}), bf16[8,40,2048]{2,1,0:T(8,128)(2,1)S(1)}, u32[]{:S(2)}, u32[]{:S(2)}) async-start(bf16[8,40,2048]{2,1,0:T(8,128)(2,1)} %bitcast.51), calls=%async_computation.1 | async-start | bytes 2621440 | tf_op jit(solution)/shard_map/all_to_all | solution.py:538
  127.4 1.5 collective-permute-start.20
  129.4 1.3 collective-permute-start.18
  130.7 1.3 collective-permute-start.22
  132.0 13.6 %all-to-all-done.1 = bf16[8,40,2048]{2,1,0:T(8,128)(2,1)S(1)} async-done(((bf16[8,40,2048]{2,1,0:T(8,128)(2,1)}), bf16[8,40,2048]{2,1,0:T(8,128)(2,1)S(1)}, u32[]{:S(2)}, u32[]{:S(2)}) %all-to-all-start.1) | async-done | bytes 1310752 | tf_op jit(solution)/shard_map/all_to_all | solution.py:538
  145.6 1.1 copy-done.6
  146.7 5.2 %shard_map.135.refs_2_ = f32[320,704]{1,0:T(8,128)} custom-call(s32[10]{0:T(128)} %dynamic-slice_bitcast_fusion.refs_0_, bf16[320,2048]{1,0:T(8,128)(2,1)} %bitcast.42, bf16[704,512]{1,0:T(8,128)(2,1)} %bitcast.48, bf16[704,512]{1,0:T(8,128)(2,1)} %collective-permute-done.7.refs_3_.refs_9_, bf16[704,512]{1,0:T(8,128)(2,1)} %copy-done.7, ...), custom_call_target="tpu_custom_call" | custom-call | flops 922746880 | bytes 5095424 | tf_op jit(solution)/shard_map/pallas_call | solution.py:35
  151.9 3.7 %collective-permute-done.18.refs_9_.refs_21_ = bf16[704,512]{1,0:T(8,128)(2,1)S(1)} collective-permute-done((bf16[704,512]{1,0:T(8,128)(2,1)}, bf16[704,512]{1,0:T(8,128)(2,1)S(1)}, u32[]{:S(2)}, u32[]{:S(2)}) %collective-permute-start.18) | collective-permute-done | bytes 720928 | tf_op jit(solution)/shard_map/ppermute | solution.py:516
  155.6 1.3 collective-permute-start.23
  156.9 6.0 %shard_map.136 = (bf16[320,704]{1,0:T(8,128)(2,1)}, f32[320,704]{1,0:T(8,128)}, f32[320,704]{1,0:T(8,128)}) custom-call(s32[10]{0:T(128)} %dynamic-slice_bitcast_fusion.refs_0_, bf16[320,2048]{1,0:T(8,128)(2,1)} %bitcast.43, f32[320,704]{1,0:T(8,128)} %shard_map.135.refs_2_, bf16[704,512]{1,0:T(8,128)(2,1)} %bitcast.13.refs_3_.refs_15_, ...), custom_call_target="tpu_custom_call" | custom-call | flops 922746880 | bytes 7348224 | tf_op jit(solution)/shard_map/pallas_call | solution.py:35
  162.9 8.3 %collective-permute-done.22.refs_7_ = bf16[704,512]{1,0:T(8,128)(2,1)} collective-permute-done((bf16[704,512]{1,0:T(8,128)(2,1)}, bf16[704,512]{1,0:T(8,128)(2,1)}, u32[]{:S(2)}, u32[]{:S(2)}) %collective-permute-start.22) | collective-permute-done | bytes 720928 | tf_op jit(solution)/shard_map/ppermute | solution.py:516
  171.2 5.9 %shard_map.137 = (bf16[320,1536]{1,0:T(8,128)(2,1)}, f32[320,704]{1,0:T(8,128)}) custom-call(s32[10]{0:T(128)} %dynamic-slice_bitcast_fusion.refs_0_, bf16[320,704]{1,0:T(8,128)(2,1)} %get-tuple-element.60.refs_1_, bf16[320,2048]{1,0:T(8,128)(2,1)} %bitcast.40, bf16[704,512]{1,0:T(8,128)(2,1)} %bitcast.17.refs_3_, bf16[704,512]{1,0:T(8,128)(2,1)} %copy-done.15, ...), custom_call_target="tpu_custom_call" | custom-call | flops 1384120320 | bytes 6856704 | tf_op jit(solution)/shard_map/pallas_call | solution.py:35
  177.1 3.7 %all-to-all-start.2 = ((bf16[8,40,1536]{2,1,0:T(8,128)(2,1)}), bf16[8,40,1536]{2,1,0:T(8,128)(2,1)S(1)}, u32[]{:S(2)}, u32[]{:S(2)}) async-start(bf16[8,40,1536]{2,1,0:T(8,128)(2,1)} %bitcast.52), calls=%async_computation.2 | async-start | bytes 1966080 | tf_op jit(solution)/shard_map/all_to_all | solution.py:538
  180.8 1.5 collective-permute-done.23.refs_7_
  182.4 0.9 copy-done.16
  183.2 7.8 %shard_map.138 = bf16[320,2560]{1,0:T(8,128)(2,1)} custom-call(s32[10]{0:T(128)} %dynamic-slice_bitcast_fusion.refs_0_, bf16[320,704]{1,0:T(8,128)(2,1)} %get-tuple-element.60.refs_1_, bf16[320,2048]{1,0:T(8,128)(2,1)} %bitcast.41, f32[320,704]{1,0:T(8,128)} %get-tuple-element.64.refs_3_, f32[320,704]{1,0:T(8,128)} %get-tuple-element.65.refs_4_, ...), custom_call_target="tpu_custom_call" | custom-call | flops 2306867200 | bytes 11542528 | tf_op jit(solution)/shard_map/pallas_call | solution.py:35
  191.0 4.5 %all-to-all-done.2 = bf16[8,40,1536]{2,1,0:T(8,128)(2,1)S(1)} async-done(((bf16[8,40,1536]{2,1,0:T(8,128)(2,1)}), bf16[8,40,1536]{2,1,0:T(8,128)(2,1)S(1)}, u32[]{:S(2)}, u32[]{:S(2)}) %all-to-all-start.2) | async-done | bytes 983072 | tf_op jit(solution)/shard_map/all_to_all | solution.py:538
  195.5 25.3 %all_to_all.20 = bf16[8,40,2560]{2,1,0:T(8,128)(2,1)S(1)} all-to-all(bf16[8,40,2560]{2,1,0:T(8,128)(2,1)} %bitcast.44), channel_id=1, replica_groups=mesh['seq'=4,'exp'=8] {'exp'}, dimensions={0} | all-to-all | bytes 3276800 | tf_op jit(solution)/shard_map/all_to_all | solution.py:538
  220.9 3.1 %shard_map.139 = (bf16[128,2048]{1,0:T(8,128)(2,1)}, bf16[128,2048]{1,0:T(8,128)(2,1)}) custom-call(s32[10]{0:T(128)S(1)} %copy-done.4, s32[128,2]{1,0:T(8,128)S(1)} %bitcast.36, f32[128,2]{1,0:T(8,128)S(1)} %bitcast.34, f32[1,2048]{1,0:T(1,128)S(1)} %bitcast.38, bf16[128,2048]{1,0:T(8,128)(2,1)S(1)} %copy-done.2, bf16[128,2048]{1,0:T(8,128)(2,1)S(1)} %bitcast.32, ...), custom_call_target="tpu_custom_call" | custom-call | flops 503316480 | bytes 4718592 | tf_op jit(solution)/shard_map/pallas_call | solution.py:35
  (64 shorter events, 5.7 us)
Async XLA Ops:
  0.6 32.5 %copy-start.20 = (s32[1,128,2]{1,2,0:T(2,128)S(1)}, s32[1,128,2]{1,2,0:T(2,128)}, u32[]{:S(2)}) copy-start(s32[1,128,2]{1,2,0:T(2,128)} %param.20) | copy-start | bytes 3076
  0.6 32.6 %copy-start.21 = (f32[1,128,2]{1,2,0:T(2,128)S(1)}, f32[1,128,2]{1,2,0:T(2,128)}, u32[]{:S(2)}) copy-start(f32[1,128,2]{1,2,0:T(2,128)} %param.21) | copy-start | bytes 3076
  0.6 6.1 %collective-permute-start = (bf16[704,512]{1,0:T(8,128)(2,1)}, bf16[704,512]{1,0:T(8,128)(2,1)S(1)}, u32[]{:S(2)}, u32[]{:S(2)}) collective-permute-start(bf16[704,512]{1,0:T(8,128)(2,1)} %bitcast.46), channel_id=1, source_target_pairs={{8,16},{16,8},{9,17},{17,9},{10,18},{18,10},{11,19},{19,11},{12,20... | collective-permute-start | bytes 2162696 | tf_op jit(solution)/shard_map/ppermute | solution.py:516
  1.5 23.1 %collective-permute-start.1 = (bf16[704,512]{1,0:T(8,128)(2,1)}, bf16[704,512]{1,0:T(8,128)(2,1)S(1)}, u32[]{:S(2)}, u32[]{:S(2)}) collective-permute-start(bf16[704,512]{1,0:T(8,128)(2,1)} %bitcast.47), channel_id=1, source_target_pairs={{8,0},{16,24},{9,1},{17,25},{10,2},{18,26},{11,3},{19,27},{12,4},{... | collective-permute-start | bytes 2162696 | tf_op jit(solution)/shard_map/ppermute | solution.py:516
  6.7 25.1 %copy-start.12 = (bf16[704,512]{1,0:T(8,128)(2,1)}, bf16[704,512]{1,0:T(8,128)(2,1)S(1)}, u32[]{:S(2)}) copy-start(bf16[704,512]{1,0:T(8,128)(2,1)S(1)} %collective-permute-done.refs_5_.refs_11_) | copy-start | bytes 2162692
  24.6 13.1 %copy-start.7 = (bf16[704,512]{1,0:T(8,128)(2,1)}, bf16[704,512]{1,0:T(8,128)(2,1)S(1)}, u32[]{:S(2)}) copy-start(bf16[704,512]{1,0:T(8,128)(2,1)S(1)} %collective-permute-done.1.refs_5_.refs_4_.refs_10_) | copy-start | bytes 2162692
  24.6 19.8 %collective-permute-start.2 = (bf16[384,1024]{1,0:T(8,128)(2,1)}, bf16[384,1024]{1,0:T(8,128)(2,1)}, u32[]{:S(2)}, u32[]{:S(2)}) collective-permute-start(bf16[384,1024]{1,0:T(8,128)(2,1)} %get-tuple-element.37.refs_1_), channel_id=1, source_target_pairs={{0,8},{24,16},{1,9},{25,17},{2,10},{26,18},{3,11},{27,19},{4,12},{... | collective-permute-start | bytes 2359304 | tf_op jit(solution)/shard_map/ppermute | solution.py:516
  27.1 17.4 %collective-permute-start.3 = (bf16[384,1024]{1,0:T(8,128)(2,1)}, bf16[384,1024]{1,0:T(8,128)(2,1)}, u32[]{:S(2)}, u32[]{:S(2)}) collective-permute-start(bf16[384,1024]{1,0:T(8,128)(2,1)} %get-tuple-element.39), channel_id=1, source_target_pairs={{8,16},{16,8},{9,17},{17,9},{10,18},{18,10},{11,19},{19,11},{12,20... | collective-permute-start | bytes 2359304 | tf_op jit(solution)/shard_map/ppermute | solution.py:516
  28.7 30.6 %collective-permute-start.4 = (bf16[384,1024]{1,0:T(8,128)(2,1)}, bf16[384,1024]{1,0:T(8,128)(2,1)}, u32[]{:S(2)}, u32[]{:S(2)}) collective-permute-start(bf16[384,1024]{1,0:T(8,128)(2,1)} %get-tuple-element.39), channel_id=1, source_target_pairs={{0,16},{24,8},{1,17},{25,9},{2,18},{26,10},{3,19},{27,11},{4,20},{... | collective-permute-start | bytes 2359304 | tf_op jit(solution)/shard_map/ppermute | solution.py:516
  31.8 29.0 %collective-permute-start.5 = (bf16[704,512]{1,0:T(8,128)(2,1)}, bf16[704,512]{1,0:T(8,128)(2,1)S(1)}, u32[]{:S(2)}, u32[]{:S(2)}) collective-permute-start(bf16[704,512]{1,0:T(8,128)(2,1)} %bitcast.13.refs_3_.refs_15_), channel_id=1, source_target_pairs={{8,0},{16,24},{9,1},{17,25},{10,2},{18,26},{11,3},{19,27},{12,4},{... | collective-permute-start | bytes 2162696 | tf_op jit(solution)/shard_map/ppermute | solution.py:516
  37.7 23.1 %copy-start.11 = (bf16[1,512,704]{1,2,0:T(8,128)(2,1)S(1)}, bf16[1,512,704]{1,2,0:T(8,128)(2,1)}, u32[]{:S(2)}) copy-start(bf16[1,512,704]{1,2,0:T(8,128)(2,1)} %param.17) | copy-start | bytes 2162692
  37.7 32.4 %all-to-all-start = ((bf16[8,40,2048]{2,1,0:T(8,128)(2,1)}), bf16[8,40,2048]{2,1,0:T(8,128)(2,1)S(1)}, u32[]{:S(2)}, u32[]{:S(2)}) async-start(bf16[8,40,2048]{2,1,0:T(8,128)(2,1)} %bitcast.45), calls=%async_computation | async-start | bytes 2621440 | tf_op jit(solution)/shard_map/all_to_all | solution.py:538
  41.6 28.6 %collective-permute-start.6 = (bf16[704,512]{1,0:T(8,128)(2,1)}, bf16[704,512]{1,0:T(8,128)(2,1)S(1)}, u32[]{:S(2)}, u32[]{:S(2)}) collective-permute-start(bf16[704,512]{1,0:T(8,128)(2,1)} %copy-done.12), channel_id=1, source_target_pairs={{8,0},{16,24},{9,1},{17,25},{10,2},{18,26},{11,3},{19,27},{12,4},{... | collective-permute-start | bytes 2162696 | tf_op jit(solution)/shard_map/ppermute | solution.py:516
  59.3 13.8 %collective-permute-start.9 = (bf16[704,512]{1,0:T(8,128)(2,1)}, bf16[704,512]{1,0:T(8,128)(2,1)}, u32[]{:S(2)}, u32[]{:S(2)}) collective-permute-start(bf16[704,512]{1,0:T(8,128)(2,1)} %bitcast.13.refs_3_.refs_15_), channel_id=1, source_target_pairs={{8,16},{16,8},{9,17},{17,9},{10,18},{18,10},{11,19},{19,11},{12,20... | collective-permute-start | bytes 2162696 | tf_op jit(solution)/shard_map/ppermute | solution.py:516
  60.8 9.4 %copy-start.8 = (bf16[704,512]{1,0:T(8,128)(2,1)}, bf16[704,512]{1,0:T(8,128)(2,1)S(1)}, u32[]{:S(2)}) copy-start(bf16[704,512]{1,0:T(8,128)(2,1)S(1)} %collective-permute-done.5.refs_6_.refs_5_.refs_17_) | copy-start | bytes 2162692
  60.8 26.9 %collective-permute-start.7 = (bf16[704,512]{1,0:T(8,128)(2,1)S(1)}, bf16[704,512]{1,0:T(8,128)(2,1)}, u32[]{:S(2)}, u32[]{:S(2)}) collective-permute-start(bf16[704,512]{1,0:T(8,128)(2,1)S(1)} %bitcast.50), channel_id=1, source_target_pairs={{0,8},{24,16},{1,9},{25,17},{2,10},{26,18},{3,11},{27,19},{4,12},{... | collective-permute-start | bytes 2162696 | tf_op jit(solution)/shard_map/ppermute | solution.py:516
  68.9 20.2 %collective-permute-start.8 = (bf16[704,512]{1,0:T(8,128)(2,1)}, bf16[704,512]{1,0:T(8,128)(2,1)}, u32[]{:S(2)}, u32[]{:S(2)}) collective-permute-start(bf16[704,512]{1,0:T(8,128)(2,1)} %bitcast.17.refs_3_), channel_id=1, source_target_pairs={{8,0},{16,24},{9,1},{17,25},{10,2},{18,26},{11,3},{19,27},{12,4},{... | collective-permute-start | bytes 2162696 | tf_op jit(solution)/shard_map/ppermute | solution.py:516
  70.2 1.1 copy-start.5
  70.2 1.3 copy-start.9
  73.2 27.9 %collective-permute-start.10 = (bf16[704,512]{1,0:T(8,128)(2,1)}, bf16[704,512]{1,0:T(8,128)(2,1)S(1)}, u32[]{:S(2)}, u32[]{:S(2)}) collective-permute-start(bf16[704,512]{1,0:T(8,128)(2,1)} %collective-permute-done.9.refs_6_.refs_18_), channel_id=1, source_target_pairs={{8,0},{16,24},{9,1},{17,25},{10,2},{18,26},{11,3},{19,27},{12,4},{... | collective-permute-start | bytes 2162696 | tf_op jit(solution)/shard_map/ppermute | solution.py:516
  74.5 27.9 %collective-permute-start.16 = (bf16[704,512]{1,0:T(8,128)(2,1)}, bf16[704,512]{1,0:T(8,128)(2,1)}, u32[]{:S(2)}, u32[]{:S(2)}) collective-permute-start(bf16[704,512]{1,0:T(8,128)(2,1)} %bitcast.13.refs_3_.refs_15_), channel_id=1, source_target_pairs={{0,8},{24,16},{1,9},{25,17},{2,10},{26,18},{3,11},{27,19},{4,12},{... | collective-permute-start | bytes 2162696 | tf_op jit(solution)/shard_map/ppermute | solution.py:516
  87.7 27.3 %collective-permute-start.14 = (bf16[704,512]{1,0:T(8,128)(2,1)}, bf16[704,512]{1,0:T(8,128)(2,1)S(1)}, u32[]{:S(2)}, u32[]{:S(2)}) collective-permute-start(bf16[704,512]{1,0:T(8,128)(2,1)} %collective-permute-done.7.refs_3_.refs_9_), channel_id=1, source_target_pairs={{8,16},{16,8},{9,17},{17,9},{10,18},{18,10},{11,19},{19,11},{12,20... | collective-permute-start | bytes 2162696 | tf_op jit(solution)/shard_map/ppermute | solution.py:516
  89.0 15.0 %collective-permute-start.12 = (bf16[128,1024]{1,0:T(8,128)(2,1)}, bf16[128,1024]{1,0:T(8,128)(2,1)S(1)}, u32[]{:S(2)}, u32[]{:S(2)}) collective-permute-start(bf16[128,1024]{1,0:T(8,128)(2,1)} %get-tuple-element.51), channel_id=1, source_target_pairs={{8,16},{16,8},{9,17},{17,9},{10,18},{18,10},{11,19},{19,11},{12,20... | collective-permute-start | bytes 786440 | tf_op jit(solution)/shard_map/ppermute | solution.py:516
  89.7 28.4 %collective-permute-start.13 = (bf16[128,1024]{1,0:T(8,128)(2,1)}, bf16[128,1024]{1,0:T(8,128)(2,1)S(1)}, u32[]{:S(2)}, u32[]{:S(2)}) collective-permute-start(bf16[128,1024]{1,0:T(8,128)(2,1)} %get-tuple-element.52), channel_id=1, source_target_pairs={{16,0},{8,24},{17,1},{9,25},{18,2},{10,26},{19,3},{11,27},{20,4},{... | collective-permute-start | bytes 786440 | tf_op jit(solution)/shard_map/ppermute | solution.py:516
  101.1 50.8 %copy-start.13 = (bf16[704,512]{1,0:T(8,128)(2,1)}, bf16[704,512]{1,0:T(8,128)(2,1)S(1)}, u32[]{:S(2)}) copy-start(bf16[704,512]{1,0:T(8,128)(2,1)S(1)} %collective-permute-done.10.refs_7_.refs_19_) | copy-start | bytes 2162692
  101.1 18.6 %collective-permute-start.11 = (bf16[128,1024]{1,0:T(8,128)(2,1)}, bf16[128,1024]{1,0:T(8,128)(2,1)S(1)}, u32[]{:S(2)}, u32[]{:S(2)}) collective-permute-start(bf16[128,1024]{1,0:T(8,128)(2,1)} %get-tuple-element.50), channel_id=1, source_target_pairs={{8,0},{16,24},{9,1},{17,25},{10,2},{18,26},{11,3},{19,27},{12,4},{... | collective-permute-start | bytes 786440 | tf_op jit(solution)/shard_map/ppermute | solution.py:516
  102.4 25.0 %collective-permute-start.17 = (bf16[704,512]{1,0:T(8,128)(2,1)}, bf16[704,512]{1,0:T(8,128)(2,1)}, u32[]{:S(2)}, u32[]{:S(2)}) collective-permute-start(bf16[704,512]{1,0:T(8,128)(2,1)} %collective-permute-done.16.refs_4_.refs_16_), channel_id=1, source_target_pairs={{8,16},{16,8},{9,17},{17,9},{10,18},{18,10},{11,19},{19,11},{12,20... | collective-permute-start | bytes 2162696 | tf_op jit(solution)/shard_map/ppermute | solution.py:516
  104.0 15.6 %copy-start.17 = (bf16[128,1024]{1,0:T(8,128)(2,1)}, bf16[128,1024]{1,0:T(8,128)(2,1)S(1)}, u32[]{:S(2)}) copy-start(bf16[128,1024]{1,0:T(8,128)(2,1)S(1)} %collective-permute-done.12.refs_6_) | copy-start | bytes 786436
  104.0 23.4 %collective-permute-start.19 = (bf16[704,512]{1,0:T(8,128)(2,1)}, bf16[704,512]{1,0:T(8,128)(2,1)S(1)}, u32[]{:S(2)}, u32[]{:S(2)}) collective-permute-start(bf16[704,512]{1,0:T(8,128)(2,1)} %bitcast.17.refs_3_), channel_id=1, source_target_pairs={{0,8},{24,16},{1,9},{25,17},{2,10},{26,18},{3,11},{27,19},{4,12},{... | collective-permute-start | bytes 2162696 | tf_op jit(solution)/shard_map/ppermute | solution.py:516
  115.0 4.6 %copy-start.10 = (bf16[704,512]{1,0:T(8,128)(2,1)}, bf16[704,512]{1,0:T(8,128)(2,1)S(1)}, u32[]{:S(2)}) copy-start(bf16[704,512]{1,0:T(8,128)(2,1)S(1)} %collective-permute-done.14.refs_8_.refs_7_.refs_13_) | copy-start | bytes 2162692
  115.0 14.4 %collective-permute-start.15 = (bf16[704,512]{1,0:T(8,128)(2,1)S(1)}, bf16[704,512]{1,0:T(8,128)(2,1)}, u32[]{:S(2)}, u32[]{:S(2)}) collective-permute-start(bf16[704,512]{1,0:T(8,128)(2,1)S(1)} %collective-permute-done.14.refs_8_.refs_7_.refs_13_), channel_id=1, source_target_pairs={{8,0},{16,24},{9,1},{17,25},{10,2},{18,26},{11,3},{19,27},{12,4},{... | collective-permute-start | bytes 2162696 | tf_op jit(solution)/shard_map/ppermute | solution.py:516
  118.1 1.6 copy-start.18
  118.1 12.6 %collective-permute-start.21 = (bf16[704,512]{1,0:T(8,128)(2,1)}, bf16[704,512]{1,0:T(8,128)(2,1)}, u32[]{:S(2)}, u32[]{:S(2)}) collective-permute-start(bf16[704,512]{1,0:T(8,128)(2,1)} %bitcast.17.refs_3_), channel_id=1, source_target_pairs={{8,16},{16,8},{9,17},{17,9},{10,18},{18,10},{11,19},{19,11},{12,20... | collective-permute-start | bytes 2162696 | tf_op jit(solution)/shard_map/ppermute | solution.py:516
  123.7 21.9 %all-to-all-start.1 = ((bf16[8,40,2048]{2,1,0:T(8,128)(2,1)}), bf16[8,40,2048]{2,1,0:T(8,128)(2,1)S(1)}, u32[]{:S(2)}, u32[]{:S(2)}) async-start(bf16[8,40,2048]{2,1,0:T(8,128)(2,1)} %bitcast.51), calls=%async_computation.1 | async-start | bytes 2621440 | tf_op jit(solution)/shard_map/all_to_all | solution.py:538
  127.4 35.5 %copy-start.15 = (bf16[704,512]{1,0:T(8,128)(2,1)}, bf16[704,512]{1,0:T(8,128)(2,1)S(1)}, u32[]{:S(2)}) copy-start(bf16[704,512]{1,0:T(8,128)(2,1)S(1)} %collective-permute-done.19.refs_4_) | copy-start | bytes 2162692
  127.4 24.5 %collective-permute-start.20 = (bf16[704,512]{1,0:T(8,128)(2,1)S(1)}, bf16[704,512]{1,0:T(8,128)(2,1)}, u32[]{:S(2)}, u32[]{:S(2)}) collective-permute-start(bf16[704,512]{1,0:T(8,128)(2,1)S(1)} %collective-permute-done.19.refs_4_), channel_id=1, source_target_pairs={{8,16},{16,8},{9,17},{17,9},{10,18},{18,10},{11,19},{19,11},{12,20... | collective-permute-start | bytes 2162696 | tf_op jit(solution)/shard_map/ppermute | solution.py:516
  129.4 26.2 %collective-permute-start.18 = (bf16[704,512]{1,0:T(8,128)(2,1)}, bf16[704,512]{1,0:T(8,128)(2,1)S(1)}, u32[]{:S(2)}, u32[]{:S(2)}) collective-permute-start(bf16[704,512]{1,0:T(8,128)(2,1)} %collective-permute-done.17.refs_8_.refs_20_), channel_id=1, source_target_pairs={{8,0},{16,24},{9,1},{17,25},{10,2},{18,26},{11,3},{19,27},{12,4},{... | collective-permute-start | bytes 2162696 | tf_op jit(solution)/shard_map/ppermute | solution.py:516
  130.7 40.5 %collective-permute-start.22 = (bf16[704,512]{1,0:T(8,128)(2,1)}, bf16[704,512]{1,0:T(8,128)(2,1)}, u32[]{:S(2)}, u32[]{:S(2)}) collective-permute-start(bf16[704,512]{1,0:T(8,128)(2,1)} %collective-permute-done.21.refs_6_), channel_id=1, source_target_pairs={{8,0},{16,24},{9,1},{17,25},{10,2},{18,26},{11,3},{19,27},{12,4},{... | collective-permute-start | bytes 2162696 | tf_op jit(solution)/shard_map/ppermute | solution.py:516
  145.6 1.1 copy-start.6
  155.6 1.3 copy-start.14
  155.6 26.7 %collective-permute-start.23 = (bf16[704,512]{1,0:T(8,128)(2,1)}, bf16[704,512]{1,0:T(8,128)(2,1)S(1)}, u32[]{:S(2)}, u32[]{:S(2)}) collective-permute-start(bf16[704,512]{1,0:T(8,128)(2,1)} %collective-permute-done.20.refs_10_.refs_6_), channel_id=1, source_target_pairs={{8,0},{16,24},{9,1},{17,25},{10,2},{18,26},{11,3},{19,27},{12,4},{... | collective-permute-start | bytes 2162696 | tf_op jit(solution)/shard_map/ppermute | solution.py:516
  177.1 18.4 %all-to-all-start.2 = ((bf16[8,40,1536]{2,1,0:T(8,128)(2,1)}), bf16[8,40,1536]{2,1,0:T(8,128)(2,1)S(1)}, u32[]{:S(2)}, u32[]{:S(2)}) async-start(bf16[8,40,1536]{2,1,0:T(8,128)(2,1)} %bitcast.52), calls=%async_computation.2 | async-start | bytes 1966080 | tf_op jit(solution)/shard_map/all_to_all | solution.py:538
  182.4 0.9 copy-start.16
  195.5 25.3 %copy-start = (bf16[1,128,2048]{2,1,0:T(8,128)(2,1)S(1)}, bf16[1,128,2048]{2,1,0:T(8,128)(2,1)}, u32[]{:S(2)}) copy-start(bf16[1,128,2048]{2,1,0:T(8,128)(2,1)} %param.22) | copy-start | bytes 1572868
  195.5 25.3 %copy-start.1 = (f32[1,128,2]{2,1,0:T(8,128)S(1)}, f32[1,128,2]{2,1,0:T(8,128)}, u32[]{:S(2)}) copy-start(f32[1,128,2]{2,1,0:T(8,128)} %copy.15) | copy-start | bytes 3076
  195.5 25.3 %copy-start.2 = (bf16[128,2048]{1,0:T(8,128)(2,1)S(1)}, bf16[128,2048]{1,0:T(8,128)(2,1)}, u32[]{:S(2)}) copy-start(bf16[128,2048]{1,0:T(8,128)(2,1)} %get-tuple-element.53.refs_4_) | copy-start | bytes 1572868
  195.5 25.3 %copy-start.3 = (f32[2048]{0:T(1024)S(1)}, f32[2048]{0:T(1024)}, u32[]{:S(2)}) copy-start(f32[2048]{0:T(1024)} %param.16) | copy-start | bytes 24580
  195.5 25.3 %copy-start.4 = (s32[10]{0:T(128)S(1)}, s32[10]{0:T(128)}, u32[]{:S(2)}) copy-start(s32[10]{0:T(128)} %dynamic-slice_bitcast_fusion.refs_0_) | copy-start | bytes 124
  (1 other events, 0.7 us)

commit v10 on v9

--- a/solution.py
+++ b/solution.py
@@ -394,17 +394,18 @@
     to_gate_ref[...] = up * to_gate_ref[...]
 
 
-def down_kernel(shape, place_ref, hidden_ref, cot_ref, *refs):
+def down_kernel(shape, first, place_ref, hidden_ref, cot_ref, *refs):
     slots = len(shape)
+    refs = list(refs)
+    total = refs.pop(0)[...] if first else None
     down_in, refs = regroup(refs, shape)
     out_ref, d_hidden_ref, down_w, sems = refs
     part = down_w.shape[2]
     inner = place_ref[INNER]
     for j in range(slots):
         fetch(inner, down_in[j], down_w.at[j], sems.at[j])
-    total = None
     for j in range(slots):
-        rows = cot_ref[:, cols_of(place_ref, j, part)]
+        rows = cot_ref[:, cols_of(place_ref, first + j, part)]
         arrived(down_in[j], down_w.at[j], sems.at[j])
         term = mm(rows, down_w[j], NT)
         total = term if total is None else total + term
@@ -465,15 +466,17 @@
     stream_ref,
     cot_ref,
     first_ref,
+    second_ref,
     last_ref,
     output_ref,
     grad_ref,
     d_normed_ref,
 ):
     tokens, width = stream_ref.shape
-    done = first_ref.shape[1]
+    done = first_ref.shape[1] + second_ref.shape[1]
     part = width - done
     slots = width // part
+    early = first_ref.shape[1] // part
     at0, at1 = slot_cols(ids_ref[...], owners, cap)
     rows = lax.broadcasted_iota(jnp.int32, (tokens, owners * cap), 1)
     pick0, pick1 = one_hot(rows == at0), one_hot(rows == at1)
@@ -483,8 +486,10 @@
     dot = jnp.zeros((tokens, 1), F32)
     for j in range(slots):
         cols = cols_of(place_ref, j, part)
-        if j < slots - 1:
+        if j < early:
             pairs = first_ref[:, j * part : (j + 1) * part]
+        elif j < slots - 1:
+            pairs = second_ref[:, (j - early) * part : (j - early + 1) * part]
         else:
             pairs = last_ref[:, width:]
         stream = stream_ref[:, cols].astype(F32)
@@ -628,19 +633,24 @@
         moved=2 * width * ffw + 2 * total * width + 14 * total * ffw,
         after=up_after,
     )
-    out_first, d_hidden = call(
-        functools.partial(down_kernel, shape[:-1]),
-        (sds((total, width - part)), sds((total, ffw), F32)),
-        (place, hidden, cot_rows, *flat(down_in[:-1])),
-        [SMEM, VMEM, VMEM] + [HBM] * sum(shape[:-1]),
-        [
-            pltpu.VMEM((groups - 1, ffw, part), BF),
-            pltpu.SemaphoreType.DMA((groups - 1,)),
-        ],
-        flops=2 * one * (groups - 1) // groups,
-        moved=2 * width * ffw + 4 * total * width + 6 * total * ffw,
-    )
-    back_first = exchange(out_first, owners, "exp")
+    d_hidden = ()
+    backs = []
+    early = groups // 2
+    for first, end in ((0, early), (early, groups - 1)):
+        here = shape[first:end]
+        out, d_hidden = call(
+            functools.partial(down_kernel, here, first),
+            (sds((total, len(here) * part)), sds((total, ffw), F32)),
+            (place, hidden, cot_rows, *([d_hidden] if first else []), *flat(down_in[first:end])),
+            [SMEM] + [VMEM] * (3 if first else 2) + [HBM] * sum(here),
+            [
+                pltpu.VMEM((len(here), ffw, part), BF),
+                pltpu.SemaphoreType.DMA((len(here),)),
+            ],
+            flops=2 * one * len(here) // groups,
+            moved=2 * width * ffw * len(here) // groups + 4 * total * width + 10 * total * ffw,
+        )
+        backs.append(exchange(out, owners, "exp"))
     back = call(
         functools.partial(grad_kernel, [*shape, shape[-1]]),
         sds((total, width + part)),
@@ -674,8 +684,8 @@
     output, stream_grad = call(
         functools.partial(final_kernel, owners, cap),
         (sds((tokens, width)), sds((tokens, width))),
-        (place, ids, weights, gain, stream, cot, back_first, back_last),
-        [SMEM] + [VMEM] * 7,
+        (place, ids, weights, gain, stream, cot, *backs, back_last),
+        [SMEM] + [VMEM] * 8,
         [pltpu.VMEM((tokens, width), F32)],
         flops=6 * total * tokens * width,
         moved=4 * total * width + 8 * tokens * width,

time: 225 us -> 231 us (1.027)
  blocking collectives: 25.3 us -> 36.7 us
  waiting for transfers between devices: 78.9 us -> 69.9 us
  Pallas kernels: 38.7 us -> 42.4 us
    all_to_all x1 -> x2, blocking collectives: 25.3 us -> 36.7 us  [exchange(): rows = lax.all_to_all(rows, axis, split_axis=0, concat_axis=0, tiled=True)]
    ppermute x24, waiting for transfers between devices: 60.8 us -> 54.1 us  [send(): return lax.ppermute(gated(array, *first), 'seq', pairs)]
    pallas_call x9 -> x10, Pallas kernels: 38.7 us -> 42.4 us  [call(): pl.pallas_call(body, grid=() if held else (1,), out_shape=outs, in_specs=...]
    all_to_all x3, waiting for transfers between devices: 18.1 us -> 15.8 us  [exchange(): rows = lax.all_to_all(rows, axis, split_axis=0, concat_axis=0, tiled=True)]
  transfers between devices with their start and end apart: 27 -> 27, of which waited for: 12 -> 11; matrix products, arithmetic and copies ran while one was open for 1% -> 1% of each run, Pallas kernels for 16% -> 17%
where the time goes in v10:
time: 231 us; the launch traced here: 230 us
  starting transfers between devices  73.2 us (32%)
  waiting for transfers between devices  69.9 us (30%)
  Pallas kernels  42.4 us (18%)
  blocking collectives  36.7 us (16%)
  local copies, waits for them, and re-layouts  6.74 us (3%)
    ppermute x24, starting transfers between devices, send(): return lax.ppermute(gated(array, *first), 'seq', pairs)  61.9 us
    ppermute x24, waiting for transfers between devices, send(): return lax.ppermute(gated(array, *first), 'seq', pairs)  54.1 us
    pallas_call x10, Pallas kernels, call(): pl.pallas_call(body, grid=() if held else (1,), out_shape=outs, in_specs=...  42.4 us
    all_to_all x2, blocking collectives, exchange(): rows = lax.all_to_all(rows, axis, split_axis=0, concat_axis=0, tiled=True)  36.7 us
    all_to_all x3, waiting for transfers between devices, exchange(): rows = lax.all_to_all(rows, axis, split_axis=0, concat_axis=0, tiled=True)  15.8 us
    all_to_all x3, starting transfers between devices, exchange(): rows = lax.all_to_all(rows, axis, split_axis=0, concat_axis=0, tiled=True)  11.3 us
    unnamed x46, local copies, waits for them, and re-layouts  4.9 us
  transfers between devices with their start and end apart: 27, of which 11 were waited for; matrix products, arithmetic and copies ran while one was open for 1% of the time, Pallas kernels for 17%

profile of v10, /device:TPU:0, one launch (start us, length us, event | category | flops | bytes accessed | tf_op | source)
XLA Modules:
  0.0 230.0 jit_solution(5012425137912641572)
XLA Ops:
  1.5 1.3 collective-permute-start.1
  2.8 1.2 dynamic-slice_bitcast_fusion.refs_0_
  4.0 2.6 %shard_map.131 = (bf16[384,1024]{1,0:T(8,128)(2,1)}, bf16[384,1024]{1,0:T(8,128)(2,1)}) custom-call(s32[10]{0:T(128)} %dynamic-slice_bitcast_fusion.refs_0_, bf16[128,2048]{1,0:T(8,128)(2,1)} %bitcast.56, bf16[128,2048]{1,0:T(8,128)(2,1)} %bitcast.57, bf16[128,2048]{1,0:T(8,128)(2,1)} %bitcast.58), custom_call_target="tpu_custom_call" | custom-call | bytes 3145728 | tf_op jit(solution)/shard_map/pallas_call | solution.py:35
  6.7 18.0 %collective-permute-done.1.refs_5_.refs_4_.refs_10_ = bf16[704,512]{1,0:T(8,128)(2,1)S(1)} collective-permute-done((bf16[704,512]{1,0:T(8,128)(2,1)}, bf16[704,512]{1,0:T(8,128)(2,1)S(1)}, u32[]{:S(2)}, u32[]{:S(2)}) %collective-permute-start.1) | collective-permute-done | bytes 720928 | tf_op jit(solution)/shard_map/ppermute | solution.py:521
  24.6 2.4 %collective-permute-start.2 = (bf16[384,1024]{1,0:T(8,128)(2,1)}, bf16[384,1024]{1,0:T(8,128)(2,1)}, u32[]{:S(2)}, u32[]{:S(2)}) collective-permute-start(bf16[384,1024]{1,0:T(8,128)(2,1)} %get-tuple-element.39.refs_1_), channel_id=1, source_target_pairs={{0,8},{24,16},{1,9},{25,17},{2,10},{26,18},{3,11},{27,19},{4,12},{... | collective-permute-start | bytes 2359304 | tf_op jit(solution)/shard_map/ppermute | solution.py:521
  27.1 1.6 collective-permute-start.3
  28.7 3.1 %collective-permute-start.4 = (bf16[384,1024]{1,0:T(8,128)(2,1)}, bf16[384,1024]{1,0:T(8,128)(2,1)}, u32[]{:S(2)}, u32[]{:S(2)}) collective-permute-start(bf16[384,1024]{1,0:T(8,128)(2,1)} %get-tuple-element.41), channel_id=1, source_target_pairs={{0,16},{24,8},{1,17},{25,9},{2,18},{26,10},{3,19},{27,11},{4,20},{... | collective-permute-start | bytes 2359304 | tf_op jit(solution)/shard_map/ppermute | solution.py:521
  31.8 1.3 collective-permute-start.5
  34.6 3.2 %shard_map.132 = bf16[320,2048]{1,0:T(8,128)(2,1)} custom-call(s32[2,128]{1,0:T(2,128)} %copy.17.refs_0_.refs_1_, f32[128,2]{1,0:T(8,128)} %bitcast.36, bf16[128,2048]{1,0:T(8,128)(2,1)} %bitcast.33), custom_call_target="tpu_custom_call" | custom-call | flops 335544320 | bytes 1835008 | tf_op jit(solution)/shard_map/pallas_call | solution.py:35
  37.7 3.9 %all-to-all-start = ((bf16[8,40,2048]{2,1,0:T(8,128)(2,1)}), bf16[8,40,2048]{2,1,0:T(8,128)(2,1)S(1)}, u32[]{:S(2)}, u32[]{:S(2)}) async-start(bf16[8,40,2048]{2,1,0:T(8,128)(2,1)} %bitcast.49), calls=%async_computation | async-start | bytes 2621440 | tf_op jit(solution)/shard_map/all_to_all | solution.py:543
  41.6 1.3 collective-permute-start.6
  42.9 1.6 collective-permute-done.2.refs_2_
  44.5 14.8 %collective-permute-done.4.refs_4_ = bf16[384,1024]{1,0:T(8,128)(2,1)} collective-permute-done((bf16[384,1024]{1,0:T(8,128)(2,1)}, bf16[384,1024]{1,0:T(8,128)(2,1)}, u32[]{:S(2)}, u32[]{:S(2)}) %collective-permute-start.4) | collective-permute-done | bytes 786464 | tf_op jit(solution)/shard_map/ppermute | solution.py:521
  59.3 1.5 collective-permute-start.9
  60.9 8.0 %collective-permute-start.7 = (bf16[704,512]{1,0:T(8,128)(2,1)S(1)}, bf16[704,512]{1,0:T(8,128)(2,1)}, u32[]{:S(2)}, u32[]{:S(2)}) collective-permute-start(bf16[704,512]{1,0:T(8,128)(2,1)S(1)} %bitcast.54), channel_id=1, source_target_pairs={{0,8},{24,16},{1,9},{25,17},{2,10},{26,18},{3,11},{27,19},{4,12},{... | collective-permute-start | bytes 2162696 | tf_op jit(solution)/shard_map/ppermute | solution.py:521
  68.9 1.3 collective-permute-start.8
  70.2 1.1 copy-done.5
  71.5 1.7 shard_map.133
  73.2 1.3 collective-permute-start.10
  74.5 13.3 %collective-permute-start.16 = (bf16[704,512]{1,0:T(8,128)(2,1)}, bf16[704,512]{1,0:T(8,128)(2,1)}, u32[]{:S(2)}, u32[]{:S(2)}) collective-permute-start(bf16[704,512]{1,0:T(8,128)(2,1)} %bitcast.13.refs_3_.refs_15_), channel_id=1, source_target_pairs={{0,8},{24,16},{1,9},{25,17},{2,10},{26,18},{3,11},{27,19},{4,12},{... | collective-permute-start | bytes 2162696 | tf_op jit(solution)/shard_map/ppermute | solution.py:521
  89.7 1.3 collective-permute-start.13
  91.0 10.1 %collective-permute-done.10.refs_7_.refs_19_ = bf16[704,512]{1,0:T(8,128)(2,1)S(1)} collective-permute-done((bf16[704,512]{1,0:T(8,128)(2,1)}, bf16[704,512]{1,0:T(8,128)(2,1)S(1)}, u32[]{:S(2)}, u32[]{:S(2)}) %collective-permute-start.10) | collective-permute-done | bytes 720928 | tf_op jit(solution)/shard_map/ppermute | solution.py:521
  101.1 1.3 collective-permute-start.11
  102.4 1.6 collective-permute-start.17
  104.0 11.0 %collective-permute-start.19 = (bf16[704,512]{1,0:T(8,128)(2,1)}, bf16[704,512]{1,0:T(8,128)(2,1)S(1)}, u32[]{:S(2)}, u32[]{:S(2)}) collective-permute-start(bf16[704,512]{1,0:T(8,128)(2,1)} %bitcast.17.refs_3_), channel_id=1, source_target_pairs={{0,8},{24,16},{1,9},{25,17},{2,10},{26,18},{3,11},{27,19},{4,12},{... | collective-permute-start | bytes 2162696 | tf_op jit(solution)/shard_map/ppermute | solution.py:521
  115.0 1.3 collective-permute-start.15
  116.3 1.8 collective-permute-done.13.refs_7_
  118.1 1.5 collective-permute-start.21
  120.4 3.3 %shard_map.134 = (bf16[128,2048]{1,0:T(8,128)(2,1)}, bf16[320,2048]{1,0:T(8,128)(2,1)}) custom-call(s32[10]{0:T(128)} %dynamic-slice_bitcast_fusion.refs_0_, s32[2,128]{1,0:T(2,128)} %copy.17.refs_0_.refs_1_, bf16[128,2048]{1,0:T(8,128)(2,1)} %bitcast.59, f32[1,2048]{1,0:T(1,128)} %bitcast.40, bf16[128,1024]{1,0:T(8,128)(2,1)} %get-tuple-element.48.refs_4_, ...), custom_call_target="tpu_custom_call" | custom-call | flops 167772160 | bytes 2883584 | tf_op jit(solution)/shard_map/pallas_call | solution.py:35
  123.7 3.7 %all-to-all-start.1 = ((bf16[8,40,2048]{2,1,0:T(8,128)(2,1)}), bf16[8,40,2048]{2,1,0:T(8,128)(2,1)S(1)}, u32[]{:S(2)}, u32[]{:S(2)}) async-start(bf16[8,40,2048]{2,1,0:T(8,128)(2,1)} %bitcast.55), calls=%async_computation.1 | async-start | bytes 2621440 | tf_op jit(solution)/shard_map/all_to_all | solution.py:543
  127.4 1.5 collective-permute-start.20
  129.4 1.3 collective-permute-start.18
  130.7 1.3 collective-permute-start.22
  132.0 13.6 %all-to-all-done.1 = bf16[8,40,2048]{2,1,0:T(8,128)(2,1)S(1)} async-done(((bf16[8,40,2048]{2,1,0:T(8,128)(2,1)}), bf16[8,40,2048]{2,1,0:T(8,128)(2,1)S(1)}, u32[]{:S(2)}, u32[]{:S(2)}) %all-to-all-start.1) | async-done | bytes 1310752 | tf_op jit(solution)/shard_map/all_to_all | solution.py:543
  145.6 1.1 copy-done.6
  146.7 5.2 %shard_map.135.refs_2_ = f32[320,704]{1,0:T(8,128)} custom-call(s32[10]{0:T(128)} %dynamic-slice_bitcast_fusion.refs_0_, bf16[320,2048]{1,0:T(8,128)(2,1)} %bitcast.46, bf16[704,512]{1,0:T(8,128)(2,1)} %bitcast.52, bf16[704,512]{1,0:T(8,128)(2,1)} %collective-permute-done.7.refs_3_.refs_9_, bf16[704,512]{1,0:T(8,128)(2,1)} %copy-done.7, ...), custom_call_target="tpu_custom_call" | custom-call | flops 922746880 | bytes 5095424 | tf_op jit(solution)/shard_map/pallas_call | solution.py:35
  151.9 3.7 %collective-permute-done.18.refs_9_.refs_21_ = bf16[704,512]{1,0:T(8,128)(2,1)S(1)} collective-permute-done((bf16[704,512]{1,0:T(8,128)(2,1)}, bf16[704,512]{1,0:T(8,128)(2,1)S(1)}, u32[]{:S(2)}, u32[]{:S(2)}) %collective-permute-start.18) | collective-permute-done | bytes 720928 | tf_op jit(solution)/shard_map/ppermute | solution.py:521
  155.6 1.3 collective-permute-start.23
  156.9 6.0 %shard_map.136 = (bf16[320,704]{1,0:T(8,128)(2,1)}, f32[320,704]{1,0:T(8,128)}, f32[320,704]{1,0:T(8,128)}) custom-call(s32[10]{0:T(128)} %dynamic-slice_bitcast_fusion.refs_0_, bf16[320,2048]{1,0:T(8,128)(2,1)} %bitcast.47, f32[320,704]{1,0:T(8,128)} %shard_map.135.refs_2_, bf16[704,512]{1,0:T(8,128)(2,1)} %bitcast.13.refs_3_.refs_15_, ...), custom_call_target="tpu_custom_call" | custom-call | flops 922746880 | bytes 7348224 | tf_op jit(solution)/shard_map/pallas_call | solution.py:35
  162.9 5.2 %shard_map.137 = (bf16[320,1024]{1,0:T(8,128)(2,1)}, f32[320,704]{1,0:T(8,128)}) custom-call(s32[10]{0:T(128)} %dynamic-slice_bitcast_fusion.refs_0_, bf16[320,704]{1,0:T(8,128)(2,1)} %get-tuple-element.62.refs_1_, bf16[320,2048]{1,0:T(8,128)(2,1)} %bitcast.43, bf16[704,512]{1,0:T(8,128)(2,1)} %bitcast.17.refs_3_, bf16[704,512]{1,0:T(8,128)(2,1)} %copy-done.15, ...), custom_call_target="tpu_custom_call" | custom-call | flops 922746880 | bytes 6316032 | tf_op jit(solution)/shard_map/pallas_call | solution.py:35
  168.1 3.1 %collective-permute-done.22.refs_5_ = bf16[704,512]{1,0:T(8,128)(2,1)} collective-permute-done((bf16[704,512]{1,0:T(8,128)(2,1)}, bf16[704,512]{1,0:T(8,128)(2,1)}, u32[]{:S(2)}, u32[]{:S(2)}) %collective-permute-start.22) | collective-permute-done | bytes 720928 | tf_op jit(solution)/shard_map/ppermute | solution.py:521
  171.2 4.4 %shard_map.138 = (bf16[320,512]{1,0:T(8,128)(2,1)}, f32[320,704]{1,0:T(8,128)}) custom-call(s32[10]{0:T(128)} %dynamic-slice_bitcast_fusion.refs_0_, bf16[320,704]{1,0:T(8,128)(2,1)} %get-tuple-element.62.refs_1_, bf16[320,2048]{1,0:T(8,128)(2,1)} %bitcast.44, f32[320,704]{1,0:T(8,128)} %get-tuple-element.64.refs_3_, ...), custom_call_target="tpu_custom_call" | custom-call | flops 461373440 | bytes 5595136 | tf_op jit(solution)/shard_map/pallas_call | solution.py:35
  175.6 11.4 %all_to_all.25 = bf16[8,40,512]{2,1,0:T(8,128)(2,1)S(1)} all-to-all(bf16[8,40,512]{2,1,0:T(8,128)(2,1)} %bitcast.60), channel_id=1, replica_groups=mesh['seq'=4,'exp'=8] {'exp'}, dimensions={0} | all-to-all | bytes 655360 | tf_op jit(solution)/shard_map/all_to_all | solution.py:543
  186.9 3.7 %all-to-all-start.2 = ((bf16[8,40,1024]{2,1,0:T(8,128)(2,1)}), bf16[8,40,1024]{2,1,0:T(8,128)(2,1)S(1)}, u32[]{:S(2)}, u32[]{:S(2)}) async-start(bf16[8,40,1024]{2,1,0:T(8,128)(2,1)} %bitcast.21), calls=%async_computation.2 | async-start | bytes 1310720 | tf_op jit(solution)/shard_map/all_to_all | solution.py:543
  191.6 7.8 %shard_map.139 = bf16[320,2560]{1,0:T(8,128)(2,1)} custom-call(s32[10]{0:T(128)} %dynamic-slice_bitcast_fusion.refs_0_, bf16[320,704]{1,0:T(8,128)(2,1)} %get-tuple-element.62.refs_1_, bf16[320,2048]{1,0:T(8,128)(2,1)} %bitcast.45, f32[320,704]{1,0:T(8,128)} %get-tuple-element.68.refs_3_, f32[320,704]{1,0:T(8,128)} %get-tuple-element.69.refs_4_, ...), custom_call_target="tpu_custom_call" | custom-call | flops 2306867200 | bytes 11542528 | tf_op jit(solution)/shard_map/pallas_call | solution.py:35
  199.4 2.2 all-to-all-done.2
  201.6 25.3 %all_to_all.26 = bf16[8,40,2560]{2,1,0:T(8,128)(2,1)S(1)} all-to-all(bf16[8,40,2560]{2,1,0:T(8,128)(2,1)} %bitcast.48), channel_id=1, replica_groups=mesh['seq'=4,'exp'=8] {'exp'}, dimensions={0} | all-to-all | bytes 3276800 | tf_op jit(solution)/shard_map/all_to_all | solution.py:543
  226.9 3.1 %shard_map.140 = (bf16[128,2048]{1,0:T(8,128)(2,1)}, bf16[128,2048]{1,0:T(8,128)(2,1)}) custom-call(s32[10]{0:T(128)S(1)} %copy-done.3, s32[128,2]{1,0:T(8,128)S(1)} %bitcast.39, f32[128,2]{1,0:T(8,128)S(1)} %bitcast.37, f32[1,2048]{1,0:T(1,128)S(1)} %bitcast.41, bf16[128,2048]{1,0:T(8,128)(2,1)S(1)} %copy-done.2, bf16[128,2048]{1,0:T(8,128)(2,1)S(1)} %bitcast.34, ...), custom_call_target="tpu_custom_call" | custom-call | flops 503316480 | bytes 4718592 | tf_op jit(solution)/shard_map/pallas_call | solution.py:35
  (66 shorter events, 6.6 us)
Async XLA Ops:
  0.6 32.5 %copy-start.20 = (s32[1,128,2]{1,2,0:T(2,128)S(1)}, s32[1,128,2]{1,2,0:T(2,128)}, u32[]{:S(2)}) copy-start(s32[1,128,2]{1,2,0:T(2,128)} %param.20) | copy-start | bytes 3076
  0.6 32.6 %copy-start.21 = (f32[1,128,2]{1,2,0:T(2,128)S(1)}, f32[1,128,2]{1,2,0:T(2,128)}, u32[]{:S(2)}) copy-start(f32[1,128,2]{1,2,0:T(2,128)} %param.21) | copy-start | bytes 3076
  0.6 6.0 %collective-permute-start = (bf16[704,512]{1,0:T(8,128)(2,1)}, bf16[704,512]{1,0:T(8,128)(2,1)S(1)}, u32[]{:S(2)}, u32[]{:S(2)}) collective-permute-start(bf16[704,512]{1,0:T(8,128)(2,1)} %bitcast.50), channel_id=1, source_target_pairs={{8,16},{16,8},{9,17},{17,9},{10,18},{18,10},{11,19},{19,11},{12,20... | collective-permute-start | bytes 2162696 | tf_op jit(solution)/shard_map/ppermute | solution.py:521
  1.5 23.1 %collective-permute-start.1 = (bf16[704,512]{1,0:T(8,128)(2,1)}, bf16[704,512]{1,0:T(8,128)(2,1)S(1)}, u32[]{:S(2)}, u32[]{:S(2)}) collective-permute-start(bf16[704,512]{1,0:T(8,128)(2,1)} %bitcast.51), channel_id=1, source_target_pairs={{8,0},{16,24},{9,1},{17,25},{10,2},{18,26},{11,3},{19,27},{12,4},{... | collective-permute-start | bytes 2162696 | tf_op jit(solution)/shard_map/ppermute | solution.py:521
  6.7 25.1 %copy-start.12 = (bf16[704,512]{1,0:T(8,128)(2,1)}, bf16[704,512]{1,0:T(8,128)(2,1)S(1)}, u32[]{:S(2)}) copy-start(bf16[704,512]{1,0:T(8,128)(2,1)S(1)} %collective-permute-done.refs_5_.refs_11_) | copy-start | bytes 2162692
  24.6 13.1 %copy-start.7 = (bf16[704,512]{1,0:T(8,128)(2,1)}, bf16[704,512]{1,0:T(8,128)(2,1)S(1)}, u32[]{:S(2)}) copy-start(bf16[704,512]{1,0:T(8,128)(2,1)S(1)} %collective-permute-done.1.refs_5_.refs_4_.refs_10_) | copy-start | bytes 2162692
  24.6 19.8 %collective-permute-start.2 = (bf16[384,1024]{1,0:T(8,128)(2,1)}, bf16[384,1024]{1,0:T(8,128)(2,1)}, u32[]{:S(2)}, u32[]{:S(2)}) collective-permute-start(bf16[384,1024]{1,0:T(8,128)(2,1)} %get-tuple-element.39.refs_1_), channel_id=1, source_target_pairs={{0,8},{24,16},{1,9},{25,17},{2,10},{26,18},{3,11},{27,19},{4,12},{... | collective-permute-start | bytes 2359304 | tf_op jit(solution)/shard_map/ppermute | solution.py:521
  27.1 17.4 %collective-permute-start.3 = (bf16[384,1024]{1,0:T(8,128)(2,1)}, bf16[384,1024]{1,0:T(8,128)(2,1)}, u32[]{:S(2)}, u32[]{:S(2)}) collective-permute-start(bf16[384,1024]{1,0:T(8,128)(2,1)} %get-tuple-element.41), channel_id=1, source_target_pairs={{8,16},{16,8},{9,17},{17,9},{10,18},{18,10},{11,19},{19,11},{12,20... | collective-permute-start | bytes 2359304 | tf_op jit(solution)/shard_map/ppermute | solution.py:521
  28.7 30.6 %collective-permute-start.4 = (bf16[384,1024]{1,0:T(8,128)(2,1)}, bf16[384,1024]{1,0:T(8,128)(2,1)}, u32[]{:S(2)}, u32[]{:S(2)}) collective-permute-start(bf16[384,1024]{1,0:T(8,128)(2,1)} %get-tuple-element.41), channel_id=1, source_target_pairs={{0,16},{24,8},{1,17},{25,9},{2,18},{26,10},{3,19},{27,11},{4,20},{... | collective-permute-start | bytes 2359304 | tf_op jit(solution)/shard_map/ppermute | solution.py:521
  31.8 29.0 %collective-permute-start.5 = (bf16[704,512]{1,0:T(8,128)(2,1)}, bf16[704,512]{1,0:T(8,128)(2,1)S(1)}, u32[]{:S(2)}, u32[]{:S(2)}) collective-permute-start(bf16[704,512]{1,0:T(8,128)(2,1)} %bitcast.13.refs_3_.refs_15_), channel_id=1, source_target_pairs={{8,0},{16,24},{9,1},{17,25},{10,2},{18,26},{11,3},{19,27},{12,4},{... | collective-permute-start | bytes 2162696 | tf_op jit(solution)/shard_map/ppermute | solution.py:521
  37.7 23.1 %copy-start.11 = (bf16[1,512,704]{1,2,0:T(8,128)(2,1)S(1)}, bf16[1,512,704]{1,2,0:T(8,128)(2,1)}, u32[]{:S(2)}) copy-start(bf16[1,512,704]{1,2,0:T(8,128)(2,1)} %param.17) | copy-start | bytes 2162692
  37.7 32.4 %all-to-all-start = ((bf16[8,40,2048]{2,1,0:T(8,128)(2,1)}), bf16[8,40,2048]{2,1,0:T(8,128)(2,1)S(1)}, u32[]{:S(2)}, u32[]{:S(2)}) async-start(bf16[8,40,2048]{2,1,0:T(8,128)(2,1)} %bitcast.49), calls=%async_computation | async-start | bytes 2621440 | tf_op jit(solution)/shard_map/all_to_all | solution.py:543
  41.6 28.6 %collective-permute-start.6 = (bf16[704,512]{1,0:T(8,128)(2,1)}, bf16[704,512]{1,0:T(8,128)(2,1)S(1)}, u32[]{:S(2)}, u32[]{:S(2)}) collective-permute-start(bf16[704,512]{1,0:T(8,128)(2,1)} %copy-done.12), channel_id=1, source_target_pairs={{8,0},{16,24},{9,1},{17,25},{10,2},{18,26},{11,3},{19,27},{12,4},{... | collective-permute-start | bytes 2162696 | tf_op jit(solution)/shard_map/ppermute | solution.py:521
  59.3 13.8 %collective-permute-start.9 = (bf16[704,512]{1,0:T(8,128)(2,1)}, bf16[704,512]{1,0:T(8,128)(2,1)}, u32[]{:S(2)}, u32[]{:S(2)}) collective-permute-start(bf16[704,512]{1,0:T(8,128)(2,1)} %bitcast.13.refs_3_.refs_15_), channel_id=1, source_target_pairs={{8,16},{16,8},{9,17},{17,9},{10,18},{18,10},{11,19},{19,11},{12,20... | collective-permute-start | bytes 2162696 | tf_op jit(solution)/shard_map/ppermute | solution.py:521
  60.9 9.3 %copy-start.8 = (bf16[704,512]{1,0:T(8,128)(2,1)}, bf16[704,512]{1,0:T(8,128)(2,1)S(1)}, u32[]{:S(2)}) copy-start(bf16[704,512]{1,0:T(8,128)(2,1)S(1)} %collective-permute-done.5.refs_6_.refs_5_.refs_17_) | copy-start | bytes 2162692
  60.9 26.9 %collective-permute-start.7 = (bf16[704,512]{1,0:T(8,128)(2,1)S(1)}, bf16[704,512]{1,0:T(8,128)(2,1)}, u32[]{:S(2)}, u32[]{:S(2)}) collective-permute-start(bf16[704,512]{1,0:T(8,128)(2,1)S(1)} %bitcast.54), channel_id=1, source_target_pairs={{0,8},{24,16},{1,9},{25,17},{2,10},{26,18},{3,11},{27,19},{4,12},{... | collective-permute-start | bytes 2162696 | tf_op jit(solution)/shard_map/ppermute | solution.py:521
  68.9 20.2 %collective-permute-start.8 = (bf16[704,512]{1,0:T(8,128)(2,1)}, bf16[704,512]{1,0:T(8,128)(2,1)}, u32[]{:S(2)}, u32[]{:S(2)}) collective-permute-start(bf16[704,512]{1,0:T(8,128)(2,1)} %bitcast.17.refs_3_), channel_id=1, source_target_pairs={{8,0},{16,24},{9,1},{17,25},{10,2},{18,26},{11,3},{19,27},{12,4},{... | collective-permute-start | bytes 2162696 | tf_op jit(solution)/shard_map/ppermute | solution.py:521
  70.2 1.1 copy-start.5
  70.2 1.3 copy-start.9
  73.2 27.9 %collective-permute-start.10 = (bf16[704,512]{1,0:T(8,128)(2,1)}, bf16[704,512]{1,0:T(8,128)(2,1)S(1)}, u32[]{:S(2)}, u32[]{:S(2)}) collective-permute-start(bf16[704,512]{1,0:T(8,128)(2,1)} %collective-permute-done.9.refs_6_.refs_18_), channel_id=1, source_target_pairs={{8,0},{16,24},{9,1},{17,25},{10,2},{18,26},{11,3},{19,27},{12,4},{... | collective-permute-start | bytes 2162696 | tf_op jit(solution)/shard_map/ppermute | solution.py:521
  74.5 27.9 %collective-permute-start.16 = (bf16[704,512]{1,0:T(8,128)(2,1)}, bf16[704,512]{1,0:T(8,128)(2,1)}, u32[]{:S(2)}, u32[]{:S(2)}) collective-permute-start(bf16[704,512]{1,0:T(8,128)(2,1)} %bitcast.13.refs_3_.refs_15_), channel_id=1, source_target_pairs={{0,8},{24,16},{1,9},{25,17},{2,10},{26,18},{3,11},{27,19},{4,12},{... | collective-permute-start | bytes 2162696 | tf_op jit(solution)/shard_map/ppermute | solution.py:521
  87.7 27.3 %collective-permute-start.14 = (bf16[704,512]{1,0:T(8,128)(2,1)}, bf16[704,512]{1,0:T(8,128)(2,1)S(1)}, u32[]{:S(2)}, u32[]{:S(2)}) collective-permute-start(bf16[704,512]{1,0:T(8,128)(2,1)} %collective-permute-done.7.refs_3_.refs_9_), channel_id=1, source_target_pairs={{8,16},{16,8},{9,17},{17,9},{10,18},{18,10},{11,19},{19,11},{12,20... | collective-permute-start | bytes 2162696 | tf_op jit(solution)/shard_map/ppermute | solution.py:521
  89.0 15.0 %collective-permute-start.12 = (bf16[128,1024]{1,0:T(8,128)(2,1)}, bf16[128,1024]{1,0:T(8,128)(2,1)S(1)}, u32[]{:S(2)}, u32[]{:S(2)}) collective-permute-start(bf16[128,1024]{1,0:T(8,128)(2,1)} %get-tuple-element.53), channel_id=1, source_target_pairs={{8,16},{16,8},{9,17},{17,9},{10,18},{18,10},{11,19},{19,11},{12,20... | collective-permute-start | bytes 786440 | tf_op jit(solution)/shard_map/ppermute | solution.py:521
  89.7 28.4 %collective-permute-start.13 = (bf16[128,1024]{1,0:T(8,128)(2,1)}, bf16[128,1024]{1,0:T(8,128)(2,1)S(1)}, u32[]{:S(2)}, u32[]{:S(2)}) collective-permute-start(bf16[128,1024]{1,0:T(8,128)(2,1)} %get-tuple-element.54), channel_id=1, source_target_pairs={{16,0},{8,24},{17,1},{9,25},{18,2},{10,26},{19,3},{11,27},{20,4},{... | collective-permute-start | bytes 786440 | tf_op jit(solution)/shard_map/ppermute | solution.py:521
  101.1 50.8 %copy-start.13 = (bf16[704,512]{1,0:T(8,128)(2,1)}, bf16[704,512]{1,0:T(8,128)(2,1)S(1)}, u32[]{:S(2)}) copy-start(bf16[704,512]{1,0:T(8,128)(2,1)S(1)} %collective-permute-done.10.refs_7_.refs_19_) | copy-start | bytes 2162692
  101.1 18.6 %collective-permute-start.11 = (bf16[128,1024]{1,0:T(8,128)(2,1)}, bf16[128,1024]{1,0:T(8,128)(2,1)S(1)}, u32[]{:S(2)}, u32[]{:S(2)}) collective-permute-start(bf16[128,1024]{1,0:T(8,128)(2,1)} %get-tuple-element.52), channel_id=1, source_target_pairs={{8,0},{16,24},{9,1},{17,25},{10,2},{18,26},{11,3},{19,27},{12,4},{... | collective-permute-start | bytes 786440 | tf_op jit(solution)/shard_map/ppermute | solution.py:521
  102.4 25.0 %collective-permute-start.17 = (bf16[704,512]{1,0:T(8,128)(2,1)}, bf16[704,512]{1,0:T(8,128)(2,1)}, u32[]{:S(2)}, u32[]{:S(2)}) collective-permute-start(bf16[704,512]{1,0:T(8,128)(2,1)} %collective-permute-done.16.refs_4_.refs_16_), channel_id=1, source_target_pairs={{8,16},{16,8},{9,17},{17,9},{10,18},{18,10},{11,19},{19,11},{12,20... | collective-permute-start | bytes 2162696 | tf_op jit(solution)/shard_map/ppermute | solution.py:521
  104.0 15.7 %copy-start.17 = (bf16[128,1024]{1,0:T(8,128)(2,1)}, bf16[128,1024]{1,0:T(8,128)(2,1)S(1)}, u32[]{:S(2)}) copy-start(bf16[128,1024]{1,0:T(8,128)(2,1)S(1)} %collective-permute-done.12.refs_6_) | copy-start | bytes 786436
  104.0 23.4 %collective-permute-start.19 = (bf16[704,512]{1,0:T(8,128)(2,1)}, bf16[704,512]{1,0:T(8,128)(2,1)S(1)}, u32[]{:S(2)}, u32[]{:S(2)}) collective-permute-start(bf16[704,512]{1,0:T(8,128)(2,1)} %bitcast.17.refs_3_), channel_id=1, source_target_pairs={{0,8},{24,16},{1,9},{25,17},{2,10},{26,18},{3,11},{27,19},{4,12},{... | collective-permute-start | bytes 2162696 | tf_op jit(solution)/shard_map/ppermute | solution.py:521
  115.0 4.7 %copy-start.10 = (bf16[704,512]{1,0:T(8,128)(2,1)}, bf16[704,512]{1,0:T(8,128)(2,1)S(1)}, u32[]{:S(2)}) copy-start(bf16[704,512]{1,0:T(8,128)(2,1)S(1)} %collective-permute-done.14.refs_8_.refs_7_.refs_13_) | copy-start | bytes 2162692
  115.0 14.4 %collective-permute-start.15 = (bf16[704,512]{1,0:T(8,128)(2,1)S(1)}, bf16[704,512]{1,0:T(8,128)(2,1)}, u32[]{:S(2)}, u32[]{:S(2)}) collective-permute-start(bf16[704,512]{1,0:T(8,128)(2,1)S(1)} %collective-permute-done.14.refs_8_.refs_7_.refs_13_), channel_id=1, source_target_pairs={{8,0},{16,24},{9,1},{17,25},{10,2},{18,26},{11,3},{19,27},{12,4},{... | collective-permute-start | bytes 2162696 | tf_op jit(solution)/shard_map/ppermute | solution.py:521
  118.1 1.6 copy-start.18
  118.1 12.6 %collective-permute-start.21 = (bf16[704,512]{1,0:T(8,128)(2,1)}, bf16[704,512]{1,0:T(8,128)(2,1)}, u32[]{:S(2)}, u32[]{:S(2)}) collective-permute-start(bf16[704,512]{1,0:T(8,128)(2,1)} %bitcast.17.refs_3_), channel_id=1, source_target_pairs={{8,16},{16,8},{9,17},{17,9},{10,18},{18,10},{11,19},{19,11},{12,20... | collective-permute-start | bytes 2162696 | tf_op jit(solution)/shard_map/ppermute | solution.py:521
  123.7 21.9 %all-to-all-start.1 = ((bf16[8,40,2048]{2,1,0:T(8,128)(2,1)}), bf16[8,40,2048]{2,1,0:T(8,128)(2,1)S(1)}, u32[]{:S(2)}, u32[]{:S(2)}) async-start(bf16[8,40,2048]{2,1,0:T(8,128)(2,1)} %bitcast.55), calls=%async_computation.1 | async-start | bytes 2621440 | tf_op jit(solution)/shard_map/all_to_all | solution.py:543
  127.4 35.5 %copy-start.15 = (bf16[704,512]{1,0:T(8,128)(2,1)}, bf16[704,512]{1,0:T(8,128)(2,1)S(1)}, u32[]{:S(2)}) copy-start(bf16[704,512]{1,0:T(8,128)(2,1)S(1)} %collective-permute-done.19.refs_4_) | copy-start | bytes 2162692
  127.4 24.5 %collective-permute-start.20 = (bf16[704,512]{1,0:T(8,128)(2,1)S(1)}, bf16[704,512]{1,0:T(8,128)(2,1)}, u32[]{:S(2)}, u32[]{:S(2)}) collective-permute-start(bf16[704,512]{1,0:T(8,128)(2,1)S(1)} %collective-permute-done.19.refs_4_), channel_id=1, source_target_pairs={{8,16},{16,8},{9,17},{17,9},{10,18},{18,10},{11,19},{19,11},{12,20... | collective-permute-start | bytes 2162696 | tf_op jit(solution)/shard_map/ppermute | solution.py:521
  129.4 26.2 %collective-permute-start.18 = (bf16[704,512]{1,0:T(8,128)(2,1)}, bf16[704,512]{1,0:T(8,128)(2,1)S(1)}, u32[]{:S(2)}, u32[]{:S(2)}) collective-permute-start(bf16[704,512]{1,0:T(8,128)(2,1)} %collective-permute-done.17.refs_8_.refs_20_), channel_id=1, source_target_pairs={{8,0},{16,24},{9,1},{17,25},{10,2},{18,26},{11,3},{19,27},{12,4},{... | collective-permute-start | bytes 2162696 | tf_op jit(solution)/shard_map/ppermute | solution.py:521
  130.7 40.5 %collective-permute-start.22 = (bf16[704,512]{1,0:T(8,128)(2,1)}, bf16[704,512]{1,0:T(8,128)(2,1)}, u32[]{:S(2)}, u32[]{:S(2)}) collective-permute-start(bf16[704,512]{1,0:T(8,128)(2,1)} %collective-permute-done.21.refs_4_), channel_id=1, source_target_pairs={{8,0},{16,24},{9,1},{17,25},{10,2},{18,26},{11,3},{19,27},{12,4},{... | collective-permute-start | bytes 2162696 | tf_op jit(solution)/shard_map/ppermute | solution.py:521
  145.6 1.1 copy-start.6
  155.6 1.3 copy-start.14
  155.6 35.1 %collective-permute-start.23 = (bf16[704,512]{1,0:T(8,128)(2,1)}, bf16[704,512]{1,0:T(8,128)(2,1)S(1)}, u32[]{:S(2)}, u32[]{:S(2)}) collective-permute-start(bf16[704,512]{1,0:T(8,128)(2,1)} %collective-permute-done.20.refs_10_.refs_6_), channel_id=1, source_target_pairs={{8,0},{16,24},{9,1},{17,25},{10,2},{18,26},{11,3},{19,27},{12,4},{... | collective-permute-start | bytes 2162696 | tf_op jit(solution)/shard_map/ppermute | solution.py:521
  186.9 14.6 %all-to-all-start.2 = ((bf16[8,40,1024]{2,1,0:T(8,128)(2,1)}), bf16[8,40,1024]{2,1,0:T(8,128)(2,1)S(1)}, u32[]{:S(2)}, u32[]{:S(2)}) async-start(bf16[8,40,1024]{2,1,0:T(8,128)(2,1)} %bitcast.21), calls=%async_computation.2 | async-start | bytes 1310720 | tf_op jit(solution)/shard_map/all_to_all | solution.py:543
  190.7 0.9 copy-start.16
  201.6 25.3 %copy-start = (bf16[1,128,2048]{2,1,0:T(8,128)(2,1)S(1)}, bf16[1,128,2048]{2,1,0:T(8,128)(2,1)}, u32[]{:S(2)}) copy-start(bf16[1,128,2048]{2,1,0:T(8,128)(2,1)} %param.22) | copy-start | bytes 1572868
  201.6 25.3 %copy-start.1 = (f32[1,128,2]{2,1,0:T(8,128)S(1)}, f32[1,128,2]{2,1,0:T(8,128)}, u32[]{:S(2)}) copy-start(f32[1,128,2]{2,1,0:T(8,128)} %copy.15) | copy-start | bytes 3076
  201.6 25.3 %copy-start.2 = (bf16[128,2048]{1,0:T(8,128)(2,1)S(1)}, bf16[128,2048]{1,0:T(8,128)(2,1)}, u32[]{:S(2)}) copy-start(bf16[128,2048]{1,0:T(8,128)(2,1)} %get-tuple-element.55.refs_4_) | copy-start | bytes 1572868
  201.6 25.3 %copy-start.3 = (s32[10]{0:T(128)S(1)}, s32[10]{0:T(128)}, u32[]{:S(2)}) copy-start(s32[10]{0:T(128)} %dynamic-slice_bitcast_fusion.refs_0_) | copy-start | bytes 124
  201.6 25.4 %copy-start.4 = (f32[2048]{0:T(1024)S(1)}, f32[2048]{0:T(1024)}, u32[]{:S(2)}) copy-start(f32[2048]{0:T(1024)} %param.16) | copy-start | bytes 24580
  (1 other events, 0.7 us)

commit v11 on v9

--- a/solution.py
+++ b/solution.py
@@ -413,25 +413,28 @@
 
 
 def grad_kernel(
-    shape, place_ref, hidden_in, cot_in, d_hidden_in, to_gate_in, to_up_in, *refs
+    shape, late, place_ref, hidden_in, cot_in, d_hidden_in, to_gate_in, to_up_in, *refs
 ):
-    slots = len(shape) - 1
-    down_in, refs = regroup(refs, shape[-1:])
-    gate_in, refs = regroup(refs, shape[:-1])
-    up_in, refs = regroup(refs, shape[:-1])
+    slots = len(shape)
+    down_in, refs = regroup(refs, shape[slots - late :])
+    gate_in, refs = regroup(refs, shape)
+    up_in, refs = regroup(refs, shape)
     o_ref, down_w, gate_w, up_w, sems = refs[:5]
     hidden_ref, cot_ref, d_hidden_ref, to_gate_ref, to_up_ref = refs[5:]
-    part = down_w.shape[1]
+    part = down_w.shape[2]
     inner = place_ref[INNER]
-    last = place_ref[COLS + cot_in.shape[1] // part - 1]
     pairs = [
-        (cot_in.at[:, pl.ds(pl.multiple_of(last * part, part), part)], cot_ref),
+        (cot_in.at[:, cols_of(place_ref, slots - late + j, part)], cot_ref.at[j])
+        for j in range(late)
+    ]
+    pairs += [
         (d_hidden_in, d_hidden_ref),
         (to_gate_in, to_gate_ref),
         (to_up_in, to_up_ref),
         (hidden_in, hidden_ref),
     ]
-    fetch(inner, down_in[0], down_w, sems.at[2, 0])
+    for j in range(late):
+        fetch(inner, down_in[j], down_w.at[j], sems.at[2, j])
     copies = [
         pltpu.make_async_copy(src, dst, sems.at[3 + i, 0]) for i, (src, dst) in enumerate(pairs)
     ]
@@ -440,13 +443,19 @@
     for j in range(slots):
         fetch(inner, gate_in[j], gate_w.at[j], sems.at[0, j])
         fetch(inner, up_in[j], up_w.at[j], sems.at[1, j])
-    arrived(down_in[0], down_w, sems.at[2, 0])
+    for j in range(late):
+        arrived(down_in[j], down_w.at[j], sems.at[2, j])
     for copy in copies:
         copy.wait()
-    d_hidden = d_hidden_ref[...] + mm(cot_ref[...], down_w[...], NT)
+    d_hidden = d_hidden_ref[...]
+    for j in range(late):
+        d_hidden = d_hidden + mm(cot_ref[j], down_w[j], NT)
     d_gate = (d_hidden * to_gate_ref[...]).astype(BF)
     d_up = (d_hidden * to_up_ref[...]).astype(BF)
-    o_ref[:, slots * part :] = mm(hidden_ref[...], down_w[...], NN).astype(BF)
+    for j in range(late):
+        o_ref[:, (slots + j) * part : (slots + j + 1) * part] = mm(
+            hidden_ref[...], down_w[j], NN
+        ).astype(BF)
     for j in range(slots):
         arrived(gate_in[j], gate_w.at[j], sems.at[0, j])
         arrived(up_in[j], up_w.at[j], sems.at[1, j])
@@ -458,6 +467,7 @@
 def final_kernel(
     owners,
     cap,
+    slots,
     place_ref,
     ids_ref,
     w_ref,
@@ -471,9 +481,8 @@
     d_normed_ref,
 ):
     tokens, width = stream_ref.shape
-    done = first_ref.shape[1]
-    part = width - done
-    slots = width // part
+    part = width // slots
+    early = slots // 2
     at0, at1 = slot_cols(ids_ref[...], owners, cap)
     rows = lax.broadcasted_iota(jnp.int32, (tokens, owners * cap), 1)
     pick0, pick1 = one_hot(rows == at0), one_hot(rows == at1)
@@ -483,10 +492,11 @@
     dot = jnp.zeros((tokens, 1), F32)
     for j in range(slots):
         cols = cols_of(place_ref, j, part)
-        if j < slots - 1:
+        if j < early:
             pairs = first_ref[:, j * part : (j + 1) * part]
         else:
-            pairs = last_ref[:, width:]
+            at = width + (j - early) * part
+            pairs = last_ref[:, at : at + part]
         stream = stream_ref[:, cols].astype(F32)
         mixed = w0 * mm(pick0, pairs, NN) + w1 * mm(pick1, pairs, NN)
         output_ref[:, cols] = (stream + mixed).astype(BF)
@@ -628,22 +638,21 @@
         moved=2 * width * ffw + 2 * total * width + 14 * total * ffw,
         after=up_after,
     )
+    early = groups // 2
+    late = groups - early
     out_first, d_hidden = call(
-        functools.partial(down_kernel, shape[:-1]),
-        (sds((total, width - part)), sds((total, ffw), F32)),
-        (place, hidden, cot_rows, *flat(down_in[:-1])),
-        [SMEM, VMEM, VMEM] + [HBM] * sum(shape[:-1]),
-        [
-            pltpu.VMEM((groups - 1, ffw, part), BF),
-            pltpu.SemaphoreType.DMA((groups - 1,)),
-        ],
-        flops=2 * one * (groups - 1) // groups,
-        moved=2 * width * ffw + 4 * total * width + 6 * total * ffw,
+        functools.partial(down_kernel, shape[:early]),
+        (sds((total, early * part)), sds((total, ffw), F32)),
+        (place, hidden, cot_rows, *flat(down_in[:early])),
+        [SMEM, VMEM, VMEM] + [HBM] * sum(shape[:early]),
+        [pltpu.VMEM((early, ffw, part), BF), pltpu.SemaphoreType.DMA((early,))],
+        flops=2 * one * early // groups,
+        moved=width * ffw + 3 * total * width + 6 * total * ffw,
     )
     back_first = exchange(out_first, owners, "exp")
     back = call(
-        functools.partial(grad_kernel, [*shape, shape[-1]]),
-        sds((total, width + part)),
+        functools.partial(grad_kernel, shape, late),
+        sds((total, width + late * part)),
         (
             place,
             hidden,
@@ -651,28 +660,28 @@
             d_hidden,
             to_gate,
             to_up,
-            *flat(down_in[-1:]),
+            *flat(down_in[early:]),
             *flat(gate_in),
             *flat(up_in),
         ),
-        [SMEM] + [HBM] * (5 + shape[-1] + 2 * sum(shape)),
+        [SMEM] + [HBM] * (5 + sum(shape[early:]) + 2 * sum(shape)),
         [
-            pltpu.VMEM((ffw, part), BF),
+            pltpu.VMEM((late, ffw, part), BF),
             full_w,
             full_w,
-            pltpu.SemaphoreType.DMA((8, groups)),
+            pltpu.SemaphoreType.DMA((7 + late, groups)),
             pltpu.VMEM((total, ffw), BF),
-            pltpu.VMEM((total, part), BF),
+            pltpu.VMEM((late, total, part), BF),
             pltpu.VMEM((total, ffw), F32),
             pltpu.VMEM((total, ffw), F32),
             pltpu.VMEM((total, ffw), F32),
         ],
-        flops=2 * one + 2 * one // groups,
-        moved=4 * width * ffw + 4 * total * width + 14 * total * ffw,
+        flops=2 * one + 2 * one * late // groups,
+        moved=5 * width * ffw + 4 * total * width + 14 * total * ffw,
     )
     back_last = exchange(back, owners, "exp")
     output, stream_grad = call(
-        functools.partial(final_kernel, owners, cap),
+        functools.partial(final_kernel, owners, cap, groups),
         (sds((tokens, width)), sds((tokens, width))),
         (place, ids, weights, gain, stream, cot, back_first, back_last),
         [SMEM] + [VMEM] * 7,

time: 225 us -> 250 us (1.11)
  the two profiles are of different devices: /device:TPU:0 before, /device:TPU:8 now
where the time goes in v11:
time: 250 us; the launch traced here: 249 us
  waiting for transfers between devices  90.3 us (36%)
  starting transfers between devices  75.8 us (30%)
  Pallas kernels  45.8 us (18%)
  blocking collectives  28.8 us (12%)
  local copies, waits for them, and re-layouts  6.77 us (3%)
    ppermute x24, waiting for transfers between devices, send(): return lax.ppermute(gated(array, *first), 'seq', pairs)  87.9 us
    ppermute x24, starting transfers between devices, send(): return lax.ppermute(gated(array, *first), 'seq', pairs)  64.4 us
    pallas_call x9, Pallas kernels, call(): pl.pallas_call(body, grid=() if held else (1,), out_shape=outs, in_specs=...  45.8 us
    all_to_all x1, blocking collectives, exchange(): rows = lax.all_to_all(rows, axis, split_axis=0, concat_axis=0, tiled=True)  28.8 us
    all_to_all x3, starting transfers between devices, exchange(): rows = lax.all_to_all(rows, axis, split_axis=0, concat_axis=0, tiled=True)  11.4 us
  transfers between devices with their start and end apart: 27, of which 13 were waited for; matrix products, arithmetic and copies ran while one was open for 1% of the time, Pallas kernels for 17%

profile of v11, /device:TPU:8, one launch (start us, length us, event | category | flops | bytes accessed | tf_op | source)
XLA Modules:
  0.0 248.6 jit_solution(6485591467266778407)
XLA Ops:
  0.6 3.6 %collective-permute-start = (bf16[704,512]{1,0:T(8,128)(2,1)}, bf16[704,512]{1,0:T(8,128)(2,1)S(1)}, u32[]{:S(2)}, u32[]{:S(2)}) collective-permute-start(bf16[704,512]{1,0:T(8,128)(2,1)} %bitcast.46), channel_id=1, source_target_pairs={{8,16},{16,8},{9,17},{17,9},{10,18},{18,10},{11,19},{19,11},{12,20... | collective-permute-start | bytes 2162696 | tf_op jit(solution)/shard_map/ppermute | solution.py:526
  4.3 1.3 collective-permute-start.1
  6.9 2.6 %shard_map.131 = (bf16[384,1024]{1,0:T(8,128)(2,1)}, bf16[384,1024]{1,0:T(8,128)(2,1)}) custom-call(s32[10]{0:T(128)} %dynamic-slice_bitcast_fusion.refs_0_, bf16[128,2048]{1,0:T(8,128)(2,1)} %bitcast.53, bf16[128,2048]{1,0:T(8,128)(2,1)} %bitcast.54, bf16[128,2048]{1,0:T(8,128)(2,1)} %bitcast.55), custom_call_target="tpu_custom_call" | custom-call | bytes 3145728 | tf_op jit(solution)/shard_map/pallas_call | solution.py:35
  9.5 11.3 %collective-permute-done.refs_5_.refs_13_ = bf16[704,512]{1,0:T(8,128)(2,1)S(1)} collective-permute-done((bf16[704,512]{1,0:T(8,128)(2,1)}, bf16[704,512]{1,0:T(8,128)(2,1)S(1)}, u32[]{:S(2)}, u32[]{:S(2)}) %collective-permute-start) | collective-permute-done | bytes 720928 | tf_op jit(solution)/shard_map/ppermute | solution.py:526
  21.3 1.3 collective-permute-start.2
  22.6 1.3 collective-permute-start.4
  23.9 6.4 %collective-permute-start.5 = (bf16[704,512]{1,0:T(8,128)(2,1)}, bf16[704,512]{1,0:T(8,128)(2,1)S(1)}, u32[]{:S(2)}, u32[]{:S(2)}) collective-permute-start(bf16[704,512]{1,0:T(8,128)(2,1)} %bitcast.13.refs_3_.refs_17_), channel_id=1, source_target_pairs={{8,0},{16,24},{9,1},{17,25},{10,2},{18,26},{11,3},{19,27},{12,4},{... | collective-permute-start | bytes 2162696 | tf_op jit(solution)/shard_map/ppermute | solution.py:526
  30.3 3.0 %collective-permute-start.3 = (bf16[384,1024]{1,0:T(8,128)(2,1)}, bf16[384,1024]{1,0:T(8,128)(2,1)}, u32[]{:S(2)}, u32[]{:S(2)}) collective-permute-start(bf16[384,1024]{1,0:T(8,128)(2,1)} %get-tuple-element.39), channel_id=1, source_target_pairs={{8,16},{16,8},{9,17},{17,9},{10,18},{18,10},{11,19},{19,11},{12,20... | collective-permute-start | bytes 2359304 | tf_op jit(solution)/shard_map/ppermute | solution.py:526
  34.8 3.2 %shard_map.132 = bf16[320,2048]{1,0:T(8,128)(2,1)} custom-call(s32[2,128]{1,0:T(2,128)} %copy.17.refs_0_.refs_1_, f32[128,2]{1,0:T(8,128)} %bitcast.33, bf16[128,2048]{1,0:T(8,128)(2,1)} %bitcast.31), custom_call_target="tpu_custom_call" | custom-call | flops 335544320 | bytes 1835008 | tf_op jit(solution)/shard_map/pallas_call | solution.py:35
  38.0 3.8 %all-to-all-start = ((bf16[8,40,2048]{2,1,0:T(8,128)(2,1)}), bf16[8,40,2048]{2,1,0:T(8,128)(2,1)S(1)}, u32[]{:S(2)}, u32[]{:S(2)}) async-start(bf16[8,40,2048]{2,1,0:T(8,128)(2,1)} %bitcast.45), calls=%async_computation | async-start | bytes 2621440 | tf_op jit(solution)/shard_map/all_to_all | solution.py:548
  41.8 2.9 %collective-permute-done.5.refs_6_.refs_5_.refs_19_ = bf16[704,512]{1,0:T(8,128)(2,1)S(1)} collective-permute-done((bf16[704,512]{1,0:T(8,128)(2,1)}, bf16[704,512]{1,0:T(8,128)(2,1)S(1)}, u32[]{:S(2)}, u32[]{:S(2)}) %collective-permute-start.5) | collective-permute-done | bytes 720928 | tf_op jit(solution)/shard_map/ppermute | solution.py:526
  44.8 14.6 %collective-permute-done.4.refs_4_ = bf16[384,1024]{1,0:T(8,128)(2,1)} collective-permute-done((bf16[384,1024]{1,0:T(8,128)(2,1)}, bf16[384,1024]{1,0:T(8,128)(2,1)}, u32[]{:S(2)}, u32[]{:S(2)}) %collective-permute-start.4) | collective-permute-done | bytes 786464 | tf_op jit(solution)/shard_map/ppermute | solution.py:526
  59.4 1.3 collective-permute-start.7
  60.7 5.4 %collective-permute-start.6 = (bf16[704,512]{1,0:T(8,128)(2,1)}, bf16[704,512]{1,0:T(8,128)(2,1)S(1)}, u32[]{:S(2)}, u32[]{:S(2)}) collective-permute-start(bf16[704,512]{1,0:T(8,128)(2,1)} %copy-done.11), channel_id=1, source_target_pairs={{8,0},{16,24},{9,1},{17,25},{10,2},{18,26},{11,3},{19,27},{12,4},{... | collective-permute-start | bytes 2162696 | tf_op jit(solution)/shard_map/ppermute | solution.py:526
  67.2 3.0 %collective-permute-start.9 = (bf16[704,512]{1,0:T(8,128)(2,1)}, bf16[704,512]{1,0:T(8,128)(2,1)}, u32[]{:S(2)}, u32[]{:S(2)}) collective-permute-start(bf16[704,512]{1,0:T(8,128)(2,1)} %bitcast.13.refs_3_.refs_17_), channel_id=1, source_target_pairs={{8,16},{16,8},{9,17},{17,9},{10,18},{18,10},{11,19},{19,11},{12,20... | collective-permute-start | bytes 2162696 | tf_op jit(solution)/shard_map/ppermute | solution.py:526
  70.2 2.2 collective-permute-start.8
  72.4 1.3 collective-permute-start.16
  73.7 6.6 %collective-permute-done.7.refs_3_.refs_11_ = bf16[704,512]{1,0:T(8,128)(2,1)} collective-permute-done((bf16[704,512]{1,0:T(8,128)(2,1)S(1)}, bf16[704,512]{1,0:T(8,128)(2,1)}, u32[]{:S(2)}, u32[]{:S(2)}) %collective-permute-start.7) | collective-permute-done | bytes 720928 | tf_op jit(solution)/shard_map/ppermute | solution.py:526
  80.3 2.9 %collective-permute-start.14 = (bf16[704,512]{1,0:T(8,128)(2,1)}, bf16[704,512]{1,0:T(8,128)(2,1)}, u32[]{:S(2)}, u32[]{:S(2)}) collective-permute-start(bf16[704,512]{1,0:T(8,128)(2,1)} %collective-permute-done.7.refs_3_.refs_11_), channel_id=1, source_target_pairs={{8,16},{16,8},{9,17},{17,9},{10,18},{18,10},{11,19},{19,11},{12,20... | collective-permute-start | bytes 2162696 | tf_op jit(solution)/shard_map/ppermute | solution.py:526
  84.5 8.5 %shard_map.133 = (bf16[128,1024]{1,0:T(8,128)(2,1)}, bf16[128,1024]{1,0:T(8,128)(2,1)}, bf16[128,1024]{1,0:T(8,128)(2,1)}, bf16[128,1024]{1,0:T(8,128)(2,1)}) custom-call(s32[10]{0:T(128)} %dynamic-slice_bitcast_fusion.refs_0_, bf16[384,1024]{1,0:T(8,128)(2,1)} %get-tuple-element.37.refs_1_, bf16[384,1024]{1,0:T(8,128)(2,1)} %collective-permute-done.2.refs_2_, ...), custom_call_target="tpu_custom_call" | custom-call | flops 1073741824 | bytes 4194304 | tf_op jit(solution)/shard_map/pallas_call | solution.py:35
  93.0 1.3 collective-permute-start.10
  94.4 4.0 %collective-permute-done.8.refs_5_ = bf16[704,512]{1,0:T(8,128)(2,1)} collective-permute-done((bf16[704,512]{1,0:T(8,128)(2,1)}, bf16[704,512]{1,0:T(8,128)(2,1)}, u32[]{:S(2)}, u32[]{:S(2)}) %collective-permute-start.8) | collective-permute-done | bytes 720928 | tf_op jit(solution)/shard_map/ppermute | solution.py:526
  98.4 2.9 %collective-permute-start.12 = (bf16[128,1024]{1,0:T(8,128)(2,1)}, bf16[128,1024]{1,0:T(8,128)(2,1)S(1)}, u32[]{:S(2)}, u32[]{:S(2)}) collective-permute-start(bf16[128,1024]{1,0:T(8,128)(2,1)} %get-tuple-element.51), channel_id=1, source_target_pairs={{8,16},{16,8},{9,17},{17,9},{10,18},{18,10},{11,19},{19,11},{12,20... | collective-permute-start | bytes 786440 | tf_op jit(solution)/shard_map/ppermute | solution.py:526
  101.3 3.0 %collective-permute-start.17 = (bf16[704,512]{1,0:T(8,128)(2,1)}, bf16[704,512]{1,0:T(8,128)(2,1)S(1)}, u32[]{:S(2)}, u32[]{:S(2)}) collective-permute-start(bf16[704,512]{1,0:T(8,128)(2,1)} %collective-permute-done.16.refs_4_.refs_18_), channel_id=1, source_target_pairs={{8,16},{16,8},{9,17},{17,9},{10,18},{18,10},{11,19},{19,11},{12,20... | collective-permute-start | bytes 2162696 | tf_op jit(solution)/shard_map/ppermute | solution.py:526
  104.3 1.3 collective-permute-start.19
  105.6 5.4 %collective-permute-start.15 = (bf16[704,512]{1,0:T(8,128)(2,1)}, bf16[704,512]{1,0:T(8,128)(2,1)S(1)}, u32[]{:S(2)}, u32[]{:S(2)}) collective-permute-start(bf16[704,512]{1,0:T(8,128)(2,1)} %collective-permute-done.14.refs_8_.refs_7_.refs_15_), channel_id=1, source_target_pairs={{8,0},{16,24},{9,1},{17,25},{10,2},{18,26},{11,3},{19,27},{12,4},{... | collective-permute-start | bytes 2162696 | tf_op jit(solution)/shard_map/ppermute | solution.py:526
  111.0 2.8 %collective-permute-done.10.refs_7_.refs_21_ = bf16[704,512]{1,0:T(8,128)(2,1)S(1)} collective-permute-done((bf16[704,512]{1,0:T(8,128)(2,1)}, bf16[704,512]{1,0:T(8,128)(2,1)S(1)}, u32[]{:S(2)}, u32[]{:S(2)}) %collective-permute-start.10) | collective-permute-done | bytes 720928 | tf_op jit(solution)/shard_map/ppermute | solution.py:526
  113.8 4.7 %collective-permute-start.13 = (bf16[128,1024]{1,0:T(8,128)(2,1)}, bf16[128,1024]{1,0:T(8,128)(2,1)S(1)}, u32[]{:S(2)}, u32[]{:S(2)}) collective-permute-start(bf16[128,1024]{1,0:T(8,128)(2,1)} %get-tuple-element.52), channel_id=1, source_target_pairs={{16,0},{8,24},{17,1},{9,25},{18,2},{10,26},{19,3},{11,27},{20,4},{... | collective-permute-start | bytes 786440 | tf_op jit(solution)/shard_map/ppermute | solution.py:526
  118.6 1.3 collective-permute-start.11
  119.9 5.8 %collective-permute-done.13.refs_7_ = bf16[128,1024]{1,0:T(8,128)(2,1)S(1)} collective-permute-done((bf16[128,1024]{1,0:T(8,128)(2,1)}, bf16[128,1024]{1,0:T(8,128)(2,1)S(1)}, u32[]{:S(2)}, u32[]{:S(2)}) %collective-permute-start.13) | collective-permute-done | bytes 262176 | tf_op jit(solution)/shard_map/ppermute | solution.py:526
  125.7 11.5 %collective-permute-done.11.refs_5_ = bf16[128,1024]{1,0:T(8,128)(2,1)S(1)} collective-permute-done((bf16[128,1024]{1,0:T(8,128)(2,1)}, bf16[128,1024]{1,0:T(8,128)(2,1)S(1)}, u32[]{:S(2)}, u32[]{:S(2)}) %collective-permute-start.11) | collective-permute-done | bytes 262176 | tf_op jit(solution)/shard_map/ppermute | solution.py:526
  137.9 3.3 %shard_map.134 = (bf16[128,2048]{1,0:T(8,128)(2,1)}, bf16[320,2048]{1,0:T(8,128)(2,1)}) custom-call(s32[10]{0:T(128)} %dynamic-slice_bitcast_fusion.refs_0_, s32[2,128]{1,0:T(2,128)} %copy.17.refs_0_.refs_1_, bf16[128,2048]{1,0:T(8,128)(2,1)} %bitcast.56, f32[1,2048]{1,0:T(1,128)} %bitcast.37, bf16[128,1024]{1,0:T(8,128)(2,1)} %get-tuple-element.46.refs_4_, ...), custom_call_target="tpu_custom_call" | custom-call | flops 167772160 | bytes 2883584 | tf_op jit(solution)/shard_map/pallas_call | solution.py:35
  141.2 3.7 %all-to-all-start.1 = ((bf16[8,40,2048]{2,1,0:T(8,128)(2,1)}), bf16[8,40,2048]{2,1,0:T(8,128)(2,1)S(1)}, u32[]{:S(2)}, u32[]{:S(2)}) async-start(bf16[8,40,2048]{2,1,0:T(8,128)(2,1)} %bitcast.51), calls=%async_computation.1 | async-start | bytes 2621440 | tf_op jit(solution)/shard_map/all_to_all | solution.py:548
  144.9 2.9 %collective-permute-start.21 = (bf16[704,512]{1,0:T(8,128)(2,1)}, bf16[704,512]{1,0:T(8,128)(2,1)}, u32[]{:S(2)}, u32[]{:S(2)}) collective-permute-start(bf16[704,512]{1,0:T(8,128)(2,1)} %bitcast.17.refs_3_), channel_id=1, source_target_pairs={{8,16},{16,8},{9,17},{17,9},{10,18},{18,10},{11,19},{19,11},{12,20... | collective-permute-start | bytes 2162696 | tf_op jit(solution)/shard_map/ppermute | solution.py:526
  147.8 3.0 %collective-permute-start.20 = (bf16[704,512]{1,0:T(8,128)(2,1)}, bf16[704,512]{1,0:T(8,128)(2,1)S(1)}, u32[]{:S(2)}, u32[]{:S(2)}) collective-permute-start(bf16[704,512]{1,0:T(8,128)(2,1)} %collective-permute-done.19.refs_4_), channel_id=1, source_target_pairs={{8,16},{16,8},{9,17},{17,9},{10,18},{18,10},{11,19},{19,11},{12,20... | collective-permute-start | bytes 2162696 | tf_op jit(solution)/shard_map/ppermute | solution.py:526
  150.8 1.3 collective-permute-start.18
  152.1 13.9 %collective-permute-done.21.refs_6_ = bf16[704,512]{1,0:T(8,128)(2,1)} collective-permute-done((bf16[704,512]{1,0:T(8,128)(2,1)}, bf16[704,512]{1,0:T(8,128)(2,1)}, u32[]{:S(2)}, u32[]{:S(2)}) %collective-permute-start.21) | collective-permute-done | bytes 720928 | tf_op jit(solution)/shard_map/ppermute | solution.py:526
  166.1 2.2 collective-permute-start.22
  168.2 12.8 %collective-permute-done.20.refs_10_.refs_8_ = bf16[704,512]{1,0:T(8,128)(2,1)S(1)} collective-permute-done((bf16[704,512]{1,0:T(8,128)(2,1)}, bf16[704,512]{1,0:T(8,128)(2,1)S(1)}, u32[]{:S(2)}, u32[]{:S(2)}) %collective-permute-start.20) | collective-permute-done | bytes 720928 | tf_op jit(solution)/shard_map/ppermute | solution.py:526
  181.9 2.2 collective-permute-start.23
  185.2 5.2 %shard_map.135.refs_2_ = f32[320,704]{1,0:T(8,128)} custom-call(s32[10]{0:T(128)} %dynamic-slice_bitcast_fusion.refs_0_, bf16[320,2048]{1,0:T(8,128)(2,1)} %bitcast.42, bf16[704,512]{1,0:T(8,128)(2,1)} %bitcast.48, bf16[704,512]{1,0:T(8,128)(2,1)} %collective-permute-done.7.refs_3_.refs_11_, bf16[704,512]{1,0:T(8,128)(2,1)} %copy-done.7, ...), custom_call_target="tpu_custom_call" | custom-call | flops 922746880 | bytes 5095424 | tf_op jit(solution)/shard_map/pallas_call | solution.py:35
  190.4 6.0 %shard_map.136 = (bf16[320,704]{1,0:T(8,128)(2,1)}, f32[320,704]{1,0:T(8,128)}, f32[320,704]{1,0:T(8,128)}) custom-call(s32[10]{0:T(128)} %dynamic-slice_bitcast_fusion.refs_0_, bf16[320,2048]{1,0:T(8,128)(2,1)} %bitcast.43, f32[320,704]{1,0:T(8,128)} %shard_map.135.refs_2_, bf16[704,512]{1,0:T(8,128)(2,1)} %bitcast.13.refs_3_.refs_17_, ...), custom_call_target="tpu_custom_call" | custom-call | flops 922746880 | bytes 7348224 | tf_op jit(solution)/shard_map/pallas_call | solution.py:35
  196.4 5.2 %shard_map.137 = (bf16[320,1024]{1,0:T(8,128)(2,1)}, f32[320,704]{1,0:T(8,128)}) custom-call(s32[10]{0:T(128)} %dynamic-slice_bitcast_fusion.refs_0_, bf16[320,704]{1,0:T(8,128)(2,1)} %get-tuple-element.60.refs_1_, bf16[320,2048]{1,0:T(8,128)(2,1)} %bitcast.40, bf16[704,512]{1,0:T(8,128)(2,1)} %bitcast.17.refs_3_, ...), custom_call_target="tpu_custom_call" | custom-call | flops 922746880 | bytes 4759552 | tf_op jit(solution)/shard_map/pallas_call | solution.py:35
  201.6 3.9 %all-to-all-start.2 = ((bf16[8,40,1024]{2,1,0:T(8,128)(2,1)}), bf16[8,40,1024]{2,1,0:T(8,128)(2,1)S(1)}, u32[]{:S(2)}, u32[]{:S(2)}) async-start(bf16[8,40,1024]{2,1,0:T(8,128)(2,1)} %bitcast.52), calls=%async_computation.2 | async-start | bytes 1310720 | tf_op jit(solution)/shard_map/all_to_all | solution.py:548
  205.5 8.7 %shard_map.138 = bf16[320,3072]{1,0:T(8,128)(2,1)} custom-call(s32[10]{0:T(128)} %dynamic-slice_bitcast_fusion.refs_0_, bf16[320,704]{1,0:T(8,128)(2,1)} %get-tuple-element.60.refs_1_, bf16[320,2048]{1,0:T(8,128)(2,1)} %bitcast.41, f32[320,704]{1,0:T(8,128)} %get-tuple-element.62.refs_3_, f32[320,704]{1,0:T(8,128)} %get-tuple-element.63.refs_4_, ...), custom_call_target="tpu_custom_call" | custom-call | flops 2768240640 | bytes 12984320 | tf_op jit(solution)/shard_map/pallas_call | solution.py:35
  214.2 2.4 all-to-all-done.2
  216.6 28.8 %all_to_all.20 = bf16[8,40,3072]{2,1,0:T(8,128)(2,1)S(1)} all-to-all(bf16[8,40,3072]{2,1,0:T(8,128)(2,1)} %bitcast.44), channel_id=1, replica_groups=mesh['seq'=4,'exp'=8] {'exp'}, dimensions={0} | all-to-all | bytes 3932160 | tf_op jit(solution)/shard_map/all_to_all | solution.py:548
  245.5 3.1 %shard_map.139 = (bf16[128,2048]{1,0:T(8,128)(2,1)}, bf16[128,2048]{1,0:T(8,128)(2,1)}) custom-call(s32[10]{0:T(128)S(1)} %copy-done.4, s32[128,2]{1,0:T(8,128)S(1)} %bitcast.36, f32[128,2]{1,0:T(8,128)S(1)} %bitcast.34, f32[1,2048]{1,0:T(1,128)S(1)} %bitcast.38, bf16[128,2048]{1,0:T(8,128)(2,1)S(1)} %copy-done.2, bf16[128,2048]{1,0:T(8,128)(2,1)S(1)} %bitcast.32, ...), custom_call_target="tpu_custom_call" | custom-call | flops 503316480 | bytes 4718592 | tf_op jit(solution)/shard_map/pallas_call | solution.py:35
  (64 shorter events, 8.4 us)
Async XLA Ops:
  0.6 32.6 %copy-start.20 = (s32[1,128,2]{1,2,0:T(2,128)S(1)}, s32[1,128,2]{1,2,0:T(2,128)}, u32[]{:S(2)}) copy-start(s32[1,128,2]{1,2,0:T(2,128)} %param.20) | copy-start | bytes 3076
  0.6 32.7 %copy-start.21 = (f32[1,128,2]{1,2,0:T(2,128)S(1)}, f32[1,128,2]{1,2,0:T(2,128)}, u32[]{:S(2)}) copy-start(f32[1,128,2]{1,2,0:T(2,128)} %param.21) | copy-start | bytes 3076
  0.6 20.1 %collective-permute-start = (bf16[704,512]{1,0:T(8,128)(2,1)}, bf16[704,512]{1,0:T(8,128)(2,1)S(1)}, u32[]{:S(2)}, u32[]{:S(2)}) collective-permute-start(bf16[704,512]{1,0:T(8,128)(2,1)} %bitcast.46), channel_id=1, source_target_pairs={{8,16},{16,8},{9,17},{17,9},{10,18},{18,10},{11,19},{19,11},{12,20... | collective-permute-start | bytes 2162696 | tf_op jit(solution)/shard_map/ppermute | solution.py:526
  4.3 17.0 %collective-permute-start.1 = (bf16[704,512]{1,0:T(8,128)(2,1)}, bf16[704,512]{1,0:T(8,128)(2,1)S(1)}, u32[]{:S(2)}, u32[]{:S(2)}) collective-permute-start(bf16[704,512]{1,0:T(8,128)(2,1)} %bitcast.47), channel_id=1, source_target_pairs={{8,0},{16,24},{9,1},{17,25},{10,2},{18,26},{11,3},{19,27},{12,4},{... | collective-permute-start | bytes 2162696 | tf_op jit(solution)/shard_map/ppermute | solution.py:526
  20.8 3.1 %copy-start.11 = (bf16[704,512]{1,0:T(8,128)(2,1)}, bf16[704,512]{1,0:T(8,128)(2,1)S(1)}, u32[]{:S(2)}) copy-start(bf16[704,512]{1,0:T(8,128)(2,1)S(1)} %collective-permute-done.refs_5_.refs_13_) | copy-start | bytes 2162692
  21.3 16.7 %copy-start.7 = (bf16[704,512]{1,0:T(8,128)(2,1)}, bf16[704,512]{1,0:T(8,128)(2,1)S(1)}, u32[]{:S(2)}) copy-start(bf16[704,512]{1,0:T(8,128)(2,1)S(1)} %collective-permute-done.1.refs_5_.refs_4_.refs_12_) | copy-start | bytes 2162692
  21.3 23.5 %collective-permute-start.2 = (bf16[384,1024]{1,0:T(8,128)(2,1)}, bf16[384,1024]{1,0:T(8,128)(2,1)}, u32[]{:S(2)}, u32[]{:S(2)}) collective-permute-start(bf16[384,1024]{1,0:T(8,128)(2,1)} %get-tuple-element.37.refs_1_), channel_id=1, source_target_pairs={{0,8},{24,16},{1,9},{25,17},{2,10},{26,18},{3,11},{27,19},{4,12},{... | collective-permute-start | bytes 2359304 | tf_op jit(solution)/shard_map/ppermute | solution.py:526
  22.6 36.8 %collective-permute-start.4 = (bf16[384,1024]{1,0:T(8,128)(2,1)}, bf16[384,1024]{1,0:T(8,128)(2,1)}, u32[]{:S(2)}, u32[]{:S(2)}) collective-permute-start(bf16[384,1024]{1,0:T(8,128)(2,1)} %get-tuple-element.39), channel_id=1, source_target_pairs={{0,16},{24,8},{1,17},{25,9},{2,18},{26,10},{3,19},{27,11},{4,20},{... | collective-permute-start | bytes 2359304 | tf_op jit(solution)/shard_map/ppermute | solution.py:526
  23.9 20.9 %collective-permute-start.5 = (bf16[704,512]{1,0:T(8,128)(2,1)}, bf16[704,512]{1,0:T(8,128)(2,1)S(1)}, u32[]{:S(2)}, u32[]{:S(2)}) collective-permute-start(bf16[704,512]{1,0:T(8,128)(2,1)} %bitcast.13.refs_3_.refs_17_), channel_id=1, source_target_pairs={{8,0},{16,24},{9,1},{17,25},{10,2},{18,26},{11,3},{19,27},{12,4},{... | collective-permute-start | bytes 2162696 | tf_op jit(solution)/shard_map/ppermute | solution.py:526
  30.3 36.9 %collective-permute-start.3 = (bf16[384,1024]{1,0:T(8,128)(2,1)}, bf16[384,1024]{1,0:T(8,128)(2,1)}, u32[]{:S(2)}, u32[]{:S(2)}) collective-permute-start(bf16[384,1024]{1,0:T(8,128)(2,1)} %get-tuple-element.39), channel_id=1, source_target_pairs={{8,16},{16,8},{9,17},{17,9},{10,18},{18,10},{11,19},{19,11},{12,20... | collective-permute-start | bytes 2359304 | tf_op jit(solution)/shard_map/ppermute | solution.py:526
  38.0 21.4 %copy-start.10 = (bf16[1,512,704]{1,2,0:T(8,128)(2,1)S(1)}, bf16[1,512,704]{1,2,0:T(8,128)(2,1)}, u32[]{:S(2)}) copy-start(bf16[1,512,704]{1,2,0:T(8,128)(2,1)} %param.17) | copy-start | bytes 2162692
  38.0 45.2 %all-to-all-start = ((bf16[8,40,2048]{2,1,0:T(8,128)(2,1)}), bf16[8,40,2048]{2,1,0:T(8,128)(2,1)S(1)}, u32[]{:S(2)}, u32[]{:S(2)}) async-start(bf16[8,40,2048]{2,1,0:T(8,128)(2,1)} %bitcast.45), calls=%async_computation | async-start | bytes 2621440 | tf_op jit(solution)/shard_map/all_to_all | solution.py:548
  44.8 38.4 %copy-start.8 = (bf16[704,512]{1,0:T(8,128)(2,1)}, bf16[704,512]{1,0:T(8,128)(2,1)S(1)}, u32[]{:S(2)}) copy-start(bf16[704,512]{1,0:T(8,128)(2,1)S(1)} %collective-permute-done.5.refs_6_.refs_5_.refs_19_) | copy-start | bytes 2162692
  59.4 20.9 %collective-permute-start.7 = (bf16[704,512]{1,0:T(8,128)(2,1)S(1)}, bf16[704,512]{1,0:T(8,128)(2,1)}, u32[]{:S(2)}, u32[]{:S(2)}) collective-permute-start(bf16[704,512]{1,0:T(8,128)(2,1)S(1)} %bitcast.50), channel_id=1, source_target_pairs={{0,8},{24,16},{1,9},{25,17},{2,10},{26,18},{3,11},{27,19},{4,12},{... | collective-permute-start | bytes 2162696 | tf_op jit(solution)/shard_map/ppermute | solution.py:526
  60.7 22.5 %collective-permute-start.6 = (bf16[704,512]{1,0:T(8,128)(2,1)}, bf16[704,512]{1,0:T(8,128)(2,1)S(1)}, u32[]{:S(2)}, u32[]{:S(2)}) collective-permute-start(bf16[704,512]{1,0:T(8,128)(2,1)} %copy-done.11), channel_id=1, source_target_pairs={{8,0},{16,24},{9,1},{17,25},{10,2},{18,26},{11,3},{19,27},{12,4},{... | collective-permute-start | bytes 2162696 | tf_op jit(solution)/shard_map/ppermute | solution.py:526
  67.2 25.8 %collective-permute-start.9 = (bf16[704,512]{1,0:T(8,128)(2,1)}, bf16[704,512]{1,0:T(8,128)(2,1)}, u32[]{:S(2)}, u32[]{:S(2)}) collective-permute-start(bf16[704,512]{1,0:T(8,128)(2,1)} %bitcast.13.refs_3_.refs_17_), channel_id=1, source_target_pairs={{8,16},{16,8},{9,17},{17,9},{10,18},{18,10},{11,19},{19,11},{12,20... | collective-permute-start | bytes 2162696 | tf_op jit(solution)/shard_map/ppermute | solution.py:526
  70.2 28.2 %collective-permute-start.8 = (bf16[704,512]{1,0:T(8,128)(2,1)}, bf16[704,512]{1,0:T(8,128)(2,1)}, u32[]{:S(2)}, u32[]{:S(2)}) collective-permute-start(bf16[704,512]{1,0:T(8,128)(2,1)} %bitcast.17.refs_3_), channel_id=1, source_target_pairs={{8,0},{16,24},{9,1},{17,25},{10,2},{18,26},{11,3},{19,27},{12,4},{... | collective-permute-start | bytes 2162696 | tf_op jit(solution)/shard_map/ppermute | solution.py:526
  72.4 28.9 %collective-permute-start.16 = (bf16[704,512]{1,0:T(8,128)(2,1)}, bf16[704,512]{1,0:T(8,128)(2,1)}, u32[]{:S(2)}, u32[]{:S(2)}) collective-permute-start(bf16[704,512]{1,0:T(8,128)(2,1)} %bitcast.13.refs_3_.refs_17_), channel_id=1, source_target_pairs={{0,8},{24,16},{1,9},{25,17},{2,10},{26,18},{3,11},{27,19},{4,12},{... | collective-permute-start | bytes 2162696 | tf_op jit(solution)/shard_map/ppermute | solution.py:526
  80.3 25.3 %collective-permute-start.14 = (bf16[704,512]{1,0:T(8,128)(2,1)}, bf16[704,512]{1,0:T(8,128)(2,1)}, u32[]{:S(2)}, u32[]{:S(2)}) collective-permute-start(bf16[704,512]{1,0:T(8,128)(2,1)} %collective-permute-done.7.refs_3_.refs_11_), channel_id=1, source_target_pairs={{8,16},{16,8},{9,17},{17,9},{10,18},{18,10},{11,19},{19,11},{12,20... | collective-permute-start | bytes 2162696 | tf_op jit(solution)/shard_map/ppermute | solution.py:526
  83.2 1.1 copy-start.5
  83.2 1.3 copy-start.9
  93.0 20.8 %collective-permute-start.10 = (bf16[704,512]{1,0:T(8,128)(2,1)}, bf16[704,512]{1,0:T(8,128)(2,1)S(1)}, u32[]{:S(2)}, u32[]{:S(2)}) collective-permute-start(bf16[704,512]{1,0:T(8,128)(2,1)} %collective-permute-done.9.refs_6_.refs_20_), channel_id=1, source_target_pairs={{8,0},{16,24},{9,1},{17,25},{10,2},{18,26},{11,3},{19,27},{12,4},{... | collective-permute-start | bytes 2162696 | tf_op jit(solution)/shard_map/ppermute | solution.py:526
  98.4 20.1 %collective-permute-start.12 = (bf16[128,1024]{1,0:T(8,128)(2,1)}, bf16[128,1024]{1,0:T(8,128)(2,1)S(1)}, u32[]{:S(2)}, u32[]{:S(2)}) collective-permute-start(bf16[128,1024]{1,0:T(8,128)(2,1)} %get-tuple-element.51), channel_id=1, source_target_pairs={{8,16},{16,8},{9,17},{17,9},{10,18},{18,10},{11,19},{19,11},{12,20... | collective-permute-start | bytes 786440 | tf_op jit(solution)/shard_map/ppermute | solution.py:526
  101.3 43.6 %collective-permute-start.17 = (bf16[704,512]{1,0:T(8,128)(2,1)}, bf16[704,512]{1,0:T(8,128)(2,1)S(1)}, u32[]{:S(2)}, u32[]{:S(2)}) collective-permute-start(bf16[704,512]{1,0:T(8,128)(2,1)} %collective-permute-done.16.refs_4_.refs_18_), channel_id=1, source_target_pairs={{8,16},{16,8},{9,17},{17,9},{10,18},{18,10},{11,19},{19,11},{12,20... | collective-permute-start | bytes 2162696 | tf_op jit(solution)/shard_map/ppermute | solution.py:526
  104.3 40.7 %collective-permute-start.19 = (bf16[704,512]{1,0:T(8,128)(2,1)}, bf16[704,512]{1,0:T(8,128)(2,1)}, u32[]{:S(2)}, u32[]{:S(2)}) collective-permute-start(bf16[704,512]{1,0:T(8,128)(2,1)} %bitcast.17.refs_3_), channel_id=1, source_target_pairs={{0,8},{24,16},{1,9},{25,17},{2,10},{26,18},{3,11},{27,19},{4,12},{... | collective-permute-start | bytes 2162696 | tf_op jit(solution)/shard_map/ppermute | solution.py:526
  105.6 45.2 %collective-permute-start.15 = (bf16[704,512]{1,0:T(8,128)(2,1)}, bf16[704,512]{1,0:T(8,128)(2,1)S(1)}, u32[]{:S(2)}, u32[]{:S(2)}) collective-permute-start(bf16[704,512]{1,0:T(8,128)(2,1)} %collective-permute-done.14.refs_8_.refs_7_.refs_15_), channel_id=1, source_target_pairs={{8,0},{16,24},{9,1},{17,25},{10,2},{18,26},{11,3},{19,27},{12,4},{... | collective-permute-start | bytes 2162696 | tf_op jit(solution)/shard_map/ppermute | solution.py:526
  113.8 27.3 %copy-start.12 = (bf16[704,512]{1,0:T(8,128)(2,1)}, bf16[704,512]{1,0:T(8,128)(2,1)S(1)}, u32[]{:S(2)}) copy-start(bf16[704,512]{1,0:T(8,128)(2,1)S(1)} %collective-permute-done.10.refs_7_.refs_21_) | copy-start | bytes 2162692
  113.8 11.8 %collective-permute-start.13 = (bf16[128,1024]{1,0:T(8,128)(2,1)}, bf16[128,1024]{1,0:T(8,128)(2,1)S(1)}, u32[]{:S(2)}, u32[]{:S(2)}) collective-permute-start(bf16[128,1024]{1,0:T(8,128)(2,1)} %get-tuple-element.52), channel_id=1, source_target_pairs={{16,0},{8,24},{17,1},{9,25},{18,2},{10,26},{19,3},{11,27},{20,4},{... | collective-permute-start | bytes 786440 | tf_op jit(solution)/shard_map/ppermute | solution.py:526
  118.5 18.7 %copy-start.17 = (bf16[128,1024]{1,0:T(8,128)(2,1)}, bf16[128,1024]{1,0:T(8,128)(2,1)S(1)}, u32[]{:S(2)}) copy-start(bf16[128,1024]{1,0:T(8,128)(2,1)S(1)} %collective-permute-done.12.refs_6_) | copy-start | bytes 786436
  118.6 18.6 %collective-permute-start.11 = (bf16[128,1024]{1,0:T(8,128)(2,1)}, bf16[128,1024]{1,0:T(8,128)(2,1)S(1)}, u32[]{:S(2)}, u32[]{:S(2)}) collective-permute-start(bf16[128,1024]{1,0:T(8,128)(2,1)} %get-tuple-element.50), channel_id=1, source_target_pairs={{8,0},{16,24},{9,1},{17,25},{10,2},{18,26},{11,3},{19,27},{12,4},{... | collective-permute-start | bytes 786440 | tf_op jit(solution)/shard_map/ppermute | solution.py:526
  125.7 11.5 %copy-start.18 = (bf16[128,1024]{1,0:T(8,128)(2,1)}, bf16[128,1024]{1,0:T(8,128)(2,1)S(1)}, u32[]{:S(2)}) copy-start(bf16[128,1024]{1,0:T(8,128)(2,1)S(1)} %collective-permute-done.13.refs_7_) | copy-start | bytes 786436
  141.2 42.9 %all-to-all-start.1 = ((bf16[8,40,2048]{2,1,0:T(8,128)(2,1)}), bf16[8,40,2048]{2,1,0:T(8,128)(2,1)S(1)}, u32[]{:S(2)}, u32[]{:S(2)}) async-start(bf16[8,40,2048]{2,1,0:T(8,128)(2,1)} %bitcast.51), calls=%async_computation.1 | async-start | bytes 2621440 | tf_op jit(solution)/shard_map/all_to_all | solution.py:548
  144.9 45.5 %copy-start.13 = (bf16[704,512]{1,0:T(8,128)(2,1)}, bf16[704,512]{1,0:T(8,128)(2,1)S(1)}, u32[]{:S(2)}) copy-start(bf16[704,512]{1,0:T(8,128)(2,1)S(1)} %collective-permute-done.17.refs_8_.refs_22_) | copy-start | bytes 2162692
  144.9 21.1 %collective-permute-start.21 = (bf16[704,512]{1,0:T(8,128)(2,1)}, bf16[704,512]{1,0:T(8,128)(2,1)}, u32[]{:S(2)}, u32[]{:S(2)}) collective-permute-start(bf16[704,512]{1,0:T(8,128)(2,1)} %bitcast.17.refs_3_), channel_id=1, source_target_pairs={{8,16},{16,8},{9,17},{17,9},{10,18},{18,10},{11,19},{19,11},{12,20... | collective-permute-start | bytes 2162696 | tf_op jit(solution)/shard_map/ppermute | solution.py:526
  147.8 33.2 %collective-permute-start.20 = (bf16[704,512]{1,0:T(8,128)(2,1)}, bf16[704,512]{1,0:T(8,128)(2,1)S(1)}, u32[]{:S(2)}, u32[]{:S(2)}) collective-permute-start(bf16[704,512]{1,0:T(8,128)(2,1)} %collective-permute-done.19.refs_4_), channel_id=1, source_target_pairs={{8,16},{16,8},{9,17},{17,9},{10,18},{18,10},{11,19},{19,11},{12,20... | collective-permute-start | bytes 2162696 | tf_op jit(solution)/shard_map/ppermute | solution.py:526
  150.8 33.3 %copy-start.14 = (bf16[704,512]{1,0:T(8,128)(2,1)}, bf16[704,512]{1,0:T(8,128)(2,1)S(1)}, u32[]{:S(2)}) copy-start(bf16[704,512]{1,0:T(8,128)(2,1)S(1)} %collective-permute-done.15.refs_8_.refs_16_) | copy-start | bytes 2162692
  150.8 30.2 %collective-permute-start.18 = (bf16[704,512]{1,0:T(8,128)(2,1)S(1)}, bf16[704,512]{1,0:T(8,128)(2,1)S(1)}, u32[]{:S(2)}, u32[]{:S(2)}) collective-permute-start(bf16[704,512]{1,0:T(8,128)(2,1)S(1)} %collective-permute-done.17.refs_8_.refs_22_), channel_id=1, source_target_pairs={{8,0},{16,24},{9,1},{17,25},{10,2},{18,26},{11,3},{19,27},{12,4},{... | collective-permute-start | bytes 2162696 | tf_op jit(solution)/shard_map/ppermute | solution.py:526
  166.1 39.4 %collective-permute-start.22 = (bf16[704,512]{1,0:T(8,128)(2,1)}, bf16[704,512]{1,0:T(8,128)(2,1)}, u32[]{:S(2)}, u32[]{:S(2)}) collective-permute-start(bf16[704,512]{1,0:T(8,128)(2,1)} %collective-permute-done.21.refs_6_), channel_id=1, source_target_pairs={{8,0},{16,24},{9,1},{17,25},{10,2},{18,26},{11,3},{19,27},{12,4},{... | collective-permute-start | bytes 2162696 | tf_op jit(solution)/shard_map/ppermute | solution.py:526
  181.0 9.4 %copy-start.15 = (bf16[704,512]{1,0:T(8,128)(2,1)}, bf16[704,512]{1,0:T(8,128)(2,1)S(1)}, u32[]{:S(2)}) copy-start(bf16[704,512]{1,0:T(8,128)(2,1)S(1)} %collective-permute-done.20.refs_10_.refs_8_) | copy-start | bytes 2162692
  181.0 0.9 copy-start.16
  181.9 23.6 %collective-permute-start.23 = (bf16[704,512]{1,0:T(8,128)(2,1)S(1)}, bf16[704,512]{1,0:T(8,128)(2,1)}, u32[]{:S(2)}, u32[]{:S(2)}) collective-permute-start(bf16[704,512]{1,0:T(8,128)(2,1)S(1)} %collective-permute-done.20.refs_10_.refs_8_), channel_id=1, source_target_pairs={{8,0},{16,24},{9,1},{17,25},{10,2},{18,26},{11,3},{19,27},{12,4},{... | collective-permute-start | bytes 2162696 | tf_op jit(solution)/shard_map/ppermute | solution.py:526
  184.1 1.1 copy-start.6
  201.6 15.0 %all-to-all-start.2 = ((bf16[8,40,1024]{2,1,0:T(8,128)(2,1)}), bf16[8,40,1024]{2,1,0:T(8,128)(2,1)S(1)}, u32[]{:S(2)}, u32[]{:S(2)}) async-start(bf16[8,40,1024]{2,1,0:T(8,128)(2,1)} %bitcast.52), calls=%async_computation.2 | async-start | bytes 1310720 | tf_op jit(solution)/shard_map/all_to_all | solution.py:548
  216.6 28.9 %copy-start = (bf16[1,128,2048]{2,1,0:T(8,128)(2,1)S(1)}, bf16[1,128,2048]{2,1,0:T(8,128)(2,1)}, u32[]{:S(2)}) copy-start(bf16[1,128,2048]{2,1,0:T(8,128)(2,1)} %param.22) | copy-start | bytes 1572868
  216.6 28.9 %copy-start.1 = (f32[1,128,2]{2,1,0:T(8,128)S(1)}, f32[1,128,2]{2,1,0:T(8,128)}, u32[]{:S(2)}) copy-start(f32[1,128,2]{2,1,0:T(8,128)} %copy.15) | copy-start | bytes 3076
  216.6 28.9 %copy-start.2 = (bf16[128,2048]{1,0:T(8,128)(2,1)S(1)}, bf16[128,2048]{1,0:T(8,128)(2,1)}, u32[]{:S(2)}) copy-start(bf16[128,2048]{1,0:T(8,128)(2,1)} %get-tuple-element.53.refs_4_) | copy-start | bytes 1572868
  216.6 28.9 %copy-start.3 = (f32[2048]{0:T(1024)S(1)}, f32[2048]{0:T(1024)}, u32[]{:S(2)}) copy-start(f32[2048]{0:T(1024)} %param.16) | copy-start | bytes 24580
  216.6 28.9 %copy-start.4 = (s32[10]{0:T(128)S(1)}, s32[10]{0:T(128)}, u32[]{:S(2)}) copy-start(s32[10]{0:T(128)} %dynamic-slice_bitcast_fusion.refs_0_) | copy-start | bytes 124
  (1 other events, 0.7 us)

commit v12 on v11

--- a/solution.py
+++ b/solution.py
@@ -225,15 +225,14 @@
     mid = send(mid, MIDDLE)
     far = send(far, [(2, 0), (1, 3)])
     up_far = send(up_mid, OUTWARD, pieces[0])
-    near = send(near, OUTWARD, up_far)
-    gate_mid_near = send(gate_inner, MIDDLE)
+    near = send(near, OUTWARD, up_far, far)
+    gate_mid_near = send(gate_inner, MIDDLE, pieces[0])
     up_mid_near = send(up_inner, MIDDLE, pieces[0])
     down_mid = send(down, MIDDLE, gate_mid_near)
     down_mid_near = send(down_inner, MIDDLE, up_mid_near)
     gate_far_near = send(gate_mid_near, OUTWARD)
     up_far_near = send(up_mid_near, OUTWARD, gate_far_near)
     down_far = send(down_mid, OUTWARD, gate_far_near)
-    down_far_near = send(down_mid_near, OUTWARD, up_far_near)
     norm_after = (gate_mid_near,)
     up_after = (down_mid_near,)
     gate_in = [
@@ -247,7 +246,7 @@
         [down],
         [down_inner, down_end],
         [down_mid, down_far],
-        [down_mid_near, down_far_near],
+        [down_mid_near],
     ]
     return (own, near, mid, far), gate_in, up_in, down_in, norm_after, up_after
 
@@ -628,6 +627,8 @@
         flops=one,
         moved=2 * width * ffw + 2 * total * width + 4 * total * ffw,
     )
+    if groups == 4:
+        down_in[3].append(send(down_in[3][0], OUTWARD, up_in[3][1], gate_pre))
     hidden, to_gate, to_up = call(
         functools.partial(up_kernel, shape),
         (sds((total, ffw)), sds((total, ffw), F32), sds((total, ffw), F32)),

time: 250 us -> 231 us (0.924)
  the two profiles are of different devices: /device:TPU:8 before, /device:TPU:0 now
where the time goes in v12:
time: 231 us; the launch traced here: 230 us
  waiting for transfers between devices  84.8 us (37%)
  starting transfers between devices  68.7 us (30%)
  Pallas kernels  39.1 us (17%)
  blocking collectives  29.2 us (13%)
  local copies, waits for them, and re-layouts  6.71 us (3%)
    ppermute x24, waiting for transfers between devices, send(): return lax.ppermute(gated(array, *first), 'seq', pairs)  74.3 us
    ppermute x24, starting transfers between devices, send(): return lax.ppermute(gated(array, *first), 'seq', pairs)  56.9 us
    pallas_call x9, Pallas kernels, call(): pl.pallas_call(body, grid=() if held else (1,), out_shape=outs, in_specs=...  39.1 us
    all_to_all x1, blocking collectives, exchange(): rows = lax.all_to_all(rows, axis, split_axis=0, concat_axis=0, tiled=True)  29.2 us
    all_to_all x3, starting transfers between devices, exchange(): rows = lax.all_to_all(rows, axis, split_axis=0, concat_axis=0, tiled=True)  11.8 us
    all_to_all x3, waiting for transfers between devices, exchange(): rows = lax.all_to_all(rows, axis, split_axis=0, concat_axis=0, tiled=True)  10.5 us
    unnamed x46, local copies, waits for them, and re-layouts  4.83 us
  transfers between devices with their start and end apart: 27, of which 10 were waited for; matrix products, arithmetic and copies ran while one was open for 1% of the time, Pallas kernels for 16%

profile of v12, /device:TPU:0, one launch (start us, length us, event | category | flops | bytes accessed | tf_op | source)
XLA Modules:
  0.0 229.5 jit_solution(3938904968461826946)
XLA Ops:
  0.6 0.8 collective-permute-start
  1.5 1.3 collective-permute-start.1
  2.8 1.3 dynamic-slice_bitcast_fusion.refs_0_
  4.1 2.7 %shard_map.131 = (bf16[384,1024]{1,0:T(8,128)(2,1)}, bf16[384,1024]{1,0:T(8,128)(2,1)}) custom-call(s32[10]{0:T(128)} %dynamic-slice_bitcast_fusion.refs_0_, bf16[128,2048]{1,0:T(8,128)(2,1)} %bitcast.53, bf16[128,2048]{1,0:T(8,128)(2,1)} %bitcast.54, bf16[128,2048]{1,0:T(8,128)(2,1)} %bitcast.55), custom_call_target="tpu_custom_call" | custom-call | bytes 3145728 | tf_op jit(solution)/shard_map/pallas_call | solution.py:35
  6.8 17.9 %collective-permute-done.1.refs_5_.refs_4_.refs_12_ = bf16[704,512]{1,0:T(8,128)(2,1)S(1)} collective-permute-done((bf16[704,512]{1,0:T(8,128)(2,1)}, bf16[704,512]{1,0:T(8,128)(2,1)S(1)}, u32[]{:S(2)}, u32[]{:S(2)}) %collective-permute-start.1) | collective-permute-done | bytes 720928 | tf_op jit(solution)/shard_map/ppermute | solution.py:525
  24.6 2.5 %collective-permute-start.2 = (bf16[384,1024]{1,0:T(8,128)(2,1)}, bf16[384,1024]{1,0:T(8,128)(2,1)}, u32[]{:S(2)}, u32[]{:S(2)}) collective-permute-start(bf16[384,1024]{1,0:T(8,128)(2,1)} %get-tuple-element.38.refs_1_), channel_id=1, source_target_pairs={{0,8},{24,16},{1,9},{25,17},{2,10},{26,18},{3,11},{27,19},{4,12},{... | collective-permute-start | bytes 2359304 | tf_op jit(solution)/shard_map/ppermute | solution.py:525
  27.2 1.6 collective-permute-start.3
  28.7 3.0 %collective-permute-start.4 = (bf16[384,1024]{1,0:T(8,128)(2,1)}, bf16[384,1024]{1,0:T(8,128)(2,1)}, u32[]{:S(2)}, u32[]{:S(2)}) collective-permute-start(bf16[384,1024]{1,0:T(8,128)(2,1)} %get-tuple-element.40), channel_id=1, source_target_pairs={{0,16},{24,8},{1,17},{25,9},{2,18},{26,10},{3,19},{27,11},{4,20},{... | collective-permute-start | bytes 2359304 | tf_op jit(solution)/shard_map/ppermute | solution.py:525
  31.8 1.3 collective-permute-start.5
  33.2 0.7 copy.15
  34.5 3.2 %shard_map.132 = bf16[320,2048]{1,0:T(8,128)(2,1)} custom-call(s32[2,128]{1,0:T(2,128)} %copy.17.refs_0_.refs_1_, f32[128,2]{1,0:T(8,128)} %bitcast.33, bf16[128,2048]{1,0:T(8,128)(2,1)} %bitcast.31), custom_call_target="tpu_custom_call" | custom-call | flops 335544320 | bytes 1835008 | tf_op jit(solution)/shard_map/pallas_call | solution.py:35
  37.7 3.9 %all-to-all-start = ((bf16[8,40,2048]{2,1,0:T(8,128)(2,1)}), bf16[8,40,2048]{2,1,0:T(8,128)(2,1)S(1)}, u32[]{:S(2)}, u32[]{:S(2)}) async-start(bf16[8,40,2048]{2,1,0:T(8,128)(2,1)} %bitcast.45), calls=%async_computation | async-start | bytes 2621440 | tf_op jit(solution)/shard_map/all_to_all | solution.py:547
  41.6 1.3 collective-permute-start.6
  42.9 1.6 collective-permute-done.2.refs_2_
  44.5 14.8 %collective-permute-done.4.refs_4_ = bf16[384,1024]{1,0:T(8,128)(2,1)} collective-permute-done((bf16[384,1024]{1,0:T(8,128)(2,1)}, bf16[384,1024]{1,0:T(8,128)(2,1)}, u32[]{:S(2)}, u32[]{:S(2)}) %collective-permute-start.4) | collective-permute-done | bytes 786464 | tf_op jit(solution)/shard_map/ppermute | solution.py:525
  59.3 1.5 collective-permute-start.9
  60.8 8.0 %collective-permute-start.7 = (bf16[704,512]{1,0:T(8,128)(2,1)S(1)}, bf16[704,512]{1,0:T(8,128)(2,1)}, u32[]{:S(2)}, u32[]{:S(2)}) collective-permute-start(bf16[704,512]{1,0:T(8,128)(2,1)S(1)} %bitcast.50), channel_id=1, source_target_pairs={{0,8},{24,16},{1,9},{25,17},{2,10},{26,18},{3,11},{27,19},{4,12},{... | collective-permute-start | bytes 2162696 | tf_op jit(solution)/shard_map/ppermute | solution.py:525
  68.9 1.3 collective-permute-start.8
  70.2 1.1 copy-done.5
  71.5 1.7 shard_map.133
  73.2 1.3 collective-permute-start.10
  74.5 13.2 %collective-permute-start.16 = (bf16[704,512]{1,0:T(8,128)(2,1)}, bf16[704,512]{1,0:T(8,128)(2,1)}, u32[]{:S(2)}, u32[]{:S(2)}) collective-permute-start(bf16[704,512]{1,0:T(8,128)(2,1)} %bitcast.13.refs_3_.refs_17_), channel_id=1, source_target_pairs={{0,8},{24,16},{1,9},{25,17},{2,10},{26,18},{3,11},{27,19},{4,12},{... | collective-permute-start | bytes 2162696 | tf_op jit(solution)/shard_map/ppermute | solution.py:525
  87.7 0.7 collective-permute-start.14
  89.1 1.3 collective-permute-start.11
  91.0 19.6 %collective-permute-done.11.refs_7_ = bf16[128,1024]{1,0:T(8,128)(2,1)S(1)} collective-permute-done((bf16[128,1024]{1,0:T(8,128)(2,1)}, bf16[128,1024]{1,0:T(8,128)(2,1)S(1)}, u32[]{:S(2)}, u32[]{:S(2)}) %collective-permute-start.11) | collective-permute-done | bytes 262176 | tf_op jit(solution)/shard_map/ppermute | solution.py:525
  110.7 1.3 collective-permute-start.12
  112.0 1.6 collective-permute-start.17
  113.6 6.8 %collective-permute-start.19 = (bf16[704,512]{1,0:T(8,128)(2,1)}, bf16[704,512]{1,0:T(8,128)(2,1)}, u32[]{:S(2)}, u32[]{:S(2)}) collective-permute-start(bf16[704,512]{1,0:T(8,128)(2,1)} %bitcast.17.refs_3_), channel_id=1, source_target_pairs={{0,8},{24,16},{1,9},{25,17},{2,10},{26,18},{3,11},{27,19},{4,12},{... | collective-permute-start | bytes 2162696 | tf_op jit(solution)/shard_map/ppermute | solution.py:525
  120.4 1.3 collective-permute-start.15
  122.6 3.3 %shard_map.134 = (bf16[128,2048]{1,0:T(8,128)(2,1)}, bf16[320,2048]{1,0:T(8,128)(2,1)}) custom-call(s32[10]{0:T(128)} %dynamic-slice_bitcast_fusion.refs_0_, s32[2,128]{1,0:T(2,128)} %copy.17.refs_0_.refs_1_, bf16[128,2048]{1,0:T(8,128)(2,1)} %bitcast.56, f32[1,2048]{1,0:T(1,128)} %bitcast.37, bf16[128,1024]{1,0:T(8,128)(2,1)} %get-tuple-element.47.refs_4_, ...), custom_call_target="tpu_custom_call" | custom-call | flops 167772160 | bytes 2883584 | tf_op jit(solution)/shard_map/pallas_call | solution.py:35
  125.9 3.7 %all-to-all-start.1 = ((bf16[8,40,2048]{2,1,0:T(8,128)(2,1)}), bf16[8,40,2048]{2,1,0:T(8,128)(2,1)S(1)}, u32[]{:S(2)}, u32[]{:S(2)}) async-start(bf16[8,40,2048]{2,1,0:T(8,128)(2,1)} %bitcast.51), calls=%async_computation.1 | async-start | bytes 2621440 | tf_op jit(solution)/shard_map/all_to_all | solution.py:547
  130.3 1.5 collective-permute-start.20
  131.9 2.8 %collective-permute-done.15.refs_8_.refs_16_ = bf16[704,512]{1,0:T(8,128)(2,1)} collective-permute-done((bf16[704,512]{1,0:T(8,128)(2,1)S(1)}, bf16[704,512]{1,0:T(8,128)(2,1)}, u32[]{:S(2)}, u32[]{:S(2)}) %collective-permute-start.15) | collective-permute-done | bytes 720928 | tf_op jit(solution)/shard_map/ppermute | solution.py:525
  134.7 1.3 collective-permute-start.18
  136.0 1.3 collective-permute-start.22
  137.3 10.5 %all-to-all-done.1 = bf16[8,40,2048]{2,1,0:T(8,128)(2,1)S(1)} async-done(((bf16[8,40,2048]{2,1,0:T(8,128)(2,1)}), bf16[8,40,2048]{2,1,0:T(8,128)(2,1)S(1)}, u32[]{:S(2)}, u32[]{:S(2)}) %all-to-all-start.1) | async-done | bytes 1310752 | tf_op jit(solution)/shard_map/all_to_all | solution.py:547
  147.8 1.1 copy-done.6
  148.9 5.3 %shard_map.135.refs_2_ = f32[320,704]{1,0:T(8,128)} custom-call(s32[10]{0:T(128)} %dynamic-slice_bitcast_fusion.refs_0_, bf16[320,2048]{1,0:T(8,128)(2,1)} %bitcast.42, bf16[704,512]{1,0:T(8,128)(2,1)} %bitcast.48, bf16[704,512]{1,0:T(8,128)(2,1)} %collective-permute-done.7.refs_3_.refs_11_, bf16[704,512]{1,0:T(8,128)(2,1)} %copy-done.7, ...), custom_call_target="tpu_custom_call" | custom-call | flops 922746880 | bytes 5095424 | tf_op jit(solution)/shard_map/pallas_call | solution.py:35
  154.2 3.2 %collective-permute-done.18.refs_9_.refs_23_ = bf16[704,512]{1,0:T(8,128)(2,1)S(1)} collective-permute-done((bf16[704,512]{1,0:T(8,128)(2,1)}, bf16[704,512]{1,0:T(8,128)(2,1)S(1)}, u32[]{:S(2)}, u32[]{:S(2)}) %collective-permute-start.18) | collective-permute-done | bytes 720928 | tf_op jit(solution)/shard_map/ppermute | solution.py:525
  157.4 1.3 collective-permute-start.23
  158.7 6.0 %shard_map.136 = (bf16[320,704]{1,0:T(8,128)(2,1)}, f32[320,704]{1,0:T(8,128)}, f32[320,704]{1,0:T(8,128)}) custom-call(s32[10]{0:T(128)} %dynamic-slice_bitcast_fusion.refs_0_, bf16[320,2048]{1,0:T(8,128)(2,1)} %bitcast.43, f32[320,704]{1,0:T(8,128)} %shard_map.135.refs_2_, bf16[704,512]{1,0:T(8,128)(2,1)} %bitcast.13.refs_3_.refs_17_, ...), custom_call_target="tpu_custom_call" | custom-call | flops 922746880 | bytes 7348224 | tf_op jit(solution)/shard_map/pallas_call | solution.py:35
  164.7 5.2 %shard_map.137 = (bf16[320,1024]{1,0:T(8,128)(2,1)}, f32[320,704]{1,0:T(8,128)}) custom-call(s32[10]{0:T(128)} %dynamic-slice_bitcast_fusion.refs_0_, bf16[320,704]{1,0:T(8,128)(2,1)} %get-tuple-element.62.refs_1_, bf16[320,2048]{1,0:T(8,128)(2,1)} %bitcast.40, bf16[704,512]{1,0:T(8,128)(2,1)} %bitcast.17.refs_3_, ...), custom_call_target="tpu_custom_call" | custom-call | flops 922746880 | bytes 4759552 | tf_op jit(solution)/shard_map/pallas_call | solution.py:35
  169.9 4.3 %all-to-all-start.2 = ((bf16[8,40,1024]{2,1,0:T(8,128)(2,1)}), bf16[8,40,1024]{2,1,0:T(8,128)(2,1)S(1)}, u32[]{:S(2)}, u32[]{:S(2)}) async-start(bf16[8,40,1024]{2,1,0:T(8,128)(2,1)} %bitcast.52), calls=%async_computation.2 | async-start | bytes 1310720 | tf_op jit(solution)/shard_map/all_to_all | solution.py:547
  174.1 13.4 %collective-permute-done.23.refs_9_ = bf16[704,512]{1,0:T(8,128)(2,1)S(1)} collective-permute-done((bf16[704,512]{1,0:T(8,128)(2,1)}, bf16[704,512]{1,0:T(8,128)(2,1)S(1)}, u32[]{:S(2)}, u32[]{:S(2)}) %collective-permute-start.23) | collective-permute-done | bytes 720928 | tf_op jit(solution)/shard_map/ppermute | solution.py:525
  187.6 0.9 copy-done.16
  188.4 8.7 %shard_map.138 = bf16[320,3072]{1,0:T(8,128)(2,1)} custom-call(s32[10]{0:T(128)} %dynamic-slice_bitcast_fusion.refs_0_, bf16[320,704]{1,0:T(8,128)(2,1)} %get-tuple-element.62.refs_1_, bf16[320,2048]{1,0:T(8,128)(2,1)} %bitcast.41, f32[320,704]{1,0:T(8,128)} %get-tuple-element.64.refs_3_, f32[320,704]{1,0:T(8,128)} %get-tuple-element.65.refs_4_, ...), custom_call_target="tpu_custom_call" | custom-call | flops 2768240640 | bytes 12984320 | tf_op jit(solution)/shard_map/pallas_call | solution.py:35
  197.2 29.2 %all_to_all.20 = bf16[8,40,3072]{2,1,0:T(8,128)(2,1)S(1)} all-to-all(bf16[8,40,3072]{2,1,0:T(8,128)(2,1)} %bitcast.44), channel_id=1, replica_groups=mesh['seq'=4,'exp'=8] {'exp'}, dimensions={0} | all-to-all | bytes 3932160 | tf_op jit(solution)/shard_map/all_to_all | solution.py:547
  226.4 3.1 %shard_map.139 = (bf16[128,2048]{1,0:T(8,128)(2,1)}, bf16[128,2048]{1,0:T(8,128)(2,1)}) custom-call(s32[10]{0:T(128)S(1)} %copy-done.4, s32[128,2]{1,0:T(8,128)S(1)} %bitcast.36, f32[128,2]{1,0:T(8,128)S(1)} %bitcast.34, f32[1,2048]{1,0:T(1,128)S(1)} %bitcast.38, bf16[128,2048]{1,0:T(8,128)(2,1)S(1)} %copy-done.2, bf16[128,2048]{1,0:T(8,128)(2,1)S(1)} %bitcast.32, ...), custom_call_target="tpu_custom_call" | custom-call | flops 503316480 | bytes 4718592 | tf_op jit(solution)/shard_map/pallas_call | solution.py:35
  (64 shorter events, 4.0 us)
Async XLA Ops:
  0.6 32.4 %copy-start.20 = (s32[1,128,2]{1,2,0:T(2,128)S(1)}, s32[1,128,2]{1,2,0:T(2,128)}, u32[]{:S(2)}) copy-start(s32[1,128,2]{1,2,0:T(2,128)} %param.20) | copy-start | bytes 3076
  0.6 32.6 %copy-start.21 = (f32[1,128,2]{1,2,0:T(2,128)S(1)}, f32[1,128,2]{1,2,0:T(2,128)}, u32[]{:S(2)}) copy-start(f32[1,128,2]{1,2,0:T(2,128)} %param.21) | copy-start | bytes 3076
  0.6 6.1 %collective-permute-start = (bf16[704,512]{1,0:T(8,128)(2,1)}, bf16[704,512]{1,0:T(8,128)(2,1)S(1)}, u32[]{:S(2)}, u32[]{:S(2)}) collective-permute-start(bf16[704,512]{1,0:T(8,128)(2,1)} %bitcast.46), channel_id=1, source_target_pairs={{8,16},{16,8},{9,17},{17,9},{10,18},{18,10},{11,19},{19,11},{12,20... | collective-permute-start | bytes 2162696 | tf_op jit(solution)/shard_map/ppermute | solution.py:525
  1.5 23.1 %collective-permute-start.1 = (bf16[704,512]{1,0:T(8,128)(2,1)}, bf16[704,512]{1,0:T(8,128)(2,1)S(1)}, u32[]{:S(2)}, u32[]{:S(2)}) collective-permute-start(bf16[704,512]{1,0:T(8,128)(2,1)} %bitcast.47), channel_id=1, source_target_pairs={{8,0},{16,24},{9,1},{17,25},{10,2},{18,26},{11,3},{19,27},{12,4},{... | collective-permute-start | bytes 2162696 | tf_op jit(solution)/shard_map/ppermute | solution.py:525
  6.8 25.0 %copy-start.12 = (bf16[704,512]{1,0:T(8,128)(2,1)}, bf16[704,512]{1,0:T(8,128)(2,1)S(1)}, u32[]{:S(2)}) copy-start(bf16[704,512]{1,0:T(8,128)(2,1)S(1)} %collective-permute-done.refs_5_.refs_13_) | copy-start | bytes 2162692
  24.6 13.1 %copy-start.7 = (bf16[704,512]{1,0:T(8,128)(2,1)}, bf16[704,512]{1,0:T(8,128)(2,1)S(1)}, u32[]{:S(2)}) copy-start(bf16[704,512]{1,0:T(8,128)(2,1)S(1)} %collective-permute-done.1.refs_5_.refs_4_.refs_12_) | copy-start | bytes 2162692
  24.6 19.8 %collective-permute-start.2 = (bf16[384,1024]{1,0:T(8,128)(2,1)}, bf16[384,1024]{1,0:T(8,128)(2,1)}, u32[]{:S(2)}, u32[]{:S(2)}) collective-permute-start(bf16[384,1024]{1,0:T(8,128)(2,1)} %get-tuple-element.38.refs_1_), channel_id=1, source_target_pairs={{0,8},{24,16},{1,9},{25,17},{2,10},{26,18},{3,11},{27,19},{4,12},{... | collective-permute-start | bytes 2359304 | tf_op jit(solution)/shard_map/ppermute | solution.py:525
  27.2 17.3 %collective-permute-start.3 = (bf16[384,1024]{1,0:T(8,128)(2,1)}, bf16[384,1024]{1,0:T(8,128)(2,1)}, u32[]{:S(2)}, u32[]{:S(2)}) collective-permute-start(bf16[384,1024]{1,0:T(8,128)(2,1)} %get-tuple-element.40), channel_id=1, source_target_pairs={{8,16},{16,8},{9,17},{17,9},{10,18},{18,10},{11,19},{19,11},{12,20... | collective-permute-start | bytes 2359304 | tf_op jit(solution)/shard_map/ppermute | solution.py:525
  28.7 30.6 %collective-permute-start.4 = (bf16[384,1024]{1,0:T(8,128)(2,1)}, bf16[384,1024]{1,0:T(8,128)(2,1)}, u32[]{:S(2)}, u32[]{:S(2)}) collective-permute-start(bf16[384,1024]{1,0:T(8,128)(2,1)} %get-tuple-element.40), channel_id=1, source_target_pairs={{0,16},{24,8},{1,17},{25,9},{2,18},{26,10},{3,19},{27,11},{4,20},{... | collective-permute-start | bytes 2359304 | tf_op jit(solution)/shard_map/ppermute | solution.py:525
  31.8 29.1 %collective-permute-start.5 = (bf16[704,512]{1,0:T(8,128)(2,1)}, bf16[704,512]{1,0:T(8,128)(2,1)S(1)}, u32[]{:S(2)}, u32[]{:S(2)}) collective-permute-start(bf16[704,512]{1,0:T(8,128)(2,1)} %bitcast.13.refs_3_.refs_17_), channel_id=1, source_target_pairs={{8,0},{16,24},{9,1},{17,25},{10,2},{18,26},{11,3},{19,27},{12,4},{... | collective-permute-start | bytes 2162696 | tf_op jit(solution)/shard_map/ppermute | solution.py:525
  37.7 23.1 %copy-start.11 = (bf16[1,512,704]{1,2,0:T(8,128)(2,1)S(1)}, bf16[1,512,704]{1,2,0:T(8,128)(2,1)}, u32[]{:S(2)}) copy-start(bf16[1,512,704]{1,2,0:T(8,128)(2,1)} %param.17) | copy-start | bytes 2162692
  37.7 32.4 %all-to-all-start = ((bf16[8,40,2048]{2,1,0:T(8,128)(2,1)}), bf16[8,40,2048]{2,1,0:T(8,128)(2,1)S(1)}, u32[]{:S(2)}, u32[]{:S(2)}) async-start(bf16[8,40,2048]{2,1,0:T(8,128)(2,1)} %bitcast.45), calls=%async_computation | async-start | bytes 2621440 | tf_op jit(solution)/shard_map/all_to_all | solution.py:547
  41.6 28.6 %collective-permute-start.6 = (bf16[704,512]{1,0:T(8,128)(2,1)}, bf16[704,512]{1,0:T(8,128)(2,1)S(1)}, u32[]{:S(2)}, u32[]{:S(2)}) collective-permute-start(bf16[704,512]{1,0:T(8,128)(2,1)} %copy-done.12), channel_id=1, source_target_pairs={{8,0},{16,24},{9,1},{17,25},{10,2},{18,26},{11,3},{19,27},{12,4},{... | collective-permute-start | bytes 2162696 | tf_op jit(solution)/shard_map/ppermute | solution.py:525
  59.3 13.8 %collective-permute-start.9 = (bf16[704,512]{1,0:T(8,128)(2,1)}, bf16[704,512]{1,0:T(8,128)(2,1)}, u32[]{:S(2)}, u32[]{:S(2)}) collective-permute-start(bf16[704,512]{1,0:T(8,128)(2,1)} %bitcast.13.refs_3_.refs_17_), channel_id=1, source_target_pairs={{8,16},{16,8},{9,17},{17,9},{10,18},{18,10},{11,19},{19,11},{12,20... | collective-permute-start | bytes 2162696 | tf_op jit(solution)/shard_map/ppermute | solution.py:525
  60.8 9.4 %copy-start.8 = (bf16[704,512]{1,0:T(8,128)(2,1)}, bf16[704,512]{1,0:T(8,128)(2,1)S(1)}, u32[]{:S(2)}) copy-start(bf16[704,512]{1,0:T(8,128)(2,1)S(1)} %collective-permute-done.5.refs_6_.refs_5_.refs_19_) | copy-start | bytes 2162692
  60.8 26.9 %collective-permute-start.7 = (bf16[704,512]{1,0:T(8,128)(2,1)S(1)}, bf16[704,512]{1,0:T(8,128)(2,1)}, u32[]{:S(2)}, u32[]{:S(2)}) collective-permute-start(bf16[704,512]{1,0:T(8,128)(2,1)S(1)} %bitcast.50), channel_id=1, source_target_pairs={{0,8},{24,16},{1,9},{25,17},{2,10},{26,18},{3,11},{27,19},{4,12},{... | collective-permute-start | bytes 2162696 | tf_op jit(solution)/shard_map/ppermute | solution.py:525
  68.9 20.2 %collective-permute-start.8 = (bf16[704,512]{1,0:T(8,128)(2,1)}, bf16[704,512]{1,0:T(8,128)(2,1)}, u32[]{:S(2)}, u32[]{:S(2)}) collective-permute-start(bf16[704,512]{1,0:T(8,128)(2,1)} %bitcast.17.refs_3_), channel_id=1, source_target_pairs={{8,0},{16,24},{9,1},{17,25},{10,2},{18,26},{11,3},{19,27},{12,4},{... | collective-permute-start | bytes 2162696 | tf_op jit(solution)/shard_map/ppermute | solution.py:525
  70.2 1.1 copy-start.5
  70.2 1.3 copy-start.9
  73.2 37.5 %collective-permute-start.10 = (bf16[704,512]{1,0:T(8,128)(2,1)}, bf16[704,512]{1,0:T(8,128)(2,1)S(1)}, u32[]{:S(2)}, u32[]{:S(2)}) collective-permute-start(bf16[704,512]{1,0:T(8,128)(2,1)} %collective-permute-done.9.refs_6_.refs_20_), channel_id=1, source_target_pairs={{8,0},{16,24},{9,1},{17,25},{10,2},{18,26},{11,3},{19,27},{12,4},{... | collective-permute-start | bytes 2162696 | tf_op jit(solution)/shard_map/ppermute | solution.py:525
  74.5 37.5 %collective-permute-start.16 = (bf16[704,512]{1,0:T(8,128)(2,1)}, bf16[704,512]{1,0:T(8,128)(2,1)}, u32[]{:S(2)}, u32[]{:S(2)}) collective-permute-start(bf16[704,512]{1,0:T(8,128)(2,1)} %bitcast.13.refs_3_.refs_17_), channel_id=1, source_target_pairs={{0,8},{24,16},{1,9},{25,17},{2,10},{26,18},{3,11},{27,19},{4,12},{... | collective-permute-start | bytes 2162696 | tf_op jit(solution)/shard_map/ppermute | solution.py:525
  87.7 32.7 %collective-permute-start.14 = (bf16[704,512]{1,0:T(8,128)(2,1)}, bf16[704,512]{1,0:T(8,128)(2,1)S(1)}, u32[]{:S(2)}, u32[]{:S(2)}) collective-permute-start(bf16[704,512]{1,0:T(8,128)(2,1)} %collective-permute-done.7.refs_3_.refs_11_), channel_id=1, source_target_pairs={{8,16},{16,8},{9,17},{17,9},{10,18},{18,10},{11,19},{19,11},{12,20... | collective-permute-start | bytes 2162696 | tf_op jit(solution)/shard_map/ppermute | solution.py:525
  89.1 21.6 %collective-permute-start.11 = (bf16[128,1024]{1,0:T(8,128)(2,1)}, bf16[128,1024]{1,0:T(8,128)(2,1)S(1)}, u32[]{:S(2)}, u32[]{:S(2)}) collective-permute-start(bf16[128,1024]{1,0:T(8,128)(2,1)} %get-tuple-element.51), channel_id=1, source_target_pairs={{16,0},{8,24},{17,1},{9,25},{18,2},{10,26},{19,3},{11,27},{20,4},{... | collective-permute-start | bytes 786440 | tf_op jit(solution)/shard_map/ppermute | solution.py:525
  90.3 31.4 %collective-permute-start.13 = (bf16[128,1024]{1,0:T(8,128)(2,1)}, bf16[128,1024]{1,0:T(8,128)(2,1)S(1)}, u32[]{:S(2)}, u32[]{:S(2)}) collective-permute-start(bf16[128,1024]{1,0:T(8,128)(2,1)} %get-tuple-element.53), channel_id=1, source_target_pairs={{8,16},{16,8},{9,17},{17,9},{10,18},{18,10},{11,19},{19,11},{12,20... | collective-permute-start | bytes 786440 | tf_op jit(solution)/shard_map/ppermute | solution.py:525
  110.7 11.2 %copy-start.17 = (bf16[128,1024]{1,0:T(8,128)(2,1)}, bf16[128,1024]{1,0:T(8,128)(2,1)S(1)}, u32[]{:S(2)}) copy-start(bf16[128,1024]{1,0:T(8,128)(2,1)S(1)} %collective-permute-done.11.refs_7_) | copy-start | bytes 786436
  110.7 43.5 %copy-start.13 = (bf16[704,512]{1,0:T(8,128)(2,1)}, bf16[704,512]{1,0:T(8,128)(2,1)S(1)}, u32[]{:S(2)}) copy-start(bf16[704,512]{1,0:T(8,128)(2,1)S(1)} %collective-permute-done.10.refs_7_.refs_21_) | copy-start | bytes 2162692
  110.7 11.2 %collective-permute-start.12 = (bf16[128,1024]{1,0:T(8,128)(2,1)}, bf16[128,1024]{1,0:T(8,128)(2,1)S(1)}, u32[]{:S(2)}, u32[]{:S(2)}) collective-permute-start(bf16[128,1024]{1,0:T(8,128)(2,1)} %get-tuple-element.52), channel_id=1, source_target_pairs={{8,0},{16,24},{9,1},{17,25},{10,2},{18,26},{11,3},{19,27},{12,4},{... | collective-permute-start | bytes 786440 | tf_op jit(solution)/shard_map/ppermute | solution.py:525
  112.0 18.3 %collective-permute-start.17 = (bf16[704,512]{1,0:T(8,128)(2,1)}, bf16[704,512]{1,0:T(8,128)(2,1)}, u32[]{:S(2)}, u32[]{:S(2)}) collective-permute-start(bf16[704,512]{1,0:T(8,128)(2,1)} %collective-permute-done.16.refs_4_.refs_18_), channel_id=1, source_target_pairs={{8,16},{16,8},{9,17},{17,9},{10,18},{18,10},{11,19},{19,11},{12,20... | collective-permute-start | bytes 2162696 | tf_op jit(solution)/shard_map/ppermute | solution.py:525
  113.6 16.7 %collective-permute-start.19 = (bf16[704,512]{1,0:T(8,128)(2,1)}, bf16[704,512]{1,0:T(8,128)(2,1)}, u32[]{:S(2)}, u32[]{:S(2)}) collective-permute-start(bf16[704,512]{1,0:T(8,128)(2,1)} %bitcast.17.refs_3_), channel_id=1, source_target_pairs={{0,8},{24,16},{1,9},{25,17},{2,10},{26,18},{3,11},{27,19},{4,12},{... | collective-permute-start | bytes 2162696 | tf_op jit(solution)/shard_map/ppermute | solution.py:525
  120.4 1.5 copy-start.10
  120.4 14.3 %collective-permute-start.15 = (bf16[704,512]{1,0:T(8,128)(2,1)S(1)}, bf16[704,512]{1,0:T(8,128)(2,1)}, u32[]{:S(2)}, u32[]{:S(2)}) collective-permute-start(bf16[704,512]{1,0:T(8,128)(2,1)S(1)} %collective-permute-done.14.refs_8_.refs_7_.refs_15_), channel_id=1, source_target_pairs={{8,0},{16,24},{9,1},{17,25},{10,2},{18,26},{11,3},{19,27},{12,4},{... | collective-permute-start | bytes 2162696 | tf_op jit(solution)/shard_map/ppermute | solution.py:525
  121.7 0.7 copy-start.18
  125.9 21.9 %all-to-all-start.1 = ((bf16[8,40,2048]{2,1,0:T(8,128)(2,1)}), bf16[8,40,2048]{2,1,0:T(8,128)(2,1)S(1)}, u32[]{:S(2)}, u32[]{:S(2)}) async-start(bf16[8,40,2048]{2,1,0:T(8,128)(2,1)} %bitcast.51), calls=%async_computation.1 | async-start | bytes 2621440 | tf_op jit(solution)/shard_map/all_to_all | solution.py:547
  129.6 6.4 %collective-permute-start.21 = (bf16[704,512]{1,0:T(8,128)(2,1)}, bf16[704,512]{1,0:T(8,128)(2,1)S(1)}, u32[]{:S(2)}, u32[]{:S(2)}) collective-permute-start(bf16[704,512]{1,0:T(8,128)(2,1)} %bitcast.17.refs_3_), channel_id=1, source_target_pairs={{8,16},{16,8},{9,17},{17,9},{10,18},{18,10},{11,19},{19,11},{12,20... | collective-permute-start | bytes 2162696 | tf_op jit(solution)/shard_map/ppermute | solution.py:525
  130.3 23.9 %collective-permute-start.20 = (bf16[704,512]{1,0:T(8,128)(2,1)}, bf16[704,512]{1,0:T(8,128)(2,1)}, u32[]{:S(2)}, u32[]{:S(2)}) collective-permute-start(bf16[704,512]{1,0:T(8,128)(2,1)} %collective-permute-done.19.refs_4_), channel_id=1, source_target_pairs={{8,16},{16,8},{9,17},{17,9},{10,18},{18,10},{11,19},{19,11},{12,20... | collective-permute-start | bytes 2162696 | tf_op jit(solution)/shard_map/ppermute | solution.py:525
  134.7 22.7 %collective-permute-start.18 = (bf16[704,512]{1,0:T(8,128)(2,1)}, bf16[704,512]{1,0:T(8,128)(2,1)S(1)}, u32[]{:S(2)}, u32[]{:S(2)}) collective-permute-start(bf16[704,512]{1,0:T(8,128)(2,1)} %collective-permute-done.17.refs_8_.refs_22_), channel_id=1, source_target_pairs={{8,0},{16,24},{9,1},{17,25},{10,2},{18,26},{11,3},{19,27},{12,4},{... | collective-permute-start | bytes 2162696 | tf_op jit(solution)/shard_map/ppermute | solution.py:525
  136.0 28.6 %copy-start.15 = (bf16[704,512]{1,0:T(8,128)(2,1)}, bf16[704,512]{1,0:T(8,128)(2,1)S(1)}, u32[]{:S(2)}) copy-start(bf16[704,512]{1,0:T(8,128)(2,1)S(1)} %collective-permute-done.21.refs_6_) | copy-start | bytes 2162692
  136.0 38.1 %collective-permute-start.22 = (bf16[704,512]{1,0:T(8,128)(2,1)S(1)}, bf16[704,512]{1,0:T(8,128)(2,1)}, u32[]{:S(2)}, u32[]{:S(2)}) collective-permute-start(bf16[704,512]{1,0:T(8,128)(2,1)S(1)} %collective-permute-done.21.refs_6_), channel_id=1, source_target_pairs={{8,0},{16,24},{9,1},{17,25},{10,2},{18,26},{11,3},{19,27},{12,4},{... | collective-permute-start | bytes 2162696 | tf_op jit(solution)/shard_map/ppermute | solution.py:525
  147.8 1.1 copy-start.6
  157.4 1.3 copy-start.14
  157.4 30.2 %collective-permute-start.23 = (bf16[704,512]{1,0:T(8,128)(2,1)}, bf16[704,512]{1,0:T(8,128)(2,1)S(1)}, u32[]{:S(2)}, u32[]{:S(2)}) collective-permute-start(bf16[704,512]{1,0:T(8,128)(2,1)} %collective-permute-done.20.refs_10_.refs_8_), channel_id=1, source_target_pairs={{8,0},{16,24},{9,1},{17,25},{10,2},{18,26},{11,3},{19,27},{12,4},{... | collective-permute-start | bytes 2162696 | tf_op jit(solution)/shard_map/ppermute | solution.py:525
  169.9 27.3 %all-to-all-start.2 = ((bf16[8,40,1024]{2,1,0:T(8,128)(2,1)}), bf16[8,40,1024]{2,1,0:T(8,128)(2,1)S(1)}, u32[]{:S(2)}, u32[]{:S(2)}) async-start(bf16[8,40,1024]{2,1,0:T(8,128)(2,1)} %bitcast.52), calls=%async_computation.2 | async-start | bytes 1310720 | tf_op jit(solution)/shard_map/all_to_all | solution.py:547
  187.6 0.9 copy-start.16
  197.2 29.2 %copy-start = (bf16[1,128,2048]{2,1,0:T(8,128)(2,1)S(1)}, bf16[1,128,2048]{2,1,0:T(8,128)(2,1)}, u32[]{:S(2)}) copy-start(bf16[1,128,2048]{2,1,0:T(8,128)(2,1)} %param.22) | copy-start | bytes 1572868
  197.2 29.2 %copy-start.1 = (f32[1,128,2]{2,1,0:T(8,128)S(1)}, f32[1,128,2]{2,1,0:T(8,128)}, u32[]{:S(2)}) copy-start(f32[1,128,2]{2,1,0:T(8,128)} %copy.15) | copy-start | bytes 3076
  197.2 29.2 %copy-start.2 = (bf16[128,2048]{1,0:T(8,128)(2,1)S(1)}, bf16[128,2048]{1,0:T(8,128)(2,1)}, u32[]{:S(2)}) copy-start(bf16[128,2048]{1,0:T(8,128)(2,1)} %get-tuple-element.55.refs_4_) | copy-start | bytes 1572868
  197.2 29.2 %copy-start.3 = (f32[2048]{0:T(1024)S(1)}, f32[2048]{0:T(1024)}, u32[]{:S(2)}) copy-start(f32[2048]{0:T(1024)} %param.16) | copy-start | bytes 24580
  197.2 29.2 %copy-start.4 = (s32[10]{0:T(128)S(1)}, s32[10]{0:T(128)}, u32[]{:S(2)}) copy-start(s32[10]{0:T(128)} %dynamic-slice_bitcast_fusion.refs_0_) | copy-start | bytes 124
  (1 other events, 0.7 us)

commit v13 on v12

--- a/solution.py
+++ b/solution.py
@@ -225,7 +225,7 @@
     mid = send(mid, MIDDLE)
     far = send(far, [(2, 0), (1, 3)])
     up_far = send(up_mid, OUTWARD, pieces[0])
-    near = send(near, OUTWARD, up_far, far)
+    near = send(near, OUTWARD, up_far)
     gate_mid_near = send(gate_inner, MIDDLE, pieces[0])
     up_mid_near = send(up_inner, MIDDLE, pieces[0])
     down_mid = send(down, MIDDLE, gate_mid_near)

time: 231 us -> 226 us (0.978)
  waiting for transfers between devices: 84.8 us -> 75 us
  starting transfers between devices: 68.7 us -> 73.8 us
    ppermute x24, waiting for transfers between devices: 74.3 us -> 63.2 us  [send(): return lax.ppermute(gated(array, *first), 'seq', pairs)]
    ppermute x24, starting transfers between devices: 56.9 us -> 62 us  [send(): return lax.ppermute(gated(array, *first), 'seq', pairs)]
where the time goes in v13:
time: 226 us; the launch traced here: 225 us
  waiting for transfers between devices  75 us (33%)
  starting transfers between devices  73.8 us (33%)
  Pallas kernels  39.1 us (17%)
  blocking collectives  29.2 us (13%)
  local copies, waits for them, and re-layouts  6.88 us (3%)
    ppermute x24, waiting for transfers between devices, send(): return lax.ppermute(gated(array, *first), 'seq', pairs)  63.2 us
    ppermute x24, starting transfers between devices, send(): return lax.ppermute(gated(array, *first), 'seq', pairs)  62 us
    pallas_call x9, Pallas kernels, call(): pl.pallas_call(body, grid=() if held else (1,), out_shape=outs, in_specs=...  39.1 us
    all_to_all x1, blocking collectives, exchange(): rows = lax.all_to_all(rows, axis, split_axis=0, concat_axis=0, tiled=True)  29.2 us
    all_to_all x3, waiting for transfers between devices, exchange(): rows = lax.all_to_all(rows, axis, split_axis=0, concat_axis=0, tiled=True)  11.9 us
    all_to_all x3, starting transfers between devices, exchange(): rows = lax.all_to_all(rows, axis, split_axis=0, concat_axis=0, tiled=True)  11.8 us
    unnamed x46, local copies, waits for them, and re-layouts  5.01 us
  transfers between devices with their start and end apart: 27, of which 10 were waited for; matrix products, arithmetic and copies ran while one was open for 1% of the time, Pallas kernels for 16%

profile of v13, /device:TPU:0, one launch (start us, length us, event | category | flops | bytes accessed | tf_op | source)
XLA Modules:
  0.0 225.0 jit_solution(14977528648057316714)
XLA Ops:
  0.6 0.8 collective-permute-start
  1.5 1.3 collective-permute-start.1
  2.8 1.3 dynamic-slice_bitcast_fusion.refs_0_
  4.1 2.7 %shard_map.131 = (bf16[384,1024]{1,0:T(8,128)(2,1)}, bf16[384,1024]{1,0:T(8,128)(2,1)}) custom-call(s32[10]{0:T(128)} %dynamic-slice_bitcast_fusion.refs_0_, bf16[128,2048]{1,0:T(8,128)(2,1)} %bitcast.53, bf16[128,2048]{1,0:T(8,128)(2,1)} %bitcast.54, bf16[128,2048]{1,0:T(8,128)(2,1)} %bitcast.55), custom_call_target="tpu_custom_call" | custom-call | bytes 3145728 | tf_op jit(solution)/shard_map/pallas_call | solution.py:35
  6.8 17.9 %collective-permute-done.1.refs_5_.refs_4_.refs_12_ = bf16[704,512]{1,0:T(8,128)(2,1)S(1)} collective-permute-done((bf16[704,512]{1,0:T(8,128)(2,1)}, bf16[704,512]{1,0:T(8,128)(2,1)S(1)}, u32[]{:S(2)}, u32[]{:S(2)}) %collective-permute-start.1) | collective-permute-done | bytes 720928 | tf_op jit(solution)/shard_map/ppermute | solution.py:525
  24.6 2.5 %collective-permute-start.2 = (bf16[384,1024]{1,0:T(8,128)(2,1)}, bf16[384,1024]{1,0:T(8,128)(2,1)}, u32[]{:S(2)}, u32[]{:S(2)}) collective-permute-start(bf16[384,1024]{1,0:T(8,128)(2,1)} %get-tuple-element.38.refs_1_), channel_id=1, source_target_pairs={{0,8},{24,16},{1,9},{25,17},{2,10},{26,18},{3,11},{27,19},{4,12},{... | collective-permute-start | bytes 2359304 | tf_op jit(solution)/shard_map/ppermute | solution.py:525
  27.1 1.5 collective-permute-start.3
  28.6 3.1 %collective-permute-start.4 = (bf16[384,1024]{1,0:T(8,128)(2,1)}, bf16[384,1024]{1,0:T(8,128)(2,1)}, u32[]{:S(2)}, u32[]{:S(2)}) collective-permute-start(bf16[384,1024]{1,0:T(8,128)(2,1)} %get-tuple-element.40), channel_id=1, source_target_pairs={{0,16},{24,8},{1,17},{25,9},{2,18},{26,10},{3,19},{27,11},{4,20},{... | collective-permute-start | bytes 2359304 | tf_op jit(solution)/shard_map/ppermute | solution.py:525
  31.8 1.3 collective-permute-start.5
  33.2 0.7 copy.15
  34.5 3.2 %shard_map.132 = bf16[320,2048]{1,0:T(8,128)(2,1)} custom-call(s32[2,128]{1,0:T(2,128)} %copy.17.refs_0_.refs_1_, f32[128,2]{1,0:T(8,128)} %bitcast.33, bf16[128,2048]{1,0:T(8,128)(2,1)} %bitcast.31), custom_call_target="tpu_custom_call" | custom-call | flops 335544320 | bytes 1835008 | tf_op jit(solution)/shard_map/pallas_call | solution.py:35
  37.7 3.9 %all-to-all-start = ((bf16[8,40,2048]{2,1,0:T(8,128)(2,1)}), bf16[8,40,2048]{2,1,0:T(8,128)(2,1)S(1)}, u32[]{:S(2)}, u32[]{:S(2)}) async-start(bf16[8,40,2048]{2,1,0:T(8,128)(2,1)} %bitcast.45), calls=%async_computation | async-start | bytes 2621440 | tf_op jit(solution)/shard_map/all_to_all | solution.py:547
  41.6 1.3 collective-permute-start.6
  42.9 1.6 collective-permute-done.2.refs_2_
  44.5 14.8 %collective-permute-done.4.refs_4_ = bf16[384,1024]{1,0:T(8,128)(2,1)} collective-permute-done((bf16[384,1024]{1,0:T(8,128)(2,1)}, bf16[384,1024]{1,0:T(8,128)(2,1)}, u32[]{:S(2)}, u32[]{:S(2)}) %collective-permute-start.4) | collective-permute-done | bytes 786464 | tf_op jit(solution)/shard_map/ppermute | solution.py:525
  59.3 1.5 collective-permute-start.9
  60.8 8.0 %collective-permute-start.7 = (bf16[704,512]{1,0:T(8,128)(2,1)S(1)}, bf16[704,512]{1,0:T(8,128)(2,1)}, u32[]{:S(2)}, u32[]{:S(2)}) collective-permute-start(bf16[704,512]{1,0:T(8,128)(2,1)S(1)} %bitcast.50), channel_id=1, source_target_pairs={{0,8},{24,16},{1,9},{25,17},{2,10},{26,18},{3,11},{27,19},{4,12},{... | collective-permute-start | bytes 2162696 | tf_op jit(solution)/shard_map/ppermute | solution.py:525
  68.9 1.3 collective-permute-start.8
  70.2 1.1 copy-done.5
  71.5 1.7 shard_map.133
  73.2 1.3 collective-permute-start.10
  74.5 13.3 %collective-permute-start.16 = (bf16[704,512]{1,0:T(8,128)(2,1)}, bf16[704,512]{1,0:T(8,128)(2,1)}, u32[]{:S(2)}, u32[]{:S(2)}) collective-permute-start(bf16[704,512]{1,0:T(8,128)(2,1)} %bitcast.13.refs_3_.refs_17_), channel_id=1, source_target_pairs={{0,8},{24,16},{1,9},{25,17},{2,10},{26,18},{3,11},{27,19},{4,12},{... | collective-permute-start | bytes 2162696 | tf_op jit(solution)/shard_map/ppermute | solution.py:525
  89.7 1.3 collective-permute-start.13
  91.0 10.1 %collective-permute-done.10.refs_7_.refs_21_ = bf16[704,512]{1,0:T(8,128)(2,1)S(1)} collective-permute-done((bf16[704,512]{1,0:T(8,128)(2,1)}, bf16[704,512]{1,0:T(8,128)(2,1)S(1)}, u32[]{:S(2)}, u32[]{:S(2)}) %collective-permute-start.10) | collective-permute-done | bytes 720928 | tf_op jit(solution)/shard_map/ppermute | solution.py:525
  101.1 1.3 collective-permute-start.11
  102.4 1.6 collective-permute-start.17
  104.0 11.9 %collective-permute-start.19 = (bf16[704,512]{1,0:T(8,128)(2,1)}, bf16[704,512]{1,0:T(8,128)(2,1)}, u32[]{:S(2)}, u32[]{:S(2)}) collective-permute-start(bf16[704,512]{1,0:T(8,128)(2,1)} %bitcast.17.refs_3_), channel_id=1, source_target_pairs={{0,8},{24,16},{1,9},{25,17},{2,10},{26,18},{3,11},{27,19},{4,12},{... | collective-permute-start | bytes 2162696 | tf_op jit(solution)/shard_map/ppermute | solution.py:525
  115.9 1.3 collective-permute-start.15
  117.2 1.0 collective-permute-done.13.refs_7_
  118.9 3.3 %shard_map.134 = (bf16[128,2048]{1,0:T(8,128)(2,1)}, bf16[320,2048]{1,0:T(8,128)(2,1)}) custom-call(s32[10]{0:T(128)} %dynamic-slice_bitcast_fusion.refs_0_, s32[2,128]{1,0:T(2,128)} %copy.17.refs_0_.refs_1_, bf16[128,2048]{1,0:T(8,128)(2,1)} %bitcast.56, f32[1,2048]{1,0:T(1,128)} %bitcast.37, bf16[128,1024]{1,0:T(8,128)(2,1)} %get-tuple-element.47.refs_4_, ...), custom_call_target="tpu_custom_call" | custom-call | flops 167772160 | bytes 2883584 | tf_op jit(solution)/shard_map/pallas_call | solution.py:35
  122.2 3.7 %all-to-all-start.1 = ((bf16[8,40,2048]{2,1,0:T(8,128)(2,1)}), bf16[8,40,2048]{2,1,0:T(8,128)(2,1)S(1)}, u32[]{:S(2)}, u32[]{:S(2)}) async-start(bf16[8,40,2048]{2,1,0:T(8,128)(2,1)} %bitcast.51), calls=%async_computation.1 | async-start | bytes 2621440 | tf_op jit(solution)/shard_map/all_to_all | solution.py:547
  126.7 1.5 collective-permute-start.20
  128.2 1.5 collective-permute-done.15.refs_8_.refs_16_
  129.7 1.3 collective-permute-start.18
  131.0 1.3 collective-permute-start.22
  132.3 11.9 %all-to-all-done.1 = bf16[8,40,2048]{2,1,0:T(8,128)(2,1)S(1)} async-done(((bf16[8,40,2048]{2,1,0:T(8,128)(2,1)}), bf16[8,40,2048]{2,1,0:T(8,128)(2,1)S(1)}, u32[]{:S(2)}, u32[]{:S(2)}) %all-to-all-start.1) | async-done | bytes 1310752 | tf_op jit(solution)/shard_map/all_to_all | solution.py:547
  144.2 1.1 copy-done.6
  145.2 5.3 %shard_map.135.refs_2_ = f32[320,704]{1,0:T(8,128)} custom-call(s32[10]{0:T(128)} %dynamic-slice_bitcast_fusion.refs_0_, bf16[320,2048]{1,0:T(8,128)(2,1)} %bitcast.42, bf16[704,512]{1,0:T(8,128)(2,1)} %bitcast.48, bf16[704,512]{1,0:T(8,128)(2,1)} %collective-permute-done.7.refs_3_.refs_11_, bf16[704,512]{1,0:T(8,128)(2,1)} %copy-done.7, ...), custom_call_target="tpu_custom_call" | custom-call | flops 922746880 | bytes 5095424 | tf_op jit(solution)/shard_map/pallas_call | solution.py:35
  150.5 2.3 %collective-permute-done.18.refs_9_.refs_23_ = bf16[704,512]{1,0:T(8,128)(2,1)S(1)} collective-permute-done((bf16[704,512]{1,0:T(8,128)(2,1)}, bf16[704,512]{1,0:T(8,128)(2,1)S(1)}, u32[]{:S(2)}, u32[]{:S(2)}) %collective-permute-start.18) | collective-permute-done | bytes 720928 | tf_op jit(solution)/shard_map/ppermute | solution.py:525
  152.8 1.3 collective-permute-start.23
  154.1 6.0 %shard_map.136 = (bf16[320,704]{1,0:T(8,128)(2,1)}, f32[320,704]{1,0:T(8,128)}, f32[320,704]{1,0:T(8,128)}) custom-call(s32[10]{0:T(128)} %dynamic-slice_bitcast_fusion.refs_0_, bf16[320,2048]{1,0:T(8,128)(2,1)} %bitcast.43, f32[320,704]{1,0:T(8,128)} %shard_map.135.refs_2_, bf16[704,512]{1,0:T(8,128)(2,1)} %bitcast.13.refs_3_.refs_17_, ...), custom_call_target="tpu_custom_call" | custom-call | flops 922746880 | bytes 7348224 | tf_op jit(solution)/shard_map/pallas_call | solution.py:35
  160.1 5.2 %shard_map.137 = (bf16[320,1024]{1,0:T(8,128)(2,1)}, f32[320,704]{1,0:T(8,128)}) custom-call(s32[10]{0:T(128)} %dynamic-slice_bitcast_fusion.refs_0_, bf16[320,704]{1,0:T(8,128)(2,1)} %get-tuple-element.62.refs_1_, bf16[320,2048]{1,0:T(8,128)(2,1)} %bitcast.40, bf16[704,512]{1,0:T(8,128)(2,1)} %bitcast.17.refs_3_, ...), custom_call_target="tpu_custom_call" | custom-call | flops 922746880 | bytes 4759552 | tf_op jit(solution)/shard_map/pallas_call | solution.py:35
  165.3 4.3 %all-to-all-start.2 = ((bf16[8,40,1024]{2,1,0:T(8,128)(2,1)}), bf16[8,40,1024]{2,1,0:T(8,128)(2,1)S(1)}, u32[]{:S(2)}, u32[]{:S(2)}) async-start(bf16[8,40,1024]{2,1,0:T(8,128)(2,1)} %bitcast.52), calls=%async_computation.2 | async-start | bytes 1310720 | tf_op jit(solution)/shard_map/all_to_all | solution.py:547
  169.6 13.4 %collective-permute-done.23.refs_9_ = bf16[704,512]{1,0:T(8,128)(2,1)S(1)} collective-permute-done((bf16[704,512]{1,0:T(8,128)(2,1)}, bf16[704,512]{1,0:T(8,128)(2,1)S(1)}, u32[]{:S(2)}, u32[]{:S(2)}) %collective-permute-start.23) | collective-permute-done | bytes 720928 | tf_op jit(solution)/shard_map/ppermute | solution.py:525
  183.0 0.9 copy-done.16
  184.0 8.7 %shard_map.138 = bf16[320,3072]{1,0:T(8,128)(2,1)} custom-call(s32[10]{0:T(128)} %dynamic-slice_bitcast_fusion.refs_0_, bf16[320,704]{1,0:T(8,128)(2,1)} %get-tuple-element.62.refs_1_, bf16[320,2048]{1,0:T(8,128)(2,1)} %bitcast.41, f32[320,704]{1,0:T(8,128)} %get-tuple-element.64.refs_3_, f32[320,704]{1,0:T(8,128)} %get-tuple-element.65.refs_4_, ...), custom_call_target="tpu_custom_call" | custom-call | flops 2768240640 | bytes 12984320 | tf_op jit(solution)/shard_map/pallas_call | solution.py:35
  192.7 29.2 %all_to_all.20 = bf16[8,40,3072]{2,1,0:T(8,128)(2,1)S(1)} all-to-all(bf16[8,40,3072]{2,1,0:T(8,128)(2,1)} %bitcast.44), channel_id=1, replica_groups=mesh['seq'=4,'exp'=8] {'exp'}, dimensions={0} | all-to-all | bytes 3932160 | tf_op jit(solution)/shard_map/all_to_all | solution.py:547
  222.0 3.1 %shard_map.139 = (bf16[128,2048]{1,0:T(8,128)(2,1)}, bf16[128,2048]{1,0:T(8,128)(2,1)}) custom-call(s32[10]{0:T(128)S(1)} %copy-done.4, s32[128,2]{1,0:T(8,128)S(1)} %bitcast.36, f32[128,2]{1,0:T(8,128)S(1)} %bitcast.34, f32[1,2048]{1,0:T(1,128)S(1)} %bitcast.38, bf16[128,2048]{1,0:T(8,128)(2,1)S(1)} %copy-done.2, bf16[128,2048]{1,0:T(8,128)(2,1)S(1)} %bitcast.32, ...), custom_call_target="tpu_custom_call" | custom-call | flops 503316480 | bytes 4718592 | tf_op jit(solution)/shard_map/pallas_call | solution.py:35
  (64 shorter events, 4.4 us)
Async XLA Ops:
  0.6 32.4 %copy-start.20 = (s32[1,128,2]{1,2,0:T(2,128)S(1)}, s32[1,128,2]{1,2,0:T(2,128)}, u32[]{:S(2)}) copy-start(s32[1,128,2]{1,2,0:T(2,128)} %param.20) | copy-start | bytes 3076
  0.6 32.6 %copy-start.21 = (f32[1,128,2]{1,2,0:T(2,128)S(1)}, f32[1,128,2]{1,2,0:T(2,128)}, u32[]{:S(2)}) copy-start(f32[1,128,2]{1,2,0:T(2,128)} %param.21) | copy-start | bytes 3076
  0.6 6.1 %collective-permute-start = (bf16[704,512]{1,0:T(8,128)(2,1)}, bf16[704,512]{1,0:T(8,128)(2,1)S(1)}, u32[]{:S(2)}, u32[]{:S(2)}) collective-permute-start(bf16[704,512]{1,0:T(8,128)(2,1)} %bitcast.46), channel_id=1, source_target_pairs={{8,16},{16,8},{9,17},{17,9},{10,18},{18,10},{11,19},{19,11},{12,20... | collective-permute-start | bytes 2162696 | tf_op jit(solution)/shard_map/ppermute | solution.py:525
  1.5 23.1 %collective-permute-start.1 = (bf16[704,512]{1,0:T(8,128)(2,1)}, bf16[704,512]{1,0:T(8,128)(2,1)S(1)}, u32[]{:S(2)}, u32[]{:S(2)}) collective-permute-start(bf16[704,512]{1,0:T(8,128)(2,1)} %bitcast.47), channel_id=1, source_target_pairs={{8,0},{16,24},{9,1},{17,25},{10,2},{18,26},{11,3},{19,27},{12,4},{... | collective-permute-start | bytes 2162696 | tf_op jit(solution)/shard_map/ppermute | solution.py:525
  6.8 25.0 %copy-start.12 = (bf16[704,512]{1,0:T(8,128)(2,1)}, bf16[704,512]{1,0:T(8,128)(2,1)S(1)}, u32[]{:S(2)}) copy-start(bf16[704,512]{1,0:T(8,128)(2,1)S(1)} %collective-permute-done.refs_5_.refs_13_) | copy-start | bytes 2162692
  24.6 13.1 %copy-start.7 = (bf16[704,512]{1,0:T(8,128)(2,1)}, bf16[704,512]{1,0:T(8,128)(2,1)S(1)}, u32[]{:S(2)}) copy-start(bf16[704,512]{1,0:T(8,128)(2,1)S(1)} %collective-permute-done.1.refs_5_.refs_4_.refs_12_) | copy-start | bytes 2162692
  24.6 19.8 %collective-permute-start.2 = (bf16[384,1024]{1,0:T(8,128)(2,1)}, bf16[384,1024]{1,0:T(8,128)(2,1)}, u32[]{:S(2)}, u32[]{:S(2)}) collective-permute-start(bf16[384,1024]{1,0:T(8,128)(2,1)} %get-tuple-element.38.refs_1_), channel_id=1, source_target_pairs={{0,8},{24,16},{1,9},{25,17},{2,10},{26,18},{3,11},{27,19},{4,12},{... | collective-permute-start | bytes 2359304 | tf_op jit(solution)/shard_map/ppermute | solution.py:525
  27.1 17.4 %collective-permute-start.3 = (bf16[384,1024]{1,0:T(8,128)(2,1)}, bf16[384,1024]{1,0:T(8,128)(2,1)}, u32[]{:S(2)}, u32[]{:S(2)}) collective-permute-start(bf16[384,1024]{1,0:T(8,128)(2,1)} %get-tuple-element.40), channel_id=1, source_target_pairs={{8,16},{16,8},{9,17},{17,9},{10,18},{18,10},{11,19},{19,11},{12,20... | collective-permute-start | bytes 2359304 | tf_op jit(solution)/shard_map/ppermute | solution.py:525
  28.6 30.7 %collective-permute-start.4 = (bf16[384,1024]{1,0:T(8,128)(2,1)}, bf16[384,1024]{1,0:T(8,128)(2,1)}, u32[]{:S(2)}, u32[]{:S(2)}) collective-permute-start(bf16[384,1024]{1,0:T(8,128)(2,1)} %get-tuple-element.40), channel_id=1, source_target_pairs={{0,16},{24,8},{1,17},{25,9},{2,18},{26,10},{3,19},{27,11},{4,20},{... | collective-permute-start | bytes 2359304 | tf_op jit(solution)/shard_map/ppermute | solution.py:525
  31.8 29.1 %collective-permute-start.5 = (bf16[704,512]{1,0:T(8,128)(2,1)}, bf16[704,512]{1,0:T(8,128)(2,1)S(1)}, u32[]{:S(2)}, u32[]{:S(2)}) collective-permute-start(bf16[704,512]{1,0:T(8,128)(2,1)} %bitcast.13.refs_3_.refs_17_), channel_id=1, source_target_pairs={{8,0},{16,24},{9,1},{17,25},{10,2},{18,26},{11,3},{19,27},{12,4},{... | collective-permute-start | bytes 2162696 | tf_op jit(solution)/shard_map/ppermute | solution.py:525
  37.7 23.1 %copy-start.11 = (bf16[1,512,704]{1,2,0:T(8,128)(2,1)S(1)}, bf16[1,512,704]{1,2,0:T(8,128)(2,1)}, u32[]{:S(2)}) copy-start(bf16[1,512,704]{1,2,0:T(8,128)(2,1)} %param.17) | copy-start | bytes 2162692
  37.7 32.4 %all-to-all-start = ((bf16[8,40,2048]{2,1,0:T(8,128)(2,1)}), bf16[8,40,2048]{2,1,0:T(8,128)(2,1)S(1)}, u32[]{:S(2)}, u32[]{:S(2)}) async-start(bf16[8,40,2048]{2,1,0:T(8,128)(2,1)} %bitcast.45), calls=%async_computation | async-start | bytes 2621440 | tf_op jit(solution)/shard_map/all_to_all | solution.py:547
  41.6 28.6 %collective-permute-start.6 = (bf16[704,512]{1,0:T(8,128)(2,1)}, bf16[704,512]{1,0:T(8,128)(2,1)S(1)}, u32[]{:S(2)}, u32[]{:S(2)}) collective-permute-start(bf16[704,512]{1,0:T(8,128)(2,1)} %copy-done.12), channel_id=1, source_target_pairs={{8,0},{16,24},{9,1},{17,25},{10,2},{18,26},{11,3},{19,27},{12,4},{... | collective-permute-start | bytes 2162696 | tf_op jit(solution)/shard_map/ppermute | solution.py:525
  59.3 13.8 %collective-permute-start.9 = (bf16[704,512]{1,0:T(8,128)(2,1)}, bf16[704,512]{1,0:T(8,128)(2,1)}, u32[]{:S(2)}, u32[]{:S(2)}) collective-permute-start(bf16[704,512]{1,0:T(8,128)(2,1)} %bitcast.13.refs_3_.refs_17_), channel_id=1, source_target_pairs={{8,16},{16,8},{9,17},{17,9},{10,18},{18,10},{11,19},{19,11},{12,20... | collective-permute-start | bytes 2162696 | tf_op jit(solution)/shard_map/ppermute | solution.py:525
  60.8 9.4 %copy-start.8 = (bf16[704,512]{1,0:T(8,128)(2,1)}, bf16[704,512]{1,0:T(8,128)(2,1)S(1)}, u32[]{:S(2)}) copy-start(bf16[704,512]{1,0:T(8,128)(2,1)S(1)} %collective-permute-done.5.refs_6_.refs_5_.refs_19_) | copy-start | bytes 2162692
  60.8 26.9 %collective-permute-start.7 = (bf16[704,512]{1,0:T(8,128)(2,1)S(1)}, bf16[704,512]{1,0:T(8,128)(2,1)}, u32[]{:S(2)}, u32[]{:S(2)}) collective-permute-start(bf16[704,512]{1,0:T(8,128)(2,1)S(1)} %bitcast.50), channel_id=1, source_target_pairs={{0,8},{24,16},{1,9},{25,17},{2,10},{26,18},{3,11},{27,19},{4,12},{... | collective-permute-start | bytes 2162696 | tf_op jit(solution)/shard_map/ppermute | solution.py:525
  68.9 20.1 %collective-permute-start.8 = (bf16[704,512]{1,0:T(8,128)(2,1)}, bf16[704,512]{1,0:T(8,128)(2,1)}, u32[]{:S(2)}, u32[]{:S(2)}) collective-permute-start(bf16[704,512]{1,0:T(8,128)(2,1)} %bitcast.17.refs_3_), channel_id=1, source_target_pairs={{8,0},{16,24},{9,1},{17,25},{10,2},{18,26},{11,3},{19,27},{12,4},{... | collective-permute-start | bytes 2162696 | tf_op jit(solution)/shard_map/ppermute | solution.py:525
  70.2 1.1 copy-start.5
  70.2 1.3 copy-start.9
  73.2 27.9 %collective-permute-start.10 = (bf16[704,512]{1,0:T(8,128)(2,1)}, bf16[704,512]{1,0:T(8,128)(2,1)S(1)}, u32[]{:S(2)}, u32[]{:S(2)}) collective-permute-start(bf16[704,512]{1,0:T(8,128)(2,1)} %collective-permute-done.9.refs_6_.refs_20_), channel_id=1, source_target_pairs={{8,0},{16,24},{9,1},{17,25},{10,2},{18,26},{11,3},{19,27},{12,4},{... | collective-permute-start | bytes 2162696 | tf_op jit(solution)/shard_map/ppermute | solution.py:525
  74.5 27.9 %collective-permute-start.16 = (bf16[704,512]{1,0:T(8,128)(2,1)}, bf16[704,512]{1,0:T(8,128)(2,1)}, u32[]{:S(2)}, u32[]{:S(2)}) collective-permute-start(bf16[704,512]{1,0:T(8,128)(2,1)} %bitcast.13.refs_3_.refs_17_), channel_id=1, source_target_pairs={{0,8},{24,16},{1,9},{25,17},{2,10},{26,18},{3,11},{27,19},{4,12},{... | collective-permute-start | bytes 2162696 | tf_op jit(solution)/shard_map/ppermute | solution.py:525
  87.8 28.1 %collective-permute-start.14 = (bf16[704,512]{1,0:T(8,128)(2,1)}, bf16[704,512]{1,0:T(8,128)(2,1)S(1)}, u32[]{:S(2)}, u32[]{:S(2)}) collective-permute-start(bf16[704,512]{1,0:T(8,128)(2,1)} %collective-permute-done.7.refs_3_.refs_11_), channel_id=1, source_target_pairs={{8,16},{16,8},{9,17},{17,9},{10,18},{18,10},{11,19},{19,11},{12,20... | collective-permute-start | bytes 2162696 | tf_op jit(solution)/shard_map/ppermute | solution.py:525
  89.0 15.0 %collective-permute-start.12 = (bf16[128,1024]{1,0:T(8,128)(2,1)}, bf16[128,1024]{1,0:T(8,128)(2,1)S(1)}, u32[]{:S(2)}, u32[]{:S(2)}) collective-permute-start(bf16[128,1024]{1,0:T(8,128)(2,1)} %get-tuple-element.52), channel_id=1, source_target_pairs={{8,16},{16,8},{9,17},{17,9},{10,18},{18,10},{11,19},{19,11},{12,20... | collective-permute-start | bytes 786440 | tf_op jit(solution)/shard_map/ppermute | solution.py:525
  89.7 28.5 %collective-permute-start.13 = (bf16[128,1024]{1,0:T(8,128)(2,1)}, bf16[128,1024]{1,0:T(8,128)(2,1)S(1)}, u32[]{:S(2)}, u32[]{:S(2)}) collective-permute-start(bf16[128,1024]{1,0:T(8,128)(2,1)} %get-tuple-element.53), channel_id=1, source_target_pairs={{16,0},{8,24},{17,1},{9,25},{18,2},{10,26},{19,3},{11,27},{20,4},{... | collective-permute-start | bytes 786440 | tf_op jit(solution)/shard_map/ppermute | solution.py:525
  101.1 49.4 %copy-start.13 = (bf16[704,512]{1,0:T(8,128)(2,1)}, bf16[704,512]{1,0:T(8,128)(2,1)S(1)}, u32[]{:S(2)}) copy-start(bf16[704,512]{1,0:T(8,128)(2,1)S(1)} %collective-permute-done.10.refs_7_.refs_21_) | copy-start | bytes 2162692
  101.1 17.0 %collective-permute-start.11 = (bf16[128,1024]{1,0:T(8,128)(2,1)}, bf16[128,1024]{1,0:T(8,128)(2,1)S(1)}, u32[]{:S(2)}, u32[]{:S(2)}) collective-permute-start(bf16[128,1024]{1,0:T(8,128)(2,1)} %get-tuple-element.51), channel_id=1, source_target_pairs={{8,0},{16,24},{9,1},{17,25},{10,2},{18,26},{11,3},{19,27},{12,4},{... | collective-permute-start | bytes 786440 | tf_op jit(solution)/shard_map/ppermute | solution.py:525
  102.4 24.3 %collective-permute-start.17 = (bf16[704,512]{1,0:T(8,128)(2,1)}, bf16[704,512]{1,0:T(8,128)(2,1)}, u32[]{:S(2)}, u32[]{:S(2)}) collective-permute-start(bf16[704,512]{1,0:T(8,128)(2,1)} %collective-permute-done.16.refs_4_.refs_18_), channel_id=1, source_target_pairs={{8,16},{16,8},{9,17},{17,9},{10,18},{18,10},{11,19},{19,11},{12,20... | collective-permute-start | bytes 2162696 | tf_op jit(solution)/shard_map/ppermute | solution.py:525
  104.0 14.1 %copy-start.17 = (bf16[128,1024]{1,0:T(8,128)(2,1)}, bf16[128,1024]{1,0:T(8,128)(2,1)S(1)}, u32[]{:S(2)}) copy-start(bf16[128,1024]{1,0:T(8,128)(2,1)S(1)} %collective-permute-done.12.refs_6_) | copy-start | bytes 786436
  104.0 22.7 %collective-permute-start.19 = (bf16[704,512]{1,0:T(8,128)(2,1)}, bf16[704,512]{1,0:T(8,128)(2,1)}, u32[]{:S(2)}, u32[]{:S(2)}) collective-permute-start(bf16[704,512]{1,0:T(8,128)(2,1)} %bitcast.17.refs_3_), channel_id=1, source_target_pairs={{0,8},{24,16},{1,9},{25,17},{2,10},{26,18},{3,11},{27,19},{4,12},{... | collective-permute-start | bytes 2162696 | tf_op jit(solution)/shard_map/ppermute | solution.py:525
  115.9 2.3 %copy-start.10 = (bf16[704,512]{1,0:T(8,128)(2,1)}, bf16[704,512]{1,0:T(8,128)(2,1)S(1)}, u32[]{:S(2)}) copy-start(bf16[704,512]{1,0:T(8,128)(2,1)S(1)} %collective-permute-done.14.refs_8_.refs_7_.refs_15_) | copy-start | bytes 2162692
  115.9 13.8 %collective-permute-start.15 = (bf16[704,512]{1,0:T(8,128)(2,1)S(1)}, bf16[704,512]{1,0:T(8,128)(2,1)}, u32[]{:S(2)}, u32[]{:S(2)}) collective-permute-start(bf16[704,512]{1,0:T(8,128)(2,1)S(1)} %collective-permute-done.14.refs_8_.refs_7_.refs_15_), channel_id=1, source_target_pairs={{8,0},{16,24},{9,1},{17,25},{10,2},{18,26},{11,3},{19,27},{12,4},{... | collective-permute-start | bytes 2162696 | tf_op jit(solution)/shard_map/ppermute | solution.py:525
  118.1 0.8 copy-start.19
  122.2 21.9 %all-to-all-start.1 = ((bf16[8,40,2048]{2,1,0:T(8,128)(2,1)}), bf16[8,40,2048]{2,1,0:T(8,128)(2,1)S(1)}, u32[]{:S(2)}, u32[]{:S(2)}) async-start(bf16[8,40,2048]{2,1,0:T(8,128)(2,1)} %bitcast.51), calls=%async_computation.1 | async-start | bytes 2621440 | tf_op jit(solution)/shard_map/all_to_all | solution.py:547
  125.9 5.0 %collective-permute-start.21 = (bf16[704,512]{1,0:T(8,128)(2,1)}, bf16[704,512]{1,0:T(8,128)(2,1)S(1)}, u32[]{:S(2)}, u32[]{:S(2)}) collective-permute-start(bf16[704,512]{1,0:T(8,128)(2,1)} %bitcast.17.refs_3_), channel_id=1, source_target_pairs={{8,16},{16,8},{9,17},{17,9},{10,18},{18,10},{11,19},{19,11},{12,20... | collective-permute-start | bytes 2162696 | tf_op jit(solution)/shard_map/ppermute | solution.py:525
  126.7 23.9 %collective-permute-start.20 = (bf16[704,512]{1,0:T(8,128)(2,1)}, bf16[704,512]{1,0:T(8,128)(2,1)}, u32[]{:S(2)}, u32[]{:S(2)}) collective-permute-start(bf16[704,512]{1,0:T(8,128)(2,1)} %collective-permute-done.19.refs_4_), channel_id=1, source_target_pairs={{8,16},{16,8},{9,17},{17,9},{10,18},{18,10},{11,19},{19,11},{12,20... | collective-permute-start | bytes 2162696 | tf_op jit(solution)/shard_map/ppermute | solution.py:525
  129.7 23.1 %collective-permute-start.18 = (bf16[704,512]{1,0:T(8,128)(2,1)}, bf16[704,512]{1,0:T(8,128)(2,1)S(1)}, u32[]{:S(2)}, u32[]{:S(2)}) collective-permute-start(bf16[704,512]{1,0:T(8,128)(2,1)} %collective-permute-done.17.refs_8_.refs_22_), channel_id=1, source_target_pairs={{8,0},{16,24},{9,1},{17,25},{10,2},{18,26},{11,3},{19,27},{12,4},{... | collective-permute-start | bytes 2162696 | tf_op jit(solution)/shard_map/ppermute | solution.py:525
  131.0 29.1 %copy-start.15 = (bf16[704,512]{1,0:T(8,128)(2,1)}, bf16[704,512]{1,0:T(8,128)(2,1)S(1)}, u32[]{:S(2)}) copy-start(bf16[704,512]{1,0:T(8,128)(2,1)S(1)} %collective-permute-done.21.refs_6_) | copy-start | bytes 2162692
  131.0 38.6 %collective-permute-start.22 = (bf16[704,512]{1,0:T(8,128)(2,1)S(1)}, bf16[704,512]{1,0:T(8,128)(2,1)}, u32[]{:S(2)}, u32[]{:S(2)}) collective-permute-start(bf16[704,512]{1,0:T(8,128)(2,1)S(1)} %collective-permute-done.21.refs_6_), channel_id=1, source_target_pairs={{8,0},{16,24},{9,1},{17,25},{10,2},{18,26},{11,3},{19,27},{12,4},{... | collective-permute-start | bytes 2162696 | tf_op jit(solution)/shard_map/ppermute | solution.py:525
  144.2 1.1 copy-start.6
  152.8 1.3 copy-start.14
  152.8 30.2 %collective-permute-start.23 = (bf16[704,512]{1,0:T(8,128)(2,1)}, bf16[704,512]{1,0:T(8,128)(2,1)S(1)}, u32[]{:S(2)}, u32[]{:S(2)}) collective-permute-start(bf16[704,512]{1,0:T(8,128)(2,1)} %collective-permute-done.20.refs_10_.refs_8_), channel_id=1, source_target_pairs={{8,0},{16,24},{9,1},{17,25},{10,2},{18,26},{11,3},{19,27},{12,4},{... | collective-permute-start | bytes 2162696 | tf_op jit(solution)/shard_map/ppermute | solution.py:525
  165.3 27.4 %all-to-all-start.2 = ((bf16[8,40,1024]{2,1,0:T(8,128)(2,1)}), bf16[8,40,1024]{2,1,0:T(8,128)(2,1)S(1)}, u32[]{:S(2)}, u32[]{:S(2)}) async-start(bf16[8,40,1024]{2,1,0:T(8,128)(2,1)} %bitcast.52), calls=%async_computation.2 | async-start | bytes 1310720 | tf_op jit(solution)/shard_map/all_to_all | solution.py:547
  183.0 0.9 copy-start.16
  192.7 29.2 %copy-start = (bf16[1,128,2048]{2,1,0:T(8,128)(2,1)S(1)}, bf16[1,128,2048]{2,1,0:T(8,128)(2,1)}, u32[]{:S(2)}) copy-start(bf16[1,128,2048]{2,1,0:T(8,128)(2,1)} %param.22) | copy-start | bytes 1572868
  192.7 29.2 %copy-start.1 = (f32[1,128,2]{2,1,0:T(8,128)S(1)}, f32[1,128,2]{2,1,0:T(8,128)}, u32[]{:S(2)}) copy-start(f32[1,128,2]{2,1,0:T(8,128)} %copy.15) | copy-start | bytes 3076
  192.7 29.2 %copy-start.2 = (bf16[128,2048]{1,0:T(8,128)(2,1)S(1)}, bf16[128,2048]{1,0:T(8,128)(2,1)}, u32[]{:S(2)}) copy-start(bf16[128,2048]{1,0:T(8,128)(2,1)} %get-tuple-element.55.refs_4_) | copy-start | bytes 1572868
  192.7 29.2 %copy-start.3 = (f32[2048]{0:T(1024)S(1)}, f32[2048]{0:T(1024)}, u32[]{:S(2)}) copy-start(f32[2048]{0:T(1024)} %param.16) | copy-start | bytes 24580
  192.7 29.2 %copy-start.4 = (s32[10]{0:T(128)S(1)}, s32[10]{0:T(128)}, u32[]{:S(2)}) copy-start(s32[10]{0:T(128)} %dynamic-slice_bitcast_fusion.refs_0_) | copy-start | bytes 124
  (1 other events, 0.7 us)

commit v14 on v10

--- a/solution.py
+++ b/solution.py
@@ -397,6 +397,7 @@
 def down_kernel(shape, first, place_ref, hidden_ref, cot_ref, *refs):
     slots = len(shape)
     refs = list(refs)
+    before_ref = refs.pop(0) if first else None
     total = refs.pop(0)[...] if first else None
     down_in, refs = regroup(refs, shape)
     out_ref, d_hidden_ref, down_w, sems = refs
@@ -404,12 +405,15 @@
     inner = place_ref[INNER]
     for j in range(slots):
         fetch(inner, down_in[j], down_w.at[j], sems.at[j])
+    if first:
+        out_ref[:, : first * part] = before_ref[...]
     for j in range(slots):
         rows = cot_ref[:, cols_of(place_ref, first + j, part)]
         arrived(down_in[j], down_w.at[j], sems.at[j])
         term = mm(rows, down_w[j], NT)
         total = term if total is None else total + term
-        out_ref[:, j * part : (j + 1) * part] = mm(hidden_ref[...], down_w[j], NN).astype(BF)
+        at = (first + j) * part
+        out_ref[:, at : at + part] = mm(hidden_ref[...], down_w[j], NN).astype(BF)
     d_hidden_ref[...] = total
 
 
@@ -466,17 +470,15 @@
     stream_ref,
     cot_ref,
     first_ref,
-    second_ref,
     last_ref,
     output_ref,
     grad_ref,
     d_normed_ref,
 ):
     tokens, width = stream_ref.shape
-    done = first_ref.shape[1] + second_ref.shape[1]
+    done = first_ref.shape[1]
     part = width - done
     slots = width // part
-    early = first_ref.shape[1] // part
     at0, at1 = slot_cols(ids_ref[...], owners, cap)
     rows = lax.broadcasted_iota(jnp.int32, (tokens, owners * cap), 1)
     pick0, pick1 = one_hot(rows == at0), one_hot(rows == at1)
@@ -486,10 +488,8 @@
     dot = jnp.zeros((tokens, 1), F32)
     for j in range(slots):
         cols = cols_of(place_ref, j, part)
-        if j < early:
+        if j < slots - 1:
             pairs = first_ref[:, j * part : (j + 1) * part]
-        elif j < slots - 1:
-            pairs = second_ref[:, (j - early) * part : (j - early + 1) * part]
         else:
             pairs = last_ref[:, width:]
         stream = stream_ref[:, cols].astype(F32)
@@ -633,16 +633,15 @@
         moved=2 * width * ffw + 2 * total * width + 14 * total * ffw,
         after=up_after,
     )
-    d_hidden = ()
-    backs = []
+    out = d_hidden = None
     early = groups // 2
     for first, end in ((0, early), (early, groups - 1)):
         here = shape[first:end]
         out, d_hidden = call(
             functools.partial(down_kernel, here, first),
-            (sds((total, len(here) * part)), sds((total, ffw), F32)),
-            (place, hidden, cot_rows, *([d_hidden] if first else []), *flat(down_in[first:end])),
-            [SMEM] + [VMEM] * (3 if first else 2) + [HBM] * sum(here),
+            (sds((total, end * part)), sds((total, ffw), F32)),
+            (place, hidden, cot_rows, *([out, d_hidden] if first else []), *flat(down_in[first:end])),
+            [SMEM] + [VMEM] * (4 if first else 2) + [HBM] * sum(here),
             [
                 pltpu.VMEM((len(here), ffw, part), BF),
                 pltpu.SemaphoreType.DMA((len(here),)),
@@ -650,7 +649,7 @@
             flops=2 * one * len(here) // groups,
             moved=2 * width * ffw * len(here) // groups + 4 * total * width + 10 * total * ffw,
         )
-        backs.append(exchange(out, owners, "exp"))
+    back_first = exchange(out, owners, "exp")
     back = call(
         functools.partial(grad_kernel, [*shape, shape[-1]]),
         sds((total, width + part)),
@@ -684,8 +683,8 @@
     output, stream_grad = call(
         functools.partial(final_kernel, owners, cap),
         (sds((tokens, width)), sds((tokens, width))),
-        (place, ids, weights, gain, stream, cot, *backs, back_last),
-        [SMEM] + [VMEM] * 8,
+        (place, ids, weights, gain, stream, cot, back_first, back_last),
+        [SMEM] + [VMEM] * 7,
         [pltpu.VMEM((tokens, width), F32)],
         flops=6 * total * tokens * width,
         moved=4 * total * width + 8 * tokens * width,

time: 231 us -> 224 us (0.970)
  blocking collectives: 36.7 us -> 25.3 us
  waiting for transfers between devices: 69.9 us -> 73.8 us
    all_to_all x2 -> x1, blocking collectives: 36.7 us -> 25.3 us  [exchange(): rows = lax.all_to_all(rows, axis, split_axis=0, concat_axis=0, tiled=True)]
    ppermute x24, waiting for transfers between devices: 54.1 us -> 58.7 us  [send(): return lax.ppermute(gated(array, *first), 'seq', pairs)]
  transfers between devices with their start and end apart: 27 -> 27, of which waited for: 11 -> 12; matrix products, arithmetic and copies ran while one was open for 1% -> 1% of each run, Pallas kernels for 17% -> 18%
where the time goes in v14:
time: 224 us; the launch traced here: 223 us
  waiting for transfers between devices  73.8 us (33%)
  starting transfers between devices  73 us (33%)
  Pallas kernels  43 us (19%)
  blocking collectives  25.3 us (11%)
  local copies, waits for them, and re-layouts  6.6 us (3%)
    ppermute x24, starting transfers between devices, send(): return lax.ppermute(gated(array, *first), 'seq', pairs)  61.7 us
    ppermute x24, waiting for transfers between devices, send(): return lax.ppermute(gated(array, *first), 'seq', pairs)  58.7 us
    pallas_call x10, Pallas kernels, call(): pl.pallas_call(body, grid=() if held else (1,), out_shape=outs, in_specs=...  43 us
    all_to_all x1, blocking collectives, exchange(): rows = lax.all_to_all(rows, axis, split_axis=0, concat_axis=0, tiled=True)  25.3 us
    all_to_all x3, waiting for transfers between devices, exchange(): rows = lax.all_to_all(rows, axis, split_axis=0, concat_axis=0, tiled=True)  15.1 us
    all_to_all x3, starting transfers between devices, exchange(): rows = lax.all_to_all(rows, axis, split_axis=0, concat_axis=0, tiled=True)  11.3 us
    unnamed x46, local copies, waits for them, and re-layouts  4.76 us
  transfers between devices with their start and end apart: 27, of which 12 were waited for; matrix products, arithmetic and copies ran while one was open for 1% of the time, Pallas kernels for 18%

profile of v14, /device:TPU:0, one launch (start us, length us, event | category | flops | bytes accessed | tf_op | source)
XLA Modules:
  0.0 222.8 jit_solution(17113425154356496902)
XLA Ops:
  1.5 1.3 collective-permute-start.1
  2.8 1.2 dynamic-slice_bitcast_fusion.refs_0_
  4.0 2.6 %shard_map.131 = (bf16[384,1024]{1,0:T(8,128)(2,1)}, bf16[384,1024]{1,0:T(8,128)(2,1)}) custom-call(s32[10]{0:T(128)} %dynamic-slice_bitcast_fusion.refs_0_, bf16[128,2048]{1,0:T(8,128)(2,1)} %bitcast.54, bf16[128,2048]{1,0:T(8,128)(2,1)} %bitcast.55, bf16[128,2048]{1,0:T(8,128)(2,1)} %bitcast.56), custom_call_target="tpu_custom_call" | custom-call | bytes 3145728 | tf_op jit(solution)/shard_map/pallas_call | solution.py:35
  6.6 18.0 %collective-permute-done.1.refs_5_.refs_4_.refs_10_ = bf16[704,512]{1,0:T(8,128)(2,1)S(1)} collective-permute-done((bf16[704,512]{1,0:T(8,128)(2,1)}, bf16[704,512]{1,0:T(8,128)(2,1)S(1)}, u32[]{:S(2)}, u32[]{:S(2)}) %collective-permute-start.1) | collective-permute-done | bytes 720928 | tf_op jit(solution)/shard_map/ppermute | solution.py:521
  24.6 2.4 %collective-permute-start.2 = (bf16[384,1024]{1,0:T(8,128)(2,1)}, bf16[384,1024]{1,0:T(8,128)(2,1)}, u32[]{:S(2)}, u32[]{:S(2)}) collective-permute-start(bf16[384,1024]{1,0:T(8,128)(2,1)} %get-tuple-element.39.refs_1_), channel_id=1, source_target_pairs={{0,8},{24,16},{1,9},{25,17},{2,10},{26,18},{3,11},{27,19},{4,12},{... | collective-permute-start | bytes 2359304 | tf_op jit(solution)/shard_map/ppermute | solution.py:521
  27.1 1.6 collective-permute-start.3
  28.7 3.1 %collective-permute-start.4 = (bf16[384,1024]{1,0:T(8,128)(2,1)}, bf16[384,1024]{1,0:T(8,128)(2,1)}, u32[]{:S(2)}, u32[]{:S(2)}) collective-permute-start(bf16[384,1024]{1,0:T(8,128)(2,1)} %get-tuple-element.41), channel_id=1, source_target_pairs={{0,16},{24,8},{1,17},{25,9},{2,18},{26,10},{3,19},{27,11},{4,20},{... | collective-permute-start | bytes 2359304 | tf_op jit(solution)/shard_map/ppermute | solution.py:521
  31.8 1.3 collective-permute-start.5
  34.5 3.2 %shard_map.132 = bf16[320,2048]{1,0:T(8,128)(2,1)} custom-call(s32[2,128]{1,0:T(2,128)} %copy.17.refs_0_.refs_1_, f32[128,2]{1,0:T(8,128)} %bitcast.33, bf16[128,2048]{1,0:T(8,128)(2,1)} %bitcast.31), custom_call_target="tpu_custom_call" | custom-call | flops 335544320 | bytes 1835008 | tf_op jit(solution)/shard_map/pallas_call | solution.py:35
  37.7 3.9 %all-to-all-start = ((bf16[8,40,2048]{2,1,0:T(8,128)(2,1)}), bf16[8,40,2048]{2,1,0:T(8,128)(2,1)S(1)}, u32[]{:S(2)}, u32[]{:S(2)}) async-start(bf16[8,40,2048]{2,1,0:T(8,128)(2,1)} %bitcast.46), calls=%async_computation | async-start | bytes 2621440 | tf_op jit(solution)/shard_map/all_to_all | solution.py:543
  41.6 1.3 collective-permute-start.6
  42.9 1.6 collective-permute-done.2.refs_2_
  44.5 14.8 %collective-permute-done.4.refs_4_ = bf16[384,1024]{1,0:T(8,128)(2,1)} collective-permute-done((bf16[384,1024]{1,0:T(8,128)(2,1)}, bf16[384,1024]{1,0:T(8,128)(2,1)}, u32[]{:S(2)}, u32[]{:S(2)}) %collective-permute-start.4) | collective-permute-done | bytes 786464 | tf_op jit(solution)/shard_map/ppermute | solution.py:521
  59.3 1.5 collective-permute-start.9
  60.9 8.0 %collective-permute-start.7 = (bf16[704,512]{1,0:T(8,128)(2,1)S(1)}, bf16[704,512]{1,0:T(8,128)(2,1)}, u32[]{:S(2)}, u32[]{:S(2)}) collective-permute-start(bf16[704,512]{1,0:T(8,128)(2,1)S(1)} %bitcast.51), channel_id=1, source_target_pairs={{0,8},{24,16},{1,9},{25,17},{2,10},{26,18},{3,11},{27,19},{4,12},{... | collective-permute-start | bytes 2162696 | tf_op jit(solution)/shard_map/ppermute | solution.py:521
  68.9 1.3 collective-permute-start.8
  70.2 1.0 copy-done.5
  71.4 1.7 shard_map.133
  73.1 1.3 collective-permute-start.10
  74.4 13.2 %collective-permute-start.16 = (bf16[704,512]{1,0:T(8,128)(2,1)}, bf16[704,512]{1,0:T(8,128)(2,1)}, u32[]{:S(2)}, u32[]{:S(2)}) collective-permute-start(bf16[704,512]{1,0:T(8,128)(2,1)} %bitcast.13.refs_3_.refs_15_), channel_id=1, source_target_pairs={{0,8},{24,16},{1,9},{25,17},{2,10},{26,18},{3,11},{27,19},{4,12},{... | collective-permute-start | bytes 2162696 | tf_op jit(solution)/shard_map/ppermute | solution.py:521
  89.8 1.3 collective-permute-start.13
  91.1 10.0 %collective-permute-done.10.refs_7_.refs_19_ = bf16[704,512]{1,0:T(8,128)(2,1)S(1)} collective-permute-done((bf16[704,512]{1,0:T(8,128)(2,1)}, bf16[704,512]{1,0:T(8,128)(2,1)S(1)}, u32[]{:S(2)}, u32[]{:S(2)}) %collective-permute-start.10) | collective-permute-done | bytes 720928 | tf_op jit(solution)/shard_map/ppermute | solution.py:521
  101.1 1.3 collective-permute-start.11
  102.4 1.5 collective-permute-start.17
  103.9 11.8 %collective-permute-start.19 = (bf16[704,512]{1,0:T(8,128)(2,1)}, bf16[704,512]{1,0:T(8,128)(2,1)}, u32[]{:S(2)}, u32[]{:S(2)}) collective-permute-start(bf16[704,512]{1,0:T(8,128)(2,1)} %bitcast.17.refs_3_), channel_id=1, source_target_pairs={{0,8},{24,16},{1,9},{25,17},{2,10},{26,18},{3,11},{27,19},{4,12},{... | collective-permute-start | bytes 2162696 | tf_op jit(solution)/shard_map/ppermute | solution.py:521
  115.7 1.3 collective-permute-start.15
  117.0 1.0 collective-permute-done.13.refs_7_
  119.4 3.3 %shard_map.134 = (bf16[128,2048]{1,0:T(8,128)(2,1)}, bf16[320,2048]{1,0:T(8,128)(2,1)}) custom-call(s32[10]{0:T(128)} %dynamic-slice_bitcast_fusion.refs_0_, s32[2,128]{1,0:T(2,128)} %copy.17.refs_0_.refs_1_, bf16[128,2048]{1,0:T(8,128)(2,1)} %bitcast.57, f32[1,2048]{1,0:T(1,128)} %bitcast.37, bf16[128,1024]{1,0:T(8,128)(2,1)} %get-tuple-element.48.refs_4_, ...), custom_call_target="tpu_custom_call" | custom-call | flops 167772160 | bytes 2883584 | tf_op jit(solution)/shard_map/pallas_call | solution.py:35
  122.7 3.7 %all-to-all-start.1 = ((bf16[8,40,2048]{2,1,0:T(8,128)(2,1)}), bf16[8,40,2048]{2,1,0:T(8,128)(2,1)S(1)}, u32[]{:S(2)}, u32[]{:S(2)}) async-start(bf16[8,40,2048]{2,1,0:T(8,128)(2,1)} %bitcast.52), calls=%async_computation.1 | async-start | bytes 2621440 | tf_op jit(solution)/shard_map/all_to_all | solution.py:543
  126.4 1.6 collective-permute-start.20
  128.0 1.5 collective-permute-done.15.refs_8_.refs_14_
  129.5 1.3 collective-permute-start.18
  130.8 1.3 collective-permute-start.22
  132.1 12.5 %all-to-all-done.1 = bf16[8,40,2048]{2,1,0:T(8,128)(2,1)S(1)} async-done(((bf16[8,40,2048]{2,1,0:T(8,128)(2,1)}), bf16[8,40,2048]{2,1,0:T(8,128)(2,1)S(1)}, u32[]{:S(2)}, u32[]{:S(2)}) %all-to-all-start.1) | async-done | bytes 1310752 | tf_op jit(solution)/shard_map/all_to_all | solution.py:543
  144.6 1.1 copy-done.6
  145.7 5.2 %shard_map.135.refs_2_ = f32[320,704]{1,0:T(8,128)} custom-call(s32[10]{0:T(128)} %dynamic-slice_bitcast_fusion.refs_0_, bf16[320,2048]{1,0:T(8,128)(2,1)} %bitcast.43, bf16[704,512]{1,0:T(8,128)(2,1)} %bitcast.49, bf16[704,512]{1,0:T(8,128)(2,1)} %collective-permute-done.7.refs_3_.refs_9_, bf16[704,512]{1,0:T(8,128)(2,1)} %copy-done.7, ...), custom_call_target="tpu_custom_call" | custom-call | flops 922746880 | bytes 5095424 | tf_op jit(solution)/shard_map/pallas_call | solution.py:35
  151.0 4.5 %collective-permute-done.18.refs_9_.refs_21_ = bf16[704,512]{1,0:T(8,128)(2,1)S(1)} collective-permute-done((bf16[704,512]{1,0:T(8,128)(2,1)}, bf16[704,512]{1,0:T(8,128)(2,1)S(1)}, u32[]{:S(2)}, u32[]{:S(2)}) %collective-permute-start.18) | collective-permute-done | bytes 720928 | tf_op jit(solution)/shard_map/ppermute | solution.py:521
  155.5 1.3 collective-permute-start.23
  156.8 6.0 %shard_map.136 = (bf16[320,704]{1,0:T(8,128)(2,1)}, f32[320,704]{1,0:T(8,128)}, f32[320,704]{1,0:T(8,128)}) custom-call(s32[10]{0:T(128)} %dynamic-slice_bitcast_fusion.refs_0_, bf16[320,2048]{1,0:T(8,128)(2,1)} %bitcast.44, f32[320,704]{1,0:T(8,128)} %shard_map.135.refs_2_, bf16[704,512]{1,0:T(8,128)(2,1)} %bitcast.13.refs_3_.refs_15_, ...), custom_call_target="tpu_custom_call" | custom-call | flops 922746880 | bytes 7348224 | tf_op jit(solution)/shard_map/pallas_call | solution.py:35
  162.8 5.2 %shard_map.137 = (bf16[320,1024]{1,0:T(8,128)(2,1)}, f32[320,704]{1,0:T(8,128)}) custom-call(s32[10]{0:T(128)} %dynamic-slice_bitcast_fusion.refs_0_, bf16[320,704]{1,0:T(8,128)(2,1)} %get-tuple-element.62.refs_1_, bf16[320,2048]{1,0:T(8,128)(2,1)} %bitcast.40, bf16[704,512]{1,0:T(8,128)(2,1)} %bitcast.17.refs_3_, ...), custom_call_target="tpu_custom_call" | custom-call | flops 922746880 | bytes 6316032 | tf_op jit(solution)/shard_map/pallas_call | solution.py:35
  168.0 3.0 %collective-permute-done.22.refs_6_ = bf16[704,512]{1,0:T(8,128)(2,1)} collective-permute-done((bf16[704,512]{1,0:T(8,128)(2,1)S(1)}, bf16[704,512]{1,0:T(8,128)(2,1)}, u32[]{:S(2)}, u32[]{:S(2)}) %collective-permute-start.22) | collective-permute-done | bytes 720928 | tf_op jit(solution)/shard_map/ppermute | solution.py:521
  171.0 4.8 %shard_map.138 = (bf16[320,1536]{1,0:T(8,128)(2,1)}, f32[320,704]{1,0:T(8,128)}) custom-call(s32[10]{0:T(128)} %dynamic-slice_bitcast_fusion.refs_0_, bf16[320,704]{1,0:T(8,128)(2,1)} %get-tuple-element.62.refs_1_, bf16[320,2048]{1,0:T(8,128)(2,1)} %bitcast.41, bf16[320,1024]{1,0:T(8,128)(2,1)} %get-tuple-element.63.refs_3_, ...), custom_call_target="tpu_custom_call" | custom-call | flops 461373440 | bytes 5595136 | tf_op jit(solution)/shard_map/pallas_call | solution.py:35
  175.9 3.7 %all-to-all-start.2 = ((bf16[8,40,1536]{2,1,0:T(8,128)(2,1)}), bf16[8,40,1536]{2,1,0:T(8,128)(2,1)S(1)}, u32[]{:S(2)}, u32[]{:S(2)}) async-start(bf16[8,40,1536]{2,1,0:T(8,128)(2,1)} %bitcast.53), calls=%async_computation.2 | async-start | bytes 1966080 | tf_op jit(solution)/shard_map/all_to_all | solution.py:543
  179.6 3.4 %collective-permute-done.23.refs_7_ = bf16[704,512]{1,0:T(8,128)(2,1)S(1)} collective-permute-done((bf16[704,512]{1,0:T(8,128)(2,1)}, bf16[704,512]{1,0:T(8,128)(2,1)S(1)}, u32[]{:S(2)}, u32[]{:S(2)}) %collective-permute-start.23) | collective-permute-done | bytes 720928 | tf_op jit(solution)/shard_map/ppermute | solution.py:521
  183.9 7.8 %shard_map.139 = bf16[320,2560]{1,0:T(8,128)(2,1)} custom-call(s32[10]{0:T(128)} %dynamic-slice_bitcast_fusion.refs_0_, bf16[320,704]{1,0:T(8,128)(2,1)} %get-tuple-element.62.refs_1_, bf16[320,2048]{1,0:T(8,128)(2,1)} %bitcast.42, f32[320,704]{1,0:T(8,128)} %get-tuple-element.68.refs_3_, f32[320,704]{1,0:T(8,128)} %get-tuple-element.69.refs_4_, ...), custom_call_target="tpu_custom_call" | custom-call | flops 2306867200 | bytes 11542528 | tf_op jit(solution)/shard_map/pallas_call | solution.py:35
  191.7 2.6 %all-to-all-done.2 = bf16[8,40,1536]{2,1,0:T(8,128)(2,1)S(1)} async-done(((bf16[8,40,1536]{2,1,0:T(8,128)(2,1)}), bf16[8,40,1536]{2,1,0:T(8,128)(2,1)S(1)}, u32[]{:S(2)}, u32[]{:S(2)}) %all-to-all-start.2) | async-done | bytes 983072 | tf_op jit(solution)/shard_map/all_to_all | solution.py:543
  194.3 25.3 %all_to_all.20 = bf16[8,40,2560]{2,1,0:T(8,128)(2,1)S(1)} all-to-all(bf16[8,40,2560]{2,1,0:T(8,128)(2,1)} %bitcast.45), channel_id=1, replica_groups=mesh['seq'=4,'exp'=8] {'exp'}, dimensions={0} | all-to-all | bytes 3276800 | tf_op jit(solution)/shard_map/all_to_all | solution.py:543
  219.7 3.1 %shard_map.140 = (bf16[128,2048]{1,0:T(8,128)(2,1)}, bf16[128,2048]{1,0:T(8,128)(2,1)}) custom-call(s32[10]{0:T(128)S(1)} %copy-done.3, s32[128,2]{1,0:T(8,128)S(1)} %bitcast.36, f32[128,2]{1,0:T(8,128)S(1)} %bitcast.34, f32[1,2048]{1,0:T(1,128)S(1)} %bitcast.38, bf16[128,2048]{1,0:T(8,128)(2,1)S(1)} %copy-done.2, bf16[128,2048]{1,0:T(8,128)(2,1)S(1)} %bitcast.32, ...), custom_call_target="tpu_custom_call" | custom-call | flops 503316480 | bytes 4718592 | tf_op jit(solution)/shard_map/pallas_call | solution.py:35
  (65 shorter events, 7.0 us)
Async XLA Ops:
  0.6 32.4 %copy-start.20 = (s32[1,128,2]{1,2,0:T(2,128)S(1)}, s32[1,128,2]{1,2,0:T(2,128)}, u32[]{:S(2)}) copy-start(s32[1,128,2]{1,2,0:T(2,128)} %param.20) | copy-start | bytes 3076
  0.6 32.5 %copy-start.21 = (f32[1,128,2]{1,2,0:T(2,128)S(1)}, f32[1,128,2]{1,2,0:T(2,128)}, u32[]{:S(2)}) copy-start(f32[1,128,2]{1,2,0:T(2,128)} %param.21) | copy-start | bytes 3076
  0.6 6.0 %collective-permute-start = (bf16[704,512]{1,0:T(8,128)(2,1)}, bf16[704,512]{1,0:T(8,128)(2,1)S(1)}, u32[]{:S(2)}, u32[]{:S(2)}) collective-permute-start(bf16[704,512]{1,0:T(8,128)(2,1)} %bitcast.47), channel_id=1, source_target_pairs={{8,16},{16,8},{9,17},{17,9},{10,18},{18,10},{11,19},{19,11},{12,20... | collective-permute-start | bytes 2162696 | tf_op jit(solution)/shard_map/ppermute | solution.py:521
  1.5 23.1 %collective-permute-start.1 = (bf16[704,512]{1,0:T(8,128)(2,1)}, bf16[704,512]{1,0:T(8,128)(2,1)S(1)}, u32[]{:S(2)}, u32[]{:S(2)}) collective-permute-start(bf16[704,512]{1,0:T(8,128)(2,1)} %bitcast.48), channel_id=1, source_target_pairs={{8,0},{16,24},{9,1},{17,25},{10,2},{18,26},{11,3},{19,27},{12,4},{... | collective-permute-start | bytes 2162696 | tf_op jit(solution)/shard_map/ppermute | solution.py:521
  6.6 25.1 %copy-start.12 = (bf16[704,512]{1,0:T(8,128)(2,1)}, bf16[704,512]{1,0:T(8,128)(2,1)S(1)}, u32[]{:S(2)}) copy-start(bf16[704,512]{1,0:T(8,128)(2,1)S(1)} %collective-permute-done.refs_5_.refs_11_) | copy-start | bytes 2162692
  24.6 13.1 %copy-start.7 = (bf16[704,512]{1,0:T(8,128)(2,1)}, bf16[704,512]{1,0:T(8,128)(2,1)S(1)}, u32[]{:S(2)}) copy-start(bf16[704,512]{1,0:T(8,128)(2,1)S(1)} %collective-permute-done.1.refs_5_.refs_4_.refs_10_) | copy-start | bytes 2162692
  24.6 19.8 %collective-permute-start.2 = (bf16[384,1024]{1,0:T(8,128)(2,1)}, bf16[384,1024]{1,0:T(8,128)(2,1)}, u32[]{:S(2)}, u32[]{:S(2)}) collective-permute-start(bf16[384,1024]{1,0:T(8,128)(2,1)} %get-tuple-element.39.refs_1_), channel_id=1, source_target_pairs={{0,8},{24,16},{1,9},{25,17},{2,10},{26,18},{3,11},{27,19},{4,12},{... | collective-permute-start | bytes 2359304 | tf_op jit(solution)/shard_map/ppermute | solution.py:521
  27.1 17.4 %collective-permute-start.3 = (bf16[384,1024]{1,0:T(8,128)(2,1)}, bf16[384,1024]{1,0:T(8,128)(2,1)}, u32[]{:S(2)}, u32[]{:S(2)}) collective-permute-start(bf16[384,1024]{1,0:T(8,128)(2,1)} %get-tuple-element.41), channel_id=1, source_target_pairs={{8,16},{16,8},{9,17},{17,9},{10,18},{18,10},{11,19},{19,11},{12,20... | collective-permute-start | bytes 2359304 | tf_op jit(solution)/shard_map/ppermute | solution.py:521
  28.7 30.7 %collective-permute-start.4 = (bf16[384,1024]{1,0:T(8,128)(2,1)}, bf16[384,1024]{1,0:T(8,128)(2,1)}, u32[]{:S(2)}, u32[]{:S(2)}) collective-permute-start(bf16[384,1024]{1,0:T(8,128)(2,1)} %get-tuple-element.41), channel_id=1, source_target_pairs={{0,16},{24,8},{1,17},{25,9},{2,18},{26,10},{3,19},{27,11},{4,20},{... | collective-permute-start | bytes 2359304 | tf_op jit(solution)/shard_map/ppermute | solution.py:521
  31.8 29.1 %collective-permute-start.5 = (bf16[704,512]{1,0:T(8,128)(2,1)}, bf16[704,512]{1,0:T(8,128)(2,1)S(1)}, u32[]{:S(2)}, u32[]{:S(2)}) collective-permute-start(bf16[704,512]{1,0:T(8,128)(2,1)} %bitcast.13.refs_3_.refs_15_), channel_id=1, source_target_pairs={{8,0},{16,24},{9,1},{17,25},{10,2},{18,26},{11,3},{19,27},{12,4},{... | collective-permute-start | bytes 2162696 | tf_op jit(solution)/shard_map/ppermute | solution.py:521
  37.7 23.2 %copy-start.11 = (bf16[1,512,704]{1,2,0:T(8,128)(2,1)S(1)}, bf16[1,512,704]{1,2,0:T(8,128)(2,1)}, u32[]{:S(2)}) copy-start(bf16[1,512,704]{1,2,0:T(8,128)(2,1)} %param.17) | copy-start | bytes 2162692
  37.7 32.4 %all-to-all-start = ((bf16[8,40,2048]{2,1,0:T(8,128)(2,1)}), bf16[8,40,2048]{2,1,0:T(8,128)(2,1)S(1)}, u32[]{:S(2)}, u32[]{:S(2)}) async-start(bf16[8,40,2048]{2,1,0:T(8,128)(2,1)} %bitcast.46), calls=%async_computation | async-start | bytes 2621440 | tf_op jit(solution)/shard_map/all_to_all | solution.py:543
  41.6 28.6 %collective-permute-start.6 = (bf16[704,512]{1,0:T(8,128)(2,1)}, bf16[704,512]{1,0:T(8,128)(2,1)S(1)}, u32[]{:S(2)}, u32[]{:S(2)}) collective-permute-start(bf16[704,512]{1,0:T(8,128)(2,1)} %copy-done.12), channel_id=1, source_target_pairs={{8,0},{16,24},{9,1},{17,25},{10,2},{18,26},{11,3},{19,27},{12,4},{... | collective-permute-start | bytes 2162696 | tf_op jit(solution)/shard_map/ppermute | solution.py:521
  59.3 13.8 %collective-permute-start.9 = (bf16[704,512]{1,0:T(8,128)(2,1)}, bf16[704,512]{1,0:T(8,128)(2,1)}, u32[]{:S(2)}, u32[]{:S(2)}) collective-permute-start(bf16[704,512]{1,0:T(8,128)(2,1)} %bitcast.13.refs_3_.refs_15_), channel_id=1, source_target_pairs={{8,16},{16,8},{9,17},{17,9},{10,18},{18,10},{11,19},{19,11},{12,20... | collective-permute-start | bytes 2162696 | tf_op jit(solution)/shard_map/ppermute | solution.py:521
  60.9 9.3 %copy-start.8 = (bf16[704,512]{1,0:T(8,128)(2,1)}, bf16[704,512]{1,0:T(8,128)(2,1)S(1)}, u32[]{:S(2)}) copy-start(bf16[704,512]{1,0:T(8,128)(2,1)S(1)} %collective-permute-done.5.refs_6_.refs_5_.refs_17_) | copy-start | bytes 2162692
  60.9 26.7 %collective-permute-start.7 = (bf16[704,512]{1,0:T(8,128)(2,1)S(1)}, bf16[704,512]{1,0:T(8,128)(2,1)}, u32[]{:S(2)}, u32[]{:S(2)}) collective-permute-start(bf16[704,512]{1,0:T(8,128)(2,1)S(1)} %bitcast.51), channel_id=1, source_target_pairs={{0,8},{24,16},{1,9},{25,17},{2,10},{26,18},{3,11},{27,19},{4,12},{... | collective-permute-start | bytes 2162696 | tf_op jit(solution)/shard_map/ppermute | solution.py:521
  68.9 20.3 %collective-permute-start.8 = (bf16[704,512]{1,0:T(8,128)(2,1)}, bf16[704,512]{1,0:T(8,128)(2,1)}, u32[]{:S(2)}, u32[]{:S(2)}) collective-permute-start(bf16[704,512]{1,0:T(8,128)(2,1)} %bitcast.17.refs_3_), channel_id=1, source_target_pairs={{8,0},{16,24},{9,1},{17,25},{10,2},{18,26},{11,3},{19,27},{12,4},{... | collective-permute-start | bytes 2162696 | tf_op jit(solution)/shard_map/ppermute | solution.py:521
  70.2 1.1 copy-start.5
  70.2 1.2 copy-start.9
  73.1 28.0 %collective-permute-start.10 = (bf16[704,512]{1,0:T(8,128)(2,1)}, bf16[704,512]{1,0:T(8,128)(2,1)S(1)}, u32[]{:S(2)}, u32[]{:S(2)}) collective-permute-start(bf16[704,512]{1,0:T(8,128)(2,1)} %collective-permute-done.9.refs_6_.refs_18_), channel_id=1, source_target_pairs={{8,0},{16,24},{9,1},{17,25},{10,2},{18,26},{11,3},{19,27},{12,4},{... | collective-permute-start | bytes 2162696 | tf_op jit(solution)/shard_map/ppermute | solution.py:521
  74.4 28.0 %collective-permute-start.16 = (bf16[704,512]{1,0:T(8,128)(2,1)}, bf16[704,512]{1,0:T(8,128)(2,1)}, u32[]{:S(2)}, u32[]{:S(2)}) collective-permute-start(bf16[704,512]{1,0:T(8,128)(2,1)} %bitcast.13.refs_3_.refs_15_), channel_id=1, source_target_pairs={{0,8},{24,16},{1,9},{25,17},{2,10},{26,18},{3,11},{27,19},{4,12},{... | collective-permute-start | bytes 2162696 | tf_op jit(solution)/shard_map/ppermute | solution.py:521
  87.6 28.1 %collective-permute-start.14 = (bf16[704,512]{1,0:T(8,128)(2,1)}, bf16[704,512]{1,0:T(8,128)(2,1)S(1)}, u32[]{:S(2)}, u32[]{:S(2)}) collective-permute-start(bf16[704,512]{1,0:T(8,128)(2,1)} %collective-permute-done.7.refs_3_.refs_9_), channel_id=1, source_target_pairs={{8,16},{16,8},{9,17},{17,9},{10,18},{18,10},{11,19},{19,11},{12,20... | collective-permute-start | bytes 2162696 | tf_op jit(solution)/shard_map/ppermute | solution.py:521
  89.1 14.8 %collective-permute-start.12 = (bf16[128,1024]{1,0:T(8,128)(2,1)}, bf16[128,1024]{1,0:T(8,128)(2,1)S(1)}, u32[]{:S(2)}, u32[]{:S(2)}) collective-permute-start(bf16[128,1024]{1,0:T(8,128)(2,1)} %get-tuple-element.53), channel_id=1, source_target_pairs={{8,16},{16,8},{9,17},{17,9},{10,18},{18,10},{11,19},{19,11},{12,20... | collective-permute-start | bytes 786440 | tf_op jit(solution)/shard_map/ppermute | solution.py:521
  89.8 28.2 %collective-permute-start.13 = (bf16[128,1024]{1,0:T(8,128)(2,1)}, bf16[128,1024]{1,0:T(8,128)(2,1)S(1)}, u32[]{:S(2)}, u32[]{:S(2)}) collective-permute-start(bf16[128,1024]{1,0:T(8,128)(2,1)} %get-tuple-element.54), channel_id=1, source_target_pairs={{16,0},{8,24},{17,1},{9,25},{18,2},{10,26},{19,3},{11,27},{20,4},{... | collective-permute-start | bytes 786440 | tf_op jit(solution)/shard_map/ppermute | solution.py:521
  101.1 49.9 %copy-start.13 = (bf16[704,512]{1,0:T(8,128)(2,1)}, bf16[704,512]{1,0:T(8,128)(2,1)S(1)}, u32[]{:S(2)}) copy-start(bf16[704,512]{1,0:T(8,128)(2,1)S(1)} %collective-permute-done.10.refs_7_.refs_19_) | copy-start | bytes 2162692
  101.1 17.6 %collective-permute-start.11 = (bf16[128,1024]{1,0:T(8,128)(2,1)}, bf16[128,1024]{1,0:T(8,128)(2,1)S(1)}, u32[]{:S(2)}, u32[]{:S(2)}) collective-permute-start(bf16[128,1024]{1,0:T(8,128)(2,1)} %get-tuple-element.52), channel_id=1, source_target_pairs={{8,0},{16,24},{9,1},{17,25},{10,2},{18,26},{11,3},{19,27},{12,4},{... | collective-permute-start | bytes 786440 | tf_op jit(solution)/shard_map/ppermute | solution.py:521
  102.4 24.1 %collective-permute-start.17 = (bf16[704,512]{1,0:T(8,128)(2,1)}, bf16[704,512]{1,0:T(8,128)(2,1)}, u32[]{:S(2)}, u32[]{:S(2)}) collective-permute-start(bf16[704,512]{1,0:T(8,128)(2,1)} %collective-permute-done.16.refs_4_.refs_16_), channel_id=1, source_target_pairs={{8,16},{16,8},{9,17},{17,9},{10,18},{18,10},{11,19},{19,11},{12,20... | collective-permute-start | bytes 2162696 | tf_op jit(solution)/shard_map/ppermute | solution.py:521
  103.9 14.8 %copy-start.17 = (bf16[128,1024]{1,0:T(8,128)(2,1)}, bf16[128,1024]{1,0:T(8,128)(2,1)S(1)}, u32[]{:S(2)}) copy-start(bf16[128,1024]{1,0:T(8,128)(2,1)S(1)} %collective-permute-done.12.refs_6_) | copy-start | bytes 786436
  103.9 22.5 %collective-permute-start.19 = (bf16[704,512]{1,0:T(8,128)(2,1)}, bf16[704,512]{1,0:T(8,128)(2,1)}, u32[]{:S(2)}, u32[]{:S(2)}) collective-permute-start(bf16[704,512]{1,0:T(8,128)(2,1)} %bitcast.17.refs_3_), channel_id=1, source_target_pairs={{0,8},{24,16},{1,9},{25,17},{2,10},{26,18},{3,11},{27,19},{4,12},{... | collective-permute-start | bytes 2162696 | tf_op jit(solution)/shard_map/ppermute | solution.py:521
  115.7 3.0 %copy-start.10 = (bf16[704,512]{1,0:T(8,128)(2,1)}, bf16[704,512]{1,0:T(8,128)(2,1)S(1)}, u32[]{:S(2)}) copy-start(bf16[704,512]{1,0:T(8,128)(2,1)S(1)} %collective-permute-done.14.refs_8_.refs_7_.refs_13_) | copy-start | bytes 2162692
  115.7 13.8 %collective-permute-start.15 = (bf16[704,512]{1,0:T(8,128)(2,1)S(1)}, bf16[704,512]{1,0:T(8,128)(2,1)}, u32[]{:S(2)}, u32[]{:S(2)}) collective-permute-start(bf16[704,512]{1,0:T(8,128)(2,1)S(1)} %collective-permute-done.14.refs_8_.refs_7_.refs_13_), channel_id=1, source_target_pairs={{8,0},{16,24},{9,1},{17,25},{10,2},{18,26},{11,3},{19,27},{12,4},{... | collective-permute-start | bytes 2162696 | tf_op jit(solution)/shard_map/ppermute | solution.py:521
  118.0 0.7 copy-start.18
  118.0 12.8 %collective-permute-start.21 = (bf16[704,512]{1,0:T(8,128)(2,1)}, bf16[704,512]{1,0:T(8,128)(2,1)S(1)}, u32[]{:S(2)}, u32[]{:S(2)}) collective-permute-start(bf16[704,512]{1,0:T(8,128)(2,1)} %bitcast.17.refs_3_), channel_id=1, source_target_pairs={{8,16},{16,8},{9,17},{17,9},{10,18},{18,10},{11,19},{19,11},{12,20... | collective-permute-start | bytes 2162696 | tf_op jit(solution)/shard_map/ppermute | solution.py:521
  122.7 21.9 %all-to-all-start.1 = ((bf16[8,40,2048]{2,1,0:T(8,128)(2,1)}), bf16[8,40,2048]{2,1,0:T(8,128)(2,1)S(1)}, u32[]{:S(2)}, u32[]{:S(2)}) async-start(bf16[8,40,2048]{2,1,0:T(8,128)(2,1)} %bitcast.52), calls=%async_computation.1 | async-start | bytes 2621440 | tf_op jit(solution)/shard_map/all_to_all | solution.py:543
  126.4 24.6 %collective-permute-start.20 = (bf16[704,512]{1,0:T(8,128)(2,1)}, bf16[704,512]{1,0:T(8,128)(2,1)}, u32[]{:S(2)}, u32[]{:S(2)}) collective-permute-start(bf16[704,512]{1,0:T(8,128)(2,1)} %collective-permute-done.19.refs_4_), channel_id=1, source_target_pairs={{8,16},{16,8},{9,17},{17,9},{10,18},{18,10},{11,19},{19,11},{12,20... | collective-permute-start | bytes 2162696 | tf_op jit(solution)/shard_map/ppermute | solution.py:521
  129.5 26.0 %collective-permute-start.18 = (bf16[704,512]{1,0:T(8,128)(2,1)}, bf16[704,512]{1,0:T(8,128)(2,1)S(1)}, u32[]{:S(2)}, u32[]{:S(2)}) collective-permute-start(bf16[704,512]{1,0:T(8,128)(2,1)} %collective-permute-done.17.refs_8_.refs_20_), channel_id=1, source_target_pairs={{8,0},{16,24},{9,1},{17,25},{10,2},{18,26},{11,3},{19,27},{12,4},{... | collective-permute-start | bytes 2162696 | tf_op jit(solution)/shard_map/ppermute | solution.py:521
  130.8 32.0 %copy-start.15 = (bf16[704,512]{1,0:T(8,128)(2,1)}, bf16[704,512]{1,0:T(8,128)(2,1)S(1)}, u32[]{:S(2)}) copy-start(bf16[704,512]{1,0:T(8,128)(2,1)S(1)} %collective-permute-done.21.refs_5_) | copy-start | bytes 2162692
  130.8 40.2 %collective-permute-start.22 = (bf16[704,512]{1,0:T(8,128)(2,1)S(1)}, bf16[704,512]{1,0:T(8,128)(2,1)}, u32[]{:S(2)}, u32[]{:S(2)}) collective-permute-start(bf16[704,512]{1,0:T(8,128)(2,1)S(1)} %collective-permute-done.21.refs_5_), channel_id=1, source_target_pairs={{8,0},{16,24},{9,1},{17,25},{10,2},{18,26},{11,3},{19,27},{12,4},{... | collective-permute-start | bytes 2162696 | tf_op jit(solution)/shard_map/ppermute | solution.py:521
  144.6 1.1 copy-start.6
  155.5 1.3 copy-start.14
  155.5 27.6 %collective-permute-start.23 = (bf16[704,512]{1,0:T(8,128)(2,1)}, bf16[704,512]{1,0:T(8,128)(2,1)S(1)}, u32[]{:S(2)}, u32[]{:S(2)}) collective-permute-start(bf16[704,512]{1,0:T(8,128)(2,1)} %collective-permute-done.20.refs_10_.refs_6_), channel_id=1, source_target_pairs={{8,0},{16,24},{9,1},{17,25},{10,2},{18,26},{11,3},{19,27},{12,4},{... | collective-permute-start | bytes 2162696 | tf_op jit(solution)/shard_map/ppermute | solution.py:521
  175.9 18.4 %all-to-all-start.2 = ((bf16[8,40,1536]{2,1,0:T(8,128)(2,1)}), bf16[8,40,1536]{2,1,0:T(8,128)(2,1)S(1)}, u32[]{:S(2)}, u32[]{:S(2)}) async-start(bf16[8,40,1536]{2,1,0:T(8,128)(2,1)} %bitcast.53), calls=%async_computation.2 | async-start | bytes 1966080 | tf_op jit(solution)/shard_map/all_to_all | solution.py:543
  183.0 0.9 copy-start.16
  194.3 25.3 %copy-start = (bf16[1,128,2048]{2,1,0:T(8,128)(2,1)S(1)}, bf16[1,128,2048]{2,1,0:T(8,128)(2,1)}, u32[]{:S(2)}) copy-start(bf16[1,128,2048]{2,1,0:T(8,128)(2,1)} %param.22) | copy-start | bytes 1572868
  194.3 25.3 %copy-start.1 = (f32[1,128,2]{2,1,0:T(8,128)S(1)}, f32[1,128,2]{2,1,0:T(8,128)}, u32[]{:S(2)}) copy-start(f32[1,128,2]{2,1,0:T(8,128)} %copy.15) | copy-start | bytes 3076
  194.3 25.3 %copy-start.2 = (bf16[128,2048]{1,0:T(8,128)(2,1)S(1)}, bf16[128,2048]{1,0:T(8,128)(2,1)}, u32[]{:S(2)}) copy-start(bf16[128,2048]{1,0:T(8,128)(2,1)} %get-tuple-element.55.refs_4_) | copy-start | bytes 1572868
  194.3 25.3 %copy-start.3 = (s32[10]{0:T(128)S(1)}, s32[10]{0:T(128)}, u32[]{:S(2)}) copy-start(s32[10]{0:T(128)} %dynamic-slice_bitcast_fusion.refs_0_) | copy-start | bytes 124
  194.3 25.4 %copy-start.4 = (f32[2048]{0:T(1024)S(1)}, f32[2048]{0:T(1024)}, u32[]{:S(2)}) copy-start(f32[2048]{0:T(1024)} %param.16) | copy-start | bytes 24580
  (1 other events, 0.7 us)
